TPU v7x, 32 devices: a whole 2x2x4 slice. The times are simulated.
32 devices in a mesh: space: 8 (over z, x), chan: 4 (over y, core).
Axes of the slice: x: 2, y: 2, z: 4, core: 2. Of those that a mesh axis runs over, the one named last changes fastest.
Arguments:
- features: bfloat16 [256, 8, 1024], P('chan', 'space'), may hold values from -6 to 6
- filters: bfloat16 [27, 256, 256], P(None, 'chan'), may hold values from -0.078125 to 0.078125
- out_bias: float32 [256], P('chan'), may hold values from -1 to 1
- loss_grad: bfloat16 [256, 8, 1024], P('chan', 'space'), may hold values from -6 to 6
Outputs:
- activated: float32 [256, 8, 1024], P('chan', 'space')
- in_grad: float32 [256, 8, 1024], P('chan', 'space')
- filter_grad: float32 [27, 256, 256], P(None, 'chan')
- bias_grad: float32 [256], replicated
All inputs are finite; a program needn't handle non-finite values.
Results may differ from a plain program's by a relative error of at most 0.0031.
Values may be sent and summed in bfloat16 or wider, within the bound.
No kernel may reach another device: no remote copies, remote signals or barrier semaphores. Data moves between devices by JAX's collectives and lax.ppermute only.
A program may use at most 128 MiB of HBM per device.

v0:
```python
import math

import jax
import jax.numpy as jnp
from jax import lax
from jax.sharding import PartitionSpec as P

TAPS = 27
PLANE_H = 32
PLANE_W = 32


def extended(cells, sides, width):
    for axis, dim in sides:
        count = lax.axis_size(axis)
        ends = count - 1
        head = lax.slice_in_dim(cells, 0, width, axis=dim)
        tail = lax.slice_in_dim(cells, cells.shape[dim] - width, cells.shape[dim], axis=dim)
        cells = jnp.concatenate(
            [
                lax.ppermute(tail, axis, [(i, (i + 1) % count) for i in range(ends)]),
                cells,
                lax.ppermute(head, axis, [((i + 1) % count, i) for i in range(ends)]),
            ],
            axis=dim,
        )
    return cells


def plane_pad(volume):
    chans, planes, cells = volume.shape
    grid = volume.reshape(chans, planes, PLANE_H, PLANE_W)
    return jnp.pad(grid, ((0, 0), (0, 0), (1, 1), (1, 1)))


def window(padded, depth_off, row_off, col_off, planes):
    chans = padded.shape[0]
    piece = lax.slice(
        padded,
        (0, depth_off, row_off, col_off),
        (chans, depth_off + planes, row_off + PLANE_H, col_off + PLANE_W),
    )
    return piece.reshape(chans, planes * PLANE_H * PLANE_W)


def contract_lead(left, right):
    return lax.dot_general(
        left, right, (((0,), (0,)), ((), ())), preferred_element_type=jnp.float32
    )


def contract_last(left, right):
    return lax.dot_general(
        left, right, (((1,), (1,)), ((), ())), preferred_element_type=jnp.float32
    )


def depth_rim(volume):
    return extended(volume, (("space", 1),), 1)


def all_channels(volume):
    return lax.all_gather(volume, "chan", axis=0, tiled=True)


def full_view(volume):
    return depth_rim(all_channels(volume))


def body(features, filters, out_bias, loss_grad):
    local_in, planes, cells = features.shape
    local_out = out_bias.shape[0]
    total_out = filters.shape[2]
    voxels = planes * cells
    offsets = [(tap // 9, tap // 3 % 3, tap % 3) for tap in range(TAPS)]
    padded_all = plane_pad(full_view(features))
    columns = lax.all_to_all(filters, "chan", split_axis=2, concat_axis=1, tiled=True)
    summed = jnp.zeros((local_out, voxels), jnp.float32)
    for tap_index, (depth_off, row_off, col_off) in enumerate(offsets):
        piece = window(padded_all, depth_off, row_off, col_off, planes)
        summed = summed + contract_lead(columns[tap_index], piece)
    padded_own = lax.dynamic_slice_in_dim(
        padded_all, lax.axis_index("chan") * local_in, local_in, 0
    )
    pre_act = summed + out_bias[:, None]
    sigmoid = jax.nn.sigmoid(pre_act)
    activated = (pre_act * sigmoid).reshape(local_out, planes, cells)
    grad_pre = (
        loss_grad.reshape(local_out, voxels).astype(jnp.float32)
        * sigmoid
        * (1.0 + pre_act * (1.0 - sigmoid))
    ).astype(jnp.bfloat16)
    grad_full = full_view(grad_pre.reshape(local_out, planes, cells))
    padded_grad = plane_pad(grad_full)
    grad_inner = lax.slice_in_dim(grad_full, 1, 1 + planes, axis=1).reshape(total_out, voxels)
    in_total = jnp.zeros((local_in, voxels), jnp.float32)
    filter_list = []
    for tap_index, (depth_off, row_off, col_off) in enumerate(offsets):
        shifted = window(padded_grad, 2 - depth_off, 2 - row_off, 2 - col_off, planes)
        in_total = in_total + jnp.dot(
            filters[tap_index], shifted, preferred_element_type=jnp.float32
        )
        piece = window(padded_own, depth_off, row_off, col_off, planes)
        filter_list.append(contract_last(piece, grad_inner))
    factor = 1.0 / math.sqrt(voxels * lax.axis_size("space"))
    filter_part = jnp.stack(filter_list, axis=0) * factor
    bias_part = jnp.sum(grad_inner.astype(jnp.float32), axis=1) * factor
    filter_grad, bias_grad = lax.psum((filter_part, bias_part), "space")
    in_grad = in_total.reshape(local_in, planes, cells)
    return (activated, in_grad, filter_grad, bias_grad)


def solution(mesh):
    in_specs = (
        P("chan", "space", None),
        P(None, "chan", None),
        P("chan"),
        P("chan", "space", None),
    )
    out_specs = (P("chan", "space", None), P("chan", "space", None), P(None, "chan", None), P())
    return jax.shard_map(body, mesh=mesh, in_specs=in_specs, out_specs=out_specs, check_vma=False)
```

profile of v0, /device:TPU:0, one launch (start us, length us, event | category | flops | bytes accessed | tf_op | source)
XLA Modules:
  0.0 211.8 jit_solution(13178048618152019697)
XLA Ops:
  7.2 9.0 %all_gather.6 = bf16[256,1,1024]{2,0,1:T(8,128)(2,1)S(1)} all-gather(bf16[64,1,1024]{2,0,1:T(8,128)(2,1)} %param.4), channel_id=1, replica_groups=mesh['space'=8,'chan'=4] {'chan'}, dimensions={0}, use_global_device_ids=true | all-gather | bytes 655360 | tf_op jit(solution)/shard_map/all_gather | solution.py:63
  16.4 1.3 collective-permute-start.1
  17.7 5.3 %collective-permute-start = (bf16[256,1,1024]{0,2,1:T(8,128)(2,1)S(1)}, bf16[256,1,1024]{0,2,1:T(8,128)(2,1)}, u32[]{:S(2)}, u32[]{:S(2)}) collective-permute-start(bf16[256,1,1024]{0,2,1:T(8,128)(2,1)S(1)} %copy.15), channel_id=1, source_target_pairs={{0,4},{4,8},{8,12},{12,16},{16,20},{20,24},{24,28},{1,5},{5,9},{9,... | collective-permute-start | bytes 1572872 | tf_op jit(solution)/shard_map/ppermute | solution.py:21
  23.0 3.0 %copy.18 = bf16[27,64,256]{1,0,2:T(8,128)(2,1)S(1)} copy(bf16[27,64,256]{2,1,0:T(8,128)(2,1)S(1)} %copy-done) | data formatting | bytes 1769472 | tf_op args[1]
  26.1 2.4 %reshape.417 = bf16[4,2,55296]{2,1,0:T(2,128)(2,1)} reshape(bf16[256,27,64]{2,1,0:T(8,128)(2,1)S(1)} %bitcast.575) | data formatting | bytes 1769472
  28.5 3.5 %all-to-all-start = ((bf16[4,2,55296]{2,1,0:T(2,128)(2,1)}), bf16[4,2,55296]{2,1,0:T(2,128)(2,1)S(1)}, u32[]{:S(2)}, u32[]{:S(2)}) async-start(bf16[4,2,55296]{2,1,0:T(2,128)(2,1)} %reshape.417), calls=%async_computation | async-start | bytes 1769472 | tf_op jit(solution)/shard_map/all_to_all | solution.py:77
  32.6 11.0 %collective-permute-done = bf16[256,1,1024]{0,2,1:T(8,128)(2,1)} collective-permute-done((bf16[256,1,1024]{0,2,1:T(8,128)(2,1)S(1)}, bf16[256,1,1024]{0,2,1:T(8,128)(2,1)}, u32[]{:S(2)}, u32[]{:S(2)}) %collective-permute-start) | collective-permute-done | bytes 524320 | tf_op jit(solution)/shard_map/ppermute | solution.py:21
  43.6 1.4 pad_maximum_fusion
  45.0 3.4 %pad_dynamic-slice_fusion.15 = (bf16[64,1,32,32]{0,3,2,1:T(8,128)(2,1)}, bf16[64,1,32,32]{0,3,2,1:T(8,128)(2,1)}, bf16[64,1,32,32]{0,3,2,1:T(8,128)(2,1)}, bf16[...) fusion(s32[]{:T(128)S(6)} %select_n.3, ...), kind=kLoop, calls=%fused_computation.15 | loop fusion | bytes 3014668 | tf_op jit(solution)/shard_map/slice | solution.py:38
  48.3 4.7 %pad_dynamic-slice_fusion.26 = (bf16[64,1,32,32]{0,3,2,1:T(8,128)(2,1)}, bf16[64,1,32,32]{0,3,2,1:T(8,128)(2,1)}, bf16[64,1,32,32]{0,3,2,1:T(8,128)(2,1)}, bf16[...) fusion(s32[]{:T(128)S(6)} %select_n.3, ...), kind=kLoop, calls=%fused_computation.26 | loop fusion | bytes 3670028 | tf_op jit(solution)/shard_map/slice | solution.py:38
  53.0 2.1 pad_slice_fusion.1
  55.1 4.8 %pad_slice_fusion = (bf16[256,1,32,32]{0,3,2,1:T(8,128)(2,1)}, bf16[256,1,32,32]{0,3,2,1:T(8,128)(2,1)}, bf16[256,1,32,32]{0,3,2,1:T(8,128)(2,1)}, bf16[256,1,32...) fusion(bf16[256,3,32,32]{0,3,2,1:T(8,128)(2,1)S(1)} %bitcast.571), kind=kLoop, calls=%fused_computation.27 | loop fusion | bytes 11534336 | tf_op jit(solution)/shard_map/slice | solution.py:38
  59.9 1.9 reshape.418
  61.8 1.4 copy.24
  64.0 0.7 squeeze.163
  64.8 0.7 squeeze.162
  65.5 0.7 squeeze.164
  66.2 0.7 squeeze.165
  66.9 0.7 squeeze.166
  70.2 1.0 fusion.110
  71.2 1.1 convolution_add_fusion.31
  81.2 7.1 %all-gather = bf16[256,1024]{1,0:T(8,128)(2,1)S(1)} all-gather(bf16[64,1024]{1,0:T(8,128)(2,1)S(1)} %get-tuple-element.124), channel_id=2, replica_groups=mesh['space'=8,'chan'=4] {'chan'}, dimensions={0}, use_global_device_ids=true | all-gather | bytes 655360 | tf_op jit(solution)/shard_map/all_gather | solution.py:63
  88.3 1.3 collective-permute-start.3
  89.6 5.4 %collective-permute-start.2 = (bf16[256,1,1024]{2,0,1:T(8,128)(2,1)S(1)}, bf16[256,1,1024]{2,0,1:T(8,128)(2,1)S(1)}, u32[]{:S(2)}, u32[]{:S(2)}) collective-permute-start(bf16[256,1,1024]{2,0,1:T(8,128)(2,1)S(1)} %bitcast.566), channel_id=1, source_target_pairs={{0,4},{4,8},{8,12},{12,16},{16,20},{20,24},{24,28},{1,5},{5,9},{9,... | collective-permute-start | bytes 1572872 | tf_op jit(solution)/shard_map/ppermute | solution.py:21
  95.0 1.0 copy.21
  104.4 1.4 broadcast_multiply_fusion
  106.0 28.3 %psum.15 = f32[256]{0:T(256)} all-reduce(f32[256]{0:T(256)S(1)} %broadcast_multiply_fusion.1), channel_id=1, replica_groups=mesh['space'=8,'chan'=4] {'space'}, use_global_device_ids=true, to_apply=%region_2.3 | all-reduce | flops 256 | bytes 2048 | tf_op jit(solution)/shard_map/psum | solution.py:108
  135.2 0.9 pad_slice_fusion.25
  136.1 3.7 %pad_slice_fusion.24 = (bf16[256,1,32,32]{0,3,2,1:T(8,128)(2,1)S(1)}, bf16[256,1,32,32]{0,3,2,1:T(8,128)(2,1)S(1)}, bf16[256,1,32,32]{0,3,2,1:T(8,128)(2,1)S(1)}...) fusion(bf16[256,3,32,32]{0,3,2,1:T(8,128)(2,1)S(1)} %bitcast.573), kind=kLoop, calls=%fused_computation.51 | loop fusion | bytes 11534336 | tf_op jit(solution)/shard_map/slice | solution.py:38
  147.5 1.0 copy.22
  148.5 53.6 %all-reduce.4.cloned.1.call-done = f32[27,64,256]{2,1,0:T(8,128)} async-done(((f32[27,64,256]{2,1,0:T(8,128)}), f32[27,64,256]{2,1,0:T(8,128)}) %all-reduce.4.cloned.1.call-update) | async-done | bytes 1769488 | tf_op jit(solution)/shard_map/psum | solution.py:108
  202.1 2.9 %copy.52 = f32[27,64,256]{2,1,0:T(8,128)} copy(f32[27,64,256]{2,1,0:T(8,128)} %all-reduce.4.cloned.1.call-done) | data formatting | bytes 3538944
  (234 shorter events, 29.6 us)
Async XLA Ops:
  7.2 15.9 %copy-start = (bf16[27,64,256]{2,1,0:T(8,128)(2,1)S(1)}, bf16[27,64,256]{2,1,0:T(8,128)(2,1)}, u32[]{:S(2)}) copy-start(bf16[27,64,256]{2,1,0:T(8,128)(2,1)} %param.5) | copy-start | bytes 2654212
  16.4 16.2 %collective-permute-start.1 = (bf16[256,1,1024]{0,2,1:T(8,128)(2,1)S(1)}, bf16[256,1,1024]{0,2,1:T(8,128)(2,1)}, u32[]{:S(2)}, u32[]{:S(2)}) collective-permute-start(bf16[256,1,1024]{0,2,1:T(8,128)(2,1)S(1)} %copy.15), channel_id=1, source_target_pairs={{4,0},{8,4},{12,8},{16,12},{20,16},{24,20},{28,24},{5,1},{9,5},{13... | collective-permute-start | bytes 1572872 | tf_op jit(solution)/shard_map/ppermute | solution.py:23
  17.7 25.9 %collective-permute-start = (bf16[256,1,1024]{0,2,1:T(8,128)(2,1)S(1)}, bf16[256,1,1024]{0,2,1:T(8,128)(2,1)}, u32[]{:S(2)}, u32[]{:S(2)}) collective-permute-start(bf16[256,1,1024]{0,2,1:T(8,128)(2,1)S(1)} %copy.15), channel_id=1, source_target_pairs={{0,4},{4,8},{8,12},{12,16},{16,20},{20,24},{24,28},{1,5},{5,9},{9,... | collective-permute-start | bytes 1572872 | tf_op jit(solution)/shard_map/ppermute | solution.py:21
  28.5 31.5 %all-to-all-start = ((bf16[4,2,55296]{2,1,0:T(2,128)(2,1)}), bf16[4,2,55296]{2,1,0:T(2,128)(2,1)S(1)}, u32[]{:S(2)}, u32[]{:S(2)}) async-start(bf16[4,2,55296]{2,1,0:T(2,128)(2,1)} %reshape.417), calls=%async_computation | async-start | bytes 1769472 | tf_op jit(solution)/shard_map/all_to_all | solution.py:77
  32.0 170.1 %all-reduce.4.cloned.1.call-start = ((), (), s32[]{:S(2)}) async-start(), calls=%async_computation.1 | async-start | bytes 3538944 | tf_op jit(solution)/shard_map/psum | solution.py:108
  64.0 6.1 %copy-start.26 = (bf16[256,1,32,32]{0,3,2,1:T(8,128)(2,1)S(1)}, bf16[256,1,32,32]{0,3,2,1:T(8,128)(2,1)}, u32[]{:S(2)}) copy-start(bf16[256,1,32,32]{0,3,2,1:T(8,128)(2,1)} %get-tuple-element.98) | copy-start | bytes 1572868
  64.0 7.2 %copy-start.8 = (bf16[256,1,32,32]{0,3,2,1:T(8,128)(2,1)S(1)}, bf16[256,1,32,32]{0,3,2,1:T(8,128)(2,1)}, u32[]{:S(2)}) copy-start(bf16[256,1,32,32]{0,3,2,1:T(8,128)(2,1)} %get-tuple-element.123) | copy-start | bytes 1572868
  68.3 4.0 %copy-start.25 = (bf16[256,1,32,32]{0,3,2,1:T(8,128)(2,1)S(1)}, bf16[256,1,32,32]{0,3,2,1:T(8,128)(2,1)}, u32[]{:S(2)}) copy-start(bf16[256,1,32,32]{0,3,2,1:T(8,128)(2,1)} %get-tuple-element.99) | copy-start | bytes 1572868
  69.6 3.1 %copy-start.24 = (bf16[256,1,32,32]{0,3,2,1:T(8,128)(2,1)S(1)}, bf16[256,1,32,32]{0,3,2,1:T(8,128)(2,1)}, u32[]{:S(2)}) copy-start(bf16[256,1,32,32]{0,3,2,1:T(8,128)(2,1)} %get-tuple-element.100) | copy-start | bytes 1572868
  69.7 3.0 %copy-start.56 = (bf16[256,64]{0,1:T(8,128)(2,1)S(1)}, bf16[256,64]{0,1:T(8,128)(2,1)}, u32[]{:S(2)}) copy-start(bf16[256,64]{0,1:T(8,128)(2,1)} %squeeze.165) | copy-start | bytes 98308
  69.8 2.5 %copy-start.57 = (bf16[256,64]{0,1:T(8,128)(2,1)S(1)}, bf16[256,64]{0,1:T(8,128)(2,1)}, u32[]{:S(2)}) copy-start(bf16[256,64]{0,1:T(8,128)(2,1)} %squeeze.164) | copy-start | bytes 98308
  71.2 1.8 copy-start.7
  71.2 1.8 copy-start.55
  80.7 15.2 %copy-start.53 = (bf16[64,1,32,32]{0,3,2,1:T(8,128)(2,1)S(1)}, bf16[64,1,32,32]{0,3,2,1:T(8,128)(2,1)}, u32[]{:S(2)}) copy-start(bf16[64,1,32,32]{0,3,2,1:T(8,128)(2,1)} %get-tuple-element.69) | copy-start | bytes 393220
  80.8 15.4 %copy-start.52 = (bf16[64,1,32,32]{0,3,2,1:T(8,128)(2,1)S(1)}, bf16[64,1,32,32]{0,3,2,1:T(8,128)(2,1)}, u32[]{:S(2)}) copy-start(bf16[64,1,32,32]{0,3,2,1:T(8,128)(2,1)} %get-tuple-element.68) | copy-start | bytes 393220
  81.2 15.4 %copy-start.51 = (bf16[64,1,32,32]{0,3,2,1:T(8,128)(2,1)S(1)}, bf16[64,1,32,32]{0,3,2,1:T(8,128)(2,1)}, u32[]{:S(2)}) copy-start(bf16[64,1,32,32]{0,3,2,1:T(8,128)(2,1)} %get-tuple-element.67) | copy-start | bytes 393220
  81.2 15.7 %copy-start.50 = (bf16[64,1,32,32]{0,3,2,1:T(8,128)(2,1)S(1)}, bf16[64,1,32,32]{0,3,2,1:T(8,128)(2,1)}, u32[]{:S(2)}) copy-start(bf16[64,1,32,32]{0,3,2,1:T(8,128)(2,1)} %get-tuple-element.66) | copy-start | bytes 393220
  88.3 46.0 %collective-permute-start.3 = (bf16[256,1,1024]{2,0,1:T(8,128)(2,1)S(1)}, bf16[256,1,1024]{2,0,1:T(8,128)(2,1)S(1)}, u32[]{:S(2)}, u32[]{:S(2)}) collective-permute-start(bf16[256,1,1024]{2,0,1:T(8,128)(2,1)S(1)} %bitcast.565), channel_id=1, source_target_pairs={{4,0},{8,4},{12,8},{16,12},{20,16},{24,20},{28,24},{5,1},{9,5},{13... | collective-permute-start | bytes 1572872 | tf_op jit(solution)/shard_map/ppermute | solution.py:23
  89.6 44.7 %collective-permute-start.2 = (bf16[256,1,1024]{2,0,1:T(8,128)(2,1)S(1)}, bf16[256,1,1024]{2,0,1:T(8,128)(2,1)S(1)}, u32[]{:S(2)}, u32[]{:S(2)}) collective-permute-start(bf16[256,1,1024]{2,0,1:T(8,128)(2,1)S(1)} %bitcast.566), channel_id=1, source_target_pairs={{0,4},{4,8},{8,12},{12,16},{16,20},{20,24},{24,28},{1,5},{5,9},{9,... | collective-permute-start | bytes 1572872 | tf_op jit(solution)/shard_map/ppermute | solution.py:21
  96.2 1.3 copy-start.48
  96.5 1.3 copy-start.47
  96.9 1.3 copy-start.46
  97.2 1.3 copy-start.45
  97.5 1.3 copy-start.44
  97.8 1.3 copy-start.43
  98.1 1.3 copy-start.42
  98.5 1.3 copy-start.41
  99.4 1.3 copy-start.38
  99.7 1.3 copy-start.37
  100.4 1.3 copy-start.35
  100.7 1.3 copy-start.34
  136.1 3.7 %copy-start.1 = (bf16[27,64,256]{2,1,0:T(8,128)(2,1)S(1)}, bf16[27,64,256]{2,1,0:T(8,128)(2,1)}, u32[]{:S(2)}) copy-start(bf16[27,64,256]{2,1,0:T(8,128)(2,1)} %param.5) | copy-start | bytes 2654212
  (34 other events, 40.0 us)
Sparse Core Ops, SparseCore 0:
  106.0 96.0 all-reduce.3
where the time goes:
time: 212 us
  waiting for transfers between devices  65.1 us (31%)
  blocking collectives  44.4 us (21%)
  local copies, waits for them, and re-layouts  42.4 us (20%)
  matrix products  25 us (12%)
  starting transfers between devices  16.8 us (8%)
  between operations  14.9 us (7%)
  other arithmetic  3.07 us (1%)
    psum x1, waiting for transfers between devices, body(): filter_grad, bias_grad = lax.psum((filter_part, bias_part), 'space')  53.6 us
    psum x1, blocking collectives, body(): filter_grad, bias_grad = lax.psum((filter_part, bias_part), 'space')  28.3 us
    slice x6, local copies, waits for them, and re-layouts, window(): lax.slice(padded, (0, depth_off, row_off, col_off), (chans, depth_off + p...  19.5 us
    all_gather x2, blocking collectives, all_channels(): return lax.all_gather(volume, 'chan', axis=0, tiled=True)  16.1 us
    unnamed x126, local copies, waits for them, and re-layouts  13.7 us
    ppermute x2, waiting for transfers between devices, extended(): lax.ppermute(tail, axis, [(i, (i + 1) % count) for i in range(ends)])  11 us
    ppermute x2, starting transfers between devices, extended(): lax.ppermute(tail, axis, [(i, (i + 1) % count) for i in range(ends)])  10.7 us
    dot_general x27, matrix products, contract_lead(): lax.dot_general(left, right, (((0,), (0,)), ((), ())), preferred_element_...  9.24 us
  transfers between devices with their start and end apart: 6, of which 3 were waited for; matrix products, arithmetic and copies ran while one was open for 22% of the time, Pallas kernels for 0%

commit v1 on v0

v1 whole, which is shorter than its diff:
```python
import functools
import math

import jax
import jax.numpy as jnp
from jax import lax
from jax.experimental import pallas as pl
from jax.experimental.pallas import tpu as pltpu
from jax.sharding import PartitionSpec as P

TAPS = 27
PLANE_H = 32
PLANE_W = 32
CELLS = PLANE_H * PLANE_W
VMEM = pl.BlockSpec(memory_space=pltpu.VMEM)
SMEM = pl.BlockSpec(memory_space=pltpu.SMEM)
BF16 = jnp.bfloat16
F32 = jnp.float32


def cell_mask(row_off, col_off):
    cell = lax.broadcasted_iota(jnp.int32, (1, CELLS), 1)
    row = cell // PLANE_W + row_off
    col = cell % PLANE_W + col_off
    inside = (row >= 0) & (row < PLANE_H) & (col >= 0) & (col < PLANE_W)
    return jnp.where(inside, 1.0, 0.0).astype(BF16)


def moved(plane, row_off, col_off):
    if row_off == 0 and col_off == 0:
        return plane
    amount = (-(row_off * PLANE_W + col_off)) % CELLS
    return pltpu.roll(plane, amount, 1) * cell_mask(row_off, col_off)


def forward_kernel(chans, parts, index, own, below, above, weights, *rest):
    outs, (stack, total) = rest[:parts], rest[parts:]
    for a, plane in enumerate((below, own, above)):
        cells = plane[...]
        for b in range(3):
            for e in range(3):
                tap = 9 * a + 3 * b + e
                stack[tap * chans : (tap + 1) * chans, :] = moved(cells, b - 1, e - 1)
    total[...] = jnp.dot(weights[...], stack[...], preferred_element_type=F32)
    for r in range(parts):
        start = pl.multiple_of((index[0] ^ r) * chans, chans)
        outs[r][...] = total[pl.ds(start, chans), :]


def forward_parts(index, own, below, above, weights, parts):
    chans = own.shape[0]
    outs = weights.shape[0]
    return pl.pallas_call(
        functools.partial(forward_kernel, chans, parts),
        out_shape=[jax.ShapeDtypeStruct((chans, CELLS), F32)] * parts,
        in_specs=[SMEM] + [VMEM] * 4,
        out_specs=[VMEM] * parts,
        scratch_shapes=[
            pltpu.VMEM((TAPS * chans, CELLS), BF16),
            pltpu.VMEM((outs, CELLS), F32),
        ],
        compiler_params=pltpu.CompilerParams(vmem_limit_bytes=40 << 20),
        cost_estimate=pl.CostEstimate(
            flops=2 * outs * TAPS * chans * CELLS, bytes_accessed=6 << 20, transcendentals=0
        ),
        name="forward_parts",
    )(index, own, below, above, weights)


def input_kernel(chans, index, mine, theirs, weights, below, own, above, stack, left):
    half = mine.shape[0]
    outs = weights.shape[2]
    for part, first in ((mine, 0), (theirs, half)):
        for u in range(half):
            start = pl.multiple_of((index[0] ^ index[1 + first + u]) * chans, chans)
            cells = part[u]
            for b in range(3):
                for e in range(3):
                    stack[3 * b + e, pl.ds(start, chans), :] = moved(cells, 1 - b, 1 - e)
    for a in range(3):
        for k in range(9):
            left[a * chans : (a + 1) * chans, k * outs : (k + 1) * outs] = weights[9 * a + k]
    total = jnp.dot(
        left[...], stack[...].reshape(9 * outs, CELLS), preferred_element_type=F32
    )
    below[...] = total[:chans].astype(BF16)
    own[...] = total[chans : 2 * chans]
    above[...] = total[2 * chans :].astype(BF16)


def input_parts(index, mine, theirs, weights):
    chans = weights.shape[1]
    outs = weights.shape[2]
    sides = jax.ShapeDtypeStruct((chans, CELLS), BF16)
    return pl.pallas_call(
        functools.partial(input_kernel, chans),
        out_shape=[sides, jax.ShapeDtypeStruct((chans, CELLS), F32), sides],
        in_specs=[SMEM] + [VMEM] * 3,
        out_specs=[VMEM] * 3,
        scratch_shapes=[
            pltpu.VMEM((9, outs, CELLS), BF16),
            pltpu.VMEM((3 * chans, 9 * outs), BF16),
        ],
        compiler_params=pltpu.CompilerParams(vmem_limit_bytes=40 << 20),
        cost_estimate=pl.CostEstimate(
            flops=2 * 3 * chans * 9 * outs * CELLS, bytes_accessed=6 << 20, transcendentals=0
        ),
        name="input_parts",
    )(index, mine, theirs, weights)


def filter_kernel(
    factor, flags, index, near, far, mine, theirs, out, shifted, rows, total, sums
):
    planes, chans = near.shape[0] * 2, near.shape[1]
    groups, _, share, _ = mine.shape
    width = 2 * groups * share
    space, chan = index[0], index[1]
    edge = jnp.zeros((3 * chans, CELLS), BF16)
    shifted[0] = edge
    shifted[planes + 1] = edge

    def fill(part, first):
        def step(q, _):
            depth = space ^ index[2 + first + q]
            cells = part[q]
            for e in range(3):
                shifted[depth + 1, e * chans : (e + 1) * chans, :] = moved(cells, 0, e - 1)
            return 0

        lax.fori_loop(0, part.shape[0], step, 0)

    fill(near, 0)
    fill(far, planes // 2)
    total[...] = jnp.zeros_like(total)
    sums[...] = jnp.zeros_like(sums)
    ones = jnp.ones((16, CELLS), BF16)

    def step(q, _):
        depth = space ^ index[2 + planes + q]
        for part, first in ((mine, 0), (theirs, groups)):
            for u in range(groups):
                group = chan ^ index[2 + 2 * planes + first + u]
                cells = part[u, q]
                for b in range(3):
                    start = pl.multiple_of(b * width + group * share, share)
                    rows[pl.ds(start, share), :] = moved(cells, 1 - b, 0)
        left = shifted[pl.ds(depth, 3)].reshape(9 * chans, CELLS)
        contract = (((1,), (1,)), ((), ()))
        total[...] += lax.dot_general(left, rows[...], contract, preferred_element_type=F32)
        sums[...] += lax.dot_general(
            ones, rows[width : 2 * width, :], contract, preferred_element_type=F32
        )
        return 0

    lax.fori_loop(0, planes, step, 0)
    for a in range(3):
        for e in range(3):
            for b in range(3):
                tap = 9 * a + 3 * b + e
                first = (3 * a + e) * chans
                out[tap * chans : (tap + 1) * chans, :] = (
                    total[first : first + chans, b * width : (b + 1) * width] * factor
                ).astype(BF16)
    bias = sums[...] * factor
    high = bias.astype(BF16)
    low = (bias - high.astype(F32)).astype(BF16)
    out[TAPS * chans : TAPS * chans + 16, :] = high
    out[TAPS * chans + 16 :, :] = low


def filter_half(index, near, far, mine, theirs, factor):
    half, chans, _ = near.shape
    groups, _, share, _ = mine.shape
    width = 2 * groups * share
    return pl.pallas_call(
        functools.partial(filter_kernel, factor, None),
        out_shape=jax.ShapeDtypeStruct((TAPS * chans + 32, width), BF16),
        in_specs=[SMEM] + [VMEM] * 4,
        out_specs=VMEM,
        scratch_shapes=[
            pltpu.VMEM((2 * half + 2, 3 * chans, CELLS), BF16),
            pltpu.VMEM((3 * width, CELLS), BF16),
            pltpu.VMEM((9 * chans, 3 * width), F32),
            pltpu.VMEM((16, width), F32),
        ],
        compiler_params=pltpu.CompilerParams(vmem_limit_bytes=52 << 20),
        cost_estimate=pl.CostEstimate(
            flops=2 * TAPS * chans * width * 2 * half * CELLS,
            bytes_accessed=8 << 20,
            transcendentals=0,
        ),
        name="filter_half",
    )(index, near, far, mine, theirs)


def spread(index, share, lanes, total):
    lane = lax.broadcasted_iota(jnp.int32, (lanes, total), 0)
    column = lax.broadcasted_iota(jnp.int32, (lanes, total), 1)
    home = (lane // share) * (2 * share) + index * share + lane % share
    return jnp.where(column == home, 1.0, 0.0).astype(BF16)


def join_kernel(share, index, mine, theirs, out, bias):
    lanes, total = mine.shape[1], out.shape[1]
    rows = out.shape[0]
    keep = spread(index[0], share, lanes, total)
    other = spread(1 - index[0], share, lanes, total)
    whole = jnp.dot(mine[...], keep, preferred_element_type=F32) + jnp.dot(
        theirs[...], other, preferred_element_type=F32
    )
    out[...] = whole[:rows]
    bias[...] = whole[rows : rows + 1] + whole[rows + 16 : rows + 17]


def join_halves(index, mine, theirs, share):
    rows = mine.shape[0] - 32
    total = 2 * mine.shape[1]
    return pl.pallas_call(
        functools.partial(join_kernel, share),
        out_shape=[
            jax.ShapeDtypeStruct((rows, total), F32),
            jax.ShapeDtypeStruct((1, total), F32),
        ],
        in_specs=[SMEM, VMEM, VMEM],
        out_specs=[VMEM, VMEM],
        compiler_params=pltpu.CompilerParams(vmem_limit_bytes=40 << 20),
        cost_estimate=pl.CostEstimate(
            flops=2 * rows * total * total, bytes_accessed=6 << 20, transcendentals=0
        ),
        name="join_halves",
    )(index, mine, theirs)


def swapped(value, axis, mask):
    count = lax.axis_size(axis)
    return lax.ppermute(value, axis, [(i, i ^ mask) for i in range(count)])


def doubled(value, axis, masks):
    flips = [0]
    for mask in masks[:-1]:
        value = jnp.concatenate([value, swapped(value, axis, mask)], axis=0)
        flips = flips + [f ^ mask for f in flips]
    flips = flips + [f ^ masks[-1] for f in flips]
    return value, swapped(value, axis, masks[-1]), flips


def body(features, filters, out_bias, loss_grad):
    chans, planes, cells = features.shape
    total_out = filters.shape[2]
    depth = lax.axis_size("space")
    groups = lax.axis_size("chan")
    space = lax.axis_index("space")
    chan = lax.axis_index("chan")
    share = chans // 2
    high_first = [1 << k for k in range(depth.bit_length() - 2, -1, -1)]
    chan_masks = [1 << k for k in range(groups.bit_length() - 2, -1, -1)]
    factor = 1.0 / math.sqrt(cells * planes * depth)

    own = features.reshape(chans, cells)
    up = [(i, i + 1) for i in range(depth - 1)]
    down = [(i + 1, i) for i in range(depth - 1)]
    below = lax.ppermute(own, "space", up)
    above = lax.ppermute(own, "space", down)
    weights = filters.reshape(TAPS * chans, total_out)
    parts = forward_parts(chan.reshape(1), own, below, above, weights.T, groups)
    pre_act = parts[0] + out_bias[:, None]
    for r in range(1, groups):
        pre_act = pre_act + swapped(parts[r], "chan", r)

    near, far, space_flips = doubled(own[None], "space", high_first)

    sigmoid = jax.nn.sigmoid(pre_act)
    activated = pre_act * sigmoid
    grad_pre = (
        loss_grad.reshape(chans, cells).astype(F32)
        * sigmoid
        * (1.0 + pre_act * (1.0 - sigmoid))
    ).astype(BF16)

    side = space & 1
    first, second = grad_pre[:share], grad_pre[share:]
    keep = jnp.where(side == 0, first, second)
    give = jnp.where(side == 0, second, first)
    pair = jnp.stack([keep, swapped(give, "space", 1)], axis=0)
    half, rest, grad_flips = doubled(pair, "space", high_first[:-1])
    grad_flips = [f ^ g for f in grad_flips[: depth // 2] for g in (0, 1)]
    gathered = jnp.concatenate([half, rest], axis=0)
    mine, theirs, chan_flips = doubled(gathered[None], "chan", chan_masks)

    grad_mine, grad_theirs, _ = doubled(grad_pre[None], "chan", chan_masks)
    to_below, in_own, to_above = input_parts(
        jnp.concatenate([chan.reshape(1), jnp.array(chan_flips, jnp.int32)]),
        grad_mine,
        grad_theirs,
        filters,
    )
    in_grad = (
        in_own
        + lax.ppermute(to_below, "space", down).astype(F32)
        + lax.ppermute(to_above, "space", up).astype(F32)
    )

    index = jnp.concatenate(
        [
            space.reshape(1),
            chan.reshape(1),
            jnp.array(space_flips + grad_flips + chan_flips, jnp.int32),
        ]
    )
    block = filter_half(index, near, far, mine, theirs, factor)
    joined, bias = join_halves(side.reshape(1), block, swapped(block, "space", 1), share)
    return (
        activated.reshape(chans, planes, cells),
        in_grad.reshape(chans, planes, cells),
        joined.reshape(TAPS, chans, total_out),
        bias.reshape(total_out),
    )


def solution(mesh):
    in_specs = (
        P("chan", "space", None),
        P(None, "chan", None),
        P("chan"),
        P("chan", "space", None),
    )
    out_specs = (P("chan", "space", None), P("chan", "space", None), P(None, "chan", None), P())
    return jax.shard_map(body, mesh=mesh, in_specs=in_specs, out_specs=out_specs, check_vma=False)
```

time: 212 us -> 112 us (0.53)
  blocking collectives: 44.4 us -> 0 us
  local copies, waits for them, and re-layouts: 42.4 us -> 4.42 us
  matrix products: 25 us -> 0 us
  Pallas kernels: 0 us -> 17.3 us
  starting transfers between devices: 16.8 us -> 31 us
  between operations: 14.9 us -> 0.85 us
  waiting for transfers between devices: 65.1 us -> 57.5 us
  other arithmetic: 3.07 us -> 0.8 us
    psum x1 -> x0, waiting for transfers between devices: 53.6 us -> none  [body(): filter_grad, bias_grad = lax.psum((filter_part, bias_part), 'space')]
    ppermute x4 -> x18, waiting for transfers between devices: 11.6 us -> 57.5 us  [the longest x14 53.3 us: swapped(): return lax.ppermute(value, axis, [(i, i ^ mask) for i in range(count)])]
    psum x1 -> x0, blocking collectives: 28.3 us -> none  [body(): filter_grad, bias_grad = lax.psum((filter_part, bias_part), 'space')]
    dot_general x81 -> x0, matrix products: 25 us -> none  [the longest x27 9.24 us: contract_lead(): lax.dot_general(left, right, (((0,), (0,)), ((), ())), preferred_element_...]
    slice x8 -> x0, local copies, waits for them, and re-layouts: 20.3 us -> none  [the longest x6 19.5 us: window(): lax.slice(padded, (0, depth_off, row_off, col_off), (chans, depth_off + p...]
    ppermute x4 -> x18, starting transfers between devices: 13.3 us -> 31 us  [the longest x14 18.9 us: swapped(): return lax.ppermute(value, axis, [(i, i ^ mask) for i in range(count)])]
    pallas_call x0 -> x4, Pallas kernels: none -> 17.3 us  [the longest x1 11.2 us: filter_half(): pl.pallas_call(functools.partial(filter_kernel, factor, None), out_shape=...]
    all_gather x2 -> x0, blocking collectives: 16.1 us -> none  [all_channels(): return lax.all_gather(volume, 'chan', axis=0, tiled=True)]
  transfers between devices with their start and end apart: 6 -> 18, of which waited for: 3 -> 12; matrix products, arithmetic and copies ran while one was open for 22% -> 3% of each run, Pallas kernels for 0% -> 13%
where the time goes in v1:
time: 112 us
  waiting for transfers between devices  57.5 us (51%)
  starting transfers between devices  31 us (28%)
  Pallas kernels  17.3 us (15%)
  local copies, waits for them, and re-layouts  4.42 us (4%)
    ppermute x14, waiting for transfers between devices, swapped(): return lax.ppermute(value, axis, [(i, i ^ mask) for i in range(count)])  53.3 us
    ppermute x14, starting transfers between devices, swapped(): return lax.ppermute(value, axis, [(i, i ^ mask) for i in range(count)])  18.9 us
    pallas_call x1, Pallas kernels, filter_half(): pl.pallas_call(functools.partial(filter_kernel, factor, None), out_shape=...  11.2 us
    ppermute x1, starting transfers between devices, body(): below = lax.ppermute(own, 'space', up)  4.98 us
    ppermute x1, starting transfers between devices, body(): lax.ppermute(to_above, 'space', up).astype(F32)  4.55 us
    ppermute x1, waiting for transfers between devices, body(): above = lax.ppermute(own, 'space', down)  4.03 us
    unnamed x18, local copies, waits for them, and re-layouts  2.97 us
    pallas_call x1, Pallas kernels, input_parts(): pl.pallas_call(functools.partial(input_kernel, chans), out_shape=[sides,...  2.8 us
  transfers between devices with their start and end apart: 18, of which 12 were waited for; matrix products, arithmetic and copies ran while one was open for 3% of the time, Pallas kernels for 13%

profile of v1, /device:TPU:0, one launch (start us, length us, event | category | flops | bytes accessed | tf_op | source)
XLA Modules:
  0.0 111.9 jit_solution(17099322717259532837)
XLA Ops:
  0.6 5.0 %collective-permute-start = (bf16[64,1024]{1,0:T(8,128)(2,1)}, bf16[64,1024]{1,0:T(8,128)(2,1)S(1)}, u32[]{:S(2)}, u32[]{:S(2)}) collective-permute-start(bf16[64,1024]{1,0:T(8,128)(2,1)} %bitcast.24), channel_id=1, source_target_pairs={{0,4},{4,8},{8,12},{12,16},{16,20},{20,24},{24,28},{1,5},{5,9},{9,... | collective-permute-start | bytes 393224 | tf_op jit(solution)/shard_map/ppermute | solution.py:264
  5.6 1.3 %collective-permute-start.1 = (bf16[64,1024]{1,0:T(8,128)(2,1)}, bf16[64,1024]{1,0:T(8,128)(2,1)S(1)}, u32[]{:S(2)}, u32[]{:S(2)}) collective-permute-start(bf16[64,1024]{1,0:T(8,128)(2,1)} %bitcast.25), channel_id=1, source_target_pairs={{4,0},{8,4},{12,8},{16,12},{20,16},{24,20},{28,24},{5,1},{9,5},{13... | collective-permute-start | bytes 393224 | tf_op jit(solution)/shard_map/ppermute | solution.py:265
  6.9 1.5 %copy.13 = bf16[1728,256]{0,1:T(8,128)(2,1)S(1)} copy(bf16[1728,256]{1,0:T(8,128)(2,1)} %bitcast.23) | data formatting | bytes 1769472 | tf_op jit(solution)/shard_map/reshape | solution.py:266
  8.7 4.0 %collective-permute-done.1.above = bf16[64,1024]{1,0:T(8,128)(2,1)S(1)} collective-permute-done((bf16[64,1024]{1,0:T(8,128)(2,1)}, bf16[64,1024]{1,0:T(8,128)(2,1)S(1)}, u32[]{:S(2)}, u32[]{:S(2)}) %collective-permute-start.1) | collective-permute-done | bytes 131104 | tf_op jit(solution)/shard_map/ppermute | solution.py:265
  12.7 1.4 %forward_parts.1 = (f32[64,1024]{1,0:T(8,128)S(1)}, f32[64,1024]{1,0:T(8,128)S(1)}, f32[64,1024]{1,0:T(8,128)S(1)}, f32[64,1024]{1,0:T(8,128)S(1)}) custom-call(s32[1]{0:T(128)} %bitcast.index, bf16[64,1024]{1,0:T(8,128)(2,1)S(1)} %bitcast.26, bf16[64,1024]{1,0:T(8,128)(2,1)S(1)} %collective-permute-done.below, ...), custom_call_target="tpu_custom_call" | custom-call | flops 905969664 | bytes 6291456 | tf_op jit(solution)/shard_map/forward_parts/pallas_call | solution.py:53
  14.2 1.6 %collective-permute-start.3 = (f32[64,1024]{1,0:T(8,128)S(1)}, f32[64,1024]{1,0:T(8,128)S(1)}, u32[]{:S(2)}, u32[]{:S(2)}) collective-permute-start(f32[64,1024]{1,0:T(8,128)S(1)} %get-tuple-element.15), channel_id=1, source_target_pairs={{0,2},{1,3},{2,0},{3,1},{4,6},{5,7},{6,4},{7,5},{8,10},{9,11},{10,... | collective-permute-start | bytes 786440 | tf_op jit(solution)/shard_map/ppermute | solution.py:237
  16.0 7.3 %collective-permute-done.3 = f32[64,1024]{1,0:T(8,128)S(1)} collective-permute-done((f32[64,1024]{1,0:T(8,128)S(1)}, f32[64,1024]{1,0:T(8,128)S(1)}, u32[]{:S(2)}, u32[]{:S(2)}) %collective-permute-start.3) | collective-permute-done | bytes 262176 | tf_op jit(solution)/shard_map/ppermute | solution.py:237
  23.3 4.7 %collective-permute-done.4 = f32[64,1024]{1,0:T(8,128)S(1)} collective-permute-done((f32[64,1024]{1,0:T(8,128)S(1)}, f32[64,1024]{1,0:T(8,128)S(1)}, u32[]{:S(2)}, u32[]{:S(2)}) %collective-permute-start.4) | collective-permute-done | bytes 262176 | tf_op jit(solution)/shard_map/ppermute | solution.py:237
  28.3 2.5 %collective-permute-start.12 = (bf16[32,1024]{1,0:T(8,128)(2,1)S(1)}, bf16[32,1024]{1,0:T(8,128)(2,1)S(1)}, u32[]{:S(2)}, u32[]{:S(2)}) collective-permute-start(bf16[32,1024]{1,0:T(8,128)(2,1)S(1)} %get-tuple-element.33), channel_id=1, source_target_pairs={{0,4},{4,0},{8,12},{12,8},{16,20},{20,16},{24,28},{28,24},{1,5},{5... | collective-permute-start | bytes 196616 | tf_op jit(solution)/shard_map/ppermute | solution.py:237
  30.8 2.5 %collective-permute-done.12 = bf16[32,1024]{1,0:T(8,128)(2,1)S(1)} collective-permute-done((bf16[32,1024]{1,0:T(8,128)(2,1)S(1)}, bf16[32,1024]{1,0:T(8,128)(2,1)S(1)}, u32[]{:S(2)}, u32[]{:S(2)}) %collective-permute-start.12) | collective-permute-done | bytes 65568 | tf_op jit(solution)/shard_map/ppermute | solution.py:237
  33.3 2.7 %collective-permute-start.13 = (bf16[2,32,1024]{2,1,0:T(8,128)(2,1)S(1)}, bf16[2,32,1024]{2,1,0:T(8,128)(2,1)S(1)}, u32[]{:S(2)}, u32[]{:S(2)}) collective-permute-start(bf16[2,32,1024]{2,1,0:T(8,128)(2,1)S(1)} %pad_maximum_fusion.5), channel_id=1, source_target_pairs={{0,16},{4,20},{8,24},{12,28},{16,0},{20,4},{24,8},{28,12},{1,17},{... | collective-permute-start | bytes 393224 | tf_op jit(solution)/shard_map/ppermute | solution.py:237
  36.0 6.3 %collective-permute-done.13 = bf16[2,32,1024]{2,1,0:T(8,128)(2,1)S(1)} collective-permute-done((bf16[2,32,1024]{2,1,0:T(8,128)(2,1)S(1)}, bf16[2,32,1024]{2,1,0:T(8,128)(2,1)S(1)}, u32[]{:S(2)}, u32[]{:S(2)}) %collective-permute-start.13) | collective-permute-done | bytes 131104 | tf_op jit(solution)/shard_map/ppermute | solution.py:237
  42.7 7.0 %collective-permute-done.14 = bf16[4,32,1024]{2,1,0:T(8,128)(2,1)S(1)} collective-permute-done((bf16[4,32,1024]{2,1,0:T(8,128)(2,1)S(1)}, bf16[4,32,1024]{2,1,0:T(8,128)(2,1)S(1)}, u32[]{:S(2)}, u32[]{:S(2)}) %collective-permute-start.14) | collective-permute-done | bytes 262176 | tf_op jit(solution)/shard_map/ppermute | solution.py:237
  49.8 1.6 %collective-permute-start.15 = (bf16[1,8,32,1024]{3,2,1,0:T(8,128)(2,1)S(1)}, bf16[1,8,32,1024]{3,2,1,0:T(8,128)(2,1)S(1)}, u32[]{:S(2)}, u32[]{:S(2)}) collective-permute-start(bf16[1,8,32,1024]{3,2,1,0:T(8,128)(2,1)S(1)} %maximum_bitcast_fusion), channel_id=1, source_target_pairs={{0,2},{1,3},{2,0},{3,1},{4,6},{5,7},{6,4},{7,5},{8,10},{9,11},{10,... | collective-permute-start | bytes 1572872 | tf_op jit(solution)/shard_map/ppermute | solution.py:237
  51.4 2.7 %collective-permute-start.9 = (bf16[1,64,1024]{2,1,0:T(8,128)(2,1)S(1)}, bf16[1,64,1024]{2,1,0:T(8,128)(2,1)S(1)}, u32[]{:S(2)}, u32[]{:S(2)}) collective-permute-start(bf16[1,64,1024]{2,1,0:T(8,128)(2,1)S(1)} %bitcast.27), channel_id=1, source_target_pairs={{0,16},{4,20},{8,24},{12,28},{16,0},{20,4},{24,8},{28,12},{1,17},{... | collective-permute-start | bytes 393224 | tf_op jit(solution)/shard_map/ppermute | solution.py:237
  54.1 7.8 %collective-permute-done.15 = bf16[1,8,32,1024]{3,2,1,0:T(8,128)(2,1)S(1)} collective-permute-done((bf16[1,8,32,1024]{3,2,1,0:T(8,128)(2,1)S(1)}, bf16[1,8,32,1024]{3,2,1,0:T(8,128)(2,1)S(1)}, u32[]{:S(2)}, u32[]{:S(2)}) %collective-permute-start.15) | collective-permute-done | bytes 524320 | tf_op jit(solution)/shard_map/ppermute | solution.py:237
  62.1 1.8 %collective-permute-start.10 = (bf16[2,64,1024]{2,1,0:T(8,128)(2,1)S(1)}, bf16[2,64,1024]{2,1,0:T(8,128)(2,1)S(1)}, u32[]{:S(2)}, u32[]{:S(2)}) collective-permute-start(bf16[2,64,1024]{2,1,0:T(8,128)(2,1)S(1)} %pad_maximum_fusion.3), channel_id=1, source_target_pairs={{0,8},{4,12},{8,0},{12,4},{16,24},{20,28},{24,16},{28,20},{1,9},{5... | collective-permute-start | bytes 786440 | tf_op jit(solution)/shard_map/ppermute | solution.py:237
  64.0 1.5 %collective-permute-start.5 = (bf16[1,64,1024]{2,1,0:T(8,128)(2,1)S(1)}, bf16[1,64,1024]{2,1,0:T(8,128)(2,1)S(1)}, u32[]{:S(2)}, u32[]{:S(2)}) collective-permute-start(bf16[1,64,1024]{2,1,0:T(8,128)(2,1)S(1)} %bitcast.30), channel_id=1, source_target_pairs={{0,2},{1,3},{2,0},{3,1},{4,6},{5,7},{6,4},{7,5},{8,10},{9,11},{10,... | collective-permute-start | bytes 393224 | tf_op jit(solution)/shard_map/ppermute | solution.py:237
  65.5 5.4 %collective-permute-done.10 = bf16[2,64,1024]{2,1,0:T(8,128)(2,1)S(1)} collective-permute-done((bf16[2,64,1024]{2,1,0:T(8,128)(2,1)S(1)}, bf16[2,64,1024]{2,1,0:T(8,128)(2,1)S(1)}, u32[]{:S(2)}, u32[]{:S(2)}) %collective-permute-start.10) | collective-permute-done | bytes 262176 | tf_op jit(solution)/shard_map/ppermute | solution.py:237
  71.0 1.0 collective-permute-start.11
  72.3 1.4 %collective-permute-done.6.theirs = bf16[2,64,1024]{2,1,0:T(8,128)(2,1)S(1)} collective-permute-done((bf16[2,64,1024]{2,1,0:T(8,128)(2,1)S(1)}, bf16[2,64,1024]{2,1,0:T(8,128)(2,1)S(1)}, u32[]{:S(2)}, u32[]{:S(2)}) %collective-permute-start.6) | collective-permute-done | bytes 262176 | tf_op jit(solution)/shard_map/ppermute | solution.py:237
  73.7 2.8 %input_parts.1 = (bf16[64,1024]{1,0:T(8,128)(2,1)S(1)}, f32[64,1024]{1,0:T(8,128)S(1)}, bf16[64,1024]{1,0:T(8,128)(2,1)S(1)}) custom-call(s32[5]{0:T(128)S(1)} %pad_add_fusion.index, bf16[2,64,1024]{2,1,0:T(8,128)(2,1)S(1)} %pad_maximum_fusion.2.mine, bf16[2,64,1024]{2,1,0:T(8,128)(2,1)S(1)} %collective-permute-done.6.theirs, bf16[27,64,256]{2,1,0:T(8,128)(2,1)S(1)} %copy-done), custom_call_target="tpu_custom_call" | custom-call | flops 905969664 | bytes 6291456 | tf_op jit(solution)/shard_map/input_parts/pallas_call | solution.py:95
  76.5 1.3 %collective-permute-start.7 = (bf16[64,1024]{1,0:T(8,128)(2,1)S(1)}, bf16[64,1024]{1,0:T(8,128)(2,1)S(1)}, u32[]{:S(2)}, u32[]{:S(2)}) collective-permute-start(bf16[64,1024]{1,0:T(8,128)(2,1)S(1)} %get-tuple-element.18), channel_id=1, source_target_pairs={{4,0},{8,4},{12,8},{16,12},{20,16},{24,20},{28,24},{5,1},{9,5},{13... | collective-permute-start | bytes 393224 | tf_op jit(solution)/shard_map/ppermute | solution.py:301
  77.8 4.6 %collective-permute-start.8 = (bf16[64,1024]{1,0:T(8,128)(2,1)S(1)}, bf16[64,1024]{1,0:T(8,128)(2,1)S(1)}, u32[]{:S(2)}, u32[]{:S(2)}) collective-permute-start(bf16[64,1024]{1,0:T(8,128)(2,1)S(1)} %get-tuple-element.19), channel_id=1, source_target_pairs={{0,4},{4,8},{8,12},{12,16},{16,20},{20,24},{24,28},{1,5},{5,9},{9,... | collective-permute-start | bytes 393224 | tf_op jit(solution)/shard_map/ppermute | solution.py:302
  82.4 4.8 %collective-permute-done.11.far = bf16[4,64,1024]{2,1,0:T(8,128)(2,1)S(1)} collective-permute-done((bf16[4,64,1024]{2,1,0:T(8,128)(2,1)S(1)}, bf16[4,64,1024]{2,1,0:T(8,128)(2,1)S(1)}, u32[]{:S(2)}, u32[]{:S(2)}) %collective-permute-start.11) | collective-permute-done | bytes 524320 | tf_op jit(solution)/shard_map/ppermute | solution.py:237
  87.2 1.0 copy-done.6
  88.2 11.2 %filter_half.1.mine = bf16[1760,128]{1,0:T(8,128)(2,1)S(1)} custom-call(s32[22]{0:T(128)S(1)} %pad_add_fusion.1.index, bf16[4,64,1024]{2,1,0:T(8,128)(2,1)S(1)} %pad_maximum_fusion.1.near, bf16[4,64,1024]{2,1,0:T(8,128)(2,1)S(1)} %collective-permute-done.11.far, bf16[2,8,32,1024]{3,2,1,0:T(8,128)(2,1)} %copy-done.2, bf16[2,8,32,1024]{3,2,1,0:T(8,128)(2,1)} %copy-done.6), custom_call_target="tpu_custom_call" | custom-call | flops 3623878656 | bytes 8388608 | tf_op jit(solution)/shard_map/filter_half/pallas_call | solution.py:176
  99.4 2.5 %collective-permute-start.17 = (bf16[1760,128]{1,0:T(8,128)(2,1)S(1)}, bf16[1760,128]{1,0:T(8,128)(2,1)S(1)}, u32[]{:S(2)}, u32[]{:S(2)}) collective-permute-start(bf16[1760,128]{1,0:T(8,128)(2,1)S(1)} %filter_half.1.mine), channel_id=1, source_target_pairs={{0,4},{4,0},{8,12},{12,8},{16,20},{20,16},{24,28},{28,24},{1,5},{5... | collective-permute-start | bytes 1351688 | tf_op jit(solution)/shard_map/ppermute | solution.py:237
  102.1 1.0 copy.14
  103.1 1.0 copy.15
  104.1 5.9 %collective-permute-done.17.theirs = bf16[1760,128]{1,0:T(8,128)(2,1)S(1)} collective-permute-done((bf16[1760,128]{1,0:T(8,128)(2,1)S(1)}, bf16[1760,128]{1,0:T(8,128)(2,1)S(1)}, u32[]{:S(2)}, u32[]{:S(2)}) %collective-permute-start.17) | collective-permute-done | bytes 450592 | tf_op jit(solution)/shard_map/ppermute | solution.py:237
  110.0 1.8 %join_halves.1 = (f32[1728,256]{1,0:T(8,128)}, f32[1,256]{1,0:T(1,128)}) custom-call(s32[1]{0:T(128)} %bitcast.8.index, bf16[1760,128]{1,0:T(8,128)(2,1)S(1)} %filter_half.1.mine, bf16[1760,128]{1,0:T(8,128)(2,1)S(1)} %collective-permute-done.17.theirs), custom_call_target="tpu_custom_call" | custom-call | flops 226492416 | bytes 6291456 | tf_op jit(solution)/shard_map/join_halves/pallas_call | solution.py:219
  (40 shorter events, 2.0 us)
Async XLA Ops:
  0.6 12.1 %copy-start.1 = (bf16[64,1,1024]{2,0,1:T(8,128)(2,1)S(1)}, bf16[64,1,1024]{2,0,1:T(8,128)(2,1)}, u32[]{:S(2)}) copy-start(bf16[64,1,1024]{2,0,1:T(8,128)(2,1)} %param.6) | copy-start | bytes 393220
  0.6 8.0 %collective-permute-start = (bf16[64,1024]{1,0:T(8,128)(2,1)}, bf16[64,1024]{1,0:T(8,128)(2,1)S(1)}, u32[]{:S(2)}, u32[]{:S(2)}) collective-permute-start(bf16[64,1024]{1,0:T(8,128)(2,1)} %bitcast.24), channel_id=1, source_target_pairs={{0,4},{4,8},{8,12},{12,16},{16,20},{20,24},{24,28},{1,5},{5,9},{9,... | collective-permute-start | bytes 393224 | tf_op jit(solution)/shard_map/ppermute | solution.py:264
  5.6 7.1 %collective-permute-start.1 = (bf16[64,1024]{1,0:T(8,128)(2,1)}, bf16[64,1024]{1,0:T(8,128)(2,1)S(1)}, u32[]{:S(2)}, u32[]{:S(2)}) collective-permute-start(bf16[64,1024]{1,0:T(8,128)(2,1)} %bitcast.25), channel_id=1, source_target_pairs={{4,0},{8,4},{12,8},{16,12},{20,16},{24,20},{28,24},{5,1},{9,5},{13... | collective-permute-start | bytes 393224 | tf_op jit(solution)/shard_map/ppermute | solution.py:265
  8.4 19.7 %copy-start.3 = (bf16[64,1,1024]{2,0,1:T(8,128)(2,1)S(1)}, bf16[64,1,1024]{2,0,1:T(8,128)(2,1)}, u32[]{:S(2)}) copy-start(bf16[64,1,1024]{2,0,1:T(8,128)(2,1)} %param.9) | copy-start | bytes 393220
  8.4 19.6 %copy-start.4 = (f32[64]{0:T(128)S(1)}, f32[64]{0:T(128)}, u32[]{:S(2)}) copy-start(f32[64]{0:T(128)} %param.8) | copy-start | bytes 772
  14.1 1.9 %collective-permute-start.2 = (f32[64,1024]{1,0:T(8,128)S(1)}, f32[64,1024]{1,0:T(8,128)S(1)}, u32[]{:S(2)}, u32[]{:S(2)}) collective-permute-start(f32[64,1024]{1,0:T(8,128)S(1)} %get-tuple-element.14), channel_id=1, source_target_pairs={{0,1},{1,0},{2,3},{3,2},{4,5},{5,4},{6,7},{7,6},{8,9},{9,8},{10,11... | collective-permute-start | bytes 786440 | tf_op jit(solution)/shard_map/ppermute | solution.py:237
  14.2 9.2 %collective-permute-start.3 = (f32[64,1024]{1,0:T(8,128)S(1)}, f32[64,1024]{1,0:T(8,128)S(1)}, u32[]{:S(2)}, u32[]{:S(2)}) collective-permute-start(f32[64,1024]{1,0:T(8,128)S(1)} %get-tuple-element.15), channel_id=1, source_target_pairs={{0,2},{1,3},{2,0},{3,1},{4,6},{5,7},{6,4},{7,5},{8,10},{9,11},{10,... | collective-permute-start | bytes 786440 | tf_op jit(solution)/shard_map/ppermute | solution.py:237
  15.8 12.3 %collective-permute-start.4 = (f32[64,1024]{1,0:T(8,128)S(1)}, f32[64,1024]{1,0:T(8,128)S(1)}, u32[]{:S(2)}, u32[]{:S(2)}) collective-permute-start(f32[64,1024]{1,0:T(8,128)S(1)} %get-tuple-element.16), channel_id=1, source_target_pairs={{0,3},{1,2},{2,1},{3,0},{4,7},{5,6},{6,5},{7,4},{8,11},{9,10},{10,... | collective-permute-start | bytes 786440 | tf_op jit(solution)/shard_map/ppermute | solution.py:237
  28.3 5.0 %collective-permute-start.12 = (bf16[32,1024]{1,0:T(8,128)(2,1)S(1)}, bf16[32,1024]{1,0:T(8,128)(2,1)S(1)}, u32[]{:S(2)}, u32[]{:S(2)}) collective-permute-start(bf16[32,1024]{1,0:T(8,128)(2,1)S(1)} %get-tuple-element.33), channel_id=1, source_target_pairs={{0,4},{4,0},{8,12},{12,8},{16,20},{20,16},{24,28},{28,24},{1,5},{5... | collective-permute-start | bytes 196616 | tf_op jit(solution)/shard_map/ppermute | solution.py:237
  33.3 9.0 %collective-permute-start.13 = (bf16[2,32,1024]{2,1,0:T(8,128)(2,1)S(1)}, bf16[2,32,1024]{2,1,0:T(8,128)(2,1)S(1)}, u32[]{:S(2)}, u32[]{:S(2)}) collective-permute-start(bf16[2,32,1024]{2,1,0:T(8,128)(2,1)S(1)} %pad_maximum_fusion.5), channel_id=1, source_target_pairs={{0,16},{4,20},{8,24},{12,28},{16,0},{20,4},{24,8},{28,12},{1,17},{... | collective-permute-start | bytes 393224 | tf_op jit(solution)/shard_map/ppermute | solution.py:237
  42.3 7.4 %collective-permute-start.14 = (bf16[4,32,1024]{2,1,0:T(8,128)(2,1)S(1)}, bf16[4,32,1024]{2,1,0:T(8,128)(2,1)S(1)}, u32[]{:S(2)}, u32[]{:S(2)}) collective-permute-start(bf16[4,32,1024]{2,1,0:T(8,128)(2,1)S(1)} %pad_maximum_fusion.4), channel_id=1, source_target_pairs={{0,8},{4,12},{8,0},{12,4},{16,24},{20,28},{24,16},{28,20},{1,9},{5... | collective-permute-start | bytes 786440 | tf_op jit(solution)/shard_map/ppermute | solution.py:237
  49.8 12.1 %collective-permute-start.15 = (bf16[1,8,32,1024]{3,2,1,0:T(8,128)(2,1)S(1)}, bf16[1,8,32,1024]{3,2,1,0:T(8,128)(2,1)S(1)}, u32[]{:S(2)}, u32[]{:S(2)}) collective-permute-start(bf16[1,8,32,1024]{3,2,1,0:T(8,128)(2,1)S(1)} %maximum_bitcast_fusion), channel_id=1, source_target_pairs={{0,2},{1,3},{2,0},{3,1},{4,6},{5,7},{6,4},{7,5},{8,10},{9,11},{10,... | collective-permute-start | bytes 1572872 | tf_op jit(solution)/shard_map/ppermute | solution.py:237
  51.4 20.8 %copy-start.7 = (s32[4]{0:T(128)S(1)}, s32[4]{0:T(128)}, u32[]{:S(2)}) copy-start(s32[4]{0:T(128)} %constant.19.clone) | copy-start | bytes 52
  51.4 20.9 %copy-start.5 = (s32[20]{0:T(128)S(1)}, s32[20]{0:T(128)}, u32[]{:S(2)}) copy-start(s32[20]{0:T(128)} %constant.20.clone) | copy-start | bytes 244
  51.4 22.3 %copy-start = (bf16[27,64,256]{2,1,0:T(8,128)(2,1)S(1)}, bf16[27,64,256]{2,1,0:T(8,128)(2,1)}, u32[]{:S(2)}) copy-start(bf16[27,64,256]{2,1,0:T(8,128)(2,1)} %weights.1) | copy-start | bytes 2654212
  51.4 10.7 %collective-permute-start.9 = (bf16[1,64,1024]{2,1,0:T(8,128)(2,1)S(1)}, bf16[1,64,1024]{2,1,0:T(8,128)(2,1)S(1)}, u32[]{:S(2)}, u32[]{:S(2)}) collective-permute-start(bf16[1,64,1024]{2,1,0:T(8,128)(2,1)S(1)} %bitcast.27), channel_id=1, source_target_pairs={{0,16},{4,20},{8,24},{12,28},{16,0},{20,4},{24,8},{28,12},{1,17},{... | collective-permute-start | bytes 393224 | tf_op jit(solution)/shard_map/ppermute | solution.py:237
  62.0 14.5 %copy-start.2 = (bf16[2,8,32,1024]{3,2,1,0:T(8,128)(2,1)}, bf16[2,8,32,1024]{3,2,1,0:T(8,128)(2,1)S(1)}, u32[]{:S(2)}) copy-start(bf16[2,8,32,1024]{3,2,1,0:T(8,128)(2,1)S(1)} %pad_maximum_fusion.mine) | copy-start | bytes 3145732
  62.0 25.2 %collective-permute-start.16 = (bf16[2,8,32,1024]{3,2,1,0:T(8,128)(2,1)S(1)}, bf16[2,8,32,1024]{3,2,1,0:T(8,128)(2,1)S(1)}, u32[]{:S(2)}, u32[]{:S(2)}) collective-permute-start(bf16[2,8,32,1024]{3,2,1,0:T(8,128)(2,1)S(1)} %pad_maximum_fusion.mine), channel_id=1, source_target_pairs={{0,1},{1,0},{2,3},{3,2},{4,5},{5,4},{6,7},{7,6},{8,9},{9,8},{10,11... | collective-permute-start | bytes 3145736 | tf_op jit(solution)/shard_map/ppermute | solution.py:237
  62.1 8.8 %collective-permute-start.10 = (bf16[2,64,1024]{2,1,0:T(8,128)(2,1)S(1)}, bf16[2,64,1024]{2,1,0:T(8,128)(2,1)S(1)}, u32[]{:S(2)}, u32[]{:S(2)}) collective-permute-start(bf16[2,64,1024]{2,1,0:T(8,128)(2,1)S(1)} %pad_maximum_fusion.3), channel_id=1, source_target_pairs={{0,8},{4,12},{8,0},{12,4},{16,24},{20,28},{24,16},{28,20},{1,9},{5... | collective-permute-start | bytes 786440 | tf_op jit(solution)/shard_map/ppermute | solution.py:237
  64.0 8.1 %collective-permute-start.5 = (bf16[1,64,1024]{2,1,0:T(8,128)(2,1)S(1)}, bf16[1,64,1024]{2,1,0:T(8,128)(2,1)S(1)}, u32[]{:S(2)}, u32[]{:S(2)}) collective-permute-start(bf16[1,64,1024]{2,1,0:T(8,128)(2,1)S(1)} %bitcast.30), channel_id=1, source_target_pairs={{0,2},{1,3},{2,0},{3,1},{4,6},{5,7},{6,4},{7,5},{8,10},{9,11},{10,... | collective-permute-start | bytes 393224 | tf_op jit(solution)/shard_map/ppermute | solution.py:237
  71.0 16.2 %collective-permute-start.11 = (bf16[4,64,1024]{2,1,0:T(8,128)(2,1)S(1)}, bf16[4,64,1024]{2,1,0:T(8,128)(2,1)S(1)}, u32[]{:S(2)}, u32[]{:S(2)}) collective-permute-start(bf16[4,64,1024]{2,1,0:T(8,128)(2,1)S(1)} %pad_maximum_fusion.1.near), channel_id=1, source_target_pairs={{0,4},{4,0},{8,12},{12,8},{16,20},{20,16},{24,28},{28,24},{1,5},{5... | collective-permute-start | bytes 1572872 | tf_op jit(solution)/shard_map/ppermute | solution.py:237
  72.1 1.6 %collective-permute-start.6 = (bf16[2,64,1024]{2,1,0:T(8,128)(2,1)S(1)}, bf16[2,64,1024]{2,1,0:T(8,128)(2,1)S(1)}, u32[]{:S(2)}, u32[]{:S(2)}) collective-permute-start(bf16[2,64,1024]{2,1,0:T(8,128)(2,1)S(1)} %pad_maximum_fusion.2.mine), channel_id=1, source_target_pairs={{0,1},{1,0},{2,3},{3,2},{4,5},{5,4},{6,7},{7,6},{8,9},{9,8},{10,11... | collective-permute-start | bytes 786440 | tf_op jit(solution)/shard_map/ppermute | solution.py:237
  76.5 26.5 %collective-permute-start.7 = (bf16[64,1024]{1,0:T(8,128)(2,1)S(1)}, bf16[64,1024]{1,0:T(8,128)(2,1)S(1)}, u32[]{:S(2)}, u32[]{:S(2)}) collective-permute-start(bf16[64,1024]{1,0:T(8,128)(2,1)S(1)} %get-tuple-element.18), channel_id=1, source_target_pairs={{4,0},{8,4},{12,8},{16,12},{20,16},{24,20},{28,24},{5,1},{9,5},{13... | collective-permute-start | bytes 393224 | tf_op jit(solution)/shard_map/ppermute | solution.py:301
  77.8 25.3 %collective-permute-start.8 = (bf16[64,1024]{1,0:T(8,128)(2,1)S(1)}, bf16[64,1024]{1,0:T(8,128)(2,1)S(1)}, u32[]{:S(2)}, u32[]{:S(2)}) collective-permute-start(bf16[64,1024]{1,0:T(8,128)(2,1)S(1)} %get-tuple-element.19), channel_id=1, source_target_pairs={{0,4},{4,8},{8,12},{12,16},{16,20},{20,24},{24,28},{1,5},{5,9},{9,... | collective-permute-start | bytes 393224 | tf_op jit(solution)/shard_map/ppermute | solution.py:302
  87.2 1.0 copy-start.6
  99.4 10.6 %collective-permute-start.17 = (bf16[1760,128]{1,0:T(8,128)(2,1)S(1)}, bf16[1760,128]{1,0:T(8,128)(2,1)S(1)}, u32[]{:S(2)}, u32[]{:S(2)}) collective-permute-start(bf16[1760,128]{1,0:T(8,128)(2,1)S(1)} %filter_half.1.mine), channel_id=1, source_target_pairs={{0,4},{4,0},{8,12},{12,8},{16,20},{20,16},{24,28},{28,24},{1,5},{5... | collective-permute-start | bytes 1351688 | tf_op jit(solution)/shard_map/ppermute | solution.py:237

commit v2 on v1

v2 whole, which is shorter than its diff:
```python
import functools
import math

import jax
import jax.numpy as jnp
from jax import lax
from jax.experimental import pallas as pl
from jax.experimental.pallas import tpu as pltpu
from jax.sharding import PartitionSpec as P

TAPS = 27
PLANE_H = 32
PLANE_W = 32
CELLS = PLANE_H * PLANE_W
VMEM = pl.BlockSpec(memory_space=pltpu.VMEM)
SMEM = pl.BlockSpec(memory_space=pltpu.SMEM)
BF16 = jnp.bfloat16
F32 = jnp.float32


def cell_mask(row_off, col_off):
    cell = lax.broadcasted_iota(jnp.int32, (1, CELLS), 1)
    row = cell // PLANE_W + row_off
    col = cell % PLANE_W + col_off
    inside = (row >= 0) & (row < PLANE_H) & (col >= 0) & (col < PLANE_W)
    return jnp.where(inside, 1.0, 0.0).astype(BF16)


def moved(plane, row_off, col_off):
    if row_off == 0 and col_off == 0:
        return plane
    amount = (-(row_off * PLANE_W + col_off)) % CELLS
    return pltpu.roll(plane, amount, 1) * cell_mask(row_off, col_off)


def repeat(count, step):
    if count > 8:
        lax.fori_loop(0, count, lambda q, _: (step(q), 0)[1], 0)
    else:
        for q in range(count):
            step(q)


def forward_kernel(chans, index, own, below, above, weights, keep, give, stack, total):
    for a, plane in enumerate((below, own, above)):
        cells = plane[...]
        for b in range(3):
            for e in range(3):
                tap = 9 * a + 3 * b + e
                stack[tap * chans : (tap + 1) * chans, :] = moved(cells, b - 1, e - 1)
    total[...] = jnp.dot(weights[...], stack[...], preferred_element_type=F32)
    for j in range(keep.shape[0]):
        start = pl.multiple_of((index[0] ^ (2 * j)) * chans, chans)
        keep[j] = total[pl.ds(start, chans), :]
        start = pl.multiple_of((index[0] ^ (2 * j + 1)) * chans, chans)
        give[j] = total[pl.ds(start, chans), :]


def forward_parts(index, own, below, above, weights):
    chans = own.shape[0]
    outs = weights.shape[0]
    side = jax.ShapeDtypeStruct((outs // chans // 2, chans, CELLS), F32)
    return pl.pallas_call(
        functools.partial(forward_kernel, chans),
        out_shape=[side, side],
        in_specs=[SMEM] + [VMEM] * 4,
        out_specs=[VMEM] * 2,
        scratch_shapes=[
            pltpu.VMEM((TAPS * chans, CELLS), BF16),
            pltpu.VMEM((outs, CELLS), F32),
        ],
        compiler_params=pltpu.CompilerParams(vmem_limit_bytes=20 << 20),
        cost_estimate=pl.CostEstimate(
            flops=2 * outs * TAPS * chans * CELLS, bytes_accessed=6 << 20, transcendentals=0
        ),
        name="forward_parts",
    )(index, own, below, above, weights)


def input_kernel(chans, groups, index, *refs):
    grads = refs[:groups]
    weights, below, own, above, stack, left = refs[groups:]
    outs = weights.shape[2]
    for u in range(groups):
        start = pl.multiple_of((index[0] ^ u) * chans, chans)
        cells = grads[u][...]
        for b in range(3):
            for e in range(3):
                stack[3 * b + e, pl.ds(start, chans), :] = moved(cells, 1 - b, 1 - e)
    for a in range(3):
        for k in range(9):
            left[a * chans : (a + 1) * chans, k * outs : (k + 1) * outs] = weights[9 * a + k]
    total = jnp.dot(
        left[...], stack[...].reshape(9 * outs, CELLS), preferred_element_type=F32
    )
    below[...] = total[:chans].astype(BF16)
    own[...] = total[chans : 2 * chans]
    above[...] = total[2 * chans :].astype(BF16)


def input_parts(index, grads, weights):
    chans = weights.shape[1]
    outs = weights.shape[2]
    groups = len(grads)
    sides = jax.ShapeDtypeStruct((chans, CELLS), BF16)
    return pl.pallas_call(
        functools.partial(input_kernel, chans, groups),
        out_shape=[sides, jax.ShapeDtypeStruct((chans, CELLS), F32), sides],
        in_specs=[SMEM] + [VMEM] * (groups + 1),
        out_specs=[VMEM] * 3,
        scratch_shapes=[
            pltpu.VMEM((9, outs, CELLS), BF16),
            pltpu.VMEM((3 * chans, 9 * outs), BF16),
        ],
        compiler_params=pltpu.CompilerParams(vmem_limit_bytes=20 << 20),
        cost_estimate=pl.CostEstimate(
            flops=2 * 3 * chans * 9 * outs * CELLS, bytes_accessed=6 << 20, transcendentals=0
        ),
        name="input_parts",
    )(index, *grads, weights)


def filter_kernel(factor, groups, index, near, far, *refs):
    grads = refs[:groups]
    out, shifted, rows, total, sums = refs[groups:]
    planes, share, _ = grads[0].shape
    chans = near.shape[1]
    width = groups * share
    space, chan = index[0], index[1]
    edge = jnp.zeros((3 * chans, CELLS), BF16)
    shifted[0] = edge
    shifted[planes + 1] = edge
    for part, first in ((near, 0), (far, planes // 2)):

        def fill(q):
            depth = space ^ index[2 + first + q]
            cells = part[q]
            for e in range(3):
                shifted[depth + 1, e * chans : (e + 1) * chans, :] = moved(cells, 0, e - 1)

        repeat(planes // 2, fill)
    ones = jnp.ones((16, CELLS), BF16)
    contract = (((1,), (1,)), ((), ()))
    total[...] = jnp.zeros_like(total)
    sums[...] = jnp.zeros_like(sums)

    def step(q):
        for u in range(groups):
            cells = grads[u][q]
            for b in range(3):
                rows[q & 1, b * groups + (chan ^ u)] = moved(cells, 1 - b, 0)
        right = rows[q & 1].reshape(3 * width, CELLS)
        left = shifted[pl.ds(space ^ q, 3)].reshape(9 * chans, CELLS)
        term = lax.dot_general(left, right, contract, preferred_element_type=F32)
        count = lax.dot_general(
            ones, right[width : 2 * width], contract, preferred_element_type=F32
        )
        total[...] += term
        sums[...] += count

    repeat(planes, step)
    bias = sums[...] * factor
    high = bias.astype(BF16)
    low = (bias - high.astype(F32)).astype(BF16)

    def tile(tap):
        if tap == TAPS:
            rest = jnp.zeros((chans - 32, width), BF16)
            return jnp.concatenate([high, low, rest][: 2 + (chans > 32)], axis=0)
        a, b, e = tap // 9, tap // 3 % 3, tap % 3
        first = (3 * a + e) * chans
        piece = total[first : first + chans, b * width : (b + 1) * width]
        return (piece * factor).astype(BF16)

    for pair in range((TAPS + 1) // 2):
        out[pair * chans : (pair + 1) * chans, :] = jnp.concatenate(
            [tile(2 * pair), tile(2 * pair + 1)], axis=1
        )


def filter_block(index, near, far, grads, factor):
    half, chans, _ = near.shape
    groups = len(grads)
    planes, share, _ = grads[0].shape
    width = groups * share
    return pl.pallas_call(
        functools.partial(filter_kernel, factor, groups),
        out_shape=jax.ShapeDtypeStruct(((TAPS + 1) // 2 * chans, 2 * width), BF16),
        in_specs=[SMEM] + [VMEM] * (2 + groups),
        out_specs=VMEM,
        scratch_shapes=[
            pltpu.VMEM((planes + 2, 3 * chans, CELLS), BF16),
            pltpu.VMEM((2, 3 * groups, share, CELLS), BF16),
            pltpu.VMEM((9 * chans, 3 * width), F32),
            pltpu.VMEM((16, width), F32),
        ],
        compiler_params=pltpu.CompilerParams(vmem_limit_bytes=28 << 20),
        cost_estimate=pl.CostEstimate(
            flops=2 * TAPS * chans * width * planes * CELLS,
            bytes_accessed=8 << 20,
            transcendentals=0,
        ),
        name="filter_block",
    )(index, near, far, *grads)


def join_kernel(share, chans, index, *refs):
    blocks, (out, bias, right) = refs[:4], refs[4:]
    lanes, total = blocks[0].shape[1], out.shape[2]
    width = lanes // 2
    lane = lax.broadcasted_iota(jnp.int32, (lanes, total), 0)
    column = lax.broadcasted_iota(jnp.int32, (lanes, total), 1)
    slot = lane % width
    for odd in range(2):
        for r in range(4):
            home = (slot // share) * (4 * share) + (index[0] ^ r) * share + slot % share
            hit = (column == home) & (lane // width == odd)
            right[r * lanes : (r + 1) * lanes, odd * total : (odd + 1) * total] = jnp.where(
                hit, 1.0, 0.0
            ).astype(BF16)
    for pair in range((TAPS + 1) // 2):
        at = slice(pair * chans, (pair + 1) * chans)
        left = jnp.concatenate([block[at, :] for block in blocks], axis=1)
        both = jnp.dot(left, right[...], preferred_element_type=F32)
        out[2 * pair] = both[:, :total]
        if 2 * pair + 1 < TAPS:
            out[2 * pair + 1] = both[:, total:]
        else:
            bias[...] = both[0:1, total:] + both[16:17, total:]


def join_blocks(index, blocks, share, chans):
    lanes = blocks[0].shape[1]
    total = 2 * lanes
    return pl.pallas_call(
        functools.partial(join_kernel, share, chans),
        out_shape=[
            jax.ShapeDtypeStruct((TAPS, chans, total), F32),
            jax.ShapeDtypeStruct((1, total), F32),
        ],
        in_specs=[SMEM] + [VMEM] * 4,
        out_specs=[VMEM, VMEM],
        scratch_shapes=[pltpu.VMEM((4 * lanes, 2 * total), BF16)],
        compiler_params=pltpu.CompilerParams(vmem_limit_bytes=20 << 20),
        cost_estimate=pl.CostEstimate(
            flops=4 * TAPS * chans * total * lanes * 2, bytes_accessed=4 << 20, transcendentals=0
        ),
        name="join_blocks",
    )(index, *blocks)


def swapped(value, axis, mask):
    count = lax.axis_size(axis)
    return lax.ppermute(value, axis, [(i, i ^ mask) for i in range(count)])


def other_chips(value):
    found = [value]
    for k in range(1, lax.axis_size("chan").bit_length() - 1):
        found = found + [swapped(v, "chan", 1 << k) for v in found]
    return found


def both_cores(values):
    return [v for value in values for v in (value, swapped(value, "chan", 1))]


def body(features, filters, out_bias, loss_grad):
    chans, planes, cells = features.shape
    total_out = filters.shape[2]
    depth = lax.axis_size("space")
    groups = lax.axis_size("chan")
    space = lax.axis_index("space")
    chan = lax.axis_index("chan")
    share = chans // 4
    high_masks = [1 << k for k in range(depth.bit_length() - 2, 0, -1)]
    factor = 1.0 / math.sqrt(cells * planes * depth)
    barrier = lax.optimization_barrier

    own = features.reshape(chans, cells)
    up = [(i, i + 1) for i in range(depth - 1)]
    down = [(i + 1, i) for i in range(depth - 1)]
    below = lax.ppermute(own, "space", up)
    above = lax.ppermute(own, "space", down)
    weights = filters.reshape(TAPS * chans, total_out)
    keep, give = forward_parts(chan.reshape(1), own, below, above, weights.T)

    side = space & 1
    near = jnp.stack([own, jnp.where(side == 0, above, below)], axis=0)
    flips = [0, 1]
    for mask in high_masks[:-1]:
        near = jnp.concatenate([near, swapped(near, "space", mask)], axis=0)
        flips = flips + [f ^ mask for f in flips]

    got = swapped(give, "chan", 1)
    pre_act = keep[0] + got[0] + out_bias[:, None]
    for j in range(1, groups // 2):
        pre_act = pre_act + swapped(keep[j] + got[j], "chan", 2 * j)
    pre_act, near = barrier((pre_act, near))
    far = swapped(near, "space", high_masks[-1])
    flips = flips + [f ^ high_masks[-1] for f in flips]

    sigmoid = jax.nn.sigmoid(pre_act)
    activated = pre_act * sigmoid
    grad_pre = (
        loss_grad.reshape(chans, cells).astype(F32)
        * sigmoid
        * (1.0 + pre_act * (1.0 - sigmoid))
    ).astype(BF16)

    split = grad_pre.reshape(2, 2, share, cells)
    kept = jnp.where(side == 0, split[:, 0], split[:, 1])
    given = jnp.where(side == 0, split[:, 1], split[:, 0])
    pair = jnp.stack([kept, swapped(given, "space", 1)], axis=0)
    pair, grads = barrier((pair, other_chips(grad_pre)))
    grads = both_cores(grads)
    side = (space >> 1) & 1
    kept = jnp.where(side == 0, pair[:, 0], pair[:, 1])
    given = jnp.where(side == 0, pair[:, 1], pair[:, 0])
    pieces = [kept]
    for t in range(1, depth // 2):
        pieces.append(swapped(given if t & 1 else kept, "space", 2 * t))
    block = jnp.concatenate(pieces, axis=0)

    block, far, grads = barrier((block, far, grads))
    to_below, in_own, to_above = input_parts(chan.reshape(1), grads, filters)

    blocks, to_below, in_own, to_above = barrier(
        (other_chips(block), to_below, in_own, to_above)
    )
    blocks = both_cores(blocks)
    in_grad = (
        in_own
        + lax.ppermute(to_below, "space", down).astype(F32)
        + lax.ppermute(to_above, "space", up).astype(F32)
    )

    index = jnp.concatenate([space.reshape(1), chan.reshape(1), jnp.array(flips, jnp.int32)])
    part = filter_block(index, near, far, blocks, factor)
    parts = [part] + [swapped(part, "space", r) for r in range(1, 4)]
    joined, bias = join_blocks((space & 3).reshape(1), parts, share, chans)
    return (
        activated.reshape(chans, planes, cells),
        in_grad.reshape(chans, planes, cells),
        joined,
        bias.reshape(total_out),
    )


def solution(mesh):
    in_specs = (
        P("chan", "space", None),
        P(None, "chan", None),
        P("chan"),
        P("chan", "space", None),
    )
    out_specs = (P("chan", "space", None), P("chan", "space", None), P(None, "chan", None), P())
    return jax.shard_map(body, mesh=mesh, in_specs=in_specs, out_specs=out_specs, check_vma=False)
```

time: 112 us -> 87.4 us (0.78)
  waiting for transfers between devices: 57.5 us -> 40.6 us
  Pallas kernels: 17.3 us -> 10.6 us
    ppermute x14 -> x17, waiting for transfers between devices: 53.3 us -> 37.2 us  [swapped(): return lax.ppermute(value, axis, [(i, i ^ mask) for i in range(count)])]
    pallas_call x4, Pallas kernels: 17.3 us -> 10.6 us  [the longest x1 4.54 us: filter_block(): pl.pallas_call(functools.partial(filter_kernel, factor, groups), out_shap...]
    ppermute x1, waiting for transfers between devices: 4.03 us -> 0.29 us  [body(): above = lax.ppermute(own, 'space', down)]
    ppermute x1, waiting for transfers between devices: 0.26 us -> 3.06 us  [body(): below = lax.ppermute(own, 'space', up)]
    unnamed x18 -> x12, local copies, waits for them, and re-layouts: 2.97 us -> 1.98 us
    ppermute x14 -> x17, starting transfers between devices: 18.9 us -> 18.4 us  [swapped(): return lax.ppermute(value, axis, [(i, i ^ mask) for i in range(count)])]
  transfers between devices with their start and end apart: 18 -> 21, of which waited for: 12 -> 11; matrix products, arithmetic and copies ran while one was open for 3% -> 4% of each run, Pallas kernels for 13% -> 8%
where the time goes in v2:
time: 87.4 us; the launch traced here: 87.1 us
  waiting for transfers between devices  40.6 us (46%)
  starting transfers between devices  31.1 us (36%)
  Pallas kernels  10.6 us (12%)
  local copies, waits for them, and re-layouts  3.43 us (4%)
  between operations  0.9 us (1%)
    ppermute x17, waiting for transfers between devices, swapped(): return lax.ppermute(value, axis, [(i, i ^ mask) for i in range(count)])  37.2 us
    ppermute x17, starting transfers between devices, swapped(): return lax.ppermute(value, axis, [(i, i ^ mask) for i in range(count)])  18.4 us
    ppermute x1, starting transfers between devices, body(): below = lax.ppermute(own, 'space', up)  5.48 us
    ppermute x1, starting transfers between devices, body(): lax.ppermute(to_above, 'space', up).astype(F32)  4.55 us
    pallas_call x1, Pallas kernels, filter_block(): pl.pallas_call(functools.partial(filter_kernel, factor, groups), out_shap...  4.54 us
    ppermute x1, waiting for transfers between devices, body(): below = lax.ppermute(own, 'space', up)  3.06 us
    pallas_call x1, Pallas kernels, join_blocks(): pl.pallas_call(functools.partial(join_kernel, share, chans), out_shape=[j...  2.45 us
    pallas_call x1, Pallas kernels, input_parts(): pl.pallas_call(functools.partial(input_kernel, chans, groups), out_shape=...  2.25 us
  transfers between devices with their start and end apart: 21, of which 11 were waited for; matrix products, arithmetic and copies ran while one was open for 4% of the time, Pallas kernels for 8%

profile of v2, /device:TPU:0, one launch (start us, length us, event | category | flops | bytes accessed | tf_op | source)
XLA Modules:
  0.0 87.1 jit_solution(11058968830434086510)
XLA Ops:
  0.6 1.4 %collective-permute-start.1 = (bf16[64,1024]{1,0:T(8,128)(2,1)}, bf16[64,1024]{1,0:T(8,128)(2,1)S(1)}, u32[]{:S(2)}, u32[]{:S(2)}) collective-permute-start(bf16[64,1024]{1,0:T(8,128)(2,1)} %bitcast.52), channel_id=1, source_target_pairs={{4,0},{8,4},{12,8},{16,12},{20,16},{24,20},{28,24},{5,1},{9,5},{13... | collective-permute-start | bytes 393224 | tf_op jit(solution)/shard_map/ppermute | solution.py:284
  2.1 5.5 %collective-permute-start = (bf16[64,1024]{1,0:T(8,128)(2,1)}, bf16[64,1024]{1,0:T(8,128)(2,1)S(1)}, u32[]{:S(2)}, u32[]{:S(2)}) collective-permute-start(bf16[64,1024]{1,0:T(8,128)(2,1)} %bitcast.53), channel_id=1, source_target_pairs={{0,4},{4,8},{8,12},{12,16},{16,20},{20,24},{24,28},{1,5},{5,9},{9,... | collective-permute-start | bytes 393224 | tf_op jit(solution)/shard_map/ppermute | solution.py:283
  7.6 1.5 %copy.13 = bf16[1728,256]{0,1:T(8,128)(2,1)S(1)} copy(bf16[1728,256]{1,0:T(8,128)(2,1)} %bitcast.50) | data formatting | bytes 1769472 | tf_op jit(solution)/shard_map/reshape | solution.py:285
  9.0 0.3 collective-permute-done.1.above
  9.3 3.1 %collective-permute-done.below = bf16[64,1024]{1,0:T(8,128)(2,1)S(1)} collective-permute-done((bf16[64,1024]{1,0:T(8,128)(2,1)}, bf16[64,1024]{1,0:T(8,128)(2,1)S(1)}, u32[]{:S(2)}, u32[]{:S(2)}) %collective-permute-start) | collective-permute-done | bytes 131104 | tf_op jit(solution)/shard_map/ppermute | solution.py:283
  12.4 1.4 %forward_parts.1 = (f32[2,64,1024]{2,1,0:T(8,128)S(1)}, f32[2,64,1024]{2,1,0:T(8,128)S(1)}) custom-call(s32[1]{0:T(128)} %bitcast.index, bf16[64,1024]{1,0:T(8,128)(2,1)S(1)} %bitcast.54, bf16[64,1024]{1,0:T(8,128)(2,1)S(1)} %collective-permute-done.below, bf16[64,1024]{1,0:T(8,128)(2,1)S(1)} %collective-permute-done.1.above, bf16[256,1728]{1,0:T(8,128)(2,1)S(1)} %bitcast.49), custom_call_target="tpu_custom_call" | custom-call | flops 905969664 | bytes 6291456 | tf_op jit(solution)/shard_map/forward_parts/pallas_call | solution.py:63
  13.9 3.7 %collective-permute-start.4 = (bf16[2,64,1024]{2,1,0:T(8,128)(2,1)S(1)}, bf16[2,64,1024]{2,1,0:T(8,128)(2,1)S(1)}, u32[]{:S(2)}, u32[]{:S(2)}) collective-permute-start(bf16[2,64,1024]{2,1,0:T(8,128)(2,1)S(1)} %pad_maximum_fusion.1), channel_id=1, source_target_pairs={{0,16},{4,20},{8,24},{12,28},{16,0},{20,4},{24,8},{28,12},{1,17},{... | collective-permute-start | bytes 786440 | tf_op jit(solution)/shard_map/ppermute | solution.py:254
  17.7 1.6 %collective-permute-start.3 = (f32[64,1024]{1,0:T(8,128)S(1)}, f32[64,1024]{1,0:T(8,128)S(1)}, u32[]{:S(2)}, u32[]{:S(2)}) collective-permute-start(f32[64,1024]{1,0:T(8,128)S(1)} %fusion), channel_id=1, source_target_pairs={{0,2},{1,3},{2,0},{3,1},{4,6},{5,7},{6,4},{7,5},{8,10},{9,11},{10,... | collective-permute-start | bytes 786440 | tf_op jit(solution)/shard_map/ppermute | solution.py:254
  19.3 11.0 %collective-permute-done.4 = bf16[2,64,1024]{2,1,0:T(8,128)(2,1)S(1)} collective-permute-done((bf16[2,64,1024]{2,1,0:T(8,128)(2,1)S(1)}, bf16[2,64,1024]{2,1,0:T(8,128)(2,1)S(1)}, u32[]{:S(2)}, u32[]{:S(2)}) %collective-permute-start.4) | collective-permute-done | bytes 262176 | tf_op jit(solution)/shard_map/ppermute | solution.py:254
  30.6 1.4 %collective-permute-start.5 = (bf16[2,16,1024]{2,1,0:T(8,128)(2,1)S(1)}, bf16[2,16,1024]{2,1,0:T(8,128)(2,1)S(1)}, u32[]{:S(2)}, u32[]{:S(2)}) collective-permute-start(bf16[2,16,1024]{2,1,0:T(8,128)(2,1)S(1)} %get-tuple-element.63), channel_id=1, source_target_pairs={{0,4},{4,0},{8,12},{12,8},{16,20},{20,16},{24,28},{28,24},{1,5},{5... | collective-permute-start | bytes 196616 | tf_op jit(solution)/shard_map/ppermute | solution.py:254
  32.0 1.5 %collective-permute-start.6 = (bf16[64,1024]{1,0:T(8,128)(2,1)S(1)}, bf16[64,1024]{1,0:T(8,128)(2,1)S(1)}, u32[]{:S(2)}, u32[]{:S(2)}) collective-permute-start(bf16[64,1024]{1,0:T(8,128)(2,1)S(1)} %get-tuple-element.35.refs_0_), channel_id=1, source_target_pairs={{0,2},{1,3},{2,0},{3,1},{4,6},{5,7},{6,4},{7,5},{8,10},{9,11},{10,... | collective-permute-start | bytes 393224 | tf_op jit(solution)/shard_map/ppermute | solution.py:254
  33.5 1.4 %collective-permute-done.5 = bf16[2,16,1024]{2,1,0:T(8,128)(2,1)S(1)} collective-permute-done((bf16[2,16,1024]{2,1,0:T(8,128)(2,1)S(1)}, bf16[2,16,1024]{2,1,0:T(8,128)(2,1)S(1)}, u32[]{:S(2)}, u32[]{:S(2)}) %collective-permute-start.5) | collective-permute-done | bytes 65568 | tf_op jit(solution)/shard_map/ppermute | solution.py:254
  35.0 2.0 %collective-permute-done.6.refs_2_ = bf16[64,1024]{1,0:T(8,128)(2,1)S(1)} collective-permute-done((bf16[64,1024]{1,0:T(8,128)(2,1)S(1)}, bf16[64,1024]{1,0:T(8,128)(2,1)S(1)}, u32[]{:S(2)}, u32[]{:S(2)}) %collective-permute-start.6) | collective-permute-done | bytes 131104 | tf_op jit(solution)/shard_map/ppermute | solution.py:254
  37.1 2.9 %collective-permute-start.9 = (bf16[2,16,1024]{2,1,0:T(8,128)(2,1)S(1)}, bf16[2,16,1024]{2,1,0:T(8,128)(2,1)S(1)}, u32[]{:S(2)}, u32[]{:S(2)}) collective-permute-start(bf16[2,16,1024]{2,1,0:T(8,128)(2,1)S(1)} %get-tuple-element.61), channel_id=1, source_target_pairs={{0,24},{4,28},{8,16},{12,20},{16,8},{20,12},{24,0},{28,4},{1,25},{... | collective-permute-start | bytes 196616 | tf_op jit(solution)/shard_map/ppermute | solution.py:254
  39.9 0.6 collective-permute-start.7
  40.5 6.6 %collective-permute-done.8 = bf16[2,16,1024]{2,1,0:T(8,128)(2,1)S(1)} collective-permute-done((bf16[2,16,1024]{2,1,0:T(8,128)(2,1)S(1)}, bf16[2,16,1024]{2,1,0:T(8,128)(2,1)S(1)}, u32[]{:S(2)}, u32[]{:S(2)}) %collective-permute-start.8) | collective-permute-done | bytes 65568 | tf_op jit(solution)/shard_map/ppermute | solution.py:254
  47.1 4.1 %collective-permute-done.9 = bf16[2,16,1024]{2,1,0:T(8,128)(2,1)S(1)} collective-permute-done((bf16[2,16,1024]{2,1,0:T(8,128)(2,1)S(1)}, bf16[2,16,1024]{2,1,0:T(8,128)(2,1)S(1)}, u32[]{:S(2)}, u32[]{:S(2)}) %collective-permute-start.9) | collective-permute-done | bytes 65568 | tf_op jit(solution)/shard_map/ppermute | solution.py:254
  51.3 0.6 collective-permute-start.13
  51.9 2.2 %input_parts.1 = (bf16[64,1024]{1,0:T(8,128)(2,1)S(1)}, f32[64,1024]{1,0:T(8,128)S(1)}, bf16[64,1024]{1,0:T(8,128)(2,1)S(1)}) custom-call(s32[1]{0:T(128)} %bitcast.index, bf16[64,1024]{1,0:T(8,128)(2,1)S(1)} %get-tuple-element.35.refs_0_, bf16[64,1024]{1,0:T(8,128)(2,1)S(1)} %collective-permute-done.11.refs_1_, ...), custom_call_target="tpu_custom_call" | custom-call | flops 905969664 | bytes 6291456 | tf_op jit(solution)/shard_map/input_parts/pallas_call | solution.py:106
  54.1 3.7 %collective-permute-done.13.refs_2_ = bf16[8,16,1024]{2,1,0:T(8,128)(2,1)S(1)} collective-permute-done((bf16[8,16,1024]{2,1,0:T(8,128)(2,1)S(1)}, bf16[8,16,1024]{2,1,0:T(8,128)(2,1)S(1)}, u32[]{:S(2)}, u32[]{:S(2)}) %collective-permute-start.13) | collective-permute-done | bytes 262176 | tf_op jit(solution)/shard_map/ppermute | solution.py:254
  57.8 0.5 collective-permute-start.17
  58.4 1.0 %copy.17 = f32[64,1,1024]{2,1,0:T(1,128)} copy(f32[64,1,1024]{2,0,1:T(8,128)S(1)} %get-tuple-element.59) | data formatting | bytes 524288
  59.4 1.3 %collective-permute-start.14 = (bf16[64,1024]{1,0:T(8,128)(2,1)S(1)}, bf16[64,1024]{1,0:T(8,128)(2,1)S(1)}, u32[]{:S(2)}, u32[]{:S(2)}) collective-permute-start(bf16[64,1024]{1,0:T(8,128)(2,1)S(1)} %get-tuple-element.43), channel_id=1, source_target_pairs={{4,0},{8,4},{12,8},{16,12},{20,16},{24,20},{28,24},{5,1},{9,5},{13... | collective-permute-start | bytes 393224 | tf_op jit(solution)/shard_map/ppermute | solution.py:334
  60.6 4.6 %collective-permute-start.15 = (bf16[64,1024]{1,0:T(8,128)(2,1)S(1)}, bf16[64,1024]{1,0:T(8,128)(2,1)S(1)}, u32[]{:S(2)}, u32[]{:S(2)}) collective-permute-start(bf16[64,1024]{1,0:T(8,128)(2,1)S(1)} %get-tuple-element.44), channel_id=1, source_target_pairs={{0,4},{4,8},{8,12},{12,16},{16,20},{20,24},{24,28},{1,5},{5,9},{9,... | collective-permute-start | bytes 393224 | tf_op jit(solution)/shard_map/ppermute | solution.py:335
  65.2 4.5 %filter_block.1.refs_0_ = bf16[896,128]{1,0:T(8,128)(2,1)S(1)} custom-call(s32[10]{0:T(128)S(1)} %pad_add_fusion.index, bf16[4,64,1024]{2,1,0:T(8,128)(2,1)S(1)} %pad_maximum_fusion.near, bf16[4,64,1024]{2,1,0:T(8,128)(2,1)S(1)} %collective-permute-done.10.far, bf16[8,16,1024]{2,1,0:T(8,128)(2,1)S(1)} %pad_maximum_fusion.2.refs_0_, ...), custom_call_target="tpu_custom_call" | custom-call | flops 1811939328 | bytes 8388608 | tf_op jit(solution)/shard_map/filter_block/pallas_call | solution.py:186
  69.8 4.8 %collective-permute-start.20 = (bf16[896,128]{1,0:T(8,128)(2,1)S(1)}, bf16[896,128]{1,0:T(8,128)(2,1)S(1)}, u32[]{:S(2)}, u32[]{:S(2)}) collective-permute-start(bf16[896,128]{1,0:T(8,128)(2,1)S(1)} %filter_block.1.refs_0_), channel_id=1, source_target_pairs={{0,12},{4,8},{8,4},{12,0},{16,28},{20,24},{24,20},{28,16},{1,13},{... | collective-permute-start | bytes 688136 | tf_op jit(solution)/shard_map/ppermute | solution.py:254
  74.6 0.6 collective-permute-start.18
  75.3 1.0 %copy.18 = f32[64,1,1024]{2,1,0:T(1,128)} copy(f32[64,1,1024]{2,0,1:T(8,128)S(1)} %add_bitcast_fusion) | data formatting | bytes 524288
  76.2 4.9 %collective-permute-done.20.refs_3_ = bf16[896,128]{1,0:T(8,128)(2,1)S(1)} collective-permute-done((bf16[896,128]{1,0:T(8,128)(2,1)S(1)}, bf16[896,128]{1,0:T(8,128)(2,1)S(1)}, u32[]{:S(2)}, u32[]{:S(2)}) %collective-permute-start.20) | collective-permute-done | bytes 229408 | tf_op jit(solution)/shard_map/ppermute | solution.py:254
  81.1 2.9 %collective-permute-done.19.refs_2_ = bf16[896,128]{1,0:T(8,128)(2,1)S(1)} collective-permute-done((bf16[896,128]{1,0:T(8,128)(2,1)S(1)}, bf16[896,128]{1,0:T(8,128)(2,1)S(1)}, u32[]{:S(2)}, u32[]{:S(2)}) %collective-permute-start.19) | collective-permute-done | bytes 229408 | tf_op jit(solution)/shard_map/ppermute | solution.py:254
  84.0 0.7 collective-permute-done.18.refs_1_
  84.7 2.4 %join_blocks.1 = (f32[27,64,256]{2,1,0:T(8,128)}, f32[1,256]{1,0:T(1,128)}) custom-call(s32[1]{0:T(128)} %bitcast.18.index, bf16[896,128]{1,0:T(8,128)(2,1)S(1)} %filter_block.1.refs_0_, bf16[896,128]{1,0:T(8,128)(2,1)S(1)} %collective-permute-done.18.refs_1_, bf16[896,128]{1,0:T(8,128)(2,1)S(1)} %collective-permute-done.19.refs_2_, ...), custom_call_target="tpu_custom_call" | custom-call | flops 452984832 | bytes 4194304 | tf_op jit(solution)/shard_map/join_blocks/pallas_call | solution.py:235
  (39 shorter events, 0.7 us)
Async XLA Ops:
  0.6 11.8 %copy-start.1 = (bf16[64,1,1024]{2,0,1:T(8,128)(2,1)S(1)}, bf16[64,1,1024]{2,0,1:T(8,128)(2,1)}, u32[]{:S(2)}) copy-start(bf16[64,1,1024]{2,0,1:T(8,128)(2,1)} %param.5) | copy-start | bytes 393220
  0.6 8.7 %collective-permute-start.1 = (bf16[64,1024]{1,0:T(8,128)(2,1)}, bf16[64,1024]{1,0:T(8,128)(2,1)S(1)}, u32[]{:S(2)}, u32[]{:S(2)}) collective-permute-start(bf16[64,1024]{1,0:T(8,128)(2,1)} %bitcast.52), channel_id=1, source_target_pairs={{4,0},{8,4},{12,8},{16,12},{20,16},{24,20},{28,24},{5,1},{9,5},{13... | collective-permute-start | bytes 393224 | tf_op jit(solution)/shard_map/ppermute | solution.py:284
  2.1 10.3 %collective-permute-start = (bf16[64,1024]{1,0:T(8,128)(2,1)}, bf16[64,1024]{1,0:T(8,128)(2,1)S(1)}, u32[]{:S(2)}, u32[]{:S(2)}) collective-permute-start(bf16[64,1024]{1,0:T(8,128)(2,1)} %bitcast.53), channel_id=1, source_target_pairs={{0,4},{4,8},{8,12},{12,16},{16,20},{20,24},{24,28},{1,5},{5,9},{9,... | collective-permute-start | bytes 393224 | tf_op jit(solution)/shard_map/ppermute | solution.py:283
  13.8 16.6 %copy-start.3 = (f32[64]{0:T(128)S(1)}, f32[64]{0:T(128)}, u32[]{:S(2)}) copy-start(f32[64]{0:T(128)} %param.7) | copy-start | bytes 772
  13.8 3.9 %collective-permute-start.2 = (f32[2,64,1024]{2,1,0:T(8,128)S(1)}, f32[2,64,1024]{2,1,0:T(8,128)S(1)}, u32[]{:S(2)}, u32[]{:S(2)}) collective-permute-start(f32[2,64,1024]{2,1,0:T(8,128)S(1)} %get-tuple-element.28), channel_id=1, source_target_pairs={{0,1},{1,0},{2,3},{3,2},{4,5},{5,4},{6,7},{7,6},{8,9},{9,8},{10,11... | collective-permute-start | bytes 1572872 | tf_op jit(solution)/shard_map/ppermute | solution.py:254
  13.9 16.6 %copy-start.2 = (bf16[64,1,1024]{2,0,1:T(8,128)(2,1)S(1)}, bf16[64,1,1024]{2,0,1:T(8,128)(2,1)}, u32[]{:S(2)}) copy-start(bf16[64,1,1024]{2,0,1:T(8,128)(2,1)} %param.8) | copy-start | bytes 393220
  13.9 16.3 %collective-permute-start.4 = (bf16[2,64,1024]{2,1,0:T(8,128)(2,1)S(1)}, bf16[2,64,1024]{2,1,0:T(8,128)(2,1)S(1)}, u32[]{:S(2)}, u32[]{:S(2)}) collective-permute-start(bf16[2,64,1024]{2,1,0:T(8,128)(2,1)S(1)} %pad_maximum_fusion.1), channel_id=1, source_target_pairs={{0,16},{4,20},{8,24},{12,28},{16,0},{20,4},{24,8},{28,12},{1,17},{... | collective-permute-start | bytes 786440 | tf_op jit(solution)/shard_map/ppermute | solution.py:254
  17.7 12.6 %collective-permute-start.3 = (f32[64,1024]{1,0:T(8,128)S(1)}, f32[64,1024]{1,0:T(8,128)S(1)}, u32[]{:S(2)}, u32[]{:S(2)}) collective-permute-start(f32[64,1024]{1,0:T(8,128)S(1)} %fusion), channel_id=1, source_target_pairs={{0,2},{1,3},{2,0},{3,1},{4,6},{5,7},{6,4},{7,5},{8,10},{9,11},{10,... | collective-permute-start | bytes 786440 | tf_op jit(solution)/shard_map/ppermute | solution.py:254
  30.3 21.5 %copy-start = (bf16[27,64,256]{2,1,0:T(8,128)(2,1)S(1)}, bf16[27,64,256]{2,1,0:T(8,128)(2,1)}, u32[]{:S(2)}) copy-start(bf16[27,64,256]{2,1,0:T(8,128)(2,1)} %refs_4_.1) | copy-start | bytes 2654212
  30.6 4.3 %collective-permute-start.5 = (bf16[2,16,1024]{2,1,0:T(8,128)(2,1)S(1)}, bf16[2,16,1024]{2,1,0:T(8,128)(2,1)S(1)}, u32[]{:S(2)}, u32[]{:S(2)}) collective-permute-start(bf16[2,16,1024]{2,1,0:T(8,128)(2,1)S(1)} %get-tuple-element.63), channel_id=1, source_target_pairs={{0,4},{4,0},{8,12},{12,8},{16,20},{20,16},{24,28},{28,24},{1,5},{5... | collective-permute-start | bytes 196616 | tf_op jit(solution)/shard_map/ppermute | solution.py:254
  32.0 5.0 %collective-permute-start.6 = (bf16[64,1024]{1,0:T(8,128)(2,1)S(1)}, bf16[64,1024]{1,0:T(8,128)(2,1)S(1)}, u32[]{:S(2)}, u32[]{:S(2)}) collective-permute-start(bf16[64,1024]{1,0:T(8,128)(2,1)S(1)} %get-tuple-element.35.refs_0_), channel_id=1, source_target_pairs={{0,2},{1,3},{2,0},{3,1},{4,6},{5,7},{6,4},{7,5},{8,10},{9,11},{10,... | collective-permute-start | bytes 393224 | tf_op jit(solution)/shard_map/ppermute | solution.py:254
  33.5 17.8 %collective-permute-start.10 = (bf16[4,64,1024]{2,1,0:T(8,128)(2,1)S(1)}, bf16[4,64,1024]{2,1,0:T(8,128)(2,1)S(1)}, u32[]{:S(2)}, u32[]{:S(2)}) collective-permute-start(bf16[4,64,1024]{2,1,0:T(8,128)(2,1)S(1)} %pad_maximum_fusion.near), channel_id=1, source_target_pairs={{0,8},{4,12},{8,0},{12,4},{16,24},{20,28},{24,16},{28,20},{1,9},{5... | collective-permute-start | bytes 1572872 | tf_op jit(solution)/shard_map/ppermute | solution.py:254
  37.0 10.1 %collective-permute-start.8 = (bf16[2,16,1024]{2,1,0:T(8,128)(2,1)S(1)}, bf16[2,16,1024]{2,1,0:T(8,128)(2,1)S(1)}, u32[]{:S(2)}, u32[]{:S(2)}) collective-permute-start(bf16[2,16,1024]{2,1,0:T(8,128)(2,1)S(1)} %get-tuple-element.60), channel_id=1, source_target_pairs={{0,16},{4,20},{8,24},{12,28},{16,0},{20,4},{24,8},{28,12},{1,17},{... | collective-permute-start | bytes 196616 | tf_op jit(solution)/shard_map/ppermute | solution.py:254
  37.1 14.1 %collective-permute-start.9 = (bf16[2,16,1024]{2,1,0:T(8,128)(2,1)S(1)}, bf16[2,16,1024]{2,1,0:T(8,128)(2,1)S(1)}, u32[]{:S(2)}, u32[]{:S(2)}) collective-permute-start(bf16[2,16,1024]{2,1,0:T(8,128)(2,1)S(1)} %get-tuple-element.61), channel_id=1, source_target_pairs={{0,24},{4,28},{8,16},{12,20},{16,8},{20,12},{24,0},{28,4},{1,25},{... | collective-permute-start | bytes 196616 | tf_op jit(solution)/shard_map/ppermute | solution.py:254
  39.9 11.3 %collective-permute-start.7 = (bf16[2,16,1024]{2,1,0:T(8,128)(2,1)S(1)}, bf16[2,16,1024]{2,1,0:T(8,128)(2,1)S(1)}, u32[]{:S(2)}, u32[]{:S(2)}) collective-permute-start(bf16[2,16,1024]{2,1,0:T(8,128)(2,1)S(1)} %get-tuple-element.61), channel_id=1, source_target_pairs={{0,8},{4,12},{8,0},{12,4},{16,24},{20,28},{24,16},{28,20},{1,9},{5... | collective-permute-start | bytes 196616 | tf_op jit(solution)/shard_map/ppermute | solution.py:254
  40.5 10.7 %collective-permute-start.11 = (bf16[64,1024]{1,0:T(8,128)(2,1)S(1)}, bf16[64,1024]{1,0:T(8,128)(2,1)S(1)}, u32[]{:S(2)}, u32[]{:S(2)}) collective-permute-start(bf16[64,1024]{1,0:T(8,128)(2,1)S(1)} %get-tuple-element.35.refs_0_), channel_id=1, source_target_pairs={{0,1},{1,0},{2,3},{3,2},{4,5},{5,4},{6,7},{7,6},{8,9},{9,8},{10,11... | collective-permute-start | bytes 393224 | tf_op jit(solution)/shard_map/ppermute | solution.py:254
  47.1 4.2 %collective-permute-start.12 = (bf16[64,1024]{1,0:T(8,128)(2,1)S(1)}, bf16[64,1024]{1,0:T(8,128)(2,1)S(1)}, u32[]{:S(2)}, u32[]{:S(2)}) collective-permute-start(bf16[64,1024]{1,0:T(8,128)(2,1)S(1)} %collective-permute-done.6.refs_2_), channel_id=1, source_target_pairs={{0,1},{1,0},{2,3},{3,2},{4,5},{5,4},{6,7},{7,6},{8,9},{9,8},{10,11... | collective-permute-start | bytes 393224 | tf_op jit(solution)/shard_map/ppermute | solution.py:254
  51.2 7.1 %copy-start.4 = (s32[8]{0:T(128)S(1)}, s32[8]{0:T(128)}, u32[]{:S(2)}) copy-start(s32[8]{0:T(128)} %constant.19.clone) | copy-start | bytes 100
  51.3 6.5 %collective-permute-start.13 = (bf16[8,16,1024]{2,1,0:T(8,128)(2,1)S(1)}, bf16[8,16,1024]{2,1,0:T(8,128)(2,1)S(1)}, u32[]{:S(2)}, u32[]{:S(2)}) collective-permute-start(bf16[8,16,1024]{2,1,0:T(8,128)(2,1)S(1)} %pad_maximum_fusion.2.refs_0_), channel_id=1, source_target_pairs={{0,2},{1,3},{2,0},{3,1},{4,6},{5,7},{6,4},{7,5},{8,10},{9,11},{10,... | collective-permute-start | bytes 786440 | tf_op jit(solution)/shard_map/ppermute | solution.py:254
  57.8 7.4 %collective-permute-start.16 = (bf16[8,16,1024]{2,1,0:T(8,128)(2,1)S(1)}, bf16[8,16,1024]{2,1,0:T(8,128)(2,1)S(1)}, u32[]{:S(2)}, u32[]{:S(2)}) collective-permute-start(bf16[8,16,1024]{2,1,0:T(8,128)(2,1)S(1)} %pad_maximum_fusion.2.refs_0_), channel_id=1, source_target_pairs={{0,1},{1,0},{2,3},{3,2},{4,5},{5,4},{6,7},{7,6},{8,9},{9,8},{10,11... | collective-permute-start | bytes 786440 | tf_op jit(solution)/shard_map/ppermute | solution.py:254
  57.8 7.4 %collective-permute-start.17 = (bf16[8,16,1024]{2,1,0:T(8,128)(2,1)S(1)}, bf16[8,16,1024]{2,1,0:T(8,128)(2,1)S(1)}, u32[]{:S(2)}, u32[]{:S(2)}) collective-permute-start(bf16[8,16,1024]{2,1,0:T(8,128)(2,1)S(1)} %collective-permute-done.13.refs_2_), channel_id=1, source_target_pairs={{0,1},{1,0},{2,3},{3,2},{4,5},{5,4},{6,7},{7,6},{8,9},{9,8},{10,11... | collective-permute-start | bytes 786440 | tf_op jit(solution)/shard_map/ppermute | solution.py:254
  59.4 15.8 %collective-permute-start.14 = (bf16[64,1024]{1,0:T(8,128)(2,1)S(1)}, bf16[64,1024]{1,0:T(8,128)(2,1)S(1)}, u32[]{:S(2)}, u32[]{:S(2)}) collective-permute-start(bf16[64,1024]{1,0:T(8,128)(2,1)S(1)} %get-tuple-element.43), channel_id=1, source_target_pairs={{4,0},{8,4},{12,8},{16,12},{20,16},{24,20},{28,24},{5,1},{9,5},{13... | collective-permute-start | bytes 393224 | tf_op jit(solution)/shard_map/ppermute | solution.py:334
  60.6 14.6 %collective-permute-start.15 = (bf16[64,1024]{1,0:T(8,128)(2,1)S(1)}, bf16[64,1024]{1,0:T(8,128)(2,1)S(1)}, u32[]{:S(2)}, u32[]{:S(2)}) collective-permute-start(bf16[64,1024]{1,0:T(8,128)(2,1)S(1)} %get-tuple-element.44), channel_id=1, source_target_pairs={{0,4},{4,8},{8,12},{12,16},{16,20},{20,24},{24,28},{1,5},{5,9},{9,... | collective-permute-start | bytes 393224 | tf_op jit(solution)/shard_map/ppermute | solution.py:335
  69.8 11.3 %collective-permute-start.20 = (bf16[896,128]{1,0:T(8,128)(2,1)S(1)}, bf16[896,128]{1,0:T(8,128)(2,1)S(1)}, u32[]{:S(2)}, u32[]{:S(2)}) collective-permute-start(bf16[896,128]{1,0:T(8,128)(2,1)S(1)} %filter_block.1.refs_0_), channel_id=1, source_target_pairs={{0,12},{4,8},{8,4},{12,0},{16,28},{20,24},{24,20},{28,16},{1,13},{... | collective-permute-start | bytes 688136 | tf_op jit(solution)/shard_map/ppermute | solution.py:254
  74.6 9.4 %collective-permute-start.19 = (bf16[896,128]{1,0:T(8,128)(2,1)S(1)}, bf16[896,128]{1,0:T(8,128)(2,1)S(1)}, u32[]{:S(2)}, u32[]{:S(2)}) collective-permute-start(bf16[896,128]{1,0:T(8,128)(2,1)S(1)} %filter_block.1.refs_0_), channel_id=1, source_target_pairs={{0,8},{4,12},{8,0},{12,4},{16,24},{20,28},{24,16},{28,20},{1,9},{5... | collective-permute-start | bytes 688136 | tf_op jit(solution)/shard_map/ppermute | solution.py:254
  74.6 10.1 %collective-permute-start.18 = (bf16[896,128]{1,0:T(8,128)(2,1)S(1)}, bf16[896,128]{1,0:T(8,128)(2,1)S(1)}, u32[]{:S(2)}, u32[]{:S(2)}) collective-permute-start(bf16[896,128]{1,0:T(8,128)(2,1)S(1)} %filter_block.1.refs_0_), channel_id=1, source_target_pairs={{0,4},{4,0},{8,12},{12,8},{16,20},{20,16},{24,28},{28,24},{1,5},{5... | collective-permute-start | bytes 688136 | tf_op jit(solution)/shard_map/ppermute | solution.py:254

commit v3 on v2

--- a/solution.py
+++ b/solution.py
@@ -120,25 +120,26 @@
     )(index, *grads, weights)
 
 
-def filter_kernel(factor, groups, index, near, far, *refs):
+def filter_kernel(factor, groups, index, own, partner, near, far, *refs):
     grads = refs[:groups]
     out, shifted, rows, total, sums = refs[groups:]
     planes, share, _ = grads[0].shape
-    chans = near.shape[1]
+    chans = own.shape[0]
     width = groups * share
     space, chan = index[0], index[1]
     edge = jnp.zeros((3 * chans, CELLS), BF16)
     shifted[0] = edge
     shifted[planes + 1] = edge
-    for part, first in ((near, 0), (far, planes // 2)):
-
-        def fill(q):
-            depth = space ^ index[2 + first + q]
-            cells = part[q]
-            for e in range(3):
-                shifted[depth + 1, e * chans : (e + 1) * chans, :] = moved(cells, 0, e - 1)
-
-        repeat(planes // 2, fill)
+
+    def place(depth, cells):
+        for e in range(3):
+            shifted[depth + 1, e * chans : (e + 1) * chans, :] = moved(cells, 0, e - 1)
+
+    count = planes // 2 - 1
+    place(space, own[...])
+    place(space ^ 1, partner[...])
+    repeat(count, lambda q: place(space ^ index[2 + q], near[q]))
+    repeat(count, lambda q: place(space ^ index[2 + count + q], far[q]))
     ones = jnp.ones((16, CELLS), BF16)
     contract = (((1,), (1,)), ((), ()))
     total[...] = jnp.zeros_like(total)
@@ -178,15 +179,15 @@
         )
 
 
-def filter_block(index, near, far, grads, factor):
-    half, chans, _ = near.shape
+def filter_block(index, own, partner, near, far, grads, factor):
+    chans = own.shape[0]
     groups = len(grads)
     planes, share, _ = grads[0].shape
     width = groups * share
     return pl.pallas_call(
         functools.partial(filter_kernel, factor, groups),
         out_shape=jax.ShapeDtypeStruct(((TAPS + 1) // 2 * chans, 2 * width), BF16),
-        in_specs=[SMEM] + [VMEM] * (2 + groups),
+        in_specs=[SMEM] + [VMEM] * (4 + groups),
         out_specs=VMEM,
         scratch_shapes=[
             pltpu.VMEM((planes + 2, 3 * chans, CELLS), BF16),
@@ -201,7 +202,7 @@
             transcendentals=0,
         ),
         name="filter_block",
-    )(index, near, far, *grads)
+    )(index, own, partner, near, far, *grads)
 
 
 def join_kernel(share, chans, index, *refs):
@@ -273,7 +274,7 @@
     space = lax.axis_index("space")
     chan = lax.axis_index("chan")
     share = chans // 4
-    high_masks = [1 << k for k in range(depth.bit_length() - 2, 0, -1)]
+    masks = [1 << k for k in range(depth.bit_length() - 2, -1, -1)]
     factor = 1.0 / math.sqrt(cells * planes * depth)
     barrier = lax.optimization_barrier
 
@@ -282,23 +283,23 @@
     down = [(i + 1, i) for i in range(depth - 1)]
     below = lax.ppermute(own, "space", up)
     above = lax.ppermute(own, "space", down)
+    near = [swapped(own, "space", mask) for mask in masks[:2]]
+    below, above, near = barrier((below, above, near))
     weights = filters.reshape(TAPS * chans, total_out)
     keep, give = forward_parts(chan.reshape(1), own, below, above, weights.T)
 
-    side = space & 1
-    near = jnp.stack([own, jnp.where(side == 0, above, below)], axis=0)
-    flips = [0, 1]
-    for mask in high_masks[:-1]:
-        near = jnp.concatenate([near, swapped(near, "space", mask)], axis=0)
-        flips = flips + [f ^ mask for f in flips]
-
     got = swapped(give, "chan", 1)
+    partial = [keep[j] + got[j] for j in range(1, groups // 2)]
     pre_act = keep[0] + got[0] + out_bias[:, None]
-    for j in range(1, groups // 2):
-        pre_act = pre_act + swapped(keep[j] + got[j], "chan", 2 * j)
+    for j, term in enumerate(partial):
+        pre_act = pre_act + swapped(term, "chan", 2 * (j + 1))
     pre_act, near = barrier((pre_act, near))
-    far = swapped(near, "space", high_masks[-1])
-    flips = flips + [f ^ high_masks[-1] for f in flips]
+    near = jnp.stack(near + [swapped(near[0], "space", masks[1])], axis=0)
+    flips = [masks[0], masks[1], masks[0] ^ masks[1]]
+    for mask in masks[2:-1]:
+        own_too = jnp.concatenate([own[None], near], axis=0)
+        near = jnp.concatenate([near, swapped(own_too, "space", mask)], axis=0)
+        flips = flips + [f ^ mask for f in [0] + flips]
 
     sigmoid = jax.nn.sigmoid(pre_act)
     activated = pre_act * sigmoid
@@ -309,34 +310,33 @@
     ).astype(BF16)
 
     split = grad_pre.reshape(2, 2, share, cells)
+    side = space & 1
     kept = jnp.where(side == 0, split[:, 0], split[:, 1])
     given = jnp.where(side == 0, split[:, 1], split[:, 0])
     pair = jnp.stack([kept, swapped(given, "space", 1)], axis=0)
-    pair, grads = barrier((pair, other_chips(grad_pre)))
-    grads = both_cores(grads)
+    pair, near = barrier((pair, near))
+    far = swapped(near, "space", masks[-1])
+    flips = flips + [f ^ 1 for f in flips]
+    partner = jnp.where(side == 0, above, below)
     side = (space >> 1) & 1
     kept = jnp.where(side == 0, pair[:, 0], pair[:, 1])
     given = jnp.where(side == 0, pair[:, 1], pair[:, 0])
     pieces = [kept]
     for t in range(1, depth // 2):
         pieces.append(swapped(given if t & 1 else kept, "space", 2 * t))
-    block = jnp.concatenate(pieces, axis=0)
-
-    block, far, grads = barrier((block, far, grads))
-    to_below, in_own, to_above = input_parts(chan.reshape(1), grads, filters)
-
-    blocks, to_below, in_own, to_above = barrier(
-        (other_chips(block), to_below, in_own, to_above)
-    )
+
+    grads = both_cores(other_chips(grad_pre))
+    terms = input_parts(chan.reshape(1), grads, filters)
+    pieces[0], (to_below, in_own, to_above) = barrier((pieces[0], terms))
+    from_above = lax.ppermute(to_below, "space", down)
+    from_below = lax.ppermute(to_above, "space", up)
+    blocks = other_chips(jnp.concatenate(pieces, axis=0))
+    blocks, far, from_above, from_below = barrier((blocks, far, from_above, from_below))
     blocks = both_cores(blocks)
-    in_grad = (
-        in_own
-        + lax.ppermute(to_below, "space", down).astype(F32)
-        + lax.ppermute(to_above, "space", up).astype(F32)
-    )
+    in_grad = in_own + from_above.astype(F32) + from_below.astype(F32)
 
     index = jnp.concatenate([space.reshape(1), chan.reshape(1), jnp.array(flips, jnp.int32)])
-    part = filter_block(index, near, far, blocks, factor)
+    part = filter_block(index, own, partner, near, far, blocks, factor)
     parts = [part] + [swapped(part, "space", r) for r in range(1, 4)]
     joined, bias = join_blocks((space & 3).reshape(1), parts, share, chans)
     return (

time: 87.4 us -> 80.2 us (0.918)
  waiting for transfers between devices: 40.6 us -> 28 us
  starting transfers between devices: 31.1 us -> 36.7 us
    ppermute x17 -> x19, waiting for transfers between devices: 37.2 us -> 22 us  [swapped(): return lax.ppermute(value, axis, [(i, i ^ mask) for i in range(count)])]
    ppermute x17 -> x19, starting transfers between devices: 18.4 us -> 25 us  [swapped(): return lax.ppermute(value, axis, [(i, i ^ mask) for i in range(count)])]
    ppermute x2, waiting for transfers between devices: 0.01 us -> 3.57 us  [the longest x1 2.16 us: body(): from_above = lax.ppermute(to_below, 'space', down)]
    ppermute x1, starting transfers between devices: 5.48 us -> 4.55 us  [body(): below = lax.ppermute(own, 'space', up)]
    unnamed x12 -> x15, local copies, waits for them, and re-layouts: 1.98 us -> 1.99 us
  transfers between devices with their start and end apart: 21 -> 23, of which waited for: 11 -> 11; matrix products, arithmetic and copies ran while one was open for 4% -> 5% of each run, Pallas kernels for 8% -> 3%
where the time goes in v3:
time: 80.2 us; the launch traced here: 80 us
  starting transfers between devices  36.7 us (46%)
  waiting for transfers between devices  28 us (35%)
  Pallas kernels  10.6 us (13%)
  local copies, waits for them, and re-layouts  3.45 us (4%)
  between operations  0.85 us (1%)
    ppermute x19, starting transfers between devices, swapped(): return lax.ppermute(value, axis, [(i, i ^ mask) for i in range(count)])  25 us
    ppermute x19, waiting for transfers between devices, swapped(): return lax.ppermute(value, axis, [(i, i ^ mask) for i in range(count)])  22 us
    ppermute x1, starting transfers between devices, body(): from_below = lax.ppermute(to_above, 'space', up)  4.55 us
    ppermute x1, starting transfers between devices, body(): below = lax.ppermute(own, 'space', up)  4.55 us
    pallas_call x1, Pallas kernels, filter_block(): pl.pallas_call(functools.partial(filter_kernel, factor, groups), out_shap...  4.51 us
    pallas_call x1, Pallas kernels, join_blocks(): pl.pallas_call(functools.partial(join_kernel, share, chans), out_shape=[j...  2.45 us
    ppermute x1, waiting for transfers between devices, body(): below = lax.ppermute(own, 'space', up)  2.38 us
    pallas_call x1, Pallas kernels, input_parts(): pl.pallas_call(functools.partial(input_kernel, chans, groups), out_shape=...  2.25 us
  transfers between devices with their start and end apart: 23, of which 11 were waited for; matrix products, arithmetic and copies ran while one was open for 5% of the time, Pallas kernels for 3%

profile of v3, /device:TPU:0, one launch (start us, length us, event | category | flops | bytes accessed | tf_op | source)
XLA Modules:
  0.0 80.0 jit_solution(303185849030712788)
XLA Ops:
  0.6 3.1 %collective-permute-start.3 = (bf16[64,1024]{1,0:T(8,128)(2,1)}, bf16[64,1024]{1,0:T(8,128)(2,1)S(1)}, u32[]{:S(2)}, u32[]{:S(2)}) collective-permute-start(bf16[64,1024]{1,0:T(8,128)(2,1)} %bitcast.52), channel_id=1, source_target_pairs={{0,8},{4,12},{8,0},{12,4},{16,24},{20,28},{24,16},{28,20},{1,9},{5... | collective-permute-start | bytes 393224 | tf_op jit(solution)/shard_map/ppermute | solution.py:255
  3.7 2.6 %collective-permute-start.2 = (bf16[64,1024]{1,0:T(8,128)(2,1)}, bf16[64,1024]{1,0:T(8,128)(2,1)S(1)}, u32[]{:S(2)}, u32[]{:S(2)}) collective-permute-start(bf16[64,1024]{1,0:T(8,128)(2,1)} %bitcast.53), channel_id=1, source_target_pairs={{0,16},{4,20},{8,24},{12,28},{16,0},{20,4},{24,8},{28,12},{1,17},{... | collective-permute-start | bytes 393224 | tf_op jit(solution)/shard_map/ppermute | solution.py:255
  6.3 1.3 %collective-permute-start.1 = (bf16[64,1024]{1,0:T(8,128)(2,1)}, bf16[64,1024]{1,0:T(8,128)(2,1)S(1)}, u32[]{:S(2)}, u32[]{:S(2)}) collective-permute-start(bf16[64,1024]{1,0:T(8,128)(2,1)} %bitcast.54), channel_id=1, source_target_pairs={{4,0},{8,4},{12,8},{16,12},{20,16},{24,20},{28,24},{5,1},{9,5},{13... | collective-permute-start | bytes 393224 | tf_op jit(solution)/shard_map/ppermute | solution.py:285
  7.6 4.6 %collective-permute-start = (bf16[64,1024]{1,0:T(8,128)(2,1)}, bf16[64,1024]{1,0:T(8,128)(2,1)S(1)}, u32[]{:S(2)}, u32[]{:S(2)}) collective-permute-start(bf16[64,1024]{1,0:T(8,128)(2,1)} %bitcast.55), channel_id=1, source_target_pairs={{0,4},{4,8},{8,12},{12,16},{16,20},{20,24},{24,28},{1,5},{5,9},{9,... | collective-permute-start | bytes 393224 | tf_op jit(solution)/shard_map/ppermute | solution.py:284
  12.2 1.5 %copy.13 = bf16[1728,256]{0,1:T(8,128)(2,1)S(1)} copy(bf16[1728,256]{1,0:T(8,128)(2,1)} %bitcast.50) | data formatting | bytes 1769472 | tf_op jit(solution)/shard_map/reshape | solution.py:288
  13.7 2.4 %collective-permute-done.below = bf16[64,1024]{1,0:T(8,128)(2,1)S(1)} collective-permute-done((bf16[64,1024]{1,0:T(8,128)(2,1)}, bf16[64,1024]{1,0:T(8,128)(2,1)S(1)}, u32[]{:S(2)}, u32[]{:S(2)}) %collective-permute-start) | collective-permute-done | bytes 131104 | tf_op jit(solution)/shard_map/ppermute | solution.py:284
  16.0 1.4 %forward_parts.1 = (f32[2,64,1024]{2,1,0:T(8,128)S(1)}, f32[2,64,1024]{2,1,0:T(8,128)S(1)}) custom-call(s32[1]{0:T(128)} %bitcast.index, bf16[64,1024]{1,0:T(8,128)(2,1)S(1)} %bitcast.56, bf16[64,1024]{1,0:T(8,128)(2,1)S(1)} %collective-permute-done.below, bf16[64,1024]{1,0:T(8,128)(2,1)S(1)} %collective-permute-done.1.above, bf16[256,1728]{1,0:T(8,128)(2,1)S(1)} %bitcast.49), custom_call_target="tpu_custom_call" | custom-call | flops 905969664 | bytes 6291456 | tf_op jit(solution)/shard_map/forward_parts/pallas_call | solution.py:63
  17.5 1.9 %collective-permute-done.4 = f32[2,64,1024]{2,1,0:T(8,128)S(1)} collective-permute-done((f32[2,64,1024]{2,1,0:T(8,128)S(1)}, f32[2,64,1024]{2,1,0:T(8,128)S(1)}, u32[]{:S(2)}, u32[]{:S(2)}) %collective-permute-start.4) | collective-permute-done | bytes 524320 | tf_op jit(solution)/shard_map/ppermute | solution.py:255
  19.5 1.6 %collective-permute-start.5 = (f32[64,1024]{1,0:T(8,128)S(1)}, f32[64,1024]{1,0:T(8,128)S(1)}, u32[]{:S(2)}, u32[]{:S(2)}) collective-permute-start(f32[64,1024]{1,0:T(8,128)S(1)} %fusion), channel_id=1, source_target_pairs={{0,2},{1,3},{2,0},{3,1},{4,6},{5,7},{6,4},{7,5},{8,10},{9,11},{10,... | collective-permute-start | bytes 786440 | tf_op jit(solution)/shard_map/ppermute | solution.py:255
  21.0 6.8 %collective-permute-done.5 = f32[64,1024]{1,0:T(8,128)S(1)} collective-permute-done((f32[64,1024]{1,0:T(8,128)S(1)}, f32[64,1024]{1,0:T(8,128)S(1)}, u32[]{:S(2)}, u32[]{:S(2)}) %collective-permute-start.5) | collective-permute-done | bytes 262176 | tf_op jit(solution)/shard_map/ppermute | solution.py:255
  28.1 2.4 %collective-permute-start.6 = (bf16[2,16,1024]{2,1,0:T(8,128)(2,1)S(1)}, bf16[2,16,1024]{2,1,0:T(8,128)(2,1)S(1)}, u32[]{:S(2)}, u32[]{:S(2)}) collective-permute-start(bf16[2,16,1024]{2,1,0:T(8,128)(2,1)S(1)} %get-tuple-element.67), channel_id=1, source_target_pairs={{0,4},{4,0},{8,12},{12,8},{16,20},{20,16},{24,28},{28,24},{1,5},{5... | collective-permute-start | bytes 196616 | tf_op jit(solution)/shard_map/ppermute | solution.py:255
  30.6 1.7 %collective-permute-start.7 = (bf16[64,1024]{1,0:T(8,128)(2,1)S(1)}, bf16[64,1024]{1,0:T(8,128)(2,1)S(1)}, u32[]{:S(2)}, u32[]{:S(2)}) collective-permute-start(bf16[64,1024]{1,0:T(8,128)(2,1)S(1)} %collective-permute-done.2), channel_id=1, source_target_pairs={{0,8},{4,12},{8,0},{12,4},{16,24},{20,28},{24,16},{28,20},{1,9},{5... | collective-permute-start | bytes 393224 | tf_op jit(solution)/shard_map/ppermute | solution.py:255
  32.2 1.5 %collective-permute-start.9 = (bf16[64,1024]{1,0:T(8,128)(2,1)S(1)}, bf16[64,1024]{1,0:T(8,128)(2,1)S(1)}, u32[]{:S(2)}, u32[]{:S(2)}) collective-permute-start(bf16[64,1024]{1,0:T(8,128)(2,1)S(1)} %get-tuple-element.62.refs_0_), channel_id=1, source_target_pairs={{0,2},{1,3},{2,0},{3,1},{4,6},{5,7},{6,4},{7,5},{8,10},{9,11},{10,... | collective-permute-start | bytes 393224 | tf_op jit(solution)/shard_map/ppermute | solution.py:255
  33.8 1.8 %collective-permute-done.7 = bf16[64,1024]{1,0:T(8,128)(2,1)S(1)} collective-permute-done((bf16[64,1024]{1,0:T(8,128)(2,1)S(1)}, bf16[64,1024]{1,0:T(8,128)(2,1)S(1)}, u32[]{:S(2)}, u32[]{:S(2)}) %collective-permute-start.7) | collective-permute-done | bytes 131104 | tf_op jit(solution)/shard_map/ppermute | solution.py:255
  35.6 1.6 %collective-permute-done.9.refs_2_ = bf16[64,1024]{1,0:T(8,128)(2,1)S(1)} collective-permute-done((bf16[64,1024]{1,0:T(8,128)(2,1)S(1)}, bf16[64,1024]{1,0:T(8,128)(2,1)S(1)}, u32[]{:S(2)}, u32[]{:S(2)}) %collective-permute-start.9) | collective-permute-done | bytes 131104 | tf_op jit(solution)/shard_map/ppermute | solution.py:255
  37.2 1.2 %collective-permute-start.13 = (bf16[2,16,1024]{2,1,0:T(8,128)(2,1)S(1)}, bf16[2,16,1024]{2,1,0:T(8,128)(2,1)S(1)}, u32[]{:S(2)}, u32[]{:S(2)}) collective-permute-start(bf16[2,16,1024]{2,1,0:T(8,128)(2,1)S(1)} %get-tuple-element.64), channel_id=1, source_target_pairs={{0,24},{4,28},{8,16},{12,20},{16,8},{20,12},{24,0},{28,4},{1,25},{... | collective-permute-start | bytes 196616 | tf_op jit(solution)/shard_map/ppermute | solution.py:255
  38.5 3.2 %collective-permute-start.12 = (bf16[2,16,1024]{2,1,0:T(8,128)(2,1)S(1)}, bf16[2,16,1024]{2,1,0:T(8,128)(2,1)S(1)}, u32[]{:S(2)}, u32[]{:S(2)}) collective-permute-start(bf16[2,16,1024]{2,1,0:T(8,128)(2,1)S(1)} %get-tuple-element.43), channel_id=1, source_target_pairs={{0,16},{4,20},{8,24},{12,28},{16,0},{20,4},{24,8},{28,12},{1,17},{... | collective-permute-start | bytes 196616 | tf_op jit(solution)/shard_map/ppermute | solution.py:255
  41.7 1.1 %collective-permute-start.15 = (bf16[3,64,1024]{2,1,0:T(8,128)(2,1)S(1)}, bf16[3,64,1024]{2,1,0:T(8,128)(2,1)S(1)}, u32[]{:S(2)}, u32[]{:S(2)}) collective-permute-start(bf16[3,64,1024]{2,1,0:T(8,128)(2,1)S(1)} %pad_maximum_fusion.near), channel_id=1, source_target_pairs={{0,4},{4,0},{8,12},{12,8},{16,20},{20,16},{24,28},{28,24},{1,5},{5... | collective-permute-start | bytes 1179656 | tf_op jit(solution)/shard_map/ppermute | solution.py:255
  42.8 2.2 %input_parts.1 = (bf16[64,1024]{1,0:T(8,128)(2,1)S(1)}, f32[64,1024]{1,0:T(8,128)S(1)}, bf16[64,1024]{1,0:T(8,128)(2,1)S(1)}) custom-call(s32[1]{0:T(128)} %bitcast.index, bf16[64,1024]{1,0:T(8,128)(2,1)S(1)} %get-tuple-element.62.refs_0_, bf16[64,1024]{1,0:T(8,128)(2,1)S(1)} %collective-permute-done.8.refs_1_, ...), custom_call_target="tpu_custom_call" | custom-call | flops 905969664 | bytes 6291456 | tf_op jit(solution)/shard_map/input_parts/pallas_call | solution.py:106
  45.6 1.6 %collective-permute-start.14 = (bf16[8,16,1024]{2,1,0:T(8,128)(2,1)S(1)}, bf16[8,16,1024]{2,1,0:T(8,128)(2,1)S(1)}, u32[]{:S(2)}, u32[]{:S(2)}) collective-permute-start(bf16[8,16,1024]{2,1,0:T(8,128)(2,1)S(1)} %constant_dynamic-update-slice_fusion.refs_0_), channel_id=1, source_target_pairs={{0,2},{1,3},{2,0},{3,1},{4,6},{5,7},{6,4},{7,5},{8,10},{9,11},{10,... | collective-permute-start | bytes 786440 | tf_op jit(solution)/shard_map/ppermute | solution.py:255
  47.2 1.3 %collective-permute-start.16 = (bf16[64,1024]{1,0:T(8,128)(2,1)S(1)}, bf16[64,1024]{1,0:T(8,128)(2,1)S(1)}, u32[]{:S(2)}, u32[]{:S(2)}) collective-permute-start(bf16[64,1024]{1,0:T(8,128)(2,1)S(1)} %get-tuple-element.45), channel_id=1, source_target_pairs={{4,0},{8,4},{12,8},{16,12},{20,16},{24,20},{28,24},{5,1},{9,5},{13... | collective-permute-start | bytes 393224 | tf_op jit(solution)/shard_map/ppermute | solution.py:331
  48.5 4.6 %collective-permute-start.17 = (bf16[64,1024]{1,0:T(8,128)(2,1)S(1)}, bf16[64,1024]{1,0:T(8,128)(2,1)S(1)}, u32[]{:S(2)}, u32[]{:S(2)}) collective-permute-start(bf16[64,1024]{1,0:T(8,128)(2,1)S(1)} %get-tuple-element.46), channel_id=1, source_target_pairs={{0,4},{4,8},{8,12},{12,16},{16,20},{20,24},{24,28},{1,5},{5,9},{9,... | collective-permute-start | bytes 393224 | tf_op jit(solution)/shard_map/ppermute | solution.py:332
  53.0 2.2 %collective-permute-done.16 = bf16[64,1024]{1,0:T(8,128)(2,1)S(1)} collective-permute-done((bf16[64,1024]{1,0:T(8,128)(2,1)S(1)}, bf16[64,1024]{1,0:T(8,128)(2,1)S(1)}, u32[]{:S(2)}, u32[]{:S(2)}) %collective-permute-start.16) | collective-permute-done | bytes 131104 | tf_op jit(solution)/shard_map/ppermute | solution.py:331
  55.2 1.4 %collective-permute-done.17 = bf16[64,1024]{1,0:T(8,128)(2,1)S(1)} collective-permute-done((bf16[64,1024]{1,0:T(8,128)(2,1)S(1)}, bf16[64,1024]{1,0:T(8,128)(2,1)S(1)}, u32[]{:S(2)}, u32[]{:S(2)}) %collective-permute-start.17) | collective-permute-done | bytes 131104 | tf_op jit(solution)/shard_map/ppermute | solution.py:332
  57.2 1.0 %copy.17 = f32[64,1,1024]{2,1,0:T(1,128)} copy(f32[64,1,1024]{2,0,1:T(8,128)S(1)} %get-tuple-element.63) | data formatting | bytes 524288
  58.5 4.5 %filter_block.1.refs_0_ = bf16[896,128]{1,0:T(8,128)(2,1)S(1)} custom-call(s32[8]{0:T(128)S(1)} %pad_add_fusion.index, bf16[64,1024]{1,0:T(8,128)(2,1)S(1)} %bitcast.57, bf16[64,1024]{1,0:T(8,128)(2,1)S(1)} %broadcast_select_fusion.partner, bf16[3,64,1024]{2,1,0:T(8,128)(2,1)S(1)} %pad_maximum_fusion.near, ...), custom_call_target="tpu_custom_call" | custom-call | flops 1811939328 | bytes 8388608 | tf_op jit(solution)/shard_map/filter_block/pallas_call | solution.py:187
  63.0 3.1 %collective-permute-start.22 = (bf16[896,128]{1,0:T(8,128)(2,1)S(1)}, bf16[896,128]{1,0:T(8,128)(2,1)S(1)}, u32[]{:S(2)}, u32[]{:S(2)}) collective-permute-start(bf16[896,128]{1,0:T(8,128)(2,1)S(1)} %filter_block.1.refs_0_), channel_id=1, source_target_pairs={{0,12},{4,8},{8,4},{12,0},{16,28},{20,24},{24,20},{28,16},{1,13},{... | collective-permute-start | bytes 688136 | tf_op jit(solution)/shard_map/ppermute | solution.py:255
  66.2 0.8 %collective-permute-start.21 = (bf16[896,128]{1,0:T(8,128)(2,1)S(1)}, bf16[896,128]{1,0:T(8,128)(2,1)S(1)}, u32[]{:S(2)}, u32[]{:S(2)}) collective-permute-start(bf16[896,128]{1,0:T(8,128)(2,1)S(1)} %filter_block.1.refs_0_), channel_id=1, source_target_pairs={{0,8},{4,12},{8,0},{12,4},{16,24},{20,28},{24,16},{28,20},{1,9},{5... | collective-permute-start | bytes 688136 | tf_op jit(solution)/shard_map/ppermute | solution.py:255
  67.5 1.0 %copy.18 = f32[64,1,1024]{2,1,0:T(1,128)} copy(f32[64,1,1024]{2,0,1:T(8,128)S(1)} %add_bitcast_fusion) | data formatting | bytes 524288
  68.5 4.1 %collective-permute-done.22.refs_3_ = bf16[896,128]{1,0:T(8,128)(2,1)S(1)} collective-permute-done((bf16[896,128]{1,0:T(8,128)(2,1)S(1)}, bf16[896,128]{1,0:T(8,128)(2,1)S(1)}, u32[]{:S(2)}, u32[]{:S(2)}) %collective-permute-start.22) | collective-permute-done | bytes 229408 | tf_op jit(solution)/shard_map/ppermute | solution.py:255
  72.6 5.0 %collective-permute-done.21.refs_2_ = bf16[896,128]{1,0:T(8,128)(2,1)S(1)} collective-permute-done((bf16[896,128]{1,0:T(8,128)(2,1)S(1)}, bf16[896,128]{1,0:T(8,128)(2,1)S(1)}, u32[]{:S(2)}, u32[]{:S(2)}) %collective-permute-start.21) | collective-permute-done | bytes 229408 | tf_op jit(solution)/shard_map/ppermute | solution.py:255
  77.6 2.5 %join_blocks.1 = (f32[27,64,256]{2,1,0:T(8,128)}, f32[1,256]{1,0:T(1,128)}) custom-call(s32[1]{0:T(128)} %bitcast.19.index, bf16[896,128]{1,0:T(8,128)(2,1)S(1)} %filter_block.1.refs_0_, bf16[896,128]{1,0:T(8,128)(2,1)S(1)} %collective-permute-done.20.refs_1_, bf16[896,128]{1,0:T(8,128)(2,1)S(1)} %collective-permute-done.21.refs_2_, ...), custom_call_target="tpu_custom_call" | custom-call | flops 452984832 | bytes 4194304 | tf_op jit(solution)/shard_map/join_blocks/pallas_call | solution.py:236
  (45 shorter events, 2.4 us)
Async XLA Ops:
  0.6 15.4 %copy-start.1 = (bf16[64,1,1024]{2,0,1:T(8,128)(2,1)S(1)}, bf16[64,1,1024]{2,0,1:T(8,128)(2,1)}, u32[]{:S(2)}) copy-start(bf16[64,1,1024]{2,0,1:T(8,128)(2,1)} %param.5) | copy-start | bytes 393220
  0.6 13.0 %collective-permute-start.3 = (bf16[64,1024]{1,0:T(8,128)(2,1)}, bf16[64,1024]{1,0:T(8,128)(2,1)S(1)}, u32[]{:S(2)}, u32[]{:S(2)}) collective-permute-start(bf16[64,1024]{1,0:T(8,128)(2,1)} %bitcast.52), channel_id=1, source_target_pairs={{0,8},{4,12},{8,0},{12,4},{16,24},{20,28},{24,16},{28,20},{1,9},{5... | collective-permute-start | bytes 393224 | tf_op jit(solution)/shard_map/ppermute | solution.py:255
  3.7 9.9 %collective-permute-start.2 = (bf16[64,1024]{1,0:T(8,128)(2,1)}, bf16[64,1024]{1,0:T(8,128)(2,1)S(1)}, u32[]{:S(2)}, u32[]{:S(2)}) collective-permute-start(bf16[64,1024]{1,0:T(8,128)(2,1)} %bitcast.53), channel_id=1, source_target_pairs={{0,16},{4,20},{8,24},{12,28},{16,0},{20,4},{24,8},{28,12},{1,17},{... | collective-permute-start | bytes 393224 | tf_op jit(solution)/shard_map/ppermute | solution.py:255
  6.3 7.3 %collective-permute-start.1 = (bf16[64,1024]{1,0:T(8,128)(2,1)}, bf16[64,1024]{1,0:T(8,128)(2,1)S(1)}, u32[]{:S(2)}, u32[]{:S(2)}) collective-permute-start(bf16[64,1024]{1,0:T(8,128)(2,1)} %bitcast.54), channel_id=1, source_target_pairs={{4,0},{8,4},{12,8},{16,12},{20,16},{24,20},{28,24},{5,1},{9,5},{13... | collective-permute-start | bytes 393224 | tf_op jit(solution)/shard_map/ppermute | solution.py:285
  7.6 8.4 %collective-permute-start = (bf16[64,1024]{1,0:T(8,128)(2,1)}, bf16[64,1024]{1,0:T(8,128)(2,1)S(1)}, u32[]{:S(2)}, u32[]{:S(2)}) collective-permute-start(bf16[64,1024]{1,0:T(8,128)(2,1)} %bitcast.55), channel_id=1, source_target_pairs={{0,4},{4,8},{8,12},{12,16},{16,20},{20,24},{24,28},{1,5},{5,9},{9,... | collective-permute-start | bytes 393224 | tf_op jit(solution)/shard_map/ppermute | solution.py:284
  16.0 11.8 %copy-start.3 = (f32[64]{0:T(128)S(1)}, f32[64]{0:T(128)}, u32[]{:S(2)}) copy-start(f32[64]{0:T(128)} %param.7) | copy-start | bytes 772
  16.0 11.9 %copy-start.2 = (bf16[64,1,1024]{2,0,1:T(8,128)(2,1)S(1)}, bf16[64,1,1024]{2,0,1:T(8,128)(2,1)}, u32[]{:S(2)}) copy-start(bf16[64,1,1024]{2,0,1:T(8,128)(2,1)} %param.8) | copy-start | bytes 393220
  17.4 2.0 %collective-permute-start.4 = (f32[2,64,1024]{2,1,0:T(8,128)S(1)}, f32[2,64,1024]{2,1,0:T(8,128)S(1)}, u32[]{:S(2)}, u32[]{:S(2)}) collective-permute-start(f32[2,64,1024]{2,1,0:T(8,128)S(1)} %get-tuple-element.32), channel_id=1, source_target_pairs={{0,1},{1,0},{2,3},{3,2},{4,5},{5,4},{6,7},{7,6},{8,9},{9,8},{10,11... | collective-permute-start | bytes 1572872 | tf_op jit(solution)/shard_map/ppermute | solution.py:255
  19.4 23.3 %copy-start = (bf16[27,64,256]{2,1,0:T(8,128)(2,1)S(1)}, bf16[27,64,256]{2,1,0:T(8,128)(2,1)}, u32[]{:S(2)}) copy-start(bf16[27,64,256]{2,1,0:T(8,128)(2,1)} %refs_4_.1) | copy-start | bytes 2654212
  19.5 8.4 %collective-permute-start.5 = (f32[64,1024]{1,0:T(8,128)S(1)}, f32[64,1024]{1,0:T(8,128)S(1)}, u32[]{:S(2)}, u32[]{:S(2)}) collective-permute-start(f32[64,1024]{1,0:T(8,128)S(1)} %fusion), channel_id=1, source_target_pairs={{0,2},{1,3},{2,0},{3,1},{4,6},{5,7},{6,4},{7,5},{8,10},{9,11},{10,... | collective-permute-start | bytes 786440 | tf_op jit(solution)/shard_map/ppermute | solution.py:255
  28.1 5.6 %collective-permute-start.6 = (bf16[2,16,1024]{2,1,0:T(8,128)(2,1)S(1)}, bf16[2,16,1024]{2,1,0:T(8,128)(2,1)S(1)}, u32[]{:S(2)}, u32[]{:S(2)}) collective-permute-start(bf16[2,16,1024]{2,1,0:T(8,128)(2,1)S(1)} %get-tuple-element.67), channel_id=1, source_target_pairs={{0,4},{4,0},{8,12},{12,8},{16,20},{20,16},{24,28},{28,24},{1,5},{5... | collective-permute-start | bytes 196616 | tf_op jit(solution)/shard_map/ppermute | solution.py:255
  30.6 5.0 %collective-permute-start.7 = (bf16[64,1024]{1,0:T(8,128)(2,1)S(1)}, bf16[64,1024]{1,0:T(8,128)(2,1)S(1)}, u32[]{:S(2)}, u32[]{:S(2)}) collective-permute-start(bf16[64,1024]{1,0:T(8,128)(2,1)S(1)} %collective-permute-done.2), channel_id=1, source_target_pairs={{0,8},{4,12},{8,0},{12,4},{16,24},{20,28},{24,16},{28,20},{1,9},{5... | collective-permute-start | bytes 393224 | tf_op jit(solution)/shard_map/ppermute | solution.py:255
  32.2 5.0 %collective-permute-start.9 = (bf16[64,1024]{1,0:T(8,128)(2,1)S(1)}, bf16[64,1024]{1,0:T(8,128)(2,1)S(1)}, u32[]{:S(2)}, u32[]{:S(2)}) collective-permute-start(bf16[64,1024]{1,0:T(8,128)(2,1)S(1)} %get-tuple-element.62.refs_0_), channel_id=1, source_target_pairs={{0,2},{1,3},{2,0},{3,1},{4,6},{5,7},{6,4},{7,5},{8,10},{9,11},{10,... | collective-permute-start | bytes 393224 | tf_op jit(solution)/shard_map/ppermute | solution.py:255
  33.8 7.9 %collective-permute-start.8 = (bf16[64,1024]{1,0:T(8,128)(2,1)S(1)}, bf16[64,1024]{1,0:T(8,128)(2,1)S(1)}, u32[]{:S(2)}, u32[]{:S(2)}) collective-permute-start(bf16[64,1024]{1,0:T(8,128)(2,1)S(1)} %get-tuple-element.62.refs_0_), channel_id=1, source_target_pairs={{0,1},{1,0},{2,3},{3,2},{4,5},{5,4},{6,7},{7,6},{8,9},{9,8},{10,11... | collective-permute-start | bytes 393224 | tf_op jit(solution)/shard_map/ppermute | solution.py:255
  37.2 5.6 %collective-permute-start.10 = (bf16[64,1024]{1,0:T(8,128)(2,1)S(1)}, bf16[64,1024]{1,0:T(8,128)(2,1)S(1)}, u32[]{:S(2)}, u32[]{:S(2)}) collective-permute-start(bf16[64,1024]{1,0:T(8,128)(2,1)S(1)} %collective-permute-done.9.refs_2_), channel_id=1, source_target_pairs={{0,1},{1,0},{2,3},{3,2},{4,5},{5,4},{6,7},{7,6},{8,9},{9,8},{10,11... | collective-permute-start | bytes 393224 | tf_op jit(solution)/shard_map/ppermute | solution.py:255
  37.2 8.3 %collective-permute-start.13 = (bf16[2,16,1024]{2,1,0:T(8,128)(2,1)S(1)}, bf16[2,16,1024]{2,1,0:T(8,128)(2,1)S(1)}, u32[]{:S(2)}, u32[]{:S(2)}) collective-permute-start(bf16[2,16,1024]{2,1,0:T(8,128)(2,1)S(1)} %get-tuple-element.64), channel_id=1, source_target_pairs={{0,24},{4,28},{8,16},{12,20},{16,8},{20,12},{24,0},{28,4},{1,25},{... | collective-permute-start | bytes 196616 | tf_op jit(solution)/shard_map/ppermute | solution.py:255
  38.5 7.1 %collective-permute-start.11 = (bf16[2,16,1024]{2,1,0:T(8,128)(2,1)S(1)}, bf16[2,16,1024]{2,1,0:T(8,128)(2,1)S(1)}, u32[]{:S(2)}, u32[]{:S(2)}) collective-permute-start(bf16[2,16,1024]{2,1,0:T(8,128)(2,1)S(1)} %get-tuple-element.64), channel_id=1, source_target_pairs={{0,8},{4,12},{8,0},{12,4},{16,24},{20,28},{24,16},{28,20},{1,9},{5... | collective-permute-start | bytes 196616 | tf_op jit(solution)/shard_map/ppermute | solution.py:255
  38.5 18.6 %copy-start.4 = (s32[6]{0:T(128)S(1)}, s32[6]{0:T(128)}, u32[]{:S(2)}) copy-start(s32[6]{0:T(128)} %constant.19.clone) | copy-start | bytes 76
  38.5 7.1 %collective-permute-start.12 = (bf16[2,16,1024]{2,1,0:T(8,128)(2,1)S(1)}, bf16[2,16,1024]{2,1,0:T(8,128)(2,1)S(1)}, u32[]{:S(2)}, u32[]{:S(2)}) collective-permute-start(bf16[2,16,1024]{2,1,0:T(8,128)(2,1)S(1)} %get-tuple-element.43), channel_id=1, source_target_pairs={{0,16},{4,20},{8,24},{12,28},{16,0},{20,4},{24,8},{28,12},{1,17},{... | collective-permute-start | bytes 196616 | tf_op jit(solution)/shard_map/ppermute | solution.py:255
  41.7 14.9 %collective-permute-start.15 = (bf16[3,64,1024]{2,1,0:T(8,128)(2,1)S(1)}, bf16[3,64,1024]{2,1,0:T(8,128)(2,1)S(1)}, u32[]{:S(2)}, u32[]{:S(2)}) collective-permute-start(bf16[3,64,1024]{2,1,0:T(8,128)(2,1)S(1)} %pad_maximum_fusion.near), channel_id=1, source_target_pairs={{0,4},{4,0},{8,12},{12,8},{16,20},{20,16},{24,28},{28,24},{1,5},{5... | collective-permute-start | bytes 1179656 | tf_op jit(solution)/shard_map/ppermute | solution.py:255
  45.6 11.0 %collective-permute-start.14 = (bf16[8,16,1024]{2,1,0:T(8,128)(2,1)S(1)}, bf16[8,16,1024]{2,1,0:T(8,128)(2,1)S(1)}, u32[]{:S(2)}, u32[]{:S(2)}) collective-permute-start(bf16[8,16,1024]{2,1,0:T(8,128)(2,1)S(1)} %constant_dynamic-update-slice_fusion.refs_0_), channel_id=1, source_target_pairs={{0,2},{1,3},{2,0},{3,1},{4,6},{5,7},{6,4},{7,5},{8,10},{9,11},{10,... | collective-permute-start | bytes 786440 | tf_op jit(solution)/shard_map/ppermute | solution.py:255
  47.2 8.0 %collective-permute-start.16 = (bf16[64,1024]{1,0:T(8,128)(2,1)S(1)}, bf16[64,1024]{1,0:T(8,128)(2,1)S(1)}, u32[]{:S(2)}, u32[]{:S(2)}) collective-permute-start(bf16[64,1024]{1,0:T(8,128)(2,1)S(1)} %get-tuple-element.45), channel_id=1, source_target_pairs={{4,0},{8,4},{12,8},{16,12},{20,16},{24,20},{28,24},{5,1},{9,5},{13... | collective-permute-start | bytes 393224 | tf_op jit(solution)/shard_map/ppermute | solution.py:331
  48.5 8.1 %collective-permute-start.17 = (bf16[64,1024]{1,0:T(8,128)(2,1)S(1)}, bf16[64,1024]{1,0:T(8,128)(2,1)S(1)}, u32[]{:S(2)}, u32[]{:S(2)}) collective-permute-start(bf16[64,1024]{1,0:T(8,128)(2,1)S(1)} %get-tuple-element.46), channel_id=1, source_target_pairs={{0,4},{4,8},{8,12},{12,16},{16,20},{20,24},{24,28},{1,5},{5,9},{9,... | collective-permute-start | bytes 393224 | tf_op jit(solution)/shard_map/ppermute | solution.py:332
  56.6 1.6 %collective-permute-start.18 = (bf16[8,16,1024]{2,1,0:T(8,128)(2,1)S(1)}, bf16[8,16,1024]{2,1,0:T(8,128)(2,1)S(1)}, u32[]{:S(2)}, u32[]{:S(2)}) collective-permute-start(bf16[8,16,1024]{2,1,0:T(8,128)(2,1)S(1)} %constant_dynamic-update-slice_fusion.refs_0_), channel_id=1, source_target_pairs={{0,1},{1,0},{2,3},{3,2},{4,5},{5,4},{6,7},{7,6},{8,9},{9,8},{10,11... | collective-permute-start | bytes 786440 | tf_op jit(solution)/shard_map/ppermute | solution.py:255
  56.6 1.9 %collective-permute-start.19 = (bf16[8,16,1024]{2,1,0:T(8,128)(2,1)S(1)}, bf16[8,16,1024]{2,1,0:T(8,128)(2,1)S(1)}, u32[]{:S(2)}, u32[]{:S(2)}) collective-permute-start(bf16[8,16,1024]{2,1,0:T(8,128)(2,1)S(1)} %collective-permute-done.14.refs_2_), channel_id=1, source_target_pairs={{0,1},{1,0},{2,3},{3,2},{4,5},{5,4},{6,7},{7,6},{8,9},{9,8},{10,11... | collective-permute-start | bytes 786440 | tf_op jit(solution)/shard_map/ppermute | solution.py:255
  63.0 9.6 %collective-permute-start.22 = (bf16[896,128]{1,0:T(8,128)(2,1)S(1)}, bf16[896,128]{1,0:T(8,128)(2,1)S(1)}, u32[]{:S(2)}, u32[]{:S(2)}) collective-permute-start(bf16[896,128]{1,0:T(8,128)(2,1)S(1)} %filter_block.1.refs_0_), channel_id=1, source_target_pairs={{0,12},{4,8},{8,4},{12,0},{16,28},{20,24},{24,20},{28,16},{1,13},{... | collective-permute-start | bytes 688136 | tf_op jit(solution)/shard_map/ppermute | solution.py:255
  66.2 11.4 %collective-permute-start.21 = (bf16[896,128]{1,0:T(8,128)(2,1)S(1)}, bf16[896,128]{1,0:T(8,128)(2,1)S(1)}, u32[]{:S(2)}, u32[]{:S(2)}) collective-permute-start(bf16[896,128]{1,0:T(8,128)(2,1)S(1)} %filter_block.1.refs_0_), channel_id=1, source_target_pairs={{0,8},{4,12},{8,0},{12,4},{16,24},{20,28},{24,16},{28,20},{1,9},{5... | collective-permute-start | bytes 688136 | tf_op jit(solution)/shard_map/ppermute | solution.py:255
  67.0 10.6 %collective-permute-start.20 = (bf16[896,128]{1,0:T(8,128)(2,1)S(1)}, bf16[896,128]{1,0:T(8,128)(2,1)S(1)}, u32[]{:S(2)}, u32[]{:S(2)}) collective-permute-start(bf16[896,128]{1,0:T(8,128)(2,1)S(1)} %filter_block.1.refs_0_), channel_id=1, source_target_pairs={{0,4},{4,0},{8,12},{12,8},{16,20},{20,16},{24,28},{28,24},{1,5},{5... | collective-permute-start | bytes 688136 | tf_op jit(solution)/shard_map/ppermute | solution.py:255

commit v4 on v3

--- a/solution.py
+++ b/solution.py
@@ -12,6 +12,7 @@
 PLANE_H = 32
 PLANE_W = 32
 CELLS = PLANE_H * PLANE_W
+CHUNKS = ((0, 8), (8, 16), (16, 24), (24, TAPS))
 VMEM = pl.BlockSpec(memory_space=pltpu.VMEM)
 SMEM = pl.BlockSpec(memory_space=pltpu.SMEM)
 BF16 = jnp.bfloat16
@@ -41,13 +42,16 @@
             step(q)
 
 
-def forward_kernel(chans, index, own, below, above, weights, keep, give, stack, total):
-    for a, plane in enumerate((below, own, above)):
+def forward_kernel(chans, index, own, partner, outer, weights, keep, give, stack, total):
+    above = 2 * (1 - index[1])
+    for a, plane in ((1, own), (above, partner), (2 - above, outer)):
         cells = plane[...]
         for b in range(3):
             for e in range(3):
-                tap = 9 * a + 3 * b + e
-                stack[tap * chans : (tap + 1) * chans, :] = moved(cells, b - 1, e - 1)
+                start = (9 * a + 3 * b + e) * chans
+                if plane is not own:
+                    start = pl.multiple_of(start, chans)
+                stack[pl.ds(start, chans), :] = moved(cells, b - 1, e - 1)
     total[...] = jnp.dot(weights[...], stack[...], preferred_element_type=F32)
     for j in range(keep.shape[0]):
         start = pl.multiple_of((index[0] ^ (2 * j)) * chans, chans)
@@ -56,7 +60,7 @@
         give[j] = total[pl.ds(start, chans), :]
 
 
-def forward_parts(index, own, below, above, weights):
+def forward_parts(index, own, partner, outer, weights):
     chans = own.shape[0]
     outs = weights.shape[0]
     side = jax.ShapeDtypeStruct((outs // chans // 2, chans, CELLS), F32)
@@ -74,12 +78,12 @@
             flops=2 * outs * TAPS * chans * CELLS, bytes_accessed=6 << 20, transcendentals=0
         ),
         name="forward_parts",
-    )(index, own, below, above, weights)
+    )(index, own, partner, outer, weights)
 
 
 def input_kernel(chans, groups, index, *refs):
     grads = refs[:groups]
-    weights, below, own, above, stack, left = refs[groups:]
+    weights, own, partner, outer, stack, left, total = refs[groups:]
     outs = weights.shape[2]
     for u in range(groups):
         start = pl.multiple_of((index[0] ^ u) * chans, chans)
@@ -90,12 +94,14 @@
     for a in range(3):
         for k in range(9):
             left[a * chans : (a + 1) * chans, k * outs : (k + 1) * outs] = weights[9 * a + k]
-    total = jnp.dot(
+    total[...] = jnp.dot(
         left[...], stack[...].reshape(9 * outs, CELLS), preferred_element_type=F32
     )
-    below[...] = total[:chans].astype(BF16)
+    above = pl.multiple_of(2 * (1 - index[1]) * chans, chans)
+    below = pl.multiple_of(2 * index[1] * chans, chans)
     own[...] = total[chans : 2 * chans]
-    above[...] = total[2 * chans :].astype(BF16)
+    partner[...] = total[pl.ds(above, chans), :].astype(BF16)
+    outer[...] = total[pl.ds(below, chans), :].astype(BF16)
 
 
 def input_parts(index, grads, weights):
@@ -105,12 +111,13 @@
     sides = jax.ShapeDtypeStruct((chans, CELLS), BF16)
     return pl.pallas_call(
         functools.partial(input_kernel, chans, groups),
-        out_shape=[sides, jax.ShapeDtypeStruct((chans, CELLS), F32), sides],
+        out_shape=[jax.ShapeDtypeStruct((chans, CELLS), F32), sides, sides],
         in_specs=[SMEM] + [VMEM] * (groups + 1),
         out_specs=[VMEM] * 3,
         scratch_shapes=[
             pltpu.VMEM((9, outs, CELLS), BF16),
             pltpu.VMEM((3 * chans, 9 * outs), BF16),
+            pltpu.VMEM((3 * chans, CELLS), F32),
         ],
         compiler_params=pltpu.CompilerParams(vmem_limit_bytes=20 << 20),
         cost_estimate=pl.CostEstimate(
@@ -206,7 +213,7 @@
 
 
 def join_kernel(share, chans, index, *refs):
-    blocks, (out, bias, right) = refs[:4], refs[4:]
+    blocks, (out, bias, right, held, done) = refs[:4], refs[4:]
     lanes, total = blocks[0].shape[1], out.shape[2]
     width = lanes // 2
     lane = lax.broadcasted_iota(jnp.int32, (lanes, total), 0)
@@ -219,15 +226,23 @@
             right[r * lanes : (r + 1) * lanes, odd * total : (odd + 1) * total] = jnp.where(
                 hit, 1.0, 0.0
             ).astype(BF16)
+    copies = []
     for pair in range((TAPS + 1) // 2):
         at = slice(pair * chans, (pair + 1) * chans)
         left = jnp.concatenate([block[at, :] for block in blocks], axis=1)
         both = jnp.dot(left, right[...], preferred_element_type=F32)
-        out[2 * pair] = both[:, :total]
+        held[2 * pair] = both[:, :total]
         if 2 * pair + 1 < TAPS:
-            out[2 * pair + 1] = both[:, total:]
+            held[2 * pair + 1] = both[:, total:]
         else:
             bias[...] = both[0:1, total:] + both[16:17, total:]
+        for k, (first, last) in enumerate(CHUNKS):
+            if last == min(2 * pair + 2, TAPS):
+                part = pl.ds(first, last - first)
+                copies.append(pltpu.make_async_copy(held.at[part], out.at[part], done.at[k]))
+                copies[-1].start()
+    for copy in copies:
+        copy.wait()
 
 
 def join_blocks(index, blocks, share, chans):
@@ -240,8 +255,12 @@
             jax.ShapeDtypeStruct((1, total), F32),
         ],
         in_specs=[SMEM] + [VMEM] * 4,
-        out_specs=[VMEM, VMEM],
-        scratch_shapes=[pltpu.VMEM((4 * lanes, 2 * total), BF16)],
+        out_specs=[pl.BlockSpec(memory_space=pl.ANY), VMEM],
+        scratch_shapes=[
+            pltpu.VMEM((4 * lanes, 2 * total), BF16),
+            pltpu.VMEM((TAPS, chans, total), F32),
+            pltpu.SemaphoreType.DMA((len(CHUNKS),)),
+        ],
         compiler_params=pltpu.CompilerParams(vmem_limit_bytes=20 << 20),
         cost_estimate=pl.CostEstimate(
             flops=4 * TAPS * chans * total * lanes * 2, bytes_accessed=4 << 20, transcendentals=0
@@ -253,6 +272,11 @@
 def swapped(value, axis, mask):
     count = lax.axis_size(axis)
     return lax.ppermute(value, axis, [(i, i ^ mask) for i in range(count)])
+
+
+def exchanged(value):
+    pairs = [(i, i + 1) for i in range(1, lax.axis_size("space") - 1, 2)]
+    return lax.ppermute(value, "space", pairs + [(j, i) for i, j in pairs])
 
 
 def other_chips(value):
@@ -274,32 +298,28 @@
     space = lax.axis_index("space")
     chan = lax.axis_index("chan")
     share = chans // 4
-    masks = [1 << k for k in range(depth.bit_length() - 2, -1, -1)]
     factor = 1.0 / math.sqrt(cells * planes * depth)
     barrier = lax.optimization_barrier
 
     own = features.reshape(chans, cells)
-    up = [(i, i + 1) for i in range(depth - 1)]
-    down = [(i + 1, i) for i in range(depth - 1)]
-    below = lax.ppermute(own, "space", up)
-    above = lax.ppermute(own, "space", down)
-    near = [swapped(own, "space", mask) for mask in masks[:2]]
-    below, above, near = barrier((below, above, near))
-    weights = filters.reshape(TAPS * chans, total_out)
-    keep, give = forward_parts(chan.reshape(1), own, below, above, weights.T)
+    weights, ahead = barrier((filters.reshape(TAPS * chans, total_out).T, own))
+    near = swapped(ahead, "space", 4)[None]
+    partner, outer = swapped(own, "space", 1), exchanged(own)
+    outer, partner, near = barrier((outer, partner, near))
+    side = (space & 1).reshape(1)
+    where = jnp.concatenate([chan.reshape(1), side])
+    keep, give = forward_parts(where, own, partner, outer, weights)
 
     got = swapped(give, "chan", 1)
-    partial = [keep[j] + got[j] for j in range(1, groups // 2)]
-    pre_act = keep[0] + got[0] + out_bias[:, None]
-    for j, term in enumerate(partial):
-        pre_act = pre_act + swapped(term, "chan", 2 * (j + 1))
-    pre_act, near = barrier((pre_act, near))
-    near = jnp.stack(near + [swapped(near[0], "space", masks[1])], axis=0)
-    flips = [masks[0], masks[1], masks[0] ^ masks[1]]
-    for mask in masks[2:-1]:
+    flips = [4]
+    for mask in [1 << k for k in range(depth.bit_length() - 2, 0, -1) if k != 2]:
         own_too = jnp.concatenate([own[None], near], axis=0)
         near = jnp.concatenate([near, swapped(own_too, "space", mask)], axis=0)
         flips = flips + [f ^ mask for f in [0] + flips]
+    pre_act = keep[0] + got[0] + out_bias[:, None]
+    for j in range(1, groups // 2):
+        pre_act = pre_act + swapped(keep[j] + got[j], "chan", 2 * j)
+    pre_act, near = barrier((pre_act, near))
 
     sigmoid = jax.nn.sigmoid(pre_act)
     activated = pre_act * sigmoid
@@ -315,9 +335,8 @@
     given = jnp.where(side == 0, split[:, 1], split[:, 0])
     pair = jnp.stack([kept, swapped(given, "space", 1)], axis=0)
     pair, near = barrier((pair, near))
-    far = swapped(near, "space", masks[-1])
+    far = swapped(near, "space", 1)
     flips = flips + [f ^ 1 for f in flips]
-    partner = jnp.where(side == 0, above, below)
     side = (space >> 1) & 1
     kept = jnp.where(side == 0, pair[:, 0], pair[:, 1])
     given = jnp.where(side == 0, pair[:, 1], pair[:, 0])
@@ -326,14 +345,14 @@
         pieces.append(swapped(given if t & 1 else kept, "space", 2 * t))
 
     grads = both_cores(other_chips(grad_pre))
-    terms = input_parts(chan.reshape(1), grads, filters)
-    pieces[0], (to_below, in_own, to_above) = barrier((pieces[0], terms))
-    from_above = lax.ppermute(to_below, "space", down)
-    from_below = lax.ppermute(to_above, "space", up)
+    pieces[0], grads = barrier((pieces[0], grads))
     blocks = other_chips(jnp.concatenate(pieces, axis=0))
-    blocks, far, from_above, from_below = barrier((blocks, far, from_above, from_below))
+
+    in_grad, to_partner, to_outer = input_parts(where, grads, filters)
+    from_partner, from_outer = swapped(to_partner, "space", 1), exchanged(to_outer)
+    blocks, far, from_partner, from_outer = barrier((blocks, far, from_partner, from_outer))
     blocks = both_cores(blocks)
-    in_grad = in_own + from_above.astype(F32) + from_below.astype(F32)
+    in_grad = in_grad + from_partner.astype(F32) + from_outer.astype(F32)
 
     index = jnp.concatenate([space.reshape(1), chan.reshape(1), jnp.array(flips, jnp.int32)])
     part = filter_block(index, own, partner, near, far, blocks, factor)

time: 80.2 us -> 82 us (1.022)
  starting transfers between devices: 36.7 us -> 27.4 us
  waiting for transfers between devices: 28 us -> 36.9 us
  Pallas kernels: 10.6 us -> 12.6 us
    ppermute x19 -> x20, waiting for transfers between devices: 22 us -> 36.9 us  [swapped(): return lax.ppermute(value, axis, [(i, i ^ mask) for i in range(count)])]
    ppermute x4 -> x2, starting transfers between devices: 11.7 us -> 1.31 us  [exchanged(): return lax.ppermute(value, 'space', pairs + [(j, i) for i, j in pairs])]
    ppermute x4 -> x2, waiting for transfers between devices: 5.95 us -> 0.01 us  [exchanged(): return lax.ppermute(value, 'space', pairs + [(j, i) for i, j in pairs])]
    pallas_call x1, Pallas kernels: 1.38 us -> 2.64 us  [forward_parts(): pl.pallas_call(functools.partial(forward_kernel, chans), out_shape=[side,...]
    ppermute x19 -> x20, starting transfers between devices: 25 us -> 26.1 us  [swapped(): return lax.ppermute(value, axis, [(i, i ^ mask) for i in range(count)])]
  transfers between devices with their start and end apart: 23 -> 22, of which waited for: 11 -> 12; matrix products, arithmetic and copies ran while one was open for 5% -> 5% of each run, Pallas kernels for 3% -> 3%
where the time goes in v4:
time: 82 us; the launch traced here: 81.8 us
  waiting for transfers between devices  36.9 us (45%)
  starting transfers between devices  27.4 us (33%)
  Pallas kernels  12.6 us (15%)
  local copies, waits for them, and re-layouts  3.45 us (4%)
  between operations  0.84 us (1%)
    ppermute x20, waiting for transfers between devices, swapped(): return lax.ppermute(value, axis, [(i, i ^ mask) for i in range(count)])  36.9 us
    ppermute x20, starting transfers between devices, swapped(): return lax.ppermute(value, axis, [(i, i ^ mask) for i in range(count)])  26.1 us
    pallas_call x1, Pallas kernels, filter_block(): pl.pallas_call(functools.partial(filter_kernel, factor, groups), out_shap...  4.58 us
    pallas_call x1, Pallas kernels, input_parts(): pl.pallas_call(functools.partial(input_kernel, chans, groups), out_shape=...  2.84 us
    pallas_call x1, Pallas kernels, forward_parts(): pl.pallas_call(functools.partial(forward_kernel, chans), out_shape=[side,...  2.64 us
    pallas_call x1, Pallas kernels, join_blocks(): pl.pallas_call(functools.partial(join_kernel, share, chans), out_shape=[j...  2.57 us
    unnamed x15, local copies, waits for them, and re-layouts  1.99 us
  transfers between devices with their start and end apart: 22, of which 12 were waited for; matrix products, arithmetic and copies ran while one was open for 5% of the time, Pallas kernels for 3%

profile of v4, /device:TPU:0, one launch (start us, length us, event | category | flops | bytes accessed | tf_op | source)
XLA Modules:
  0.0 81.8 jit_solution(1102961672324666727)
XLA Ops:
  0.6 3.0 %collective-permute-start.1 = (bf16[64,1024]{1,0:T(8,128)(2,1)}, bf16[64,1024]{1,0:T(8,128)(2,1)S(1)}, u32[]{:S(2)}, u32[]{:S(2)}) collective-permute-start(bf16[64,1024]{1,0:T(8,128)(2,1)} %bitcast.52), channel_id=1, source_target_pairs={{0,4},{4,0},{8,12},{12,8},{16,20},{20,16},{24,28},{28,24},{1,5},{5... | collective-permute-start | bytes 393224 | tf_op jit(solution)/shard_map/ppermute | solution.py:274
  3.6 0.7 collective-permute-start
  4.3 1.5 %copy.13 = bf16[1728,256]{0,1:T(8,128)(2,1)S(1)} copy(bf16[1728,256]{1,0:T(8,128)(2,1)} %bitcast.50) | data formatting | bytes 1769472 | tf_op jit(solution)/shard_map/reshape | solution.py:305
  5.8 4.3 %collective-permute-start.2 = (bf16[64,1024]{1,0:T(8,128)(2,1)S(1)}, bf16[64,1024]{1,0:T(8,128)(2,1)S(1)}, u32[]{:S(2)}, u32[]{:S(2)}) collective-permute-start(bf16[64,1024]{1,0:T(8,128)(2,1)S(1)} %bitcast.54), channel_id=1, source_target_pairs={{0,16},{4,20},{8,24},{12,28},{16,0},{20,4},{24,8},{28,12},{1,17},{... | collective-permute-start | bytes 393224 | tf_op jit(solution)/shard_map/ppermute | solution.py:274
  10.2 7.1 %collective-permute-done.2 = bf16[64,1024]{1,0:T(8,128)(2,1)S(1)} collective-permute-done((bf16[64,1024]{1,0:T(8,128)(2,1)S(1)}, bf16[64,1024]{1,0:T(8,128)(2,1)S(1)}, u32[]{:S(2)}, u32[]{:S(2)}) %collective-permute-start.2) | collective-permute-done | bytes 131104 | tf_op jit(solution)/shard_map/ppermute | solution.py:274
  17.3 2.6 %forward_parts.1 = (f32[2,64,1024]{2,1,0:T(8,128)S(1)}, f32[2,64,1024]{2,1,0:T(8,128)S(1)}) custom-call(s32[2]{0:T(128)S(1)} %pad_add_fusion.index, bf16[64,1024]{1,0:T(8,128)(2,1)S(1)} %bitcast.55, bf16[64,1024]{1,0:T(8,128)(2,1)S(1)} %collective-permute-done.1.partner, bf16[64,1024]{1,0:T(8,128)(2,1)S(1)} %collective-permute-done.outer, ...), custom_call_target="tpu_custom_call" | custom-call | flops 905969664 | bytes 6291456 | tf_op jit(solution)/shard_map/forward_parts/pallas_call | solution.py:67
  20.2 1.8 %collective-permute-done.3 = f32[2,64,1024]{2,1,0:T(8,128)S(1)} collective-permute-done((f32[2,64,1024]{2,1,0:T(8,128)S(1)}, f32[2,64,1024]{2,1,0:T(8,128)S(1)}, u32[]{:S(2)}, u32[]{:S(2)}) %collective-permute-start.3) | collective-permute-done | bytes 524320 | tf_op jit(solution)/shard_map/ppermute | solution.py:274
  22.0 1.6 %collective-permute-start.4 = (f32[64,1024]{1,0:T(8,128)S(1)}, f32[64,1024]{1,0:T(8,128)S(1)}, u32[]{:S(2)}, u32[]{:S(2)}) collective-permute-start(f32[64,1024]{1,0:T(8,128)S(1)} %fusion), channel_id=1, source_target_pairs={{0,2},{1,3},{2,0},{3,1},{4,6},{5,7},{6,4},{7,5},{8,10},{9,11},{10,... | collective-permute-start | bytes 786440 | tf_op jit(solution)/shard_map/ppermute | solution.py:274
  23.6 5.3 %collective-permute-done.5 = bf16[2,64,1024]{2,1,0:T(8,128)(2,1)S(1)} collective-permute-done((bf16[2,64,1024]{2,1,0:T(8,128)(2,1)S(1)}, bf16[2,64,1024]{2,1,0:T(8,128)(2,1)S(1)}, u32[]{:S(2)}, u32[]{:S(2)}) %collective-permute-start.5) | collective-permute-done | bytes 262176 | tf_op jit(solution)/shard_map/ppermute | solution.py:274
  28.9 1.5 %collective-permute-done.4 = f32[64,1024]{1,0:T(8,128)S(1)} collective-permute-done((f32[64,1024]{1,0:T(8,128)S(1)}, f32[64,1024]{1,0:T(8,128)S(1)}, u32[]{:S(2)}, u32[]{:S(2)}) %collective-permute-start.4) | collective-permute-done | bytes 262176 | tf_op jit(solution)/shard_map/ppermute | solution.py:274
  30.7 1.3 %collective-permute-start.6 = (bf16[2,16,1024]{2,1,0:T(8,128)(2,1)S(1)}, bf16[2,16,1024]{2,1,0:T(8,128)(2,1)S(1)}, u32[]{:S(2)}, u32[]{:S(2)}) collective-permute-start(bf16[2,16,1024]{2,1,0:T(8,128)(2,1)S(1)} %get-tuple-element.69), channel_id=1, source_target_pairs={{0,4},{4,0},{8,12},{12,8},{16,20},{20,16},{24,28},{28,24},{1,5},{5... | collective-permute-start | bytes 196616 | tf_op jit(solution)/shard_map/ppermute | solution.py:274
  31.9 1.5 %collective-permute-start.8 = (bf16[64,1024]{1,0:T(8,128)(2,1)S(1)}, bf16[64,1024]{1,0:T(8,128)(2,1)S(1)}, u32[]{:S(2)}, u32[]{:S(2)}) collective-permute-start(bf16[64,1024]{1,0:T(8,128)(2,1)S(1)} %get-tuple-element.40.refs_0_), channel_id=1, source_target_pairs={{0,2},{1,3},{2,0},{3,1},{4,6},{5,7},{6,4},{7,5},{8,10},{9,11},{10,... | collective-permute-start | bytes 393224 | tf_op jit(solution)/shard_map/ppermute | solution.py:274
  33.4 1.5 %collective-permute-done.6 = bf16[2,16,1024]{2,1,0:T(8,128)(2,1)S(1)} collective-permute-done((bf16[2,16,1024]{2,1,0:T(8,128)(2,1)S(1)}, bf16[2,16,1024]{2,1,0:T(8,128)(2,1)S(1)}, u32[]{:S(2)}, u32[]{:S(2)}) %collective-permute-start.6) | collective-permute-done | bytes 65568 | tf_op jit(solution)/shard_map/ppermute | solution.py:274
  35.0 1.9 %collective-permute-done.8.refs_2_ = bf16[64,1024]{1,0:T(8,128)(2,1)S(1)} collective-permute-done((bf16[64,1024]{1,0:T(8,128)(2,1)S(1)}, bf16[64,1024]{1,0:T(8,128)(2,1)S(1)}, u32[]{:S(2)}, u32[]{:S(2)}) %collective-permute-start.8) | collective-permute-done | bytes 131104 | tf_op jit(solution)/shard_map/ppermute | solution.py:274
  36.9 2.8 %collective-permute-start.12 = (bf16[2,16,1024]{2,1,0:T(8,128)(2,1)S(1)}, bf16[2,16,1024]{2,1,0:T(8,128)(2,1)S(1)}, u32[]{:S(2)}, u32[]{:S(2)}) collective-permute-start(bf16[2,16,1024]{2,1,0:T(8,128)(2,1)S(1)} %get-tuple-element.66), channel_id=1, source_target_pairs={{0,24},{4,28},{8,16},{12,20},{16,8},{20,12},{24,0},{28,4},{1,25},{... | collective-permute-start | bytes 196616 | tf_op jit(solution)/shard_map/ppermute | solution.py:274
  39.7 1.6 %collective-permute-start.11 = (bf16[2,16,1024]{2,1,0:T(8,128)(2,1)S(1)}, bf16[2,16,1024]{2,1,0:T(8,128)(2,1)S(1)}, u32[]{:S(2)}, u32[]{:S(2)}) collective-permute-start(bf16[2,16,1024]{2,1,0:T(8,128)(2,1)S(1)} %get-tuple-element.45), channel_id=1, source_target_pairs={{0,16},{4,20},{8,24},{12,28},{16,0},{20,4},{24,8},{28,12},{1,17},{... | collective-permute-start | bytes 196616 | tf_op jit(solution)/shard_map/ppermute | solution.py:274
  41.4 0.8 %collective-permute-start.14 = (bf16[3,64,1024]{2,1,0:T(8,128)(2,1)S(1)}, bf16[3,64,1024]{2,1,0:T(8,128)(2,1)S(1)}, u32[]{:S(2)}, u32[]{:S(2)}) collective-permute-start(bf16[3,64,1024]{2,1,0:T(8,128)(2,1)S(1)} %pad_maximum_fusion.near), channel_id=1, source_target_pairs={{0,4},{4,0},{8,12},{12,8},{16,20},{20,16},{24,28},{28,24},{1,5},{5... | collective-permute-start | bytes 1179656 | tf_op jit(solution)/shard_map/ppermute | solution.py:274
  42.2 3.9 %collective-permute-done.10 = bf16[2,16,1024]{2,1,0:T(8,128)(2,1)S(1)} collective-permute-done((bf16[2,16,1024]{2,1,0:T(8,128)(2,1)S(1)}, bf16[2,16,1024]{2,1,0:T(8,128)(2,1)S(1)}, u32[]{:S(2)}, u32[]{:S(2)}) %collective-permute-start.10) | collective-permute-done | bytes 65568 | tf_op jit(solution)/shard_map/ppermute | solution.py:274
  46.4 1.6 %collective-permute-start.13 = (bf16[8,16,1024]{2,1,0:T(8,128)(2,1)S(1)}, bf16[8,16,1024]{2,1,0:T(8,128)(2,1)S(1)}, u32[]{:S(2)}, u32[]{:S(2)}) collective-permute-start(bf16[8,16,1024]{2,1,0:T(8,128)(2,1)S(1)} %constant_dynamic-update-slice_fusion.refs_0_), channel_id=1, source_target_pairs={{0,2},{1,3},{2,0},{3,1},{4,6},{5,7},{6,4},{7,5},{8,10},{9,11},{10,... | collective-permute-start | bytes 786440 | tf_op jit(solution)/shard_map/ppermute | solution.py:274
  48.0 2.8 %input_parts.1 = (f32[64,1024]{1,0:T(8,128)S(1)}, bf16[64,1024]{1,0:T(8,128)(2,1)S(1)}, bf16[64,1024]{1,0:T(8,128)(2,1)S(1)}) custom-call(s32[2]{0:T(128)S(1)} %pad_add_fusion.index, bf16[64,1024]{1,0:T(8,128)(2,1)S(1)} %get-tuple-element.40.refs_0_, bf16[64,1024]{1,0:T(8,128)(2,1)S(1)} %collective-permute-done.7.refs_1_, ...), custom_call_target="tpu_custom_call" | custom-call | flops 905969664 | bytes 6291456 | tf_op jit(solution)/shard_map/input_parts/pallas_call | solution.py:112
  50.8 0.6 collective-permute-start.15
  51.5 0.7 collective-permute-start.16
  52.1 3.7 %collective-permute-done.15 = bf16[64,1024]{1,0:T(8,128)(2,1)S(1)} collective-permute-done((bf16[64,1024]{1,0:T(8,128)(2,1)S(1)}, bf16[64,1024]{1,0:T(8,128)(2,1)S(1)}, u32[]{:S(2)}, u32[]{:S(2)}) %collective-permute-start.15) | collective-permute-done | bytes 131104 | tf_op jit(solution)/shard_map/ppermute | solution.py:274
  56.0 0.5 collective-permute-start.18
  56.5 1.0 %copy.17 = f32[64,1,1024]{2,1,0:T(1,128)} copy(f32[64,1,1024]{2,0,1:T(8,128)S(1)} %get-tuple-element.65) | data formatting | bytes 524288
  57.9 4.6 %filter_block.1.refs_0_ = bf16[896,128]{1,0:T(8,128)(2,1)S(1)} custom-call(s32[8]{0:T(128)S(1)} %pad_add_fusion.1.index, bf16[64,1024]{1,0:T(8,128)(2,1)S(1)} %bitcast.57, bf16[64,1024]{1,0:T(8,128)(2,1)S(1)} %collective-permute-done.1.partner, bf16[3,64,1024]{2,1,0:T(8,128)(2,1)S(1)} %pad_maximum_fusion.near, ...), custom_call_target="tpu_custom_call" | custom-call | flops 1811939328 | bytes 8388608 | tf_op jit(solution)/shard_map/filter_block/pallas_call | solution.py:194
  62.4 4.8 %collective-permute-start.21 = (bf16[896,128]{1,0:T(8,128)(2,1)S(1)}, bf16[896,128]{1,0:T(8,128)(2,1)S(1)}, u32[]{:S(2)}, u32[]{:S(2)}) collective-permute-start(bf16[896,128]{1,0:T(8,128)(2,1)S(1)} %filter_block.1.refs_0_), channel_id=1, source_target_pairs={{0,12},{4,8},{8,4},{12,0},{16,28},{20,24},{24,20},{28,16},{1,13},{... | collective-permute-start | bytes 688136 | tf_op jit(solution)/shard_map/ppermute | solution.py:274
  67.2 1.5 %collective-permute-start.20 = (bf16[896,128]{1,0:T(8,128)(2,1)S(1)}, bf16[896,128]{1,0:T(8,128)(2,1)S(1)}, u32[]{:S(2)}, u32[]{:S(2)}) collective-permute-start(bf16[896,128]{1,0:T(8,128)(2,1)S(1)} %filter_block.1.refs_0_), channel_id=1, source_target_pairs={{0,8},{4,12},{8,0},{12,4},{16,24},{20,28},{24,16},{28,20},{1,9},{5... | collective-permute-start | bytes 688136 | tf_op jit(solution)/shard_map/ppermute | solution.py:274
  68.7 1.0 %copy.18 = f32[64,1,1024]{2,1,0:T(1,128)} copy(f32[64,1,1024]{2,0,1:T(8,128)S(1)} %add_bitcast_fusion) | data formatting | bytes 524288
  69.7 3.9 %collective-permute-done.21.refs_3_ = bf16[896,128]{1,0:T(8,128)(2,1)S(1)} collective-permute-done((bf16[896,128]{1,0:T(8,128)(2,1)S(1)}, bf16[896,128]{1,0:T(8,128)(2,1)S(1)}, u32[]{:S(2)}, u32[]{:S(2)}) %collective-permute-start.21) | collective-permute-done | bytes 229408 | tf_op jit(solution)/shard_map/ppermute | solution.py:274
  73.6 5.6 %collective-permute-done.20.refs_2_ = bf16[896,128]{1,0:T(8,128)(2,1)S(1)} collective-permute-done((bf16[896,128]{1,0:T(8,128)(2,1)S(1)}, bf16[896,128]{1,0:T(8,128)(2,1)S(1)}, u32[]{:S(2)}, u32[]{:S(2)}) %collective-permute-start.20) | collective-permute-done | bytes 229408 | tf_op jit(solution)/shard_map/ppermute | solution.py:274
  79.2 2.6 %join_blocks.1 = (f32[27,64,256]{2,1,0:T(8,128)}, f32[1,256]{1,0:T(1,128)}) custom-call(s32[1]{0:T(128)} %bitcast.19.index, bf16[896,128]{1,0:T(8,128)(2,1)S(1)} %filter_block.1.refs_0_, bf16[896,128]{1,0:T(8,128)(2,1)S(1)} %collective-permute-done.19.refs_1_, bf16[896,128]{1,0:T(8,128)(2,1)S(1)} %collective-permute-done.20.refs_2_, ...), custom_call_target="tpu_custom_call" | custom-call | flops 452984832 | bytes 4194304 | tf_op jit(solution)/shard_map/join_blocks/pallas_call | solution.py:251
  (44 shorter events, 1.5 us)
Async XLA Ops:
  0.6 5.1 %copy-start.1 = (bf16[64,1,1024]{2,0,1:T(8,128)(2,1)S(1)}, bf16[64,1,1024]{2,0,1:T(8,128)(2,1)}, u32[]{:S(2)}) copy-start(bf16[64,1,1024]{2,0,1:T(8,128)(2,1)} %param.5) | copy-start | bytes 393220
  0.6 9.5 %collective-permute-start.1 = (bf16[64,1024]{1,0:T(8,128)(2,1)}, bf16[64,1024]{1,0:T(8,128)(2,1)S(1)}, u32[]{:S(2)}, u32[]{:S(2)}) collective-permute-start(bf16[64,1024]{1,0:T(8,128)(2,1)} %bitcast.52), channel_id=1, source_target_pairs={{0,4},{4,0},{8,12},{12,8},{16,20},{20,16},{24,28},{28,24},{1,5},{5... | collective-permute-start | bytes 393224 | tf_op jit(solution)/shard_map/ppermute | solution.py:274
  3.6 6.5 %collective-permute-start = (bf16[64,1024]{1,0:T(8,128)(2,1)}, bf16[64,1024]{1,0:T(8,128)(2,1)S(1)}, u32[]{:S(2)}, u32[]{:S(2)}) collective-permute-start(bf16[64,1024]{1,0:T(8,128)(2,1)} %bitcast.53), channel_id=1, source_target_pairs={{4,8},{12,16},{20,24},{8,4},{16,12},{24,20},{5,9},{13,17},{21,25},... | collective-permute-start | bytes 393224 | tf_op jit(solution)/shard_map/ppermute | solution.py:279
  5.8 11.5 %collective-permute-start.2 = (bf16[64,1024]{1,0:T(8,128)(2,1)S(1)}, bf16[64,1024]{1,0:T(8,128)(2,1)S(1)}, u32[]{:S(2)}, u32[]{:S(2)}) collective-permute-start(bf16[64,1024]{1,0:T(8,128)(2,1)S(1)} %bitcast.54), channel_id=1, source_target_pairs={{0,16},{4,20},{8,24},{12,28},{16,0},{20,4},{24,8},{28,12},{1,17},{... | collective-permute-start | bytes 393224 | tf_op jit(solution)/shard_map/ppermute | solution.py:274
  19.9 10.4 %copy-start.3 = (f32[64]{0:T(128)S(1)}, f32[64]{0:T(128)}, u32[]{:S(2)}) copy-start(f32[64]{0:T(128)} %param.7) | copy-start | bytes 772
  20.0 10.5 %copy-start.2 = (bf16[64,1,1024]{2,0,1:T(8,128)(2,1)S(1)}, bf16[64,1,1024]{2,0,1:T(8,128)(2,1)}, u32[]{:S(2)}) copy-start(bf16[64,1,1024]{2,0,1:T(8,128)(2,1)} %param.8) | copy-start | bytes 393220
  20.0 2.0 %collective-permute-start.3 = (f32[2,64,1024]{2,1,0:T(8,128)S(1)}, f32[2,64,1024]{2,1,0:T(8,128)S(1)}, u32[]{:S(2)}, u32[]{:S(2)}) collective-permute-start(f32[2,64,1024]{2,1,0:T(8,128)S(1)} %get-tuple-element.35), channel_id=1, source_target_pairs={{0,1},{1,0},{2,3},{3,2},{4,5},{5,4},{6,7},{7,6},{8,9},{9,8},{10,11... | collective-permute-start | bytes 1572872 | tf_op jit(solution)/shard_map/ppermute | solution.py:274
  20.1 8.8 %collective-permute-start.5 = (bf16[2,64,1024]{2,1,0:T(8,128)(2,1)S(1)}, bf16[2,64,1024]{2,1,0:T(8,128)(2,1)S(1)}, u32[]{:S(2)}, u32[]{:S(2)}) collective-permute-start(bf16[2,64,1024]{2,1,0:T(8,128)(2,1)S(1)} %pad_maximum_fusion.1), channel_id=1, source_target_pairs={{0,8},{4,12},{8,0},{12,4},{16,24},{20,28},{24,16},{28,20},{1,9},{5... | collective-permute-start | bytes 786440 | tf_op jit(solution)/shard_map/ppermute | solution.py:274
  22.0 8.4 %collective-permute-start.4 = (f32[64,1024]{1,0:T(8,128)S(1)}, f32[64,1024]{1,0:T(8,128)S(1)}, u32[]{:S(2)}, u32[]{:S(2)}) collective-permute-start(f32[64,1024]{1,0:T(8,128)S(1)} %fusion), channel_id=1, source_target_pairs={{0,2},{1,3},{2,0},{3,1},{4,6},{5,7},{6,4},{7,5},{8,10},{9,11},{10,... | collective-permute-start | bytes 786440 | tf_op jit(solution)/shard_map/ppermute | solution.py:274
  28.9 19.1 %copy-start = (bf16[27,64,256]{2,1,0:T(8,128)(2,1)S(1)}, bf16[27,64,256]{2,1,0:T(8,128)(2,1)}, u32[]{:S(2)}) copy-start(bf16[27,64,256]{2,1,0:T(8,128)(2,1)} %refs_4_.1) | copy-start | bytes 2654212
  30.7 4.3 %collective-permute-start.6 = (bf16[2,16,1024]{2,1,0:T(8,128)(2,1)S(1)}, bf16[2,16,1024]{2,1,0:T(8,128)(2,1)S(1)}, u32[]{:S(2)}, u32[]{:S(2)}) collective-permute-start(bf16[2,16,1024]{2,1,0:T(8,128)(2,1)S(1)} %get-tuple-element.69), channel_id=1, source_target_pairs={{0,4},{4,0},{8,12},{12,8},{16,20},{20,16},{24,28},{28,24},{1,5},{5... | collective-permute-start | bytes 196616 | tf_op jit(solution)/shard_map/ppermute | solution.py:274
  31.9 5.0 %collective-permute-start.8 = (bf16[64,1024]{1,0:T(8,128)(2,1)S(1)}, bf16[64,1024]{1,0:T(8,128)(2,1)S(1)}, u32[]{:S(2)}, u32[]{:S(2)}) collective-permute-start(bf16[64,1024]{1,0:T(8,128)(2,1)S(1)} %get-tuple-element.40.refs_0_), channel_id=1, source_target_pairs={{0,2},{1,3},{2,0},{3,1},{4,6},{5,7},{6,4},{7,5},{8,10},{9,11},{10,... | collective-permute-start | bytes 393224 | tf_op jit(solution)/shard_map/ppermute | solution.py:274
  33.4 7.9 %collective-permute-start.7 = (bf16[64,1024]{1,0:T(8,128)(2,1)S(1)}, bf16[64,1024]{1,0:T(8,128)(2,1)S(1)}, u32[]{:S(2)}, u32[]{:S(2)}) collective-permute-start(bf16[64,1024]{1,0:T(8,128)(2,1)S(1)} %get-tuple-element.40.refs_0_), channel_id=1, source_target_pairs={{0,1},{1,0},{2,3},{3,2},{4,5},{5,4},{6,7},{7,6},{8,9},{9,8},{10,11... | collective-permute-start | bytes 393224 | tf_op jit(solution)/shard_map/ppermute | solution.py:274
  36.9 5.3 %collective-permute-start.9 = (bf16[64,1024]{1,0:T(8,128)(2,1)S(1)}, bf16[64,1024]{1,0:T(8,128)(2,1)S(1)}, u32[]{:S(2)}, u32[]{:S(2)}) collective-permute-start(bf16[64,1024]{1,0:T(8,128)(2,1)S(1)} %collective-permute-done.8.refs_2_), channel_id=1, source_target_pairs={{0,1},{1,0},{2,3},{3,2},{4,5},{5,4},{6,7},{7,6},{8,9},{9,8},{10,11... | collective-permute-start | bytes 393224 | tf_op jit(solution)/shard_map/ppermute | solution.py:274
  36.9 9.5 %collective-permute-start.12 = (bf16[2,16,1024]{2,1,0:T(8,128)(2,1)S(1)}, bf16[2,16,1024]{2,1,0:T(8,128)(2,1)S(1)}, u32[]{:S(2)}, u32[]{:S(2)}) collective-permute-start(bf16[2,16,1024]{2,1,0:T(8,128)(2,1)S(1)} %get-tuple-element.66), channel_id=1, source_target_pairs={{0,24},{4,28},{8,16},{12,20},{16,8},{20,12},{24,0},{28,4},{1,25},{... | collective-permute-start | bytes 196616 | tf_op jit(solution)/shard_map/ppermute | solution.py:274
  39.7 6.3 %collective-permute-start.10 = (bf16[2,16,1024]{2,1,0:T(8,128)(2,1)S(1)}, bf16[2,16,1024]{2,1,0:T(8,128)(2,1)S(1)}, u32[]{:S(2)}, u32[]{:S(2)}) collective-permute-start(bf16[2,16,1024]{2,1,0:T(8,128)(2,1)S(1)} %get-tuple-element.66), channel_id=1, source_target_pairs={{0,8},{4,12},{8,0},{12,4},{16,24},{20,28},{24,16},{28,20},{1,9},{5... | collective-permute-start | bytes 196616 | tf_op jit(solution)/shard_map/ppermute | solution.py:274
  39.7 6.6 %collective-permute-start.11 = (bf16[2,16,1024]{2,1,0:T(8,128)(2,1)S(1)}, bf16[2,16,1024]{2,1,0:T(8,128)(2,1)S(1)}, u32[]{:S(2)}, u32[]{:S(2)}) collective-permute-start(bf16[2,16,1024]{2,1,0:T(8,128)(2,1)S(1)} %get-tuple-element.45), channel_id=1, source_target_pairs={{0,16},{4,20},{8,24},{12,28},{16,0},{20,4},{24,8},{28,12},{1,17},{... | collective-permute-start | bytes 196616 | tf_op jit(solution)/shard_map/ppermute | solution.py:274
  41.4 14.5 %collective-permute-start.14 = (bf16[3,64,1024]{2,1,0:T(8,128)(2,1)S(1)}, bf16[3,64,1024]{2,1,0:T(8,128)(2,1)S(1)}, u32[]{:S(2)}, u32[]{:S(2)}) collective-permute-start(bf16[3,64,1024]{2,1,0:T(8,128)(2,1)S(1)} %pad_maximum_fusion.near), channel_id=1, source_target_pairs={{0,4},{4,0},{8,12},{12,8},{16,20},{20,16},{24,28},{28,24},{1,5},{5... | collective-permute-start | bytes 1179656 | tf_op jit(solution)/shard_map/ppermute | solution.py:274
  46.4 10.1 %copy-start.4 = (s32[6]{0:T(128)S(1)}, s32[6]{0:T(128)}, u32[]{:S(2)}) copy-start(s32[6]{0:T(128)} %constant.19.clone) | copy-start | bytes 76
  46.4 9.5 %collective-permute-start.13 = (bf16[8,16,1024]{2,1,0:T(8,128)(2,1)S(1)}, bf16[8,16,1024]{2,1,0:T(8,128)(2,1)S(1)}, u32[]{:S(2)}, u32[]{:S(2)}) collective-permute-start(bf16[8,16,1024]{2,1,0:T(8,128)(2,1)S(1)} %constant_dynamic-update-slice_fusion.refs_0_), channel_id=1, source_target_pairs={{0,2},{1,3},{2,0},{3,1},{4,6},{5,7},{6,4},{7,5},{8,10},{9,11},{10,... | collective-permute-start | bytes 786440 | tf_op jit(solution)/shard_map/ppermute | solution.py:274
  50.8 5.0 %collective-permute-start.15 = (bf16[64,1024]{1,0:T(8,128)(2,1)S(1)}, bf16[64,1024]{1,0:T(8,128)(2,1)S(1)}, u32[]{:S(2)}, u32[]{:S(2)}) collective-permute-start(bf16[64,1024]{1,0:T(8,128)(2,1)S(1)} %get-tuple-element.47), channel_id=1, source_target_pairs={{0,4},{4,0},{8,12},{12,8},{16,20},{20,16},{24,28},{28,24},{1,5},{5... | collective-permute-start | bytes 393224 | tf_op jit(solution)/shard_map/ppermute | solution.py:274
  51.5 4.4 %collective-permute-start.16 = (bf16[64,1024]{1,0:T(8,128)(2,1)S(1)}, bf16[64,1024]{1,0:T(8,128)(2,1)S(1)}, u32[]{:S(2)}, u32[]{:S(2)}) collective-permute-start(bf16[64,1024]{1,0:T(8,128)(2,1)S(1)} %get-tuple-element.48), channel_id=1, source_target_pairs={{4,8},{12,16},{20,24},{8,4},{16,12},{24,20},{5,9},{13,17},{21,25},... | collective-permute-start | bytes 393224 | tf_op jit(solution)/shard_map/ppermute | solution.py:279
  55.9 1.6 %collective-permute-start.17 = (bf16[8,16,1024]{2,1,0:T(8,128)(2,1)S(1)}, bf16[8,16,1024]{2,1,0:T(8,128)(2,1)S(1)}, u32[]{:S(2)}, u32[]{:S(2)}) collective-permute-start(bf16[8,16,1024]{2,1,0:T(8,128)(2,1)S(1)} %constant_dynamic-update-slice_fusion.refs_0_), channel_id=1, source_target_pairs={{0,1},{1,0},{2,3},{3,2},{4,5},{5,4},{6,7},{7,6},{8,9},{9,8},{10,11... | collective-permute-start | bytes 786440 | tf_op jit(solution)/shard_map/ppermute | solution.py:274
  56.0 1.9 %collective-permute-start.18 = (bf16[8,16,1024]{2,1,0:T(8,128)(2,1)S(1)}, bf16[8,16,1024]{2,1,0:T(8,128)(2,1)S(1)}, u32[]{:S(2)}, u32[]{:S(2)}) collective-permute-start(bf16[8,16,1024]{2,1,0:T(8,128)(2,1)S(1)} %collective-permute-done.13.refs_2_), channel_id=1, source_target_pairs={{0,1},{1,0},{2,3},{3,2},{4,5},{5,4},{6,7},{7,6},{8,9},{9,8},{10,11... | collective-permute-start | bytes 786440 | tf_op jit(solution)/shard_map/ppermute | solution.py:274
  62.4 11.2 %collective-permute-start.21 = (bf16[896,128]{1,0:T(8,128)(2,1)S(1)}, bf16[896,128]{1,0:T(8,128)(2,1)S(1)}, u32[]{:S(2)}, u32[]{:S(2)}) collective-permute-start(bf16[896,128]{1,0:T(8,128)(2,1)S(1)} %filter_block.1.refs_0_), channel_id=1, source_target_pairs={{0,12},{4,8},{8,4},{12,0},{16,28},{20,24},{24,20},{28,16},{1,13},{... | collective-permute-start | bytes 688136 | tf_op jit(solution)/shard_map/ppermute | solution.py:274
  67.2 12.0 %collective-permute-start.20 = (bf16[896,128]{1,0:T(8,128)(2,1)S(1)}, bf16[896,128]{1,0:T(8,128)(2,1)S(1)}, u32[]{:S(2)}, u32[]{:S(2)}) collective-permute-start(bf16[896,128]{1,0:T(8,128)(2,1)S(1)} %filter_block.1.refs_0_), channel_id=1, source_target_pairs={{0,8},{4,12},{8,0},{12,4},{16,24},{20,28},{24,16},{28,20},{1,9},{5... | collective-permute-start | bytes 688136 | tf_op jit(solution)/shard_map/ppermute | solution.py:274
  68.7 10.6 %collective-permute-start.19 = (bf16[896,128]{1,0:T(8,128)(2,1)S(1)}, bf16[896,128]{1,0:T(8,128)(2,1)S(1)}, u32[]{:S(2)}, u32[]{:S(2)}) collective-permute-start(bf16[896,128]{1,0:T(8,128)(2,1)S(1)} %filter_block.1.refs_0_), channel_id=1, source_target_pairs={{0,4},{4,0},{8,12},{12,8},{16,20},{20,16},{24,28},{28,24},{1,5},{5... | collective-permute-start | bytes 688136 | tf_op jit(solution)/shard_map/ppermute | solution.py:274

commit v5 on v4

--- a/solution.py
+++ b/solution.py
@@ -43,15 +43,14 @@
 
 
 def forward_kernel(chans, index, own, partner, outer, weights, keep, give, stack, total):
-    above = 2 * (1 - index[1])
-    for a, plane in ((1, own), (above, partner), (2 - above, outer)):
-        cells = plane[...]
+    low = index[1] == 0
+    below = jnp.where(low, outer[...], partner[...])
+    above = jnp.where(low, partner[...], outer[...])
+    for a, cells in enumerate((below, own[...], above)):
         for b in range(3):
             for e in range(3):
-                start = (9 * a + 3 * b + e) * chans
-                if plane is not own:
-                    start = pl.multiple_of(start, chans)
-                stack[pl.ds(start, chans), :] = moved(cells, b - 1, e - 1)
+                tap = 9 * a + 3 * b + e
+                stack[tap * chans : (tap + 1) * chans, :] = moved(cells, b - 1, e - 1)
     total[...] = jnp.dot(weights[...], stack[...], preferred_element_type=F32)
     for j in range(keep.shape[0]):
         start = pl.multiple_of((index[0] ^ (2 * j)) * chans, chans)
@@ -97,11 +96,11 @@
     total[...] = jnp.dot(
         left[...], stack[...].reshape(9 * outs, CELLS), preferred_element_type=F32
     )
-    above = pl.multiple_of(2 * (1 - index[1]) * chans, chans)
-    below = pl.multiple_of(2 * index[1] * chans, chans)
+    low = index[1] == 0
+    below, above = total[:chans], total[2 * chans :]
     own[...] = total[chans : 2 * chans]
-    partner[...] = total[pl.ds(above, chans), :].astype(BF16)
-    outer[...] = total[pl.ds(below, chans), :].astype(BF16)
+    partner[...] = jnp.where(low, above, below).astype(BF16)
+    outer[...] = jnp.where(low, below, above).astype(BF16)
 
 
 def input_parts(index, grads, weights):
@@ -227,20 +226,21 @@
                 hit, 1.0, 0.0
             ).astype(BF16)
     copies = []
-    for pair in range((TAPS + 1) // 2):
-        at = slice(pair * chans, (pair + 1) * chans)
+    for k, (first, last) in enumerate(CHUNKS):
+        pairs = range(first // 2, (last + 1) // 2)
+        at = slice(pairs[0] * chans, (pairs[-1] + 1) * chans)
         left = jnp.concatenate([block[at, :] for block in blocks], axis=1)
         both = jnp.dot(left, right[...], preferred_element_type=F32)
-        held[2 * pair] = both[:, :total]
-        if 2 * pair + 1 < TAPS:
-            held[2 * pair + 1] = both[:, total:]
-        else:
-            bias[...] = both[0:1, total:] + both[16:17, total:]
-        for k, (first, last) in enumerate(CHUNKS):
-            if last == min(2 * pair + 2, TAPS):
-                part = pl.ds(first, last - first)
-                copies.append(pltpu.make_async_copy(held.at[part], out.at[part], done.at[k]))
-                copies[-1].start()
+        for pair in pairs:
+            row = (pair - pairs[0]) * chans
+            held[2 * pair] = both[row : row + chans, :total]
+            if 2 * pair + 1 < TAPS:
+                held[2 * pair + 1] = both[row : row + chans, total:]
+            else:
+                bias[...] = both[row : row + 1, total:] + both[row + 16 : row + 17, total:]
+        part = pl.ds(first, last - first)
+        copies.append(pltpu.make_async_copy(held.at[part], out.at[part], done.at[k]))
+        copies[-1].start()
     for copy in copies:
         copy.wait()
 
@@ -302,15 +302,15 @@
     barrier = lax.optimization_barrier
 
     own = features.reshape(chans, cells)
-    weights, ahead = barrier((filters.reshape(TAPS * chans, total_out).T, own))
-    near = swapped(ahead, "space", 4)[None]
+    weights = filters.reshape(TAPS * chans, total_out).T
     partner, outer = swapped(own, "space", 1), exchanged(own)
-    outer, partner, near = barrier((outer, partner, near))
+    outer, partner = barrier((outer, partner))
     side = (space & 1).reshape(1)
     where = jnp.concatenate([chan.reshape(1), side])
     keep, give = forward_parts(where, own, partner, outer, weights)
 
     got = swapped(give, "chan", 1)
+    near = swapped(own, "space", 4)[None]
     flips = [4]
     for mask in [1 << k for k in range(depth.bit_length() - 2, 0, -1) if k != 2]:
         own_too = jnp.concatenate([own[None], near], axis=0)
@@ -319,7 +319,6 @@
     pre_act = keep[0] + got[0] + out_bias[:, None]
     for j in range(1, groups // 2):
         pre_act = pre_act + swapped(keep[j] + got[j], "chan", 2 * j)
-    pre_act, near = barrier((pre_act, near))
 
     sigmoid = jax.nn.sigmoid(pre_act)
     activated = pre_act * sigmoid
@@ -333,6 +332,7 @@
     side = space & 1
     kept = jnp.where(side == 0, split[:, 0], split[:, 1])
     given = jnp.where(side == 0, split[:, 1], split[:, 0])
+    given, grad_pre = barrier((given, grad_pre))
     pair = jnp.stack([kept, swapped(given, "space", 1)], axis=0)
     pair, near = barrier((pair, near))
     far = swapped(near, "space", 1)

time: 82 us -> 78.6 us (0.959)
  waiting for transfers between devices: 36.9 us -> 34.9 us
  Pallas kernels: 12.6 us -> 11.4 us
    ppermute x20, waiting for transfers between devices: 36.9 us -> 34.9 us  [swapped(): return lax.ppermute(value, axis, [(i, i ^ mask) for i in range(count)])]
  transfers between devices with their start and end apart: 22 -> 22, of which waited for: 12 -> 10; matrix products, arithmetic and copies ran while one was open for 5% -> 5% of each run, Pallas kernels for 3% -> 4%
where the time goes in v5:
time: 78.6 us; the launch traced here: 78.4 us
  waiting for transfers between devices  34.9 us (44%)
  starting transfers between devices  27.3 us (35%)
  Pallas kernels  11.4 us (15%)
  local copies, waits for them, and re-layouts  3.45 us (4%)
  between operations  0.85 us (1%)
    ppermute x20, waiting for transfers between devices, swapped(): return lax.ppermute(value, axis, [(i, i ^ mask) for i in range(count)])  34.9 us
    ppermute x20, starting transfers between devices, swapped(): return lax.ppermute(value, axis, [(i, i ^ mask) for i in range(count)])  26 us
    pallas_call x1, Pallas kernels, filter_block(): pl.pallas_call(functools.partial(filter_kernel, factor, groups), out_shap...  4.51 us
    pallas_call x1, Pallas kernels, input_parts(): pl.pallas_call(functools.partial(input_kernel, chans, groups), out_shape=...  2.81 us
    pallas_call x1, Pallas kernels, join_blocks(): pl.pallas_call(functools.partial(join_kernel, share, chans), out_shape=[j...  2.11 us
    unnamed x15, local copies, waits for them, and re-layouts  1.99 us
    pallas_call x1, Pallas kernels, forward_parts(): pl.pallas_call(functools.partial(forward_kernel, chans), out_shape=[side,...  1.92 us
  transfers between devices with their start and end apart: 22, of which 10 were waited for; matrix products, arithmetic and copies ran while one was open for 5% of the time, Pallas kernels for 4%

profile of v5, /device:TPU:0, one launch (start us, length us, event | category | flops | bytes accessed | tf_op | source)
XLA Modules:
  0.0 78.4 jit_solution(12160569889659765613)
XLA Ops:
  0.6 3.0 %collective-permute-start.1 = (bf16[64,1024]{1,0:T(8,128)(2,1)}, bf16[64,1024]{1,0:T(8,128)(2,1)S(1)}, u32[]{:S(2)}, u32[]{:S(2)}) collective-permute-start(bf16[64,1024]{1,0:T(8,128)(2,1)} %bitcast.53), channel_id=1, source_target_pairs={{0,4},{4,0},{8,12},{12,8},{16,20},{20,16},{24,28},{28,24},{1,5},{5... | collective-permute-start | bytes 393224 | tf_op jit(solution)/shard_map/ppermute | solution.py:274
  3.6 0.7 collective-permute-start
  4.3 1.5 %copy.13 = bf16[1728,256]{0,1:T(8,128)(2,1)S(1)} copy(bf16[1728,256]{1,0:T(8,128)(2,1)} %bitcast.51) | data formatting | bytes 1769472 | tf_op jit(solution)/shard_map/reshape | solution.py:305
  5.9 1.5 %collective-permute-done.1.partner = bf16[64,1024]{1,0:T(8,128)(2,1)S(1)} collective-permute-done((bf16[64,1024]{1,0:T(8,128)(2,1)}, bf16[64,1024]{1,0:T(8,128)(2,1)S(1)}, u32[]{:S(2)}, u32[]{:S(2)}) %collective-permute-start.1) | collective-permute-done | bytes 131104 | tf_op jit(solution)/shard_map/ppermute | solution.py:274
  7.4 1.9 %forward_parts.1 = (f32[2,64,1024]{2,1,0:T(8,128)S(1)}, f32[2,64,1024]{2,1,0:T(8,128)S(1)}) custom-call(s32[2]{0:T(128)S(1)} %pad_add_fusion.index, bf16[64,1024]{1,0:T(8,128)(2,1)S(1)} %bitcast.55, bf16[64,1024]{1,0:T(8,128)(2,1)S(1)} %collective-permute-done.1.partner, bf16[64,1024]{1,0:T(8,128)(2,1)S(1)} %collective-permute-done.outer, ...), custom_call_target="tpu_custom_call" | custom-call | flops 905969664 | bytes 6291456 | tf_op jit(solution)/shard_map/forward_parts/pallas_call | solution.py:66
  9.4 1.9 %collective-permute-done.2 = f32[2,64,1024]{2,1,0:T(8,128)S(1)} collective-permute-done((f32[2,64,1024]{2,1,0:T(8,128)S(1)}, f32[2,64,1024]{2,1,0:T(8,128)S(1)}, u32[]{:S(2)}, u32[]{:S(2)}) %collective-permute-start.2) | collective-permute-done | bytes 524320 | tf_op jit(solution)/shard_map/ppermute | solution.py:274
  11.3 1.8 %collective-permute-start.3 = (f32[64,1024]{1,0:T(8,128)S(1)}, f32[64,1024]{1,0:T(8,128)S(1)}, u32[]{:S(2)}, u32[]{:S(2)}) collective-permute-start(f32[64,1024]{1,0:T(8,128)S(1)} %fusion), channel_id=1, source_target_pairs={{0,2},{1,3},{2,0},{3,1},{4,6},{5,7},{6,4},{7,5},{8,10},{9,11},{10,... | collective-permute-start | bytes 786440 | tf_op jit(solution)/shard_map/ppermute | solution.py:274
  13.1 6.6 %collective-permute-start.5 = (bf16[64,1024]{1,0:T(8,128)(2,1)S(1)}, bf16[64,1024]{1,0:T(8,128)(2,1)S(1)}, u32[]{:S(2)}, u32[]{:S(2)}) collective-permute-start(bf16[64,1024]{1,0:T(8,128)(2,1)S(1)} %bitcast.56), channel_id=1, source_target_pairs={{0,16},{4,20},{8,24},{12,28},{16,0},{20,4},{24,8},{28,12},{1,17},{... | collective-permute-start | bytes 393224 | tf_op jit(solution)/shard_map/ppermute | solution.py:274
  19.7 6.3 %collective-permute-done.5 = bf16[64,1024]{1,0:T(8,128)(2,1)S(1)} collective-permute-done((bf16[64,1024]{1,0:T(8,128)(2,1)S(1)}, bf16[64,1024]{1,0:T(8,128)(2,1)S(1)}, u32[]{:S(2)}, u32[]{:S(2)}) %collective-permute-start.5) | collective-permute-done | bytes 131104 | tf_op jit(solution)/shard_map/ppermute | solution.py:274
  26.1 0.8 %collective-permute-start.6 = (bf16[2,64,1024]{2,1,0:T(8,128)(2,1)S(1)}, bf16[2,64,1024]{2,1,0:T(8,128)(2,1)S(1)}, u32[]{:S(2)}, u32[]{:S(2)}) collective-permute-start(bf16[2,64,1024]{2,1,0:T(8,128)(2,1)S(1)} %pad_maximum_fusion.1), channel_id=1, source_target_pairs={{0,8},{4,12},{8,0},{12,4},{16,24},{20,28},{24,16},{28,20},{1,9},{5... | collective-permute-start | bytes 786440 | tf_op jit(solution)/shard_map/ppermute | solution.py:274
  26.9 0.2 fusion.5
  27.2 0.6 collective-permute-start.8
  27.8 5.9 %collective-permute-done.6 = bf16[2,64,1024]{2,1,0:T(8,128)(2,1)S(1)} collective-permute-done((bf16[2,64,1024]{2,1,0:T(8,128)(2,1)S(1)}, bf16[2,64,1024]{2,1,0:T(8,128)(2,1)S(1)}, u32[]{:S(2)}, u32[]{:S(2)}) %collective-permute-start.6) | collective-permute-done | bytes 262176 | tf_op jit(solution)/shard_map/ppermute | solution.py:274
  33.8 0.5 collective-permute-start.9
  34.4 4.3 %collective-permute-start.12 = (bf16[2,16,1024]{2,1,0:T(8,128)(2,1)S(1)}, bf16[2,16,1024]{2,1,0:T(8,128)(2,1)S(1)}, u32[]{:S(2)}, u32[]{:S(2)}) collective-permute-start(bf16[2,16,1024]{2,1,0:T(8,128)(2,1)S(1)} %get-tuple-element.60), channel_id=1, source_target_pairs={{0,24},{4,28},{8,16},{12,20},{16,8},{20,12},{24,0},{28,4},{1,25},{... | collective-permute-start | bytes 196616 | tf_op jit(solution)/shard_map/ppermute | solution.py:274
  38.7 0.6 collective-permute-start.11
  39.4 4.1 %collective-permute-done.10 = bf16[2,16,1024]{2,1,0:T(8,128)(2,1)S(1)} collective-permute-done((bf16[2,16,1024]{2,1,0:T(8,128)(2,1)S(1)}, bf16[2,16,1024]{2,1,0:T(8,128)(2,1)S(1)}, u32[]{:S(2)}, u32[]{:S(2)}) %collective-permute-start.10) | collective-permute-done | bytes 65568 | tf_op jit(solution)/shard_map/ppermute | solution.py:274
  43.5 1.1 %collective-permute-done.11 = bf16[2,16,1024]{2,1,0:T(8,128)(2,1)S(1)} collective-permute-done((bf16[2,16,1024]{2,1,0:T(8,128)(2,1)S(1)}, bf16[2,16,1024]{2,1,0:T(8,128)(2,1)S(1)}, u32[]{:S(2)}, u32[]{:S(2)}) %collective-permute-start.11) | collective-permute-done | bytes 65568 | tf_op jit(solution)/shard_map/ppermute | solution.py:274
  44.6 0.6 collective-permute-start.13
  45.1 2.8 %input_parts.1 = (f32[64,1024]{1,0:T(8,128)S(1)}, bf16[64,1024]{1,0:T(8,128)(2,1)S(1)}, bf16[64,1024]{1,0:T(8,128)(2,1)S(1)}) custom-call(s32[2]{0:T(128)S(1)} %pad_add_fusion.index, bf16[64,1024]{1,0:T(8,128)(2,1)S(1)} %get-tuple-element.34.refs_0_, bf16[64,1024]{1,0:T(8,128)(2,1)S(1)} %collective-permute-done.7.refs_1_, ...), custom_call_target="tpu_custom_call" | custom-call | flops 905969664 | bytes 6291456 | tf_op jit(solution)/shard_map/input_parts/pallas_call | solution.py:111
  48.1 0.7 collective-permute-start.16
  48.8 4.2 %collective-permute-done.15 = bf16[64,1024]{1,0:T(8,128)(2,1)S(1)} collective-permute-done((bf16[64,1024]{1,0:T(8,128)(2,1)S(1)}, bf16[64,1024]{1,0:T(8,128)(2,1)S(1)}, u32[]{:S(2)}, u32[]{:S(2)}) %collective-permute-start.15) | collective-permute-done | bytes 131104 | tf_op jit(solution)/shard_map/ppermute | solution.py:274
  53.1 0.5 collective-permute-start.18
  53.8 1.0 %copy.17 = f32[64,1,1024]{2,1,0:T(1,128)} copy(f32[64,1,1024]{2,0,1:T(8,128)S(1)} %multiply_bitcast_fusion) | data formatting | bytes 524288
  54.7 0.3 collective-permute-done.18.refs_3_
  55.0 4.5 %filter_block.1.refs_0_ = bf16[896,128]{1,0:T(8,128)(2,1)S(1)} custom-call(s32[8]{0:T(128)S(1)} %pad_add_fusion.1.index, bf16[64,1024]{1,0:T(8,128)(2,1)S(1)} %bitcast.58, bf16[64,1024]{1,0:T(8,128)(2,1)S(1)} %collective-permute-done.1.partner, bf16[3,64,1024]{2,1,0:T(8,128)(2,1)S(1)} %pad_maximum_fusion.near, ...), custom_call_target="tpu_custom_call" | custom-call | flops 1811939328 | bytes 8388608 | tf_op jit(solution)/shard_map/filter_block/pallas_call | solution.py:193
  59.5 5.6 %collective-permute-start.21 = (bf16[896,128]{1,0:T(8,128)(2,1)S(1)}, bf16[896,128]{1,0:T(8,128)(2,1)S(1)}, u32[]{:S(2)}, u32[]{:S(2)}) collective-permute-start(bf16[896,128]{1,0:T(8,128)(2,1)S(1)} %filter_block.1.refs_0_), channel_id=1, source_target_pairs={{0,12},{4,8},{8,4},{12,0},{16,28},{20,24},{24,20},{28,16},{1,13},{... | collective-permute-start | bytes 688136 | tf_op jit(solution)/shard_map/ppermute | solution.py:274
  65.1 0.7 collective-permute-start.20
  65.8 1.0 %copy.18 = f32[64,1,1024]{2,1,0:T(1,128)} copy(f32[64,1,1024]{2,0,1:T(8,128)S(1)} %add_bitcast_fusion) | data formatting | bytes 524288
  66.7 4.8 %collective-permute-done.21.refs_3_ = bf16[896,128]{1,0:T(8,128)(2,1)S(1)} collective-permute-done((bf16[896,128]{1,0:T(8,128)(2,1)S(1)}, bf16[896,128]{1,0:T(8,128)(2,1)S(1)}, u32[]{:S(2)}, u32[]{:S(2)}) %collective-permute-start.21) | collective-permute-done | bytes 229408 | tf_op jit(solution)/shard_map/ppermute | solution.py:274
  71.5 4.8 %collective-permute-done.20.refs_2_ = bf16[896,128]{1,0:T(8,128)(2,1)S(1)} collective-permute-done((bf16[896,128]{1,0:T(8,128)(2,1)S(1)}, bf16[896,128]{1,0:T(8,128)(2,1)S(1)}, u32[]{:S(2)}, u32[]{:S(2)}) %collective-permute-start.20) | collective-permute-done | bytes 229408 | tf_op jit(solution)/shard_map/ppermute | solution.py:274
  76.3 2.1 %join_blocks.1 = (f32[27,64,256]{2,1,0:T(8,128)}, f32[1,256]{1,0:T(1,128)}) custom-call(s32[1]{0:T(128)} %bitcast.19.index, bf16[896,128]{1,0:T(8,128)(2,1)S(1)} %filter_block.1.refs_0_, bf16[896,128]{1,0:T(8,128)(2,1)S(1)} %collective-permute-done.19.refs_1_, bf16[896,128]{1,0:T(8,128)(2,1)S(1)} %collective-permute-done.20.refs_2_, ...), custom_call_target="tpu_custom_call" | custom-call | flops 452984832 | bytes 4194304 | tf_op jit(solution)/shard_map/join_blocks/pallas_call | solution.py:251
  (44 shorter events, 0.9 us)
Async XLA Ops:
  0.6 6.7 %copy-start.1 = (bf16[64,1,1024]{2,0,1:T(8,128)(2,1)S(1)}, bf16[64,1,1024]{2,0,1:T(8,128)(2,1)}, u32[]{:S(2)}) copy-start(bf16[64,1,1024]{2,0,1:T(8,128)(2,1)} %param.5) | copy-start | bytes 393220
  0.6 6.7 %collective-permute-start.1 = (bf16[64,1024]{1,0:T(8,128)(2,1)}, bf16[64,1024]{1,0:T(8,128)(2,1)S(1)}, u32[]{:S(2)}, u32[]{:S(2)}) collective-permute-start(bf16[64,1024]{1,0:T(8,128)(2,1)} %bitcast.53), channel_id=1, source_target_pairs={{0,4},{4,0},{8,12},{12,8},{16,20},{20,16},{24,28},{28,24},{1,5},{5... | collective-permute-start | bytes 393224 | tf_op jit(solution)/shard_map/ppermute | solution.py:274
  3.6 3.7 %collective-permute-start = (bf16[64,1024]{1,0:T(8,128)(2,1)}, bf16[64,1024]{1,0:T(8,128)(2,1)S(1)}, u32[]{:S(2)}, u32[]{:S(2)}) collective-permute-start(bf16[64,1024]{1,0:T(8,128)(2,1)} %bitcast.54), channel_id=1, source_target_pairs={{4,8},{12,16},{20,24},{8,4},{16,12},{24,20},{5,9},{13,17},{21,25},... | collective-permute-start | bytes 393224 | tf_op jit(solution)/shard_map/ppermute | solution.py:279
  7.4 19.5 %copy-start.2 = (bf16[64,1,1024]{2,0,1:T(8,128)(2,1)S(1)}, bf16[64,1,1024]{2,0,1:T(8,128)(2,1)}, u32[]{:S(2)}) copy-start(bf16[64,1,1024]{2,0,1:T(8,128)(2,1)} %param.8) | copy-start | bytes 393220
  7.4 19.5 %copy-start.3 = (f32[64]{0:T(128)S(1)}, f32[64]{0:T(128)}, u32[]{:S(2)}) copy-start(f32[64]{0:T(128)} %param.7) | copy-start | bytes 772
  9.3 2.0 %collective-permute-start.2 = (f32[2,64,1024]{2,1,0:T(8,128)S(1)}, f32[2,64,1024]{2,1,0:T(8,128)S(1)}, u32[]{:S(2)}, u32[]{:S(2)}) collective-permute-start(f32[2,64,1024]{2,1,0:T(8,128)S(1)} %get-tuple-element.30), channel_id=1, source_target_pairs={{0,1},{1,0},{2,3},{3,2},{4,5},{5,4},{6,7},{7,6},{8,9},{9,8},{10,11... | collective-permute-start | bytes 1572872 | tf_op jit(solution)/shard_map/ppermute | solution.py:274
  11.3 15.6 %collective-permute-start.3 = (f32[64,1024]{1,0:T(8,128)S(1)}, f32[64,1024]{1,0:T(8,128)S(1)}, u32[]{:S(2)}, u32[]{:S(2)}) collective-permute-start(f32[64,1024]{1,0:T(8,128)S(1)} %fusion), channel_id=1, source_target_pairs={{0,2},{1,3},{2,0},{3,1},{4,6},{5,7},{6,4},{7,5},{8,10},{9,11},{10,... | collective-permute-start | bytes 786440 | tf_op jit(solution)/shard_map/ppermute | solution.py:274
  13.1 12.9 %collective-permute-start.5 = (bf16[64,1024]{1,0:T(8,128)(2,1)S(1)}, bf16[64,1024]{1,0:T(8,128)(2,1)S(1)}, u32[]{:S(2)}, u32[]{:S(2)}) collective-permute-start(bf16[64,1024]{1,0:T(8,128)(2,1)S(1)} %bitcast.56), channel_id=1, source_target_pairs={{0,16},{4,20},{8,24},{12,28},{16,0},{20,4},{24,8},{28,12},{1,17},{... | collective-permute-start | bytes 393224 | tf_op jit(solution)/shard_map/ppermute | solution.py:274
  26.1 19.1 %copy-start = (bf16[27,64,256]{2,1,0:T(8,128)(2,1)S(1)}, bf16[27,64,256]{2,1,0:T(8,128)(2,1)}, u32[]{:S(2)}) copy-start(bf16[27,64,256]{2,1,0:T(8,128)(2,1)} %refs_4_.1) | copy-start | bytes 2654212
  26.1 7.6 %collective-permute-start.6 = (bf16[2,64,1024]{2,1,0:T(8,128)(2,1)S(1)}, bf16[2,64,1024]{2,1,0:T(8,128)(2,1)S(1)}, u32[]{:S(2)}, u32[]{:S(2)}) collective-permute-start(bf16[2,64,1024]{2,1,0:T(8,128)(2,1)S(1)} %pad_maximum_fusion.1), channel_id=1, source_target_pairs={{0,8},{4,12},{8,0},{12,4},{16,24},{20,28},{24,16},{28,20},{1,9},{5... | collective-permute-start | bytes 786440 | tf_op jit(solution)/shard_map/ppermute | solution.py:274
  27.1 6.7 %collective-permute-start.4 = (bf16[2,16,1024]{2,1,0:T(8,128)(2,1)S(1)}, bf16[2,16,1024]{2,1,0:T(8,128)(2,1)S(1)}, u32[]{:S(2)}, u32[]{:S(2)}) collective-permute-start(bf16[2,16,1024]{2,1,0:T(8,128)(2,1)S(1)} %get-tuple-element.31), channel_id=1, source_target_pairs={{0,4},{4,0},{8,12},{12,8},{16,20},{20,16},{24,28},{28,24},{1,5},{5... | collective-permute-start | bytes 196616 | tf_op jit(solution)/shard_map/ppermute | solution.py:274
  27.2 6.6 %collective-permute-start.8 = (bf16[64,1024]{1,0:T(8,128)(2,1)S(1)}, bf16[64,1024]{1,0:T(8,128)(2,1)S(1)}, u32[]{:S(2)}, u32[]{:S(2)}) collective-permute-start(bf16[64,1024]{1,0:T(8,128)(2,1)S(1)} %get-tuple-element.34.refs_0_), channel_id=1, source_target_pairs={{0,2},{1,3},{2,0},{3,1},{4,6},{5,7},{6,4},{7,5},{8,10},{9,11},{10,... | collective-permute-start | bytes 393224 | tf_op jit(solution)/shard_map/ppermute | solution.py:274
  33.7 5.7 %collective-permute-start.7 = (bf16[64,1024]{1,0:T(8,128)(2,1)S(1)}, bf16[64,1024]{1,0:T(8,128)(2,1)S(1)}, u32[]{:S(2)}, u32[]{:S(2)}) collective-permute-start(bf16[64,1024]{1,0:T(8,128)(2,1)S(1)} %get-tuple-element.34.refs_0_), channel_id=1, source_target_pairs={{0,1},{1,0},{2,3},{3,2},{4,5},{5,4},{6,7},{7,6},{8,9},{9,8},{10,11... | collective-permute-start | bytes 393224 | tf_op jit(solution)/shard_map/ppermute | solution.py:274
  33.8 5.5 %collective-permute-start.9 = (bf16[64,1024]{1,0:T(8,128)(2,1)S(1)}, bf16[64,1024]{1,0:T(8,128)(2,1)S(1)}, u32[]{:S(2)}, u32[]{:S(2)}) collective-permute-start(bf16[64,1024]{1,0:T(8,128)(2,1)S(1)} %collective-permute-done.8.refs_2_), channel_id=1, source_target_pairs={{0,1},{1,0},{2,3},{3,2},{4,5},{5,4},{6,7},{7,6},{8,9},{9,8},{10,11... | collective-permute-start | bytes 393224 | tf_op jit(solution)/shard_map/ppermute | solution.py:274
  34.4 10.2 %collective-permute-start.12 = (bf16[2,16,1024]{2,1,0:T(8,128)(2,1)S(1)}, bf16[2,16,1024]{2,1,0:T(8,128)(2,1)S(1)}, u32[]{:S(2)}, u32[]{:S(2)}) collective-permute-start(bf16[2,16,1024]{2,1,0:T(8,128)(2,1)S(1)} %get-tuple-element.60), channel_id=1, source_target_pairs={{0,24},{4,28},{8,16},{12,20},{16,8},{20,12},{24,0},{28,4},{1,25},{... | collective-permute-start | bytes 196616 | tf_op jit(solution)/shard_map/ppermute | solution.py:274
  38.7 4.7 %collective-permute-start.10 = (bf16[2,16,1024]{2,1,0:T(8,128)(2,1)S(1)}, bf16[2,16,1024]{2,1,0:T(8,128)(2,1)S(1)}, u32[]{:S(2)}, u32[]{:S(2)}) collective-permute-start(bf16[2,16,1024]{2,1,0:T(8,128)(2,1)S(1)} %get-tuple-element.60), channel_id=1, source_target_pairs={{0,8},{4,12},{8,0},{12,4},{16,24},{20,28},{24,16},{28,20},{1,9},{5... | collective-permute-start | bytes 196616 | tf_op jit(solution)/shard_map/ppermute | solution.py:274
  38.7 5.8 %collective-permute-start.11 = (bf16[2,16,1024]{2,1,0:T(8,128)(2,1)S(1)}, bf16[2,16,1024]{2,1,0:T(8,128)(2,1)S(1)}, u32[]{:S(2)}, u32[]{:S(2)}) collective-permute-start(bf16[2,16,1024]{2,1,0:T(8,128)(2,1)S(1)} %get-tuple-element.39), channel_id=1, source_target_pairs={{0,16},{4,20},{8,24},{12,28},{16,0},{20,4},{24,8},{28,12},{1,17},{... | collective-permute-start | bytes 196616 | tf_op jit(solution)/shard_map/ppermute | solution.py:274
  39.4 13.7 %collective-permute-start.14 = (bf16[3,64,1024]{2,1,0:T(8,128)(2,1)S(1)}, bf16[3,64,1024]{2,1,0:T(8,128)(2,1)S(1)}, u32[]{:S(2)}, u32[]{:S(2)}) collective-permute-start(bf16[3,64,1024]{2,1,0:T(8,128)(2,1)S(1)} %pad_maximum_fusion.near), channel_id=1, source_target_pairs={{0,4},{4,0},{8,12},{12,8},{16,20},{20,16},{24,28},{28,24},{1,5},{5... | collective-permute-start | bytes 1179656 | tf_op jit(solution)/shard_map/ppermute | solution.py:274
  44.5 9.1 %copy-start.4 = (s32[6]{0:T(128)S(1)}, s32[6]{0:T(128)}, u32[]{:S(2)}) copy-start(s32[6]{0:T(128)} %constant.19.clone) | copy-start | bytes 76
  44.6 8.4 %collective-permute-start.13 = (bf16[8,16,1024]{2,1,0:T(8,128)(2,1)S(1)}, bf16[8,16,1024]{2,1,0:T(8,128)(2,1)S(1)}, u32[]{:S(2)}, u32[]{:S(2)}) collective-permute-start(bf16[8,16,1024]{2,1,0:T(8,128)(2,1)S(1)} %constant_dynamic-update-slice_fusion.refs_0_), channel_id=1, source_target_pairs={{0,2},{1,3},{2,0},{3,1},{4,6},{5,7},{6,4},{7,5},{8,10},{9,11},{10,... | collective-permute-start | bytes 786440 | tf_op jit(solution)/shard_map/ppermute | solution.py:274
  48.0 5.0 %collective-permute-start.15 = (bf16[64,1024]{1,0:T(8,128)(2,1)S(1)}, bf16[64,1024]{1,0:T(8,128)(2,1)S(1)}, u32[]{:S(2)}, u32[]{:S(2)}) collective-permute-start(bf16[64,1024]{1,0:T(8,128)(2,1)S(1)} %get-tuple-element.41), channel_id=1, source_target_pairs={{0,4},{4,0},{8,12},{12,8},{16,20},{20,16},{24,28},{28,24},{1,5},{5... | collective-permute-start | bytes 393224 | tf_op jit(solution)/shard_map/ppermute | solution.py:274
  48.1 4.9 %collective-permute-start.16 = (bf16[64,1024]{1,0:T(8,128)(2,1)S(1)}, bf16[64,1024]{1,0:T(8,128)(2,1)S(1)}, u32[]{:S(2)}, u32[]{:S(2)}) collective-permute-start(bf16[64,1024]{1,0:T(8,128)(2,1)S(1)} %get-tuple-element.42), channel_id=1, source_target_pairs={{4,8},{12,16},{20,24},{8,4},{16,12},{24,20},{5,9},{13,17},{21,25},... | collective-permute-start | bytes 393224 | tf_op jit(solution)/shard_map/ppermute | solution.py:279
  53.0 1.7 %collective-permute-start.17 = (bf16[8,16,1024]{2,1,0:T(8,128)(2,1)S(1)}, bf16[8,16,1024]{2,1,0:T(8,128)(2,1)S(1)}, u32[]{:S(2)}, u32[]{:S(2)}) collective-permute-start(bf16[8,16,1024]{2,1,0:T(8,128)(2,1)S(1)} %constant_dynamic-update-slice_fusion.refs_0_), channel_id=1, source_target_pairs={{0,1},{1,0},{2,3},{3,2},{4,5},{5,4},{6,7},{7,6},{8,9},{9,8},{10,11... | collective-permute-start | bytes 786440 | tf_op jit(solution)/shard_map/ppermute | solution.py:274
  53.1 1.9 %collective-permute-start.18 = (bf16[8,16,1024]{2,1,0:T(8,128)(2,1)S(1)}, bf16[8,16,1024]{2,1,0:T(8,128)(2,1)S(1)}, u32[]{:S(2)}, u32[]{:S(2)}) collective-permute-start(bf16[8,16,1024]{2,1,0:T(8,128)(2,1)S(1)} %collective-permute-done.13.refs_2_), channel_id=1, source_target_pairs={{0,1},{1,0},{2,3},{3,2},{4,5},{5,4},{6,7},{7,6},{8,9},{9,8},{10,11... | collective-permute-start | bytes 786440 | tf_op jit(solution)/shard_map/ppermute | solution.py:274
  59.5 12.0 %collective-permute-start.21 = (bf16[896,128]{1,0:T(8,128)(2,1)S(1)}, bf16[896,128]{1,0:T(8,128)(2,1)S(1)}, u32[]{:S(2)}, u32[]{:S(2)}) collective-permute-start(bf16[896,128]{1,0:T(8,128)(2,1)S(1)} %filter_block.1.refs_0_), channel_id=1, source_target_pairs={{0,12},{4,8},{8,4},{12,0},{16,28},{20,24},{24,20},{28,16},{1,13},{... | collective-permute-start | bytes 688136 | tf_op jit(solution)/shard_map/ppermute | solution.py:274
  65.1 11.2 %collective-permute-start.20 = (bf16[896,128]{1,0:T(8,128)(2,1)S(1)}, bf16[896,128]{1,0:T(8,128)(2,1)S(1)}, u32[]{:S(2)}, u32[]{:S(2)}) collective-permute-start(bf16[896,128]{1,0:T(8,128)(2,1)S(1)} %filter_block.1.refs_0_), channel_id=1, source_target_pairs={{0,8},{4,12},{8,0},{12,4},{16,24},{20,28},{24,16},{28,20},{1,9},{5... | collective-permute-start | bytes 688136 | tf_op jit(solution)/shard_map/ppermute | solution.py:274
  65.7 10.6 %collective-permute-start.19 = (bf16[896,128]{1,0:T(8,128)(2,1)S(1)}, bf16[896,128]{1,0:T(8,128)(2,1)S(1)}, u32[]{:S(2)}, u32[]{:S(2)}) collective-permute-start(bf16[896,128]{1,0:T(8,128)(2,1)S(1)} %filter_block.1.refs_0_), channel_id=1, source_target_pairs={{0,4},{4,0},{8,12},{12,8},{16,20},{20,16},{24,28},{28,24},{1,5},{5... | collective-permute-start | bytes 688136 | tf_op jit(solution)/shard_map/ppermute | solution.py:274

commit v6 on v5

--- a/solution.py
+++ b/solution.py
@@ -43,14 +43,25 @@
 
 
 def forward_kernel(chans, index, own, partner, outer, weights, keep, give, stack, total):
-    low = index[1] == 0
-    below = jnp.where(low, outer[...], partner[...])
-    above = jnp.where(low, partner[...], outer[...])
-    for a, cells in enumerate((below, own[...], above)):
+    def place(a, plane):
+        cells = plane[...]
         for b in range(3):
             for e in range(3):
                 tap = 9 * a + 3 * b + e
                 stack[tap * chans : (tap + 1) * chans, :] = moved(cells, b - 1, e - 1)
+
+    place(1, own)
+
+    @pl.when(index[1] == 0)
+    def _():
+        place(0, outer)
+        place(2, partner)
+
+    @pl.when(index[1] != 0)
+    def _():
+        place(0, partner)
+        place(2, outer)
+
     total[...] = jnp.dot(weights[...], stack[...], preferred_element_type=F32)
     for j in range(keep.shape[0]):
         start = pl.multiple_of((index[0] ^ (2 * j)) * chans, chans)
@@ -80,13 +91,13 @@
     )(index, own, partner, outer, weights)
 
 
-def input_kernel(chans, groups, index, *refs):
-    grads = refs[:groups]
-    weights, own, partner, outer, stack, left, total = refs[groups:]
+def input_kernel(chans, chips, index, *refs):
+    grads = refs[:chips]
+    weights, own, partner, outer, stack, left, total = refs[chips:]
     outs = weights.shape[2]
-    for u in range(groups):
+    for u in range(2 * chips):
         start = pl.multiple_of((index[0] ^ u) * chans, chans)
-        cells = grads[u][...]
+        cells = grads[u // 2][u % 2]
         for b in range(3):
             for e in range(3):
                 stack[3 * b + e, pl.ds(start, chans), :] = moved(cells, 1 - b, 1 - e)
@@ -96,22 +107,28 @@
     total[...] = jnp.dot(
         left[...], stack[...].reshape(9 * outs, CELLS), preferred_element_type=F32
     )
-    low = index[1] == 0
-    below, above = total[:chans], total[2 * chans :]
     own[...] = total[chans : 2 * chans]
-    partner[...] = jnp.where(low, above, below).astype(BF16)
-    outer[...] = jnp.where(low, below, above).astype(BF16)
+
+    @pl.when(index[1] == 0)
+    def _():
+        partner[...] = total[2 * chans :].astype(BF16)
+        outer[...] = total[:chans].astype(BF16)
+
+    @pl.when(index[1] != 0)
+    def _():
+        partner[...] = total[:chans].astype(BF16)
+        outer[...] = total[2 * chans :].astype(BF16)
 
 
 def input_parts(index, grads, weights):
     chans = weights.shape[1]
     outs = weights.shape[2]
-    groups = len(grads)
+    chips = len(grads)
     sides = jax.ShapeDtypeStruct((chans, CELLS), BF16)
     return pl.pallas_call(
-        functools.partial(input_kernel, chans, groups),
+        functools.partial(input_kernel, chans, chips),
         out_shape=[jax.ShapeDtypeStruct((chans, CELLS), F32), sides, sides],
-        in_specs=[SMEM] + [VMEM] * (groups + 1),
+        in_specs=[SMEM] + [VMEM] * (chips + 1),
         out_specs=[VMEM] * 3,
         scratch_shapes=[
             pltpu.VMEM((9, outs, CELLS), BF16),
@@ -310,15 +327,18 @@
     keep, give = forward_parts(where, own, partner, outer, weights)
 
     got = swapped(give, "chan", 1)
-    near = swapped(own, "space", 4)[None]
-    flips = [4]
-    for mask in [1 << k for k in range(depth.bit_length() - 2, 0, -1) if k != 2]:
+    near = [swapped(own, "space", 4), swapped(own, "space", 2)]
+    pre_act = keep[0] + got[0] + out_bias[:, None]
+    for j in range(1, groups // 2):
+        pre_act = pre_act + swapped(keep[j] + got[j], "chan", 2 * j)
+
+    pre_act, near = barrier((pre_act, near))
+    near = jnp.stack(near + [swapped(near[0], "space", 2)], axis=0)
+    flips = [4, 2, 6]
+    for mask in [1 << k for k in range(3, depth.bit_length() - 1)]:
         own_too = jnp.concatenate([own[None], near], axis=0)
         near = jnp.concatenate([near, swapped(own_too, "space", mask)], axis=0)
         flips = flips + [f ^ mask for f in [0] + flips]
-    pre_act = keep[0] + got[0] + out_bias[:, None]
-    for j in range(1, groups // 2):
-        pre_act = pre_act + swapped(keep[j] + got[j], "chan", 2 * j)
 
     sigmoid = jax.nn.sigmoid(pre_act)
     activated = pre_act * sigmoid
@@ -334,7 +354,6 @@
     given = jnp.where(side == 0, split[:, 1], split[:, 0])
     given, grad_pre = barrier((given, grad_pre))
     pair = jnp.stack([kept, swapped(given, "space", 1)], axis=0)
-    pair, near = barrier((pair, near))
     far = swapped(near, "space", 1)
     flips = flips + [f ^ 1 for f in flips]
     side = (space >> 1) & 1
@@ -344,7 +363,7 @@
     for t in range(1, depth // 2):
         pieces.append(swapped(given if t & 1 else kept, "space", 2 * t))
 
-    grads = both_cores(other_chips(grad_pre))
+    grads = other_chips(jnp.stack([grad_pre, swapped(grad_pre, "chan", 1)], axis=0))
     pieces[0], grads = barrier((pieces[0], grads))
     blocks = other_chips(jnp.concatenate(pieces, axis=0))
 

time: 78.6 us -> 75.6 us (0.962)
  waiting for transfers between devices: 34.9 us -> 29.5 us
  starting transfers between devices: 27.3 us -> 29 us
    ppermute x20, waiting for transfers between devices: 34.9 us -> 29.5 us  [swapped(): return lax.ppermute(value, axis, [(i, i ^ mask) for i in range(count)])]
    ppermute x20, starting transfers between devices: 26 us -> 27.7 us  [swapped(): return lax.ppermute(value, axis, [(i, i ^ mask) for i in range(count)])]
  transfers between devices with their start and end apart: 22 -> 22, of which waited for: 10 -> 12; matrix products, arithmetic and copies ran while one was open for 5% -> 5% of each run, Pallas kernels for 4% -> 4%
where the time goes in v6:
time: 75.6 us; the launch traced here: 75.4 us
  waiting for transfers between devices  29.5 us (39%)
  starting transfers between devices  29 us (38%)
  Pallas kernels  12.1 us (16%)
  local copies, waits for them, and re-layouts  3.45 us (5%)
  between operations  0.83 us (1%)
    ppermute x20, waiting for transfers between devices, swapped(): return lax.ppermute(value, axis, [(i, i ^ mask) for i in range(count)])  29.5 us
    ppermute x20, starting transfers between devices, swapped(): return lax.ppermute(value, axis, [(i, i ^ mask) for i in range(count)])  27.7 us
    pallas_call x1, Pallas kernels, filter_block(): pl.pallas_call(functools.partial(filter_kernel, factor, groups), out_shap...  4.52 us
    pallas_call x1, Pallas kernels, input_parts(): pl.pallas_call(functools.partial(input_kernel, chans, chips), out_shape=[...  2.82 us
    pallas_call x1, Pallas kernels, forward_parts(): pl.pallas_call(functools.partial(forward_kernel, chans), out_shape=[side,...  2.68 us
    pallas_call x1, Pallas kernels, join_blocks(): pl.pallas_call(functools.partial(join_kernel, share, chans), out_shape=[j...  2.11 us
    unnamed x15, local copies, waits for them, and re-layouts  1.99 us
  transfers between devices with their start and end apart: 22, of which 12 were waited for; matrix products, arithmetic and copies ran while one was open for 5% of the time, Pallas kernels for 4%

profile of v6, /device:TPU:0, one launch (start us, length us, event | category | flops | bytes accessed | tf_op | source)
XLA Modules:
  0.0 75.4 jit_solution(12040087549764496946)
XLA Ops:
  0.6 3.0 %collective-permute-start.1 = (bf16[64,1024]{1,0:T(8,128)(2,1)}, bf16[64,1024]{1,0:T(8,128)(2,1)S(1)}, u32[]{:S(2)}, u32[]{:S(2)}) collective-permute-start(bf16[64,1024]{1,0:T(8,128)(2,1)} %bitcast.54), channel_id=1, source_target_pairs={{0,4},{4,0},{8,12},{12,8},{16,20},{20,16},{24,28},{28,24},{1,5},{5... | collective-permute-start | bytes 393224 | tf_op jit(solution)/shard_map/ppermute | solution.py:291
  3.6 0.7 collective-permute-start
  4.3 1.5 %copy.13 = bf16[1728,256]{0,1:T(8,128)(2,1)S(1)} copy(bf16[1728,256]{1,0:T(8,128)(2,1)} %bitcast.53) | data formatting | bytes 1769472 | tf_op jit(solution)/shard_map/reshape | solution.py:322
  5.9 1.5 %collective-permute-done.1.partner = bf16[64,1024]{1,0:T(8,128)(2,1)S(1)} collective-permute-done((bf16[64,1024]{1,0:T(8,128)(2,1)}, bf16[64,1024]{1,0:T(8,128)(2,1)S(1)}, u32[]{:S(2)}, u32[]{:S(2)}) %collective-permute-start.1) | collective-permute-done | bytes 131104 | tf_op jit(solution)/shard_map/ppermute | solution.py:291
  7.4 2.7 %forward_parts.1 = (f32[2,64,1024]{2,1,0:T(8,128)S(1)}, f32[2,64,1024]{2,1,0:T(8,128)S(1)}) custom-call(s32[2]{0:T(128)S(1)} %pad_add_fusion.index, bf16[64,1024]{1,0:T(8,128)(2,1)S(1)} %bitcast.56, bf16[64,1024]{1,0:T(8,128)(2,1)S(1)} %collective-permute-done.1.partner, bf16[64,1024]{1,0:T(8,128)(2,1)S(1)} %collective-permute-done.outer, ...), custom_call_target="tpu_custom_call" | custom-call | flops 905969664 | bytes 6291456 | tf_op jit(solution)/shard_map/forward_parts/pallas_call | solution.py:77
  10.1 1.9 %collective-permute-done.2 = f32[2,64,1024]{2,1,0:T(8,128)S(1)} collective-permute-done((f32[2,64,1024]{2,1,0:T(8,128)S(1)}, f32[2,64,1024]{2,1,0:T(8,128)S(1)}, u32[]{:S(2)}, u32[]{:S(2)}) %collective-permute-start.2) | collective-permute-done | bytes 524320 | tf_op jit(solution)/shard_map/ppermute | solution.py:291
  12.1 1.8 %collective-permute-start.3 = (f32[64,1024]{1,0:T(8,128)S(1)}, f32[64,1024]{1,0:T(8,128)S(1)}, u32[]{:S(2)}, u32[]{:S(2)}) collective-permute-start(f32[64,1024]{1,0:T(8,128)S(1)} %fusion), channel_id=1, source_target_pairs={{0,2},{1,3},{2,0},{3,1},{4,6},{5,7},{6,4},{7,5},{8,10},{9,11},{10,... | collective-permute-start | bytes 786440 | tf_op jit(solution)/shard_map/ppermute | solution.py:291
  13.9 5.6 %collective-permute-start.5 = (bf16[64,1024]{1,0:T(8,128)(2,1)S(1)}, bf16[64,1024]{1,0:T(8,128)(2,1)S(1)}, u32[]{:S(2)}, u32[]{:S(2)}) collective-permute-start(bf16[64,1024]{1,0:T(8,128)(2,1)S(1)} %bitcast.57), channel_id=1, source_target_pairs={{0,8},{4,12},{8,0},{12,4},{16,24},{20,28},{24,16},{28,20},{1,9},{5... | collective-permute-start | bytes 393224 | tf_op jit(solution)/shard_map/ppermute | solution.py:291
  19.5 2.6 %collective-permute-start.4 = (bf16[64,1024]{1,0:T(8,128)(2,1)S(1)}, bf16[64,1024]{1,0:T(8,128)(2,1)S(1)}, u32[]{:S(2)}, u32[]{:S(2)}) collective-permute-start(bf16[64,1024]{1,0:T(8,128)(2,1)S(1)} %bitcast.58), channel_id=1, source_target_pairs={{0,16},{4,20},{8,24},{12,28},{16,0},{20,4},{24,8},{28,12},{1,17},{... | collective-permute-start | bytes 393224 | tf_op jit(solution)/shard_map/ppermute | solution.py:291
  22.2 2.7 %collective-permute-done.5 = bf16[64,1024]{1,0:T(8,128)(2,1)S(1)} collective-permute-done((bf16[64,1024]{1,0:T(8,128)(2,1)S(1)}, bf16[64,1024]{1,0:T(8,128)(2,1)S(1)}, u32[]{:S(2)}, u32[]{:S(2)}) %collective-permute-start.5) | collective-permute-done | bytes 131104 | tf_op jit(solution)/shard_map/ppermute | solution.py:291
  24.9 3.4 %collective-permute-done.4 = bf16[64,1024]{1,0:T(8,128)(2,1)S(1)} collective-permute-done((bf16[64,1024]{1,0:T(8,128)(2,1)S(1)}, bf16[64,1024]{1,0:T(8,128)(2,1)S(1)}, u32[]{:S(2)}, u32[]{:S(2)}) %collective-permute-start.4) | collective-permute-done | bytes 131104 | tf_op jit(solution)/shard_map/ppermute | solution.py:291
  28.4 0.6 collective-permute-start.6
  29.0 0.7 collective-permute-done.7
  29.8 0.6 collective-permute-start.8
  30.8 2.1 %collective-permute-done.6 = bf16[2,16,1024]{2,1,0:T(8,128)(2,1)S(1)} collective-permute-done((bf16[2,16,1024]{2,1,0:T(8,128)(2,1)S(1)}, bf16[2,16,1024]{2,1,0:T(8,128)(2,1)S(1)}, u32[]{:S(2)}, u32[]{:S(2)}) %collective-permute-start.6) | collective-permute-done | bytes 65568 | tf_op jit(solution)/shard_map/ppermute | solution.py:291
  33.0 2.5 %collective-permute-start.11 = (bf16[2,16,1024]{2,1,0:T(8,128)(2,1)S(1)}, bf16[2,16,1024]{2,1,0:T(8,128)(2,1)S(1)}, u32[]{:S(2)}, u32[]{:S(2)}) collective-permute-start(bf16[2,16,1024]{2,1,0:T(8,128)(2,1)S(1)} %get-tuple-element.58), channel_id=1, source_target_pairs={{0,24},{4,28},{8,16},{12,20},{16,8},{20,12},{24,0},{28,4},{1,25},{... | collective-permute-start | bytes 196616 | tf_op jit(solution)/shard_map/ppermute | solution.py:291
  35.5 1.9 %collective-permute-start.10 = (bf16[2,16,1024]{2,1,0:T(8,128)(2,1)S(1)}, bf16[2,16,1024]{2,1,0:T(8,128)(2,1)S(1)}, u32[]{:S(2)}, u32[]{:S(2)}) collective-permute-start(bf16[2,16,1024]{2,1,0:T(8,128)(2,1)S(1)} %get-tuple-element.36), channel_id=1, source_target_pairs={{0,16},{4,20},{8,24},{12,28},{16,0},{20,4},{24,8},{28,12},{1,17},{... | collective-permute-start | bytes 196616 | tf_op jit(solution)/shard_map/ppermute | solution.py:291
  37.5 0.6 collective-permute-start.14
  38.2 3.2 %collective-permute-done.9 = bf16[2,16,1024]{2,1,0:T(8,128)(2,1)S(1)} collective-permute-done((bf16[2,16,1024]{2,1,0:T(8,128)(2,1)S(1)}, bf16[2,16,1024]{2,1,0:T(8,128)(2,1)S(1)}, u32[]{:S(2)}, u32[]{:S(2)}) %collective-permute-start.9) | collective-permute-done | bytes 65568 | tf_op jit(solution)/shard_map/ppermute | solution.py:291
  41.5 0.7 collective-permute-start.12
  42.2 2.8 %input_parts.1 = (f32[64,1024]{1,0:T(8,128)S(1)}, bf16[64,1024]{1,0:T(8,128)(2,1)S(1)}, bf16[64,1024]{1,0:T(8,128)(2,1)S(1)}) custom-call(s32[2]{0:T(128)S(1)} %pad_add_fusion.index, bf16[2,64,1024]{2,1,0:T(8,128)(2,1)S(1)} %pad_maximum_fusion.1.refs_0_, bf16[2,64,1024]{2,1,0:T(8,128)(2,1)S(1)} %collective-permute-done.8.refs_1_, ...), custom_call_target="tpu_custom_call" | custom-call | flops 905969664 | bytes 6291456 | tf_op jit(solution)/shard_map/input_parts/pallas_call | solution.py:128
  45.0 0.6 collective-permute-start.15
  45.6 0.7 collective-permute-start.16
  46.2 4.0 %collective-permute-done.15 = bf16[64,1024]{1,0:T(8,128)(2,1)S(1)} collective-permute-done((bf16[64,1024]{1,0:T(8,128)(2,1)S(1)}, bf16[64,1024]{1,0:T(8,128)(2,1)S(1)}, u32[]{:S(2)}, u32[]{:S(2)}) %collective-permute-start.15) | collective-permute-done | bytes 131104 | tf_op jit(solution)/shard_map/ppermute | solution.py:291
  50.9 1.0 %copy.17 = f32[64,1,1024]{2,1,0:T(1,128)} copy(f32[64,1,1024]{2,0,1:T(8,128)S(1)} %get-tuple-element.57) | data formatting | bytes 524288
  52.2 4.5 %filter_block.1.refs_0_ = bf16[896,128]{1,0:T(8,128)(2,1)S(1)} custom-call(s32[8]{0:T(128)S(1)} %pad_add_fusion.1.index, bf16[64,1024]{1,0:T(8,128)(2,1)S(1)} %bitcast.59, bf16[64,1024]{1,0:T(8,128)(2,1)S(1)} %collective-permute-done.1.partner, bf16[3,64,1024]{2,1,0:T(8,128)(2,1)S(1)} %pad_maximum_fusion.near, ...), custom_call_target="tpu_custom_call" | custom-call | flops 1811939328 | bytes 8388608 | tf_op jit(solution)/shard_map/filter_block/pallas_call | solution.py:210
  56.7 5.2 %collective-permute-start.21 = (bf16[896,128]{1,0:T(8,128)(2,1)S(1)}, bf16[896,128]{1,0:T(8,128)(2,1)S(1)}, u32[]{:S(2)}, u32[]{:S(2)}) collective-permute-start(bf16[896,128]{1,0:T(8,128)(2,1)S(1)} %filter_block.1.refs_0_), channel_id=1, source_target_pairs={{0,12},{4,8},{8,4},{12,0},{16,28},{20,24},{24,20},{28,16},{1,13},{... | collective-permute-start | bytes 688136 | tf_op jit(solution)/shard_map/ppermute | solution.py:291
  61.9 0.9 %collective-permute-start.20 = (bf16[896,128]{1,0:T(8,128)(2,1)S(1)}, bf16[896,128]{1,0:T(8,128)(2,1)S(1)}, u32[]{:S(2)}, u32[]{:S(2)}) collective-permute-start(bf16[896,128]{1,0:T(8,128)(2,1)S(1)} %filter_block.1.refs_0_), channel_id=1, source_target_pairs={{0,8},{4,12},{8,0},{12,4},{16,24},{20,28},{24,16},{28,20},{1,9},{5... | collective-permute-start | bytes 688136 | tf_op jit(solution)/shard_map/ppermute | solution.py:291
  62.8 1.0 %copy.18 = f32[64,1,1024]{2,1,0:T(1,128)} copy(f32[64,1,1024]{2,0,1:T(8,128)S(1)} %add_bitcast_fusion) | data formatting | bytes 524288
  63.8 4.5 %collective-permute-done.21.refs_3_ = bf16[896,128]{1,0:T(8,128)(2,1)S(1)} collective-permute-done((bf16[896,128]{1,0:T(8,128)(2,1)S(1)}, bf16[896,128]{1,0:T(8,128)(2,1)S(1)}, u32[]{:S(2)}, u32[]{:S(2)}) %collective-permute-start.21) | collective-permute-done | bytes 229408 | tf_op jit(solution)/shard_map/ppermute | solution.py:291
  68.3 5.0 %collective-permute-done.20.refs_2_ = bf16[896,128]{1,0:T(8,128)(2,1)S(1)} collective-permute-done((bf16[896,128]{1,0:T(8,128)(2,1)S(1)}, bf16[896,128]{1,0:T(8,128)(2,1)S(1)}, u32[]{:S(2)}, u32[]{:S(2)}) %collective-permute-start.20) | collective-permute-done | bytes 229408 | tf_op jit(solution)/shard_map/ppermute | solution.py:291
  73.3 2.1 %join_blocks.1 = (f32[27,64,256]{2,1,0:T(8,128)}, f32[1,256]{1,0:T(1,128)}) custom-call(s32[1]{0:T(128)} %bitcast.22.index, bf16[896,128]{1,0:T(8,128)(2,1)S(1)} %filter_block.1.refs_0_, bf16[896,128]{1,0:T(8,128)(2,1)S(1)} %collective-permute-done.19.refs_1_, bf16[896,128]{1,0:T(8,128)(2,1)S(1)} %collective-permute-done.20.refs_2_, ...), custom_call_target="tpu_custom_call" | custom-call | flops 452984832 | bytes 4194304 | tf_op jit(solution)/shard_map/join_blocks/pallas_call | solution.py:268
  (43 shorter events, 2.3 us)
Async XLA Ops:
  0.6 6.7 %copy-start.1 = (bf16[64,1,1024]{2,0,1:T(8,128)(2,1)S(1)}, bf16[64,1,1024]{2,0,1:T(8,128)(2,1)}, u32[]{:S(2)}) copy-start(bf16[64,1,1024]{2,0,1:T(8,128)(2,1)} %param.5) | copy-start | bytes 393220
  0.6 6.7 %collective-permute-start.1 = (bf16[64,1024]{1,0:T(8,128)(2,1)}, bf16[64,1024]{1,0:T(8,128)(2,1)S(1)}, u32[]{:S(2)}, u32[]{:S(2)}) collective-permute-start(bf16[64,1024]{1,0:T(8,128)(2,1)} %bitcast.54), channel_id=1, source_target_pairs={{0,4},{4,0},{8,12},{12,8},{16,20},{20,16},{24,28},{28,24},{1,5},{5... | collective-permute-start | bytes 393224 | tf_op jit(solution)/shard_map/ppermute | solution.py:291
  3.6 3.7 %collective-permute-start = (bf16[64,1024]{1,0:T(8,128)(2,1)}, bf16[64,1024]{1,0:T(8,128)(2,1)S(1)}, u32[]{:S(2)}, u32[]{:S(2)}) collective-permute-start(bf16[64,1024]{1,0:T(8,128)(2,1)} %bitcast.55), channel_id=1, source_target_pairs={{4,8},{12,16},{20,24},{8,4},{16,12},{24,20},{5,9},{13,17},{21,25},... | collective-permute-start | bytes 393224 | tf_op jit(solution)/shard_map/ppermute | solution.py:296
  7.4 14.7 %copy-start.3 = (f32[64]{0:T(128)S(1)}, f32[64]{0:T(128)}, u32[]{:S(2)}) copy-start(f32[64]{0:T(128)} %param.7) | copy-start | bytes 772
  7.4 20.8 %copy-start.2 = (bf16[64,1,1024]{2,0,1:T(8,128)(2,1)S(1)}, bf16[64,1,1024]{2,0,1:T(8,128)(2,1)}, u32[]{:S(2)}) copy-start(bf16[64,1,1024]{2,0,1:T(8,128)(2,1)} %param.8) | copy-start | bytes 393220
  10.1 2.0 %collective-permute-start.2 = (f32[2,64,1024]{2,1,0:T(8,128)S(1)}, f32[2,64,1024]{2,1,0:T(8,128)S(1)}, u32[]{:S(2)}, u32[]{:S(2)}) collective-permute-start(f32[2,64,1024]{2,1,0:T(8,128)S(1)} %get-tuple-element.29), channel_id=1, source_target_pairs={{0,1},{1,0},{2,3},{3,2},{4,5},{5,4},{6,7},{7,6},{8,9},{9,8},{10,11... | collective-permute-start | bytes 1572872 | tf_op jit(solution)/shard_map/ppermute | solution.py:291
  12.1 10.0 %collective-permute-start.3 = (f32[64,1024]{1,0:T(8,128)S(1)}, f32[64,1024]{1,0:T(8,128)S(1)}, u32[]{:S(2)}, u32[]{:S(2)}) collective-permute-start(f32[64,1024]{1,0:T(8,128)S(1)} %fusion), channel_id=1, source_target_pairs={{0,2},{1,3},{2,0},{3,1},{4,6},{5,7},{6,4},{7,5},{8,10},{9,11},{10,... | collective-permute-start | bytes 786440 | tf_op jit(solution)/shard_map/ppermute | solution.py:291
  13.9 10.9 %collective-permute-start.5 = (bf16[64,1024]{1,0:T(8,128)(2,1)S(1)}, bf16[64,1024]{1,0:T(8,128)(2,1)S(1)}, u32[]{:S(2)}, u32[]{:S(2)}) collective-permute-start(bf16[64,1024]{1,0:T(8,128)(2,1)S(1)} %bitcast.57), channel_id=1, source_target_pairs={{0,8},{4,12},{8,0},{12,4},{16,24},{20,28},{24,16},{28,20},{1,9},{5... | collective-permute-start | bytes 393224 | tf_op jit(solution)/shard_map/ppermute | solution.py:291
  19.5 8.7 %collective-permute-start.4 = (bf16[64,1024]{1,0:T(8,128)(2,1)S(1)}, bf16[64,1024]{1,0:T(8,128)(2,1)S(1)}, u32[]{:S(2)}, u32[]{:S(2)}) collective-permute-start(bf16[64,1024]{1,0:T(8,128)(2,1)S(1)} %bitcast.58), channel_id=1, source_target_pairs={{0,16},{4,20},{8,24},{12,28},{16,0},{20,4},{24,8},{28,12},{1,17},{... | collective-permute-start | bytes 393224 | tf_op jit(solution)/shard_map/ppermute | solution.py:291
  22.2 20.0 %copy-start = (bf16[27,64,256]{2,1,0:T(8,128)(2,1)S(1)}, bf16[27,64,256]{2,1,0:T(8,128)(2,1)}, u32[]{:S(2)}) copy-start(bf16[27,64,256]{2,1,0:T(8,128)(2,1)} %refs_2_.1) | copy-start | bytes 2654212
  28.4 1.4 %collective-permute-start.7 = (bf16[64,1024]{1,0:T(8,128)(2,1)S(1)}, bf16[64,1024]{1,0:T(8,128)(2,1)S(1)}, u32[]{:S(2)}, u32[]{:S(2)}) collective-permute-start(bf16[64,1024]{1,0:T(8,128)(2,1)S(1)} %get-tuple-element.32), channel_id=1, source_target_pairs={{0,1},{1,0},{2,3},{3,2},{4,5},{5,4},{6,7},{7,6},{8,9},{9,8},{10,11... | collective-permute-start | bytes 393224 | tf_op jit(solution)/shard_map/ppermute | solution.py:291
  28.4 4.5 %collective-permute-start.6 = (bf16[2,16,1024]{2,1,0:T(8,128)(2,1)S(1)}, bf16[2,16,1024]{2,1,0:T(8,128)(2,1)S(1)}, u32[]{:S(2)}, u32[]{:S(2)}) collective-permute-start(bf16[2,16,1024]{2,1,0:T(8,128)(2,1)S(1)} %get-tuple-element.31), channel_id=1, source_target_pairs={{0,4},{4,0},{8,12},{12,8},{16,20},{20,16},{24,28},{28,24},{1,5},{5... | collective-permute-start | bytes 196616 | tf_op jit(solution)/shard_map/ppermute | solution.py:291
  29.8 8.4 %collective-permute-start.8 = (bf16[2,64,1024]{2,1,0:T(8,128)(2,1)S(1)}, bf16[2,64,1024]{2,1,0:T(8,128)(2,1)S(1)}, u32[]{:S(2)}, u32[]{:S(2)}) collective-permute-start(bf16[2,64,1024]{2,1,0:T(8,128)(2,1)S(1)} %pad_maximum_fusion.1.refs_0_), channel_id=1, source_target_pairs={{0,2},{1,3},{2,0},{3,1},{4,6},{5,7},{6,4},{7,5},{8,10},{9,11},{10,... | collective-permute-start | bytes 786440 | tf_op jit(solution)/shard_map/ppermute | solution.py:291
  30.4 7.0 %collective-permute-start.13 = (bf16[64,1024]{1,0:T(8,128)(2,1)S(1)}, bf16[64,1024]{1,0:T(8,128)(2,1)S(1)}, u32[]{:S(2)}, u32[]{:S(2)}) collective-permute-start(bf16[64,1024]{1,0:T(8,128)(2,1)S(1)} %collective-permute-done.4), channel_id=1, source_target_pairs={{0,8},{4,12},{8,0},{12,4},{16,24},{20,28},{24,16},{28,20},{1,9},{5... | collective-permute-start | bytes 393224 | tf_op jit(solution)/shard_map/ppermute | solution.py:291
  33.0 8.5 %collective-permute-start.11 = (bf16[2,16,1024]{2,1,0:T(8,128)(2,1)S(1)}, bf16[2,16,1024]{2,1,0:T(8,128)(2,1)S(1)}, u32[]{:S(2)}, u32[]{:S(2)}) collective-permute-start(bf16[2,16,1024]{2,1,0:T(8,128)(2,1)S(1)} %get-tuple-element.58), channel_id=1, source_target_pairs={{0,24},{4,28},{8,16},{12,20},{16,8},{20,12},{24,0},{28,4},{1,25},{... | collective-permute-start | bytes 196616 | tf_op jit(solution)/shard_map/ppermute | solution.py:291
  35.5 5.9 %collective-permute-start.9 = (bf16[2,16,1024]{2,1,0:T(8,128)(2,1)S(1)}, bf16[2,16,1024]{2,1,0:T(8,128)(2,1)S(1)}, u32[]{:S(2)}, u32[]{:S(2)}) collective-permute-start(bf16[2,16,1024]{2,1,0:T(8,128)(2,1)S(1)} %get-tuple-element.58), channel_id=1, source_target_pairs={{0,8},{4,12},{8,0},{12,4},{16,24},{20,28},{24,16},{28,20},{1,9},{5... | collective-permute-start | bytes 196616 | tf_op jit(solution)/shard_map/ppermute | solution.py:291
  35.5 5.9 %collective-permute-start.10 = (bf16[2,16,1024]{2,1,0:T(8,128)(2,1)S(1)}, bf16[2,16,1024]{2,1,0:T(8,128)(2,1)S(1)}, u32[]{:S(2)}, u32[]{:S(2)}) collective-permute-start(bf16[2,16,1024]{2,1,0:T(8,128)(2,1)S(1)} %get-tuple-element.36), channel_id=1, source_target_pairs={{0,16},{4,20},{8,24},{12,28},{16,0},{20,4},{24,8},{28,12},{1,17},{... | collective-permute-start | bytes 196616 | tf_op jit(solution)/shard_map/ppermute | solution.py:291
  37.5 12.7 %collective-permute-start.14 = (bf16[3,64,1024]{2,1,0:T(8,128)(2,1)S(1)}, bf16[3,64,1024]{2,1,0:T(8,128)(2,1)S(1)}, u32[]{:S(2)}, u32[]{:S(2)}) collective-permute-start(bf16[3,64,1024]{2,1,0:T(8,128)(2,1)S(1)} %pad_maximum_fusion.near), channel_id=1, source_target_pairs={{0,4},{4,0},{8,12},{12,8},{16,20},{20,16},{24,28},{28,24},{1,5},{5... | collective-permute-start | bytes 1179656 | tf_op jit(solution)/shard_map/ppermute | solution.py:291
  41.4 9.4 %copy-start.4 = (s32[6]{0:T(128)S(1)}, s32[6]{0:T(128)}, u32[]{:S(2)}) copy-start(s32[6]{0:T(128)} %constant.19.clone) | copy-start | bytes 76
  41.5 8.7 %collective-permute-start.12 = (bf16[8,16,1024]{2,1,0:T(8,128)(2,1)S(1)}, bf16[8,16,1024]{2,1,0:T(8,128)(2,1)S(1)}, u32[]{:S(2)}, u32[]{:S(2)}) collective-permute-start(bf16[8,16,1024]{2,1,0:T(8,128)(2,1)S(1)} %constant_dynamic-update-slice_fusion.refs_0_), channel_id=1, source_target_pairs={{0,2},{1,3},{2,0},{3,1},{4,6},{5,7},{6,4},{7,5},{8,10},{9,11},{10,... | collective-permute-start | bytes 786440 | tf_op jit(solution)/shard_map/ppermute | solution.py:291
  45.0 5.2 %collective-permute-start.15 = (bf16[64,1024]{1,0:T(8,128)(2,1)S(1)}, bf16[64,1024]{1,0:T(8,128)(2,1)S(1)}, u32[]{:S(2)}, u32[]{:S(2)}) collective-permute-start(bf16[64,1024]{1,0:T(8,128)(2,1)S(1)} %get-tuple-element.39), channel_id=1, source_target_pairs={{0,4},{4,0},{8,12},{12,8},{16,20},{20,16},{24,28},{28,24},{1,5},{5... | collective-permute-start | bytes 393224 | tf_op jit(solution)/shard_map/ppermute | solution.py:291
  45.6 4.6 %collective-permute-start.16 = (bf16[64,1024]{1,0:T(8,128)(2,1)S(1)}, bf16[64,1024]{1,0:T(8,128)(2,1)S(1)}, u32[]{:S(2)}, u32[]{:S(2)}) collective-permute-start(bf16[64,1024]{1,0:T(8,128)(2,1)S(1)} %get-tuple-element.40), channel_id=1, source_target_pairs={{4,8},{12,16},{20,24},{8,4},{16,12},{24,20},{5,9},{13,17},{21,25},... | collective-permute-start | bytes 393224 | tf_op jit(solution)/shard_map/ppermute | solution.py:296
  50.2 1.6 %collective-permute-start.17 = (bf16[8,16,1024]{2,1,0:T(8,128)(2,1)S(1)}, bf16[8,16,1024]{2,1,0:T(8,128)(2,1)S(1)}, u32[]{:S(2)}, u32[]{:S(2)}) collective-permute-start(bf16[8,16,1024]{2,1,0:T(8,128)(2,1)S(1)} %constant_dynamic-update-slice_fusion.refs_0_), channel_id=1, source_target_pairs={{0,1},{1,0},{2,3},{3,2},{4,5},{5,4},{6,7},{7,6},{8,9},{9,8},{10,11... | collective-permute-start | bytes 786440 | tf_op jit(solution)/shard_map/ppermute | solution.py:291
  50.3 1.9 %collective-permute-start.18 = (bf16[8,16,1024]{2,1,0:T(8,128)(2,1)S(1)}, bf16[8,16,1024]{2,1,0:T(8,128)(2,1)S(1)}, u32[]{:S(2)}, u32[]{:S(2)}) collective-permute-start(bf16[8,16,1024]{2,1,0:T(8,128)(2,1)S(1)} %collective-permute-done.12.refs_2_), channel_id=1, source_target_pairs={{0,1},{1,0},{2,3},{3,2},{4,5},{5,4},{6,7},{7,6},{8,9},{9,8},{10,11... | collective-permute-start | bytes 786440 | tf_op jit(solution)/shard_map/ppermute | solution.py:291
  56.7 11.6 %collective-permute-start.21 = (bf16[896,128]{1,0:T(8,128)(2,1)S(1)}, bf16[896,128]{1,0:T(8,128)(2,1)S(1)}, u32[]{:S(2)}, u32[]{:S(2)}) collective-permute-start(bf16[896,128]{1,0:T(8,128)(2,1)S(1)} %filter_block.1.refs_0_), channel_id=1, source_target_pairs={{0,12},{4,8},{8,4},{12,0},{16,28},{20,24},{24,20},{28,16},{1,13},{... | collective-permute-start | bytes 688136 | tf_op jit(solution)/shard_map/ppermute | solution.py:291
  61.9 11.5 %collective-permute-start.20 = (bf16[896,128]{1,0:T(8,128)(2,1)S(1)}, bf16[896,128]{1,0:T(8,128)(2,1)S(1)}, u32[]{:S(2)}, u32[]{:S(2)}) collective-permute-start(bf16[896,128]{1,0:T(8,128)(2,1)S(1)} %filter_block.1.refs_0_), channel_id=1, source_target_pairs={{0,8},{4,12},{8,0},{12,4},{16,24},{20,28},{24,16},{28,20},{1,9},{5... | collective-permute-start | bytes 688136 | tf_op jit(solution)/shard_map/ppermute | solution.py:291
  62.7 10.6 %collective-permute-start.19 = (bf16[896,128]{1,0:T(8,128)(2,1)S(1)}, bf16[896,128]{1,0:T(8,128)(2,1)S(1)}, u32[]{:S(2)}, u32[]{:S(2)}) collective-permute-start(bf16[896,128]{1,0:T(8,128)(2,1)S(1)} %filter_block.1.refs_0_), channel_id=1, source_target_pairs={{0,4},{4,0},{8,12},{12,8},{16,20},{20,16},{24,28},{28,24},{1,5},{5... | collective-permute-start | bytes 688136 | tf_op jit(solution)/shard_map/ppermute | solution.py:291

commit v7 on v6

--- a/solution.py
+++ b/solution.py
@@ -43,25 +43,12 @@
 
 
 def forward_kernel(chans, index, own, partner, outer, weights, keep, give, stack, total):
-    def place(a, plane):
+    for k, plane in enumerate((own, partner, outer)):
         cells = plane[...]
         for b in range(3):
             for e in range(3):
-                tap = 9 * a + 3 * b + e
-                stack[tap * chans : (tap + 1) * chans, :] = moved(cells, b - 1, e - 1)
-
-    place(1, own)
-
-    @pl.when(index[1] == 0)
-    def _():
-        place(0, outer)
-        place(2, partner)
-
-    @pl.when(index[1] != 0)
-    def _():
-        place(0, partner)
-        place(2, outer)
-
+                start = (9 * k + 3 * b + e) * chans
+                stack[start : start + chans, :] = moved(cells, b - 1, e - 1)
     total[...] = jnp.dot(weights[...], stack[...], preferred_element_type=F32)
     for j in range(keep.shape[0]):
         start = pl.multiple_of((index[0] ^ (2 * j)) * chans, chans)
@@ -93,7 +80,7 @@
 
 def input_kernel(chans, chips, index, *refs):
     grads = refs[:chips]
-    weights, own, partner, outer, stack, left, total = refs[chips:]
+    weights, own, partner, outer, stack, left = refs[chips:]
     outs = weights.shape[2]
     for u in range(2 * chips):
         start = pl.multiple_of((index[0] ^ u) * chans, chans)
@@ -101,23 +88,15 @@
         for b in range(3):
             for e in range(3):
                 stack[3 * b + e, pl.ds(start, chans), :] = moved(cells, 1 - b, 1 - e)
-    for a in range(3):
+    for row, a in enumerate((1, 2 * (1 - index[1]), 2 * index[1])):
         for k in range(9):
-            left[a * chans : (a + 1) * chans, k * outs : (k + 1) * outs] = weights[9 * a + k]
-    total[...] = jnp.dot(
+            left[row * chans : (row + 1) * chans, k * outs : (k + 1) * outs] = weights[9 * a + k]
+    total = jnp.dot(
         left[...], stack[...].reshape(9 * outs, CELLS), preferred_element_type=F32
     )
-    own[...] = total[chans : 2 * chans]
-
-    @pl.when(index[1] == 0)
-    def _():
-        partner[...] = total[2 * chans :].astype(BF16)
-        outer[...] = total[:chans].astype(BF16)
-
-    @pl.when(index[1] != 0)
-    def _():
-        partner[...] = total[:chans].astype(BF16)
-        outer[...] = total[2 * chans :].astype(BF16)
+    own[...] = total[:chans]
+    partner[...] = total[chans : 2 * chans].astype(BF16)
+    outer[...] = total[2 * chans :].astype(BF16)
 
 
 def input_parts(index, grads, weights):
@@ -133,7 +112,6 @@
         scratch_shapes=[
             pltpu.VMEM((9, outs, CELLS), BF16),
             pltpu.VMEM((3 * chans, 9 * outs), BF16),
-            pltpu.VMEM((3 * chans, CELLS), F32),
         ],
         compiler_params=pltpu.CompilerParams(vmem_limit_bytes=20 << 20),
         cost_estimate=pl.CostEstimate(
@@ -319,11 +297,14 @@
     barrier = lax.optimization_barrier
 
     own = features.reshape(chans, cells)
-    weights = filters.reshape(TAPS * chans, total_out).T
     partner, outer = swapped(own, "space", 1), exchanged(own)
     outer, partner = barrier((outer, partner))
-    side = (space & 1).reshape(1)
-    where = jnp.concatenate([chan.reshape(1), side])
+    side = space & 1
+    where = jnp.stack([chan, side])
+    slabs = filters.reshape(3, 9 * chans, total_out)
+    weights = jnp.concatenate(
+        [slabs[1], slabs[2 * (1 - side)], slabs[2 * side]], axis=0
+    ).T
     keep, give = forward_parts(where, own, partner, outer, weights)
 
     got = swapped(give, "chan", 1)
@@ -364,10 +345,9 @@
         pieces.append(swapped(given if t & 1 else kept, "space", 2 * t))
 
     grads = other_chips(jnp.stack([grad_pre, swapped(grad_pre, "chan", 1)], axis=0))
-    pieces[0], grads = barrier((pieces[0], grads))
+    in_grad, to_partner, to_outer = input_parts(where, grads, filters)
+    pieces[0], to_partner, to_outer = barrier((pieces[0], to_partner, to_outer))
     blocks = other_chips(jnp.concatenate(pieces, axis=0))
-
-    in_grad, to_partner, to_outer = input_parts(where, grads, filters)
     from_partner, from_outer = swapped(to_partner, "space", 1), exchanged(to_outer)
     blocks, far, from_partner, from_outer = barrier((blocks, far, from_partner, from_outer))
     blocks = both_cores(blocks)

time: 75.6 us -> 73.6 us (0.974)
  starting transfers between devices: 29 us -> 27 us
  local copies, waits for them, and re-layouts: 3.45 us -> 5.15 us
  waiting for transfers between devices: 29.5 us -> 28.6 us
  Pallas kernels: 12.1 us -> 11.3 us
    ppermute x20, starting transfers between devices: 27.7 us -> 25.7 us  [swapped(): return lax.ppermute(value, axis, [(i, i ^ mask) for i in range(count)])]
    reshape x1 -> x0, local copies, waits for them, and re-layouts: 1.45 us -> none  [body(): weights = filters.reshape(TAPS * chans, total_out).T]
    dynamic_slice x0 -> x1, local copies, waits for them, and re-layouts: none -> 1.09 us  [body(): slabs[2 * side]]
    slice x0 -> x1, local copies, waits for them, and re-layouts: none -> 0.98 us  [body(): slabs[1]]
    ppermute x20, waiting for transfers between devices: 29.5 us -> 28.6 us  [swapped(): return lax.ppermute(value, axis, [(i, i ^ mask) for i in range(count)])]
    pallas_call x1, Pallas kernels: 2.68 us -> 1.91 us  [forward_parts(): pl.pallas_call(functools.partial(forward_kernel, chans), out_shape=[side,...]
    unnamed x15 -> x17, local copies, waits for them, and re-layouts: 1.99 us -> 2.4 us
  transfers between devices with their start and end apart: 22 -> 22, of which waited for: 12 -> 11; matrix products, arithmetic and copies ran while one was open for 5% -> 7% of each run, Pallas kernels for 4% -> 4%
where the time goes in v7:
time: 73.6 us; the launch traced here: 73.4 us
  waiting for transfers between devices  28.6 us (39%)
  starting transfers between devices  27 us (37%)
  Pallas kernels  11.3 us (15%)
  local copies, waits for them, and re-layouts  5.15 us (7%)
  between operations  0.85 us (1%)
    ppermute x20, waiting for transfers between devices, swapped(): return lax.ppermute(value, axis, [(i, i ^ mask) for i in range(count)])  28.6 us
    ppermute x20, starting transfers between devices, swapped(): return lax.ppermute(value, axis, [(i, i ^ mask) for i in range(count)])  25.7 us
    pallas_call x1, Pallas kernels, filter_block(): pl.pallas_call(functools.partial(filter_kernel, factor, groups), out_shap...  4.52 us
    pallas_call x1, Pallas kernels, input_parts(): pl.pallas_call(functools.partial(input_kernel, chans, chips), out_shape=[...  2.79 us
    unnamed x17, local copies, waits for them, and re-layouts  2.4 us
    pallas_call x1, Pallas kernels, join_blocks(): pl.pallas_call(functools.partial(join_kernel, share, chans), out_shape=[j...  2.11 us
    pallas_call x1, Pallas kernels, forward_parts(): pl.pallas_call(functools.partial(forward_kernel, chans), out_shape=[side,...  1.91 us
  transfers between devices with their start and end apart: 22, of which 11 were waited for; matrix products, arithmetic and copies ran while one was open for 7% of the time, Pallas kernels for 4%

profile of v7, /device:TPU:0, one launch (start us, length us, event | category | flops | bytes accessed | tf_op | source)
XLA Modules:
  0.0 73.4 jit_solution(11217316766828320764)
XLA Ops:
  0.6 3.0 %collective-permute-start.1 = (bf16[64,1024]{1,0:T(8,128)(2,1)}, bf16[64,1024]{1,0:T(8,128)(2,1)S(1)}, u32[]{:S(2)}, u32[]{:S(2)}) collective-permute-start(bf16[64,1024]{1,0:T(8,128)(2,1)} %bitcast.57), channel_id=1, source_target_pairs={{0,4},{4,0},{8,12},{12,8},{16,20},{20,16},{24,28},{28,24},{1,5},{5... | collective-permute-start | bytes 393224 | tf_op jit(solution)/shard_map/ppermute | solution.py:269
  3.6 0.7 collective-permute-start
  4.3 1.1 %constant_dynamic-slice_fusion = (bf16[1,576,256]{2,1,0:T(8,128)(2,1)S(1)}, bf16[1,576,256]{2,1,0:T(8,128)(2,1)S(1)}) fusion(bf16[3,576,256]{2,1,0:T(8,128)(2,1)} %bitcast.56, s32[]{:T(128)S(6)} %select_n.48, s32[]{:T(128)S(6)} %select_n.47), kind=kLoop, calls=%fused_computation.30 | loop fusion | bytes 1179656 | tf_op jit(solution)/shard_map/dynamic_slice | solution.py:306
  5.4 1.0 %slice.32 = bf16[9,64,256]{2,1,0:T(8,128)(2,1)S(1)} slice(bf16[27,64,256]{2,1,0:T(8,128)(2,1)} %refs_2_.1), slice={[9:18], [0:64], [0:256]} | slice | bytes 589824 | tf_op jit(solution)/shard_map/slice | solution.py:306
  7.6 1.9 %forward_parts.1 = (f32[2,64,1024]{2,1,0:T(8,128)S(1)}, f32[2,64,1024]{2,1,0:T(8,128)S(1)}) custom-call(s32[2]{0:T(128)S(1)} %pad_add_fusion.index, bf16[64,1024]{1,0:T(8,128)(2,1)S(1)} %bitcast.59, bf16[64,1024]{1,0:T(8,128)(2,1)S(1)} %collective-permute-done.1.partner, bf16[64,1024]{1,0:T(8,128)(2,1)S(1)} %collective-permute-done.outer, ...), custom_call_target="tpu_custom_call" | custom-call | flops 905969664 | bytes 6291456 | tf_op jit(solution)/shard_map/forward_parts/pallas_call | solution.py:64
  9.6 1.9 %collective-permute-done.2 = f32[2,64,1024]{2,1,0:T(8,128)S(1)} collective-permute-done((f32[2,64,1024]{2,1,0:T(8,128)S(1)}, f32[2,64,1024]{2,1,0:T(8,128)S(1)}, u32[]{:S(2)}, u32[]{:S(2)}) %collective-permute-start.2) | collective-permute-done | bytes 524320 | tf_op jit(solution)/shard_map/ppermute | solution.py:269
  11.5 1.6 %collective-permute-start.3 = (f32[64,1024]{1,0:T(8,128)S(1)}, f32[64,1024]{1,0:T(8,128)S(1)}, u32[]{:S(2)}, u32[]{:S(2)}) collective-permute-start(f32[64,1024]{1,0:T(8,128)S(1)} %fusion), channel_id=1, source_target_pairs={{0,2},{1,3},{2,0},{3,1},{4,6},{5,7},{6,4},{7,5},{8,10},{9,11},{10,... | collective-permute-start | bytes 786440 | tf_op jit(solution)/shard_map/ppermute | solution.py:269
  13.1 5.6 %collective-permute-start.5 = (bf16[64,1024]{1,0:T(8,128)(2,1)S(1)}, bf16[64,1024]{1,0:T(8,128)(2,1)S(1)}, u32[]{:S(2)}, u32[]{:S(2)}) collective-permute-start(bf16[64,1024]{1,0:T(8,128)(2,1)S(1)} %bitcast.60), channel_id=1, source_target_pairs={{0,8},{4,12},{8,0},{12,4},{16,24},{20,28},{24,16},{28,20},{1,9},{5... | collective-permute-start | bytes 393224 | tf_op jit(solution)/shard_map/ppermute | solution.py:269
  18.7 2.6 %collective-permute-start.4 = (bf16[64,1024]{1,0:T(8,128)(2,1)S(1)}, bf16[64,1024]{1,0:T(8,128)(2,1)S(1)}, u32[]{:S(2)}, u32[]{:S(2)}) collective-permute-start(bf16[64,1024]{1,0:T(8,128)(2,1)S(1)} %bitcast.61), channel_id=1, source_target_pairs={{0,16},{4,20},{8,24},{12,28},{16,0},{20,4},{24,8},{28,12},{1,17},{... | collective-permute-start | bytes 393224 | tf_op jit(solution)/shard_map/ppermute | solution.py:269
  21.4 2.7 %collective-permute-done.5 = bf16[64,1024]{1,0:T(8,128)(2,1)S(1)} collective-permute-done((bf16[64,1024]{1,0:T(8,128)(2,1)S(1)}, bf16[64,1024]{1,0:T(8,128)(2,1)S(1)}, u32[]{:S(2)}, u32[]{:S(2)}) %collective-permute-start.5) | collective-permute-done | bytes 131104 | tf_op jit(solution)/shard_map/ppermute | solution.py:269
  24.1 3.4 %collective-permute-done.4 = bf16[64,1024]{1,0:T(8,128)(2,1)S(1)} collective-permute-done((bf16[64,1024]{1,0:T(8,128)(2,1)S(1)}, bf16[64,1024]{1,0:T(8,128)(2,1)S(1)}, u32[]{:S(2)}, u32[]{:S(2)}) %collective-permute-start.4) | collective-permute-done | bytes 131104 | tf_op jit(solution)/shard_map/ppermute | solution.py:269
  27.7 0.6 collective-permute-start.8
  28.3 0.7 %collective-permute-done.6 = bf16[64,1024]{1,0:T(8,128)(2,1)S(1)} collective-permute-done((bf16[64,1024]{1,0:T(8,128)(2,1)S(1)}, bf16[64,1024]{1,0:T(8,128)(2,1)S(1)}, u32[]{:S(2)}, u32[]{:S(2)}) %collective-permute-start.6) | collective-permute-done | bytes 131104 | tf_op jit(solution)/shard_map/ppermute | solution.py:269
  29.0 0.6 collective-permute-start.7
  30.0 2.1 %collective-permute-done.8 = bf16[2,16,1024]{2,1,0:T(8,128)(2,1)S(1)} collective-permute-done((bf16[2,16,1024]{2,1,0:T(8,128)(2,1)S(1)}, bf16[2,16,1024]{2,1,0:T(8,128)(2,1)S(1)}, u32[]{:S(2)}, u32[]{:S(2)}) %collective-permute-start.8) | collective-permute-done | bytes 65568 | tf_op jit(solution)/shard_map/ppermute | solution.py:269
  32.2 2.5 %collective-permute-start.11 = (bf16[2,16,1024]{2,1,0:T(8,128)(2,1)S(1)}, bf16[2,16,1024]{2,1,0:T(8,128)(2,1)S(1)}, u32[]{:S(2)}, u32[]{:S(2)}) collective-permute-start(bf16[2,16,1024]{2,1,0:T(8,128)(2,1)S(1)} %get-tuple-element.60), channel_id=1, source_target_pairs={{0,24},{4,28},{8,16},{12,20},{16,8},{20,12},{24,0},{28,4},{1,25},{... | collective-permute-start | bytes 196616 | tf_op jit(solution)/shard_map/ppermute | solution.py:269
  34.7 1.9 %collective-permute-start.10 = (bf16[2,16,1024]{2,1,0:T(8,128)(2,1)S(1)}, bf16[2,16,1024]{2,1,0:T(8,128)(2,1)S(1)}, u32[]{:S(2)}, u32[]{:S(2)}) collective-permute-start(bf16[2,16,1024]{2,1,0:T(8,128)(2,1)S(1)} %get-tuple-element.36), channel_id=1, source_target_pairs={{0,16},{4,20},{8,24},{12,28},{16,0},{20,4},{24,8},{28,12},{1,17},{... | collective-permute-start | bytes 196616 | tf_op jit(solution)/shard_map/ppermute | solution.py:269
  36.7 0.6 collective-permute-start.14
  37.5 2.8 %input_parts.1 = (f32[64,1024]{1,0:T(8,128)S(1)}, bf16[64,1024]{1,0:T(8,128)(2,1)S(1)}, bf16[64,1024]{1,0:T(8,128)(2,1)S(1)}) custom-call(s32[2]{0:T(128)S(1)} %pad_add_fusion.index, bf16[2,64,1024]{2,1,0:T(8,128)(2,1)S(1)} %pad_maximum_fusion.1.refs_0_, bf16[2,64,1024]{2,1,0:T(8,128)(2,1)S(1)} %collective-permute-done.7.refs_1_, ...), custom_call_target="tpu_custom_call" | custom-call | flops 905969664 | bytes 6291456 | tf_op jit(solution)/shard_map/input_parts/pallas_call | solution.py:107
  40.7 0.7 collective-permute-start.12
  41.4 0.9 %collective-permute-start.15 = (bf16[64,1024]{1,0:T(8,128)(2,1)S(1)}, bf16[64,1024]{1,0:T(8,128)(2,1)S(1)}, u32[]{:S(2)}, u32[]{:S(2)}) collective-permute-start(bf16[64,1024]{1,0:T(8,128)(2,1)S(1)} %get-tuple-element.39), channel_id=1, source_target_pairs={{0,4},{4,0},{8,12},{12,8},{16,20},{20,16},{24,28},{28,24},{1,5},{5... | collective-permute-start | bytes 393224 | tf_op jit(solution)/shard_map/ppermute | solution.py:269
  42.3 0.7 collective-permute-start.16
  42.9 7.4 %collective-permute-done.15 = bf16[64,1024]{1,0:T(8,128)(2,1)S(1)} collective-permute-done((bf16[64,1024]{1,0:T(8,128)(2,1)S(1)}, bf16[64,1024]{1,0:T(8,128)(2,1)S(1)}, u32[]{:S(2)}, u32[]{:S(2)}) %collective-permute-start.15) | collective-permute-done | bytes 131104 | tf_op jit(solution)/shard_map/ppermute | solution.py:269
  50.4 0.5 collective-permute-start.18
  50.9 1.0 %copy.21 = f32[64,1,1024]{2,1,0:T(1,128)} copy(f32[64,1,1024]{2,0,1:T(8,128)S(1)} %get-tuple-element.59) | data formatting | bytes 524288
  52.3 4.5 %filter_block.1.refs_0_ = bf16[896,128]{1,0:T(8,128)(2,1)S(1)} custom-call(s32[8]{0:T(128)S(1)} %pad_add_fusion.1.index, bf16[64,1024]{1,0:T(8,128)(2,1)S(1)} %bitcast.62, bf16[64,1024]{1,0:T(8,128)(2,1)S(1)} %collective-permute-done.1.partner, bf16[3,64,1024]{2,1,0:T(8,128)(2,1)S(1)} %pad_maximum_fusion.near, ...), custom_call_target="tpu_custom_call" | custom-call | flops 1811939328 | bytes 8388608 | tf_op jit(solution)/shard_map/filter_block/pallas_call | solution.py:188
  56.8 2.3 %collective-permute-start.21 = (bf16[896,128]{1,0:T(8,128)(2,1)S(1)}, bf16[896,128]{1,0:T(8,128)(2,1)S(1)}, u32[]{:S(2)}, u32[]{:S(2)}) collective-permute-start(bf16[896,128]{1,0:T(8,128)(2,1)S(1)} %filter_block.1.refs_0_), channel_id=1, source_target_pairs={{0,12},{4,8},{8,4},{12,0},{16,28},{20,24},{24,20},{28,16},{1,13},{... | collective-permute-start | bytes 688136 | tf_op jit(solution)/shard_map/ppermute | solution.py:269
  59.1 1.7 %collective-permute-start.20 = (bf16[896,128]{1,0:T(8,128)(2,1)S(1)}, bf16[896,128]{1,0:T(8,128)(2,1)S(1)}, u32[]{:S(2)}, u32[]{:S(2)}) collective-permute-start(bf16[896,128]{1,0:T(8,128)(2,1)S(1)} %filter_block.1.refs_0_), channel_id=1, source_target_pairs={{0,8},{4,12},{8,0},{12,4},{16,24},{20,28},{24,16},{28,20},{1,9},{5... | collective-permute-start | bytes 688136 | tf_op jit(solution)/shard_map/ppermute | solution.py:269
  60.8 1.0 %copy.22 = f32[64,1,1024]{2,1,0:T(1,128)} copy(f32[64,1,1024]{2,0,1:T(8,128)S(1)} %add_bitcast_fusion) | data formatting | bytes 524288
  61.8 4.4 %collective-permute-done.21.refs_3_ = bf16[896,128]{1,0:T(8,128)(2,1)S(1)} collective-permute-done((bf16[896,128]{1,0:T(8,128)(2,1)S(1)}, bf16[896,128]{1,0:T(8,128)(2,1)S(1)}, u32[]{:S(2)}, u32[]{:S(2)}) %collective-permute-start.21) | collective-permute-done | bytes 229408 | tf_op jit(solution)/shard_map/ppermute | solution.py:269
  66.2 5.1 %collective-permute-done.20.refs_2_ = bf16[896,128]{1,0:T(8,128)(2,1)S(1)} collective-permute-done((bf16[896,128]{1,0:T(8,128)(2,1)S(1)}, bf16[896,128]{1,0:T(8,128)(2,1)S(1)}, u32[]{:S(2)}, u32[]{:S(2)}) %collective-permute-start.20) | collective-permute-done | bytes 229408 | tf_op jit(solution)/shard_map/ppermute | solution.py:269
  71.3 2.1 %join_blocks.1 = (f32[27,64,256]{2,1,0:T(8,128)}, f32[1,256]{1,0:T(1,128)}) custom-call(s32[1]{0:T(128)} %bitcast.25.index, bf16[896,128]{1,0:T(8,128)(2,1)S(1)} %filter_block.1.refs_0_, bf16[896,128]{1,0:T(8,128)(2,1)S(1)} %collective-permute-done.19.refs_1_, bf16[896,128]{1,0:T(8,128)(2,1)S(1)} %collective-permute-done.20.refs_2_, ...), custom_call_target="tpu_custom_call" | custom-call | flops 452984832 | bytes 4194304 | tf_op jit(solution)/shard_map/join_blocks/pallas_call | solution.py:246
  (48 shorter events, 3.2 us)
Async XLA Ops:
  0.6 6.9 %collective-permute-start.1 = (bf16[64,1024]{1,0:T(8,128)(2,1)}, bf16[64,1024]{1,0:T(8,128)(2,1)S(1)}, u32[]{:S(2)}, u32[]{:S(2)}) collective-permute-start(bf16[64,1024]{1,0:T(8,128)(2,1)} %bitcast.57), channel_id=1, source_target_pairs={{0,4},{4,0},{8,12},{12,8},{16,20},{20,16},{24,28},{28,24},{1,5},{5... | collective-permute-start | bytes 393224 | tf_op jit(solution)/shard_map/ppermute | solution.py:269
  3.6 3.9 %collective-permute-start = (bf16[64,1024]{1,0:T(8,128)(2,1)}, bf16[64,1024]{1,0:T(8,128)(2,1)S(1)}, u32[]{:S(2)}, u32[]{:S(2)}) collective-permute-start(bf16[64,1024]{1,0:T(8,128)(2,1)} %bitcast.58), channel_id=1, source_target_pairs={{4,8},{12,16},{20,24},{8,4},{16,12},{24,20},{5,9},{13,17},{21,25},... | collective-permute-start | bytes 393224 | tf_op jit(solution)/shard_map/ppermute | solution.py:274
  6.4 1.2 %copy-start.1 = (bf16[64,1,1024]{2,0,1:T(8,128)(2,1)S(1)}, bf16[64,1,1024]{2,0,1:T(8,128)(2,1)}, u32[]{:S(2)}) copy-start(bf16[64,1,1024]{2,0,1:T(8,128)(2,1)} %param.5) | copy-start | bytes 393220
  7.6 13.7 %copy-start.3 = (f32[64]{0:T(128)S(1)}, f32[64]{0:T(128)}, u32[]{:S(2)}) copy-start(f32[64]{0:T(128)} %param.7) | copy-start | bytes 772
  7.6 19.8 %copy-start.2 = (bf16[64,1,1024]{2,0,1:T(8,128)(2,1)S(1)}, bf16[64,1,1024]{2,0,1:T(8,128)(2,1)}, u32[]{:S(2)}) copy-start(bf16[64,1,1024]{2,0,1:T(8,128)(2,1)} %param.8) | copy-start | bytes 393220
  9.5 2.0 %collective-permute-start.2 = (f32[2,64,1024]{2,1,0:T(8,128)S(1)}, f32[2,64,1024]{2,1,0:T(8,128)S(1)}, u32[]{:S(2)}, u32[]{:S(2)}) collective-permute-start(f32[2,64,1024]{2,1,0:T(8,128)S(1)} %get-tuple-element.29), channel_id=1, source_target_pairs={{0,1},{1,0},{2,3},{3,2},{4,5},{5,4},{6,7},{7,6},{8,9},{9,8},{10,11... | collective-permute-start | bytes 1572872 | tf_op jit(solution)/shard_map/ppermute | solution.py:269
  11.5 9.8 %collective-permute-start.3 = (f32[64,1024]{1,0:T(8,128)S(1)}, f32[64,1024]{1,0:T(8,128)S(1)}, u32[]{:S(2)}, u32[]{:S(2)}) collective-permute-start(f32[64,1024]{1,0:T(8,128)S(1)} %fusion), channel_id=1, source_target_pairs={{0,2},{1,3},{2,0},{3,1},{4,6},{5,7},{6,4},{7,5},{8,10},{9,11},{10,... | collective-permute-start | bytes 786440 | tf_op jit(solution)/shard_map/ppermute | solution.py:269
  13.1 10.9 %collective-permute-start.5 = (bf16[64,1024]{1,0:T(8,128)(2,1)S(1)}, bf16[64,1024]{1,0:T(8,128)(2,1)S(1)}, u32[]{:S(2)}, u32[]{:S(2)}) collective-permute-start(bf16[64,1024]{1,0:T(8,128)(2,1)S(1)} %bitcast.60), channel_id=1, source_target_pairs={{0,8},{4,12},{8,0},{12,4},{16,24},{20,28},{24,16},{28,20},{1,9},{5... | collective-permute-start | bytes 393224 | tf_op jit(solution)/shard_map/ppermute | solution.py:269
  18.7 8.7 %collective-permute-start.4 = (bf16[64,1024]{1,0:T(8,128)(2,1)S(1)}, bf16[64,1024]{1,0:T(8,128)(2,1)S(1)}, u32[]{:S(2)}, u32[]{:S(2)}) collective-permute-start(bf16[64,1024]{1,0:T(8,128)(2,1)S(1)} %bitcast.61), channel_id=1, source_target_pairs={{0,16},{4,20},{8,24},{12,28},{16,0},{20,4},{24,8},{28,12},{1,17},{... | collective-permute-start | bytes 393224 | tf_op jit(solution)/shard_map/ppermute | solution.py:269
  21.3 16.2 %copy-start = (bf16[27,64,256]{2,1,0:T(8,128)(2,1)S(1)}, bf16[27,64,256]{2,1,0:T(8,128)(2,1)}, u32[]{:S(2)}) copy-start(bf16[27,64,256]{2,1,0:T(8,128)(2,1)} %refs_2_.1) | copy-start | bytes 2654212
  27.6 1.4 %collective-permute-start.6 = (bf16[64,1024]{1,0:T(8,128)(2,1)S(1)}, bf16[64,1024]{1,0:T(8,128)(2,1)S(1)}, u32[]{:S(2)}, u32[]{:S(2)}) collective-permute-start(bf16[64,1024]{1,0:T(8,128)(2,1)S(1)} %get-tuple-element.31), channel_id=1, source_target_pairs={{0,1},{1,0},{2,3},{3,2},{4,5},{5,4},{6,7},{7,6},{8,9},{9,8},{10,11... | collective-permute-start | bytes 393224 | tf_op jit(solution)/shard_map/ppermute | solution.py:269
  27.7 4.5 %collective-permute-start.8 = (bf16[2,16,1024]{2,1,0:T(8,128)(2,1)S(1)}, bf16[2,16,1024]{2,1,0:T(8,128)(2,1)S(1)}, u32[]{:S(2)}, u32[]{:S(2)}) collective-permute-start(bf16[2,16,1024]{2,1,0:T(8,128)(2,1)S(1)} %get-tuple-element.33), channel_id=1, source_target_pairs={{0,4},{4,0},{8,12},{12,8},{16,20},{20,16},{24,28},{28,24},{1,5},{5... | collective-permute-start | bytes 196616 | tf_op jit(solution)/shard_map/ppermute | solution.py:269
  29.0 8.4 %collective-permute-start.7 = (bf16[2,64,1024]{2,1,0:T(8,128)(2,1)S(1)}, bf16[2,64,1024]{2,1,0:T(8,128)(2,1)S(1)}, u32[]{:S(2)}, u32[]{:S(2)}) collective-permute-start(bf16[2,64,1024]{2,1,0:T(8,128)(2,1)S(1)} %pad_maximum_fusion.1.refs_0_), channel_id=1, source_target_pairs={{0,2},{1,3},{2,0},{3,1},{4,6},{5,7},{6,4},{7,5},{8,10},{9,11},{10,... | collective-permute-start | bytes 786440 | tf_op jit(solution)/shard_map/ppermute | solution.py:269
  29.6 7.0 %collective-permute-start.13 = (bf16[64,1024]{1,0:T(8,128)(2,1)S(1)}, bf16[64,1024]{1,0:T(8,128)(2,1)S(1)}, u32[]{:S(2)}, u32[]{:S(2)}) collective-permute-start(bf16[64,1024]{1,0:T(8,128)(2,1)S(1)} %collective-permute-done.4), channel_id=1, source_target_pairs={{0,8},{4,12},{8,0},{12,4},{16,24},{20,28},{24,16},{28,20},{1,9},{5... | collective-permute-start | bytes 393224 | tf_op jit(solution)/shard_map/ppermute | solution.py:269
  32.2 8.5 %collective-permute-start.11 = (bf16[2,16,1024]{2,1,0:T(8,128)(2,1)S(1)}, bf16[2,16,1024]{2,1,0:T(8,128)(2,1)S(1)}, u32[]{:S(2)}, u32[]{:S(2)}) collective-permute-start(bf16[2,16,1024]{2,1,0:T(8,128)(2,1)S(1)} %get-tuple-element.60), channel_id=1, source_target_pairs={{0,24},{4,28},{8,16},{12,20},{16,8},{20,12},{24,0},{28,4},{1,25},{... | collective-permute-start | bytes 196616 | tf_op jit(solution)/shard_map/ppermute | solution.py:269
  34.7 5.9 %collective-permute-start.9 = (bf16[2,16,1024]{2,1,0:T(8,128)(2,1)S(1)}, bf16[2,16,1024]{2,1,0:T(8,128)(2,1)S(1)}, u32[]{:S(2)}, u32[]{:S(2)}) collective-permute-start(bf16[2,16,1024]{2,1,0:T(8,128)(2,1)S(1)} %get-tuple-element.60), channel_id=1, source_target_pairs={{0,8},{4,12},{8,0},{12,4},{16,24},{20,28},{24,16},{28,20},{1,9},{5... | collective-permute-start | bytes 196616 | tf_op jit(solution)/shard_map/ppermute | solution.py:269
  34.7 5.9 %collective-permute-start.10 = (bf16[2,16,1024]{2,1,0:T(8,128)(2,1)S(1)}, bf16[2,16,1024]{2,1,0:T(8,128)(2,1)S(1)}, u32[]{:S(2)}, u32[]{:S(2)}) collective-permute-start(bf16[2,16,1024]{2,1,0:T(8,128)(2,1)S(1)} %get-tuple-element.36), channel_id=1, source_target_pairs={{0,16},{4,20},{8,24},{12,28},{16,0},{20,4},{24,8},{28,12},{1,17},{... | collective-permute-start | bytes 196616 | tf_op jit(solution)/shard_map/ppermute | solution.py:269
  36.7 14.2 %copy-start.4 = (s32[6]{0:T(128)S(1)}, s32[6]{0:T(128)}, u32[]{:S(2)}) copy-start(s32[6]{0:T(128)} %constant.21.clone) | copy-start | bytes 76
  36.7 13.6 %collective-permute-start.14 = (bf16[3,64,1024]{2,1,0:T(8,128)(2,1)S(1)}, bf16[3,64,1024]{2,1,0:T(8,128)(2,1)S(1)}, u32[]{:S(2)}, u32[]{:S(2)}) collective-permute-start(bf16[3,64,1024]{2,1,0:T(8,128)(2,1)S(1)} %pad_maximum_fusion.near), channel_id=1, source_target_pairs={{0,4},{4,0},{8,12},{12,8},{16,20},{20,16},{24,28},{28,24},{1,5},{5... | collective-permute-start | bytes 1179656 | tf_op jit(solution)/shard_map/ppermute | solution.py:269
  40.7 9.6 %collective-permute-start.12 = (bf16[8,16,1024]{2,1,0:T(8,128)(2,1)S(1)}, bf16[8,16,1024]{2,1,0:T(8,128)(2,1)S(1)}, u32[]{:S(2)}, u32[]{:S(2)}) collective-permute-start(bf16[8,16,1024]{2,1,0:T(8,128)(2,1)S(1)} %constant_dynamic-update-slice_fusion.refs_0_), channel_id=1, source_target_pairs={{0,2},{1,3},{2,0},{3,1},{4,6},{5,7},{6,4},{7,5},{8,10},{9,11},{10,... | collective-permute-start | bytes 786440 | tf_op jit(solution)/shard_map/ppermute | solution.py:269
  41.4 8.9 %collective-permute-start.15 = (bf16[64,1024]{1,0:T(8,128)(2,1)S(1)}, bf16[64,1024]{1,0:T(8,128)(2,1)S(1)}, u32[]{:S(2)}, u32[]{:S(2)}) collective-permute-start(bf16[64,1024]{1,0:T(8,128)(2,1)S(1)} %get-tuple-element.39), channel_id=1, source_target_pairs={{0,4},{4,0},{8,12},{12,8},{16,20},{20,16},{24,28},{28,24},{1,5},{5... | collective-permute-start | bytes 393224 | tf_op jit(solution)/shard_map/ppermute | solution.py:269
  42.3 8.0 %collective-permute-start.16 = (bf16[64,1024]{1,0:T(8,128)(2,1)S(1)}, bf16[64,1024]{1,0:T(8,128)(2,1)S(1)}, u32[]{:S(2)}, u32[]{:S(2)}) collective-permute-start(bf16[64,1024]{1,0:T(8,128)(2,1)S(1)} %get-tuple-element.40), channel_id=1, source_target_pairs={{4,8},{12,16},{20,24},{8,4},{16,12},{24,20},{5,9},{13,17},{21,25},... | collective-permute-start | bytes 393224 | tf_op jit(solution)/shard_map/ppermute | solution.py:274
  50.3 1.6 %collective-permute-start.17 = (bf16[8,16,1024]{2,1,0:T(8,128)(2,1)S(1)}, bf16[8,16,1024]{2,1,0:T(8,128)(2,1)S(1)}, u32[]{:S(2)}, u32[]{:S(2)}) collective-permute-start(bf16[8,16,1024]{2,1,0:T(8,128)(2,1)S(1)} %constant_dynamic-update-slice_fusion.refs_0_), channel_id=1, source_target_pairs={{0,1},{1,0},{2,3},{3,2},{4,5},{5,4},{6,7},{7,6},{8,9},{9,8},{10,11... | collective-permute-start | bytes 786440 | tf_op jit(solution)/shard_map/ppermute | solution.py:269
  50.4 1.9 %collective-permute-start.18 = (bf16[8,16,1024]{2,1,0:T(8,128)(2,1)S(1)}, bf16[8,16,1024]{2,1,0:T(8,128)(2,1)S(1)}, u32[]{:S(2)}, u32[]{:S(2)}) collective-permute-start(bf16[8,16,1024]{2,1,0:T(8,128)(2,1)S(1)} %collective-permute-done.12.refs_2_), channel_id=1, source_target_pairs={{0,1},{1,0},{2,3},{3,2},{4,5},{5,4},{6,7},{7,6},{8,9},{9,8},{10,11... | collective-permute-start | bytes 786440 | tf_op jit(solution)/shard_map/ppermute | solution.py:269
  56.8 9.4 %collective-permute-start.21 = (bf16[896,128]{1,0:T(8,128)(2,1)S(1)}, bf16[896,128]{1,0:T(8,128)(2,1)S(1)}, u32[]{:S(2)}, u32[]{:S(2)}) collective-permute-start(bf16[896,128]{1,0:T(8,128)(2,1)S(1)} %filter_block.1.refs_0_), channel_id=1, source_target_pairs={{0,12},{4,8},{8,4},{12,0},{16,28},{20,24},{24,20},{28,16},{1,13},{... | collective-permute-start | bytes 688136 | tf_op jit(solution)/shard_map/ppermute | solution.py:269
  59.1 12.3 %collective-permute-start.20 = (bf16[896,128]{1,0:T(8,128)(2,1)S(1)}, bf16[896,128]{1,0:T(8,128)(2,1)S(1)}, u32[]{:S(2)}, u32[]{:S(2)}) collective-permute-start(bf16[896,128]{1,0:T(8,128)(2,1)S(1)} %filter_block.1.refs_0_), channel_id=1, source_target_pairs={{0,8},{4,12},{8,0},{12,4},{16,24},{20,28},{24,16},{28,20},{1,9},{5... | collective-permute-start | bytes 688136 | tf_op jit(solution)/shard_map/ppermute | solution.py:269
  60.7 10.6 %collective-permute-start.19 = (bf16[896,128]{1,0:T(8,128)(2,1)S(1)}, bf16[896,128]{1,0:T(8,128)(2,1)S(1)}, u32[]{:S(2)}, u32[]{:S(2)}) collective-permute-start(bf16[896,128]{1,0:T(8,128)(2,1)S(1)} %filter_block.1.refs_0_), channel_id=1, source_target_pairs={{0,4},{4,0},{8,12},{12,8},{16,20},{20,16},{24,28},{28,24},{1,5},{5... | collective-permute-start | bytes 688136 | tf_op jit(solution)/shard_map/ppermute | solution.py:269

commit v8 on v7

--- a/solution.py
+++ b/solution.py
@@ -121,26 +121,23 @@
     )(index, *grads, weights)
 
 
-def filter_kernel(factor, groups, index, own, partner, near, far, *refs):
+def filter_kernel(factor, groups, flips, index, *refs):
+    held, refs = refs[: len(flips)], refs[len(flips) :]
     grads = refs[:groups]
     out, shifted, rows, total, sums = refs[groups:]
     planes, share, _ = grads[0].shape
-    chans = own.shape[0]
+    chans = held[0].shape[1]
     width = groups * share
     space, chan = index[0], index[1]
     edge = jnp.zeros((3 * chans, CELLS), BF16)
     shifted[0] = edge
     shifted[planes + 1] = edge
 
-    def place(depth, cells):
-        for e in range(3):
-            shifted[depth + 1, e * chans : (e + 1) * chans, :] = moved(cells, 0, e - 1)
-
-    count = planes // 2 - 1
-    place(space, own[...])
-    place(space ^ 1, partner[...])
-    repeat(count, lambda q: place(space ^ index[2 + q], near[q]))
-    repeat(count, lambda q: place(space ^ index[2 + count + q], far[q]))
+    for part, its_flips in zip(held, flips):
+        for q, flip in enumerate(its_flips):
+            at = (space ^ flip) + 1
+            for e in range(3):
+                shifted[at, e * chans : (e + 1) * chans, :] = moved(part[q], 0, e - 1)
     ones = jnp.ones((16, CELLS), BF16)
     contract = (((1,), (1,)), ((), ()))
     total[...] = jnp.zeros_like(total)
@@ -180,15 +177,15 @@
         )
 
 
-def filter_block(index, own, partner, near, far, grads, factor):
-    chans = own.shape[0]
+def filter_block(index, held, flips, grads, factor):
+    chans = held[0].shape[1]
     groups = len(grads)
     planes, share, _ = grads[0].shape
     width = groups * share
     return pl.pallas_call(
-        functools.partial(filter_kernel, factor, groups),
+        functools.partial(filter_kernel, factor, groups, flips),
         out_shape=jax.ShapeDtypeStruct(((TAPS + 1) // 2 * chans, 2 * width), BF16),
-        in_specs=[SMEM] + [VMEM] * (4 + groups),
+        in_specs=[SMEM] + [VMEM] * (len(flips) + groups),
         out_specs=VMEM,
         scratch_shapes=[
             pltpu.VMEM((planes + 2, 3 * chans, CELLS), BF16),
@@ -203,7 +200,7 @@
             transcendentals=0,
         ),
         name="filter_block",
-    )(index, own, partner, near, far, *grads)
+    )(index, *held, *grads)
 
 
 def join_kernel(share, chans, index, *refs):
@@ -308,19 +305,12 @@
     keep, give = forward_parts(where, own, partner, outer, weights)
 
     got = swapped(give, "chan", 1)
-    near = [swapped(own, "space", 4), swapped(own, "space", 2)]
+    near = [swapped(own, "space", flip) for flip in (4, 2, 3)]
     pre_act = keep[0] + got[0] + out_bias[:, None]
     for j in range(1, groups // 2):
         pre_act = pre_act + swapped(keep[j] + got[j], "chan", 2 * j)
 
     pre_act, near = barrier((pre_act, near))
-    near = jnp.stack(near + [swapped(near[0], "space", 2)], axis=0)
-    flips = [4, 2, 6]
-    for mask in [1 << k for k in range(3, depth.bit_length() - 1)]:
-        own_too = jnp.concatenate([own[None], near], axis=0)
-        near = jnp.concatenate([near, swapped(own_too, "space", mask)], axis=0)
-        flips = flips + [f ^ mask for f in [0] + flips]
-
     sigmoid = jax.nn.sigmoid(pre_act)
     activated = pre_act * sigmoid
     grad_pre = (
@@ -335,8 +325,8 @@
     given = jnp.where(side == 0, split[:, 1], split[:, 0])
     given, grad_pre = barrier((given, grad_pre))
     pair = jnp.stack([kept, swapped(given, "space", 1)], axis=0)
-    far = swapped(near, "space", 1)
-    flips = flips + [f ^ 1 for f in flips]
+    ahead = swapped(near[0], "space", 1)
+    last = swapped(jnp.stack([near[0], ahead], axis=0), "space", 2)
     side = (space >> 1) & 1
     kept = jnp.where(side == 0, pair[:, 0], pair[:, 1])
     given = jnp.where(side == 0, pair[:, 1], pair[:, 0])
@@ -349,12 +339,16 @@
     pieces[0], to_partner, to_outer = barrier((pieces[0], to_partner, to_outer))
     blocks = other_chips(jnp.concatenate(pieces, axis=0))
     from_partner, from_outer = swapped(to_partner, "space", 1), exchanged(to_outer)
-    blocks, far, from_partner, from_outer = barrier((blocks, far, from_partner, from_outer))
+    blocks, last, from_partner, from_outer = barrier((blocks, last, from_partner, from_outer))
     blocks = both_cores(blocks)
     in_grad = in_grad + from_partner.astype(F32) + from_outer.astype(F32)
 
-    index = jnp.concatenate([space.reshape(1), chan.reshape(1), jnp.array(flips, jnp.int32)])
-    part = filter_block(index, own, partner, near, far, blocks, factor)
+    held = [v[None] for v in (own, partner, *near, ahead)] + [last]
+    flips = [(0,), (1,), (4,), (2,), (3,), (5,), (6, 7)]
+    for mask in [1 << k for k in range(3, depth.bit_length() - 1)]:
+        held.append(swapped(jnp.concatenate(held, axis=0), "space", mask))
+        flips.append(tuple(f ^ mask for some in flips for f in some))
+    part = filter_block(jnp.stack([space, chan]), held, flips, blocks, factor)
     parts = [part] + [swapped(part, "space", r) for r in range(1, 4)]
     joined, bias = join_blocks((space & 3).reshape(1), parts, share, chans)
     return (

time: 73.6 us -> 73.8 us (level)
  starting transfers between devices: 27 us -> 31.6 us
  waiting for transfers between devices: 28.6 us -> 24.2 us
    ppermute x20 -> x21, starting transfers between devices: 25.7 us -> 30.3 us  [swapped(): return lax.ppermute(value, axis, [(i, i ^ mask) for i in range(count)])]
    ppermute x20 -> x21, waiting for transfers between devices: 28.6 us -> 24.2 us  [swapped(): return lax.ppermute(value, axis, [(i, i ^ mask) for i in range(count)])]
    unnamed x17 -> x15, local copies, waits for them, and re-layouts: 2.4 us -> 2.39 us
  transfers between devices with their start and end apart: 22 -> 23, of which waited for: 11 -> 12; matrix products, arithmetic and copies ran while one was open for 7% -> 7% of each run, Pallas kernels for 4% -> 4%
where the time goes in v8:
time: 73.8 us; the launch traced here: 73.6 us
  starting transfers between devices  31.6 us (43%)
  waiting for transfers between devices  24.2 us (33%)
  Pallas kernels  11.3 us (15%)
  local copies, waits for them, and re-layouts  5.14 us (7%)
  between operations  0.84 us (1%)
    ppermute x21, starting transfers between devices, swapped(): return lax.ppermute(value, axis, [(i, i ^ mask) for i in range(count)])  30.3 us
    ppermute x21, waiting for transfers between devices, swapped(): return lax.ppermute(value, axis, [(i, i ^ mask) for i in range(count)])  24.2 us
    pallas_call x1, Pallas kernels, filter_block(): pl.pallas_call(functools.partial(filter_kernel, factor, groups, flips), o...  4.5 us
    pallas_call x1, Pallas kernels, input_parts(): pl.pallas_call(functools.partial(input_kernel, chans, chips), out_shape=[...  2.8 us
    unnamed x15, local copies, waits for them, and re-layouts  2.39 us
    pallas_call x1, Pallas kernels, join_blocks(): pl.pallas_call(functools.partial(join_kernel, share, chans), out_shape=[j...  2.11 us
    pallas_call x1, Pallas kernels, forward_parts(): pl.pallas_call(functools.partial(forward_kernel, chans), out_shape=[side,...  1.91 us
  transfers between devices with their start and end apart: 23, of which 12 were waited for; matrix products, arithmetic and copies ran while one was open for 7% of the time, Pallas kernels for 4%

profile of v8, /device:TPU:0, one launch (start us, length us, event | category | flops | bytes accessed | tf_op | source)
XLA Modules:
  0.0 73.6 jit_solution(17469649281049745846)
XLA Ops:
  0.6 3.0 %collective-permute-start.1 = (bf16[64,1024]{1,0:T(8,128)(2,1)}, bf16[64,1024]{1,0:T(8,128)(2,1)S(1)}, u32[]{:S(2)}, u32[]{:S(2)}) collective-permute-start(bf16[64,1024]{1,0:T(8,128)(2,1)} %bitcast.64), channel_id=1, source_target_pairs={{0,4},{4,0},{8,12},{12,8},{16,20},{20,16},{24,28},{28,24},{1,5},{5... | collective-permute-start | bytes 393224 | tf_op jit(solution)/shard_map/ppermute | solution.py:266
  3.6 0.7 collective-permute-start
  4.3 1.1 %constant_dynamic-slice_fusion = (bf16[1,576,256]{2,1,0:T(8,128)(2,1)S(1)}, bf16[1,576,256]{2,1,0:T(8,128)(2,1)S(1)}) fusion(bf16[3,576,256]{2,1,0:T(8,128)(2,1)} %bitcast.59, s32[]{:T(128)S(6)} %select_n.48, s32[]{:T(128)S(6)} %select_n.47), kind=kLoop, calls=%fused_computation.30 | loop fusion | bytes 1179656 | tf_op jit(solution)/shard_map/dynamic_slice | solution.py:303
  5.4 1.0 %slice.32 = bf16[9,64,256]{2,1,0:T(8,128)(2,1)S(1)} slice(bf16[27,64,256]{2,1,0:T(8,128)(2,1)} %refs_2_.1), slice={[9:18], [0:64], [0:256]} | slice | bytes 589824 | tf_op jit(solution)/shard_map/slice | solution.py:303
  7.6 1.9 %forward_parts.1 = (f32[2,64,1024]{2,1,0:T(8,128)S(1)}, f32[2,64,1024]{2,1,0:T(8,128)S(1)}) custom-call(s32[2]{0:T(128)S(1)} %pad_add_fusion.index, bf16[64,1024]{1,0:T(8,128)(2,1)S(1)} %bitcast.66, bf16[64,1024]{1,0:T(8,128)(2,1)S(1)} %collective-permute-done.1.partner, bf16[64,1024]{1,0:T(8,128)(2,1)S(1)} %collective-permute-done.outer, ...), custom_call_target="tpu_custom_call" | custom-call | flops 905969664 | bytes 6291456 | tf_op jit(solution)/shard_map/forward_parts/pallas_call | solution.py:64
  9.6 1.9 %collective-permute-done.2 = f32[2,64,1024]{2,1,0:T(8,128)S(1)} collective-permute-done((f32[2,64,1024]{2,1,0:T(8,128)S(1)}, f32[2,64,1024]{2,1,0:T(8,128)S(1)}, u32[]{:S(2)}, u32[]{:S(2)}) %collective-permute-start.2) | collective-permute-done | bytes 524320 | tf_op jit(solution)/shard_map/ppermute | solution.py:266
  11.6 1.6 %collective-permute-start.3 = (f32[64,1024]{1,0:T(8,128)S(1)}, f32[64,1024]{1,0:T(8,128)S(1)}, u32[]{:S(2)}, u32[]{:S(2)}) collective-permute-start(f32[64,1024]{1,0:T(8,128)S(1)} %fusion), channel_id=1, source_target_pairs={{0,2},{1,3},{2,0},{3,1},{4,6},{5,7},{6,4},{7,5},{8,10},{9,11},{10,... | collective-permute-start | bytes 786440 | tf_op jit(solution)/shard_map/ppermute | solution.py:266
  13.2 5.5 %collective-permute-start.6 = (bf16[64,1024]{1,0:T(8,128)(2,1)S(1)}, bf16[64,1024]{1,0:T(8,128)(2,1)S(1)}, u32[]{:S(2)}, u32[]{:S(2)}) collective-permute-start(bf16[64,1024]{1,0:T(8,128)(2,1)S(1)} %bitcast.67), channel_id=1, source_target_pairs={{0,12},{4,8},{8,4},{12,0},{16,28},{20,24},{24,20},{28,16},{1,13},{... | collective-permute-start | bytes 393224 | tf_op jit(solution)/shard_map/ppermute | solution.py:266
  19.1 2.6 %collective-permute-start.4 = (bf16[64,1024]{1,0:T(8,128)(2,1)S(1)}, bf16[64,1024]{1,0:T(8,128)(2,1)S(1)}, u32[]{:S(2)}, u32[]{:S(2)}) collective-permute-start(bf16[64,1024]{1,0:T(8,128)(2,1)S(1)} %bitcast.69), channel_id=1, source_target_pairs={{0,16},{4,20},{8,24},{12,28},{16,0},{20,4},{24,8},{28,12},{1,17},{... | collective-permute-start | bytes 393224 | tf_op jit(solution)/shard_map/ppermute | solution.py:266
  21.8 0.8 %collective-permute-done.6 = bf16[64,1024]{1,0:T(8,128)(2,1)S(1)} collective-permute-done((bf16[64,1024]{1,0:T(8,128)(2,1)S(1)}, bf16[64,1024]{1,0:T(8,128)(2,1)S(1)}, u32[]{:S(2)}, u32[]{:S(2)}) %collective-permute-start.6) | collective-permute-done | bytes 131104 | tf_op jit(solution)/shard_map/ppermute | solution.py:266
  22.6 5.4 %collective-permute-done.5 = bf16[64,1024]{1,0:T(8,128)(2,1)S(1)} collective-permute-done((bf16[64,1024]{1,0:T(8,128)(2,1)S(1)}, bf16[64,1024]{1,0:T(8,128)(2,1)S(1)}, u32[]{:S(2)}, u32[]{:S(2)}) %collective-permute-start.5) | collective-permute-done | bytes 131104 | tf_op jit(solution)/shard_map/ppermute | solution.py:266
  28.2 0.6 collective-permute-start.9
  28.9 0.7 collective-permute-done.7
  30.0 0.8 %collective-permute-start.14 = (bf16[64,1024]{1,0:T(8,128)(2,1)S(1)}, bf16[64,1024]{1,0:T(8,128)(2,1)S(1)}, u32[]{:S(2)}, u32[]{:S(2)}) collective-permute-start(bf16[64,1024]{1,0:T(8,128)(2,1)S(1)} %collective-permute-done.4), channel_id=1, source_target_pairs={{0,4},{4,0},{8,12},{12,8},{16,20},{20,16},{24,28},{28,24},{1,5},{5... | collective-permute-start | bytes 393224 | tf_op jit(solution)/shard_map/ppermute | solution.py:266
  30.8 2.3 %collective-permute-done.9 = bf16[2,16,1024]{2,1,0:T(8,128)(2,1)S(1)} collective-permute-done((bf16[2,16,1024]{2,1,0:T(8,128)(2,1)S(1)}, bf16[2,16,1024]{2,1,0:T(8,128)(2,1)S(1)}, u32[]{:S(2)}, u32[]{:S(2)}) %collective-permute-start.9) | collective-permute-done | bytes 65568 | tf_op jit(solution)/shard_map/ppermute | solution.py:266
  33.1 3.1 %collective-permute-start.12 = (bf16[2,16,1024]{2,1,0:T(8,128)(2,1)S(1)}, bf16[2,16,1024]{2,1,0:T(8,128)(2,1)S(1)}, u32[]{:S(2)}, u32[]{:S(2)}) collective-permute-start(bf16[2,16,1024]{2,1,0:T(8,128)(2,1)S(1)} %get-tuple-element.62), channel_id=1, source_target_pairs={{0,24},{4,28},{8,16},{12,20},{16,8},{20,12},{24,0},{28,4},{1,25},{... | collective-permute-start | bytes 196616 | tf_op jit(solution)/shard_map/ppermute | solution.py:266
  36.2 1.4 %collective-permute-start.11 = (bf16[2,16,1024]{2,1,0:T(8,128)(2,1)S(1)}, bf16[2,16,1024]{2,1,0:T(8,128)(2,1)S(1)}, u32[]{:S(2)}, u32[]{:S(2)}) collective-permute-start(bf16[2,16,1024]{2,1,0:T(8,128)(2,1)S(1)} %get-tuple-element.37), channel_id=1, source_target_pairs={{0,16},{4,20},{8,24},{12,28},{16,0},{20,4},{24,8},{28,12},{1,17},{... | collective-permute-start | bytes 196616 | tf_op jit(solution)/shard_map/ppermute | solution.py:266
  37.5 1.4 %collective-permute-start.15 = (bf16[2,64,1024]{2,1,0:T(8,128)(2,1)S(1)}, bf16[2,64,1024]{2,1,0:T(8,128)(2,1)S(1)}, u32[]{:S(2)}, u32[]{:S(2)}) collective-permute-start(bf16[2,64,1024]{2,1,0:T(8,128)(2,1)S(1)} %pad_maximum_fusion.1), channel_id=1, source_target_pairs={{0,8},{4,12},{8,0},{12,4},{16,24},{20,28},{24,16},{28,20},{1,9},{5... | collective-permute-start | bytes 786440 | tf_op jit(solution)/shard_map/ppermute | solution.py:266
  39.0 2.8 %input_parts.1 = (f32[64,1024]{1,0:T(8,128)S(1)}, bf16[64,1024]{1,0:T(8,128)(2,1)S(1)}, bf16[64,1024]{1,0:T(8,128)(2,1)S(1)}) custom-call(s32[2]{0:T(128)S(1)} %pad_add_fusion.index, bf16[2,64,1024]{2,1,0:T(8,128)(2,1)S(1)} %pad_maximum_fusion.refs_0_, bf16[2,64,1024]{2,1,0:T(8,128)(2,1)S(1)} %collective-permute-done.8.refs_1_, bf16[27,64,256]{2,1,0:T(8,128)(2,1)S(1)} %copy-done), custom_call_target="tpu_custom_call" | custom-call | flops 905969664 | bytes 6291456 | tf_op jit(solution)/shard_map/input_parts/pallas_call | solution.py:107
  41.8 0.7 collective-permute-done.10
  43.1 1.6 %collective-permute-start.16 = (bf16[64,1024]{1,0:T(8,128)(2,1)S(1)}, bf16[64,1024]{1,0:T(8,128)(2,1)S(1)}, u32[]{:S(2)}, u32[]{:S(2)}) collective-permute-start(bf16[64,1024]{1,0:T(8,128)(2,1)S(1)} %get-tuple-element.39), channel_id=1, source_target_pairs={{0,4},{4,0},{8,12},{12,8},{16,20},{20,16},{24,28},{28,24},{1,5},{5... | collective-permute-start | bytes 393224 | tf_op jit(solution)/shard_map/ppermute | solution.py:266
  44.6 0.7 collective-permute-start.17
  45.3 2.5 %collective-permute-done.15.refs_6_ = bf16[2,64,1024]{2,1,0:T(8,128)(2,1)S(1)} collective-permute-done((bf16[2,64,1024]{2,1,0:T(8,128)(2,1)S(1)}, bf16[2,64,1024]{2,1,0:T(8,128)(2,1)S(1)}, u32[]{:S(2)}, u32[]{:S(2)}) %collective-permute-start.15) | collective-permute-done | bytes 262176 | tf_op jit(solution)/shard_map/ppermute | solution.py:266
  47.8 0.8 %collective-permute-done.16 = bf16[64,1024]{1,0:T(8,128)(2,1)S(1)} collective-permute-done((bf16[64,1024]{1,0:T(8,128)(2,1)S(1)}, bf16[64,1024]{1,0:T(8,128)(2,1)S(1)}, u32[]{:S(2)}, u32[]{:S(2)}) %collective-permute-start.16) | collective-permute-done | bytes 131104 | tf_op jit(solution)/shard_map/ppermute | solution.py:266
  49.6 1.0 %copy.20 = f32[64,1,1024]{2,1,0:T(1,128)} copy(f32[64,1,1024]{2,0,1:T(8,128)S(1)} %get-tuple-element.61) | data formatting | bytes 524288
  50.9 4.5 %filter_block.1.refs_0_ = bf16[896,128]{1,0:T(8,128)(2,1)S(1)} custom-call(s32[2]{0:T(128)S(1)} %pad_add_fusion.1.index, bf16[1,64,1024]{2,1,0:T(8,128)(2,1)S(1)} %bitcast.70, bf16[1,64,1024]{2,1,0:T(8,128)(2,1)S(1)} %bitcast.71, bf16[1,64,1024]{2,1,0:T(8,128)(2,1)S(1)} %bitcast.61, bf16[1,64,1024]{2,1,0:T(8,128)(2,1)S(1)} %bitcast.73, ...), custom_call_target="tpu_custom_call" | custom-call | flops 1811939328 | bytes 8388608 | tf_op jit(solution)/shard_map/filter_block/pallas_call | solution.py:185
  55.4 5.1 %collective-permute-start.22 = (bf16[896,128]{1,0:T(8,128)(2,1)S(1)}, bf16[896,128]{1,0:T(8,128)(2,1)S(1)}, u32[]{:S(2)}, u32[]{:S(2)}) collective-permute-start(bf16[896,128]{1,0:T(8,128)(2,1)S(1)} %filter_block.1.refs_0_), channel_id=1, source_target_pairs={{0,12},{4,8},{8,4},{12,0},{16,28},{20,24},{24,20},{28,16},{1,13},{... | collective-permute-start | bytes 688136 | tf_op jit(solution)/shard_map/ppermute | solution.py:266
  60.7 1.4 %collective-permute-start.20 = (bf16[896,128]{1,0:T(8,128)(2,1)S(1)}, bf16[896,128]{1,0:T(8,128)(2,1)S(1)}, u32[]{:S(2)}, u32[]{:S(2)}) collective-permute-start(bf16[896,128]{1,0:T(8,128)(2,1)S(1)} %filter_block.1.refs_0_), channel_id=1, source_target_pairs={{0,4},{4,0},{8,12},{12,8},{16,20},{20,16},{24,28},{28,24},{1,5},{5... | collective-permute-start | bytes 688136 | tf_op jit(solution)/shard_map/ppermute | solution.py:266
  62.2 1.0 %copy.21 = f32[64,1,1024]{2,1,0:T(1,128)} copy(f32[64,1,1024]{2,0,1:T(8,128)S(1)} %add_bitcast_fusion) | data formatting | bytes 524288
  63.1 3.9 %collective-permute-done.22.refs_3_ = bf16[896,128]{1,0:T(8,128)(2,1)S(1)} collective-permute-done((bf16[896,128]{1,0:T(8,128)(2,1)S(1)}, bf16[896,128]{1,0:T(8,128)(2,1)S(1)}, u32[]{:S(2)}, u32[]{:S(2)}) %collective-permute-start.22) | collective-permute-done | bytes 229408 | tf_op jit(solution)/shard_map/ppermute | solution.py:266
  67.0 4.5 %collective-permute-done.21.refs_2_ = bf16[896,128]{1,0:T(8,128)(2,1)S(1)} collective-permute-done((bf16[896,128]{1,0:T(8,128)(2,1)S(1)}, bf16[896,128]{1,0:T(8,128)(2,1)S(1)}, u32[]{:S(2)}, u32[]{:S(2)}) %collective-permute-start.21) | collective-permute-done | bytes 229408 | tf_op jit(solution)/shard_map/ppermute | solution.py:266
  71.5 2.1 %join_blocks.1 = (f32[27,64,256]{2,1,0:T(8,128)}, f32[1,256]{1,0:T(1,128)}) custom-call(s32[1]{0:T(128)} %bitcast.24.index, bf16[896,128]{1,0:T(8,128)(2,1)S(1)} %filter_block.1.refs_0_, bf16[896,128]{1,0:T(8,128)(2,1)S(1)} %collective-permute-done.20.refs_1_, bf16[896,128]{1,0:T(8,128)(2,1)S(1)} %collective-permute-done.21.refs_2_, ...), custom_call_target="tpu_custom_call" | custom-call | flops 452984832 | bytes 4194304 | tf_op jit(solution)/shard_map/join_blocks/pallas_call | solution.py:243
  (48 shorter events, 4.7 us)
Async XLA Ops:
  0.6 6.9 %collective-permute-start.1 = (bf16[64,1024]{1,0:T(8,128)(2,1)}, bf16[64,1024]{1,0:T(8,128)(2,1)S(1)}, u32[]{:S(2)}, u32[]{:S(2)}) collective-permute-start(bf16[64,1024]{1,0:T(8,128)(2,1)} %bitcast.64), channel_id=1, source_target_pairs={{0,4},{4,0},{8,12},{12,8},{16,20},{20,16},{24,28},{28,24},{1,5},{5... | collective-permute-start | bytes 393224 | tf_op jit(solution)/shard_map/ppermute | solution.py:266
  3.6 3.9 %collective-permute-start = (bf16[64,1024]{1,0:T(8,128)(2,1)}, bf16[64,1024]{1,0:T(8,128)(2,1)S(1)}, u32[]{:S(2)}, u32[]{:S(2)}) collective-permute-start(bf16[64,1024]{1,0:T(8,128)(2,1)} %bitcast.65), channel_id=1, source_target_pairs={{4,8},{12,16},{20,24},{8,4},{16,12},{24,20},{5,9},{13,17},{21,25},... | collective-permute-start | bytes 393224 | tf_op jit(solution)/shard_map/ppermute | solution.py:271
  6.4 1.2 %copy-start.1 = (bf16[64,1,1024]{2,0,1:T(8,128)(2,1)S(1)}, bf16[64,1,1024]{2,0,1:T(8,128)(2,1)}, u32[]{:S(2)}) copy-start(bf16[64,1,1024]{2,0,1:T(8,128)(2,1)} %param.4) | copy-start | bytes 393220
  7.6 14.1 %copy-start.3 = (f32[64]{0:T(128)S(1)}, f32[64]{0:T(128)}, u32[]{:S(2)}) copy-start(f32[64]{0:T(128)} %param.6) | copy-start | bytes 772
  7.6 20.4 %copy-start.2 = (bf16[64,1,1024]{2,0,1:T(8,128)(2,1)S(1)}, bf16[64,1,1024]{2,0,1:T(8,128)(2,1)}, u32[]{:S(2)}) copy-start(bf16[64,1,1024]{2,0,1:T(8,128)(2,1)} %param.7) | copy-start | bytes 393220
  9.5 2.0 %collective-permute-start.2 = (f32[2,64,1024]{2,1,0:T(8,128)S(1)}, f32[2,64,1024]{2,1,0:T(8,128)S(1)}, u32[]{:S(2)}, u32[]{:S(2)}) collective-permute-start(f32[2,64,1024]{2,1,0:T(8,128)S(1)} %get-tuple-element.30), channel_id=1, source_target_pairs={{0,1},{1,0},{2,3},{3,2},{4,5},{5,4},{6,7},{7,6},{8,9},{9,8},{10,11... | collective-permute-start | bytes 1572872 | tf_op jit(solution)/shard_map/ppermute | solution.py:266
  11.5 27.4 %copy-start = (bf16[27,64,256]{2,1,0:T(8,128)(2,1)S(1)}, bf16[27,64,256]{2,1,0:T(8,128)(2,1)}, u32[]{:S(2)}) copy-start(bf16[27,64,256]{2,1,0:T(8,128)(2,1)} %refs_2_.1) | copy-start | bytes 2654212
  11.6 10.2 %collective-permute-start.3 = (f32[64,1024]{1,0:T(8,128)S(1)}, f32[64,1024]{1,0:T(8,128)S(1)}, u32[]{:S(2)}, u32[]{:S(2)}) collective-permute-start(f32[64,1024]{1,0:T(8,128)S(1)} %fusion), channel_id=1, source_target_pairs={{0,2},{1,3},{2,0},{3,1},{4,6},{5,7},{6,4},{7,5},{8,10},{9,11},{10,... | collective-permute-start | bytes 786440 | tf_op jit(solution)/shard_map/ppermute | solution.py:266
  13.2 9.4 %collective-permute-start.6 = (bf16[64,1024]{1,0:T(8,128)(2,1)S(1)}, bf16[64,1024]{1,0:T(8,128)(2,1)S(1)}, u32[]{:S(2)}, u32[]{:S(2)}) collective-permute-start(bf16[64,1024]{1,0:T(8,128)(2,1)S(1)} %bitcast.67), channel_id=1, source_target_pairs={{0,12},{4,8},{8,4},{12,0},{16,28},{20,24},{24,20},{28,16},{1,13},{... | collective-permute-start | bytes 393224 | tf_op jit(solution)/shard_map/ppermute | solution.py:266
  18.7 9.3 %collective-permute-start.5 = (bf16[64,1024]{1,0:T(8,128)(2,1)S(1)}, bf16[64,1024]{1,0:T(8,128)(2,1)S(1)}, u32[]{:S(2)}, u32[]{:S(2)}) collective-permute-start(bf16[64,1024]{1,0:T(8,128)(2,1)S(1)} %bitcast.68), channel_id=1, source_target_pairs={{0,8},{4,12},{8,0},{12,4},{16,24},{20,28},{24,16},{28,20},{1,9},{5... | collective-permute-start | bytes 393224 | tf_op jit(solution)/shard_map/ppermute | solution.py:266
  19.1 8.9 %collective-permute-start.4 = (bf16[64,1024]{1,0:T(8,128)(2,1)S(1)}, bf16[64,1024]{1,0:T(8,128)(2,1)S(1)}, u32[]{:S(2)}, u32[]{:S(2)}) collective-permute-start(bf16[64,1024]{1,0:T(8,128)(2,1)S(1)} %bitcast.69), channel_id=1, source_target_pairs={{0,16},{4,20},{8,24},{12,28},{16,0},{20,4},{24,8},{28,12},{1,17},{... | collective-permute-start | bytes 393224 | tf_op jit(solution)/shard_map/ppermute | solution.py:266
  28.1 1.4 %collective-permute-start.7 = (bf16[64,1024]{1,0:T(8,128)(2,1)S(1)}, bf16[64,1024]{1,0:T(8,128)(2,1)S(1)}, u32[]{:S(2)}, u32[]{:S(2)}) collective-permute-start(bf16[64,1024]{1,0:T(8,128)(2,1)S(1)} %get-tuple-element.32), channel_id=1, source_target_pairs={{0,1},{1,0},{2,3},{3,2},{4,5},{5,4},{6,7},{7,6},{8,9},{9,8},{10,11... | collective-permute-start | bytes 393224 | tf_op jit(solution)/shard_map/ppermute | solution.py:266
  28.2 4.8 %collective-permute-start.9 = (bf16[2,16,1024]{2,1,0:T(8,128)(2,1)S(1)}, bf16[2,16,1024]{2,1,0:T(8,128)(2,1)S(1)}, u32[]{:S(2)}, u32[]{:S(2)}) collective-permute-start(bf16[2,16,1024]{2,1,0:T(8,128)(2,1)S(1)} %get-tuple-element.34), channel_id=1, source_target_pairs={{0,4},{4,0},{8,12},{12,8},{16,20},{20,16},{24,28},{28,24},{1,5},{5... | collective-permute-start | bytes 196616 | tf_op jit(solution)/shard_map/ppermute | solution.py:266
  29.6 9.4 %collective-permute-start.8 = (bf16[2,64,1024]{2,1,0:T(8,128)(2,1)S(1)}, bf16[2,64,1024]{2,1,0:T(8,128)(2,1)S(1)}, u32[]{:S(2)}, u32[]{:S(2)}) collective-permute-start(bf16[2,64,1024]{2,1,0:T(8,128)(2,1)S(1)} %pad_maximum_fusion.refs_0_), channel_id=1, source_target_pairs={{0,2},{1,3},{2,0},{3,1},{4,6},{5,7},{6,4},{7,5},{8,10},{9,11},{10,... | collective-permute-start | bytes 786440 | tf_op jit(solution)/shard_map/ppermute | solution.py:266
  30.0 7.5 %collective-permute-start.14 = (bf16[64,1024]{1,0:T(8,128)(2,1)S(1)}, bf16[64,1024]{1,0:T(8,128)(2,1)S(1)}, u32[]{:S(2)}, u32[]{:S(2)}) collective-permute-start(bf16[64,1024]{1,0:T(8,128)(2,1)S(1)} %collective-permute-done.4), channel_id=1, source_target_pairs={{0,4},{4,0},{8,12},{12,8},{16,20},{20,16},{24,28},{28,24},{1,5},{5... | collective-permute-start | bytes 393224 | tf_op jit(solution)/shard_map/ppermute | solution.py:266
  33.1 9.5 %collective-permute-start.12 = (bf16[2,16,1024]{2,1,0:T(8,128)(2,1)S(1)}, bf16[2,16,1024]{2,1,0:T(8,128)(2,1)S(1)}, u32[]{:S(2)}, u32[]{:S(2)}) collective-permute-start(bf16[2,16,1024]{2,1,0:T(8,128)(2,1)S(1)} %get-tuple-element.62), channel_id=1, source_target_pairs={{0,24},{4,28},{8,16},{12,20},{16,8},{20,12},{24,0},{28,4},{1,25},{... | collective-permute-start | bytes 196616 | tf_op jit(solution)/shard_map/ppermute | solution.py:266
  36.1 6.4 %collective-permute-start.10 = (bf16[2,16,1024]{2,1,0:T(8,128)(2,1)S(1)}, bf16[2,16,1024]{2,1,0:T(8,128)(2,1)S(1)}, u32[]{:S(2)}, u32[]{:S(2)}) collective-permute-start(bf16[2,16,1024]{2,1,0:T(8,128)(2,1)S(1)} %get-tuple-element.62), channel_id=1, source_target_pairs={{0,8},{4,12},{8,0},{12,4},{16,24},{20,28},{24,16},{28,20},{1,9},{5... | collective-permute-start | bytes 196616 | tf_op jit(solution)/shard_map/ppermute | solution.py:266
  36.2 6.4 %collective-permute-start.11 = (bf16[2,16,1024]{2,1,0:T(8,128)(2,1)S(1)}, bf16[2,16,1024]{2,1,0:T(8,128)(2,1)S(1)}, u32[]{:S(2)}, u32[]{:S(2)}) collective-permute-start(bf16[2,16,1024]{2,1,0:T(8,128)(2,1)S(1)} %get-tuple-element.37), channel_id=1, source_target_pairs={{0,16},{4,20},{8,24},{12,28},{16,0},{20,4},{24,8},{28,12},{1,17},{... | collective-permute-start | bytes 196616 | tf_op jit(solution)/shard_map/ppermute | solution.py:266
  37.5 10.2 %collective-permute-start.15 = (bf16[2,64,1024]{2,1,0:T(8,128)(2,1)S(1)}, bf16[2,64,1024]{2,1,0:T(8,128)(2,1)S(1)}, u32[]{:S(2)}, u32[]{:S(2)}) collective-permute-start(bf16[2,64,1024]{2,1,0:T(8,128)(2,1)S(1)} %pad_maximum_fusion.1), channel_id=1, source_target_pairs={{0,8},{4,12},{8,0},{12,4},{16,24},{20,28},{24,16},{28,20},{1,9},{5... | collective-permute-start | bytes 786440 | tf_op jit(solution)/shard_map/ppermute | solution.py:266
  42.6 6.4 %collective-permute-start.13 = (bf16[8,16,1024]{2,1,0:T(8,128)(2,1)S(1)}, bf16[8,16,1024]{2,1,0:T(8,128)(2,1)S(1)}, u32[]{:S(2)}, u32[]{:S(2)}) collective-permute-start(bf16[8,16,1024]{2,1,0:T(8,128)(2,1)S(1)} %constant_dynamic-update-slice_fusion.refs_7_), channel_id=1, source_target_pairs={{0,2},{1,3},{2,0},{3,1},{4,6},{5,7},{6,4},{7,5},{8,10},{9,11},{10,... | collective-permute-start | bytes 786440 | tf_op jit(solution)/shard_map/ppermute | solution.py:266
  43.1 5.5 %collective-permute-start.16 = (bf16[64,1024]{1,0:T(8,128)(2,1)S(1)}, bf16[64,1024]{1,0:T(8,128)(2,1)S(1)}, u32[]{:S(2)}, u32[]{:S(2)}) collective-permute-start(bf16[64,1024]{1,0:T(8,128)(2,1)S(1)} %get-tuple-element.39), channel_id=1, source_target_pairs={{0,4},{4,0},{8,12},{12,8},{16,20},{20,16},{24,28},{28,24},{1,5},{5... | collective-permute-start | bytes 393224 | tf_op jit(solution)/shard_map/ppermute | solution.py:266
  44.6 3.9 %collective-permute-start.17 = (bf16[64,1024]{1,0:T(8,128)(2,1)S(1)}, bf16[64,1024]{1,0:T(8,128)(2,1)S(1)}, u32[]{:S(2)}, u32[]{:S(2)}) collective-permute-start(bf16[64,1024]{1,0:T(8,128)(2,1)S(1)} %get-tuple-element.40), channel_id=1, source_target_pairs={{4,8},{12,16},{20,24},{8,4},{16,12},{24,20},{5,9},{13,17},{21,25},... | collective-permute-start | bytes 393224 | tf_op jit(solution)/shard_map/ppermute | solution.py:271
  49.0 1.6 %collective-permute-start.18 = (bf16[8,16,1024]{2,1,0:T(8,128)(2,1)S(1)}, bf16[8,16,1024]{2,1,0:T(8,128)(2,1)S(1)}, u32[]{:S(2)}, u32[]{:S(2)}) collective-permute-start(bf16[8,16,1024]{2,1,0:T(8,128)(2,1)S(1)} %constant_dynamic-update-slice_fusion.refs_7_), channel_id=1, source_target_pairs={{0,1},{1,0},{2,3},{3,2},{4,5},{5,4},{6,7},{7,6},{8,9},{9,8},{10,11... | collective-permute-start | bytes 786440 | tf_op jit(solution)/shard_map/ppermute | solution.py:266
  49.0 1.9 %collective-permute-start.19 = (bf16[8,16,1024]{2,1,0:T(8,128)(2,1)S(1)}, bf16[8,16,1024]{2,1,0:T(8,128)(2,1)S(1)}, u32[]{:S(2)}, u32[]{:S(2)}) collective-permute-start(bf16[8,16,1024]{2,1,0:T(8,128)(2,1)S(1)} %collective-permute-done.13.refs_9_), channel_id=1, source_target_pairs={{0,1},{1,0},{2,3},{3,2},{4,5},{5,4},{6,7},{7,6},{8,9},{9,8},{10,11... | collective-permute-start | bytes 786440 | tf_op jit(solution)/shard_map/ppermute | solution.py:266
  55.4 11.6 %collective-permute-start.22 = (bf16[896,128]{1,0:T(8,128)(2,1)S(1)}, bf16[896,128]{1,0:T(8,128)(2,1)S(1)}, u32[]{:S(2)}, u32[]{:S(2)}) collective-permute-start(bf16[896,128]{1,0:T(8,128)(2,1)S(1)} %filter_block.1.refs_0_), channel_id=1, source_target_pairs={{0,12},{4,8},{8,4},{12,0},{16,28},{20,24},{24,20},{28,16},{1,13},{... | collective-permute-start | bytes 688136 | tf_op jit(solution)/shard_map/ppermute | solution.py:266
  60.6 11.0 %collective-permute-start.21 = (bf16[896,128]{1,0:T(8,128)(2,1)S(1)}, bf16[896,128]{1,0:T(8,128)(2,1)S(1)}, u32[]{:S(2)}, u32[]{:S(2)}) collective-permute-start(bf16[896,128]{1,0:T(8,128)(2,1)S(1)} %filter_block.1.refs_0_), channel_id=1, source_target_pairs={{0,8},{4,12},{8,0},{12,4},{16,24},{20,28},{24,16},{28,20},{1,9},{5... | collective-permute-start | bytes 688136 | tf_op jit(solution)/shard_map/ppermute | solution.py:266
  60.7 10.8 %collective-permute-start.20 = (bf16[896,128]{1,0:T(8,128)(2,1)S(1)}, bf16[896,128]{1,0:T(8,128)(2,1)S(1)}, u32[]{:S(2)}, u32[]{:S(2)}) collective-permute-start(bf16[896,128]{1,0:T(8,128)(2,1)S(1)} %filter_block.1.refs_0_), channel_id=1, source_target_pairs={{0,4},{4,0},{8,12},{12,8},{16,20},{20,16},{24,28},{28,24},{1,5},{5... | collective-permute-start | bytes 688136 | tf_op jit(solution)/shard_map/ppermute | solution.py:266

commit v9 on v8

--- a/solution.py
+++ b/solution.py
@@ -305,7 +305,7 @@
     keep, give = forward_parts(where, own, partner, outer, weights)
 
     got = swapped(give, "chan", 1)
-    near = [swapped(own, "space", flip) for flip in (4, 2, 3)]
+    near = [swapped(own, "space", flip) for flip in (4, 2)]
     pre_act = keep[0] + got[0] + out_bias[:, None]
     for j in range(1, groups // 2):
         pre_act = pre_act + swapped(keep[j] + got[j], "chan", 2 * j)
@@ -325,8 +325,8 @@
     given = jnp.where(side == 0, split[:, 1], split[:, 0])
     given, grad_pre = barrier((given, grad_pre))
     pair = jnp.stack([kept, swapped(given, "space", 1)], axis=0)
-    ahead = swapped(near[0], "space", 1)
-    last = swapped(jnp.stack([near[0], ahead], axis=0), "space", 2)
+    ahead = swapped(jnp.stack(near, axis=0), "space", 1)
+    last = swapped(jnp.stack([near[0], ahead[0]], axis=0), "space", 2)
     side = (space >> 1) & 1
     kept = jnp.where(side == 0, pair[:, 0], pair[:, 1])
     given = jnp.where(side == 0, pair[:, 1], pair[:, 0])
@@ -343,8 +343,8 @@
     blocks = both_cores(blocks)
     in_grad = in_grad + from_partner.astype(F32) + from_outer.astype(F32)
 
-    held = [v[None] for v in (own, partner, *near, ahead)] + [last]
-    flips = [(0,), (1,), (4,), (2,), (3,), (5,), (6, 7)]
+    held = [v[None] for v in (own, partner, *near)] + [ahead, last]
+    flips = [(0,), (1,), (4,), (2,), (5, 3), (6, 7)]
     for mask in [1 << k for k in range(3, depth.bit_length() - 1)]:
         held.append(swapped(jnp.concatenate(held, axis=0), "space", mask))
         flips.append(tuple(f ^ mask for some in flips for f in some))

time: 73.8 us -> 72.4 us (0.981)
  starting transfers between devices: 31.6 us -> 28.2 us
  waiting for transfers between devices: 24.2 us -> 26.2 us
    ppermute x21 -> x20, starting transfers between devices: 30.3 us -> 26.8 us  [swapped(): return lax.ppermute(value, axis, [(i, i ^ mask) for i in range(count)])]
    ppermute x21 -> x20, waiting for transfers between devices: 24.2 us -> 26.2 us  [swapped(): return lax.ppermute(value, axis, [(i, i ^ mask) for i in range(count)])]
  transfers between devices with their start and end apart: 23 -> 22, of which waited for: 12 -> 10; matrix products, arithmetic and copies ran while one was open for 7% -> 8% of each run, Pallas kernels for 4% -> 4%
where the time goes in v9:
time: 72.4 us; the launch traced here: 72.2 us
  starting transfers between devices  28.2 us (39%)
  waiting for transfers between devices  26.2 us (36%)
  Pallas kernels  11.3 us (16%)
  local copies, waits for them, and re-layouts  5.15 us (7%)
  between operations  0.87 us (1%)
    ppermute x20, starting transfers between devices, swapped(): return lax.ppermute(value, axis, [(i, i ^ mask) for i in range(count)])  26.8 us
    ppermute x20, waiting for transfers between devices, swapped(): return lax.ppermute(value, axis, [(i, i ^ mask) for i in range(count)])  26.2 us
    pallas_call x1, Pallas kernels, filter_block(): pl.pallas_call(functools.partial(filter_kernel, factor, groups, flips), o...  4.5 us
    pallas_call x1, Pallas kernels, input_parts(): pl.pallas_call(functools.partial(input_kernel, chans, chips), out_shape=[...  2.79 us
    unnamed x15, local copies, waits for them, and re-layouts  2.4 us
    pallas_call x1, Pallas kernels, join_blocks(): pl.pallas_call(functools.partial(join_kernel, share, chans), out_shape=[j...  2.11 us
    pallas_call x1, Pallas kernels, forward_parts(): pl.pallas_call(functools.partial(forward_kernel, chans), out_shape=[side,...  1.91 us
  transfers between devices with their start and end apart: 22, of which 10 were waited for; matrix products, arithmetic and copies ran while one was open for 8% of the time, Pallas kernels for 4%

profile of v9, /device:TPU:0, one launch (start us, length us, event | category | flops | bytes accessed | tf_op | source)
XLA Modules:
  0.0 72.2 jit_solution(3406027018900399055)
XLA Ops:
  0.6 3.0 %collective-permute-start.1 = (bf16[64,1024]{1,0:T(8,128)(2,1)}, bf16[64,1024]{1,0:T(8,128)(2,1)S(1)}, u32[]{:S(2)}, u32[]{:S(2)}) collective-permute-start(bf16[64,1024]{1,0:T(8,128)(2,1)} %bitcast.63), channel_id=1, source_target_pairs={{0,4},{4,0},{8,12},{12,8},{16,20},{20,16},{24,28},{28,24},{1,5},{5... | collective-permute-start | bytes 393224 | tf_op jit(solution)/shard_map/ppermute | solution.py:266
  3.6 0.7 collective-permute-start
  4.3 1.1 %constant_dynamic-slice_fusion = (bf16[1,576,256]{2,1,0:T(8,128)(2,1)S(1)}, bf16[1,576,256]{2,1,0:T(8,128)(2,1)S(1)}) fusion(bf16[3,576,256]{2,1,0:T(8,128)(2,1)} %bitcast.57, s32[]{:T(128)S(6)} %select_n.48, s32[]{:T(128)S(6)} %select_n.47), kind=kLoop, calls=%fused_computation.31 | loop fusion | bytes 1179656 | tf_op jit(solution)/shard_map/dynamic_slice | solution.py:303
  5.4 1.0 %slice.35 = bf16[9,64,256]{2,1,0:T(8,128)(2,1)S(1)} slice(bf16[27,64,256]{2,1,0:T(8,128)(2,1)} %refs_2_.1), slice={[9:18], [0:64], [0:256]} | slice | bytes 589824 | tf_op jit(solution)/shard_map/slice | solution.py:303
  7.6 1.9 %forward_parts.1 = (f32[2,64,1024]{2,1,0:T(8,128)S(1)}, f32[2,64,1024]{2,1,0:T(8,128)S(1)}) custom-call(s32[2]{0:T(128)S(1)} %pad_add_fusion.index, bf16[64,1024]{1,0:T(8,128)(2,1)S(1)} %bitcast.65, bf16[64,1024]{1,0:T(8,128)(2,1)S(1)} %collective-permute-done.1.partner, bf16[64,1024]{1,0:T(8,128)(2,1)S(1)} %collective-permute-done.outer, ...), custom_call_target="tpu_custom_call" | custom-call | flops 905969664 | bytes 6291456 | tf_op jit(solution)/shard_map/forward_parts/pallas_call | solution.py:64
  9.6 1.9 %collective-permute-done.2 = f32[2,64,1024]{2,1,0:T(8,128)S(1)} collective-permute-done((f32[2,64,1024]{2,1,0:T(8,128)S(1)}, f32[2,64,1024]{2,1,0:T(8,128)S(1)}, u32[]{:S(2)}, u32[]{:S(2)}) %collective-permute-start.2) | collective-permute-done | bytes 524320 | tf_op jit(solution)/shard_map/ppermute | solution.py:266
  11.5 1.6 %collective-permute-start.3 = (f32[64,1024]{1,0:T(8,128)S(1)}, f32[64,1024]{1,0:T(8,128)S(1)}, u32[]{:S(2)}, u32[]{:S(2)}) collective-permute-start(f32[64,1024]{1,0:T(8,128)S(1)} %fusion), channel_id=1, source_target_pairs={{0,2},{1,3},{2,0},{3,1},{4,6},{5,7},{6,4},{7,5},{8,10},{9,11},{10,... | collective-permute-start | bytes 786440 | tf_op jit(solution)/shard_map/ppermute | solution.py:266
  13.1 5.6 %collective-permute-start.5 = (bf16[64,1024]{1,0:T(8,128)(2,1)S(1)}, bf16[64,1024]{1,0:T(8,128)(2,1)S(1)}, u32[]{:S(2)}, u32[]{:S(2)}) collective-permute-start(bf16[64,1024]{1,0:T(8,128)(2,1)S(1)} %bitcast.66), channel_id=1, source_target_pairs={{0,8},{4,12},{8,0},{12,4},{16,24},{20,28},{24,16},{28,20},{1,9},{5... | collective-permute-start | bytes 393224 | tf_op jit(solution)/shard_map/ppermute | solution.py:266
  18.7 2.6 %collective-permute-start.4 = (bf16[64,1024]{1,0:T(8,128)(2,1)S(1)}, bf16[64,1024]{1,0:T(8,128)(2,1)S(1)}, u32[]{:S(2)}, u32[]{:S(2)}) collective-permute-start(bf16[64,1024]{1,0:T(8,128)(2,1)S(1)} %bitcast.67), channel_id=1, source_target_pairs={{0,16},{4,20},{8,24},{12,28},{16,0},{20,4},{24,8},{28,12},{1,17},{... | collective-permute-start | bytes 393224 | tf_op jit(solution)/shard_map/ppermute | solution.py:266
  21.4 2.7 %collective-permute-done.5 = bf16[64,1024]{1,0:T(8,128)(2,1)S(1)} collective-permute-done((bf16[64,1024]{1,0:T(8,128)(2,1)S(1)}, bf16[64,1024]{1,0:T(8,128)(2,1)S(1)}, u32[]{:S(2)}, u32[]{:S(2)}) %collective-permute-start.5) | collective-permute-done | bytes 131104 | tf_op jit(solution)/shard_map/ppermute | solution.py:266
  24.1 3.4 %collective-permute-done.4 = bf16[64,1024]{1,0:T(8,128)(2,1)S(1)} collective-permute-done((bf16[64,1024]{1,0:T(8,128)(2,1)S(1)}, bf16[64,1024]{1,0:T(8,128)(2,1)S(1)}, u32[]{:S(2)}, u32[]{:S(2)}) %collective-permute-start.4) | collective-permute-done | bytes 131104 | tf_op jit(solution)/shard_map/ppermute | solution.py:266
  27.7 0.6 collective-permute-start.8
  28.3 1.6 %collective-permute-start.13 = (bf16[2,64,1024]{2,1,0:T(8,128)(2,1)S(1)}, bf16[2,64,1024]{2,1,0:T(8,128)(2,1)S(1)}, u32[]{:S(2)}, u32[]{:S(2)}) collective-permute-start(bf16[2,64,1024]{2,1,0:T(8,128)(2,1)S(1)} %pad_maximum_fusion), channel_id=1, source_target_pairs={{0,4},{4,0},{8,12},{12,8},{16,20},{20,16},{24,28},{28,24},{1,5},{5... | collective-permute-start | bytes 786440 | tf_op jit(solution)/shard_map/ppermute | solution.py:266
  29.9 0.6 collective-permute-start.7
  30.5 2.2 %collective-permute-done.8 = bf16[2,16,1024]{2,1,0:T(8,128)(2,1)S(1)} collective-permute-done((bf16[2,16,1024]{2,1,0:T(8,128)(2,1)S(1)}, bf16[2,16,1024]{2,1,0:T(8,128)(2,1)S(1)}, u32[]{:S(2)}, u32[]{:S(2)}) %collective-permute-start.8) | collective-permute-done | bytes 65568 | tf_op jit(solution)/shard_map/ppermute | solution.py:266
  32.6 2.5 %collective-permute-start.11 = (bf16[2,16,1024]{2,1,0:T(8,128)(2,1)S(1)}, bf16[2,16,1024]{2,1,0:T(8,128)(2,1)S(1)}, u32[]{:S(2)}, u32[]{:S(2)}) collective-permute-start(bf16[2,16,1024]{2,1,0:T(8,128)(2,1)S(1)} %get-tuple-element.60), channel_id=1, source_target_pairs={{0,24},{4,28},{8,16},{12,20},{16,8},{20,12},{24,0},{28,4},{1,25},{... | collective-permute-start | bytes 196616 | tf_op jit(solution)/shard_map/ppermute | solution.py:266
  35.2 1.9 %collective-permute-start.10 = (bf16[2,16,1024]{2,1,0:T(8,128)(2,1)S(1)}, bf16[2,16,1024]{2,1,0:T(8,128)(2,1)S(1)}, u32[]{:S(2)}, u32[]{:S(2)}) collective-permute-start(bf16[2,16,1024]{2,1,0:T(8,128)(2,1)S(1)} %get-tuple-element.36), channel_id=1, source_target_pairs={{0,16},{4,20},{8,24},{12,28},{16,0},{20,4},{24,8},{28,12},{1,17},{... | collective-permute-start | bytes 196616 | tf_op jit(solution)/shard_map/ppermute | solution.py:266
  37.1 0.7 collective-permute-done.13.refs_4_
  37.8 0.5 collective-permute-start.14
  38.4 2.8 %input_parts.1 = (f32[64,1024]{1,0:T(8,128)S(1)}, bf16[64,1024]{1,0:T(8,128)(2,1)S(1)}, bf16[64,1024]{1,0:T(8,128)(2,1)S(1)}) custom-call(s32[2]{0:T(128)S(1)} %pad_add_fusion.index, bf16[2,64,1024]{2,1,0:T(8,128)(2,1)S(1)} %pad_maximum_fusion.2.refs_0_, bf16[2,64,1024]{2,1,0:T(8,128)(2,1)S(1)} %collective-permute-done.7.refs_1_, ...), custom_call_target="tpu_custom_call" | custom-call | flops 905969664 | bytes 6291456 | tf_op jit(solution)/shard_map/input_parts/pallas_call | solution.py:107
  41.2 0.6 collective-permute-start.12
  41.8 0.5 collective-permute-start.15
  42.3 0.7 collective-permute-start.16
  43.0 3.8 %collective-permute-done.15 = bf16[64,1024]{1,0:T(8,128)(2,1)S(1)} collective-permute-done((bf16[64,1024]{1,0:T(8,128)(2,1)S(1)}, bf16[64,1024]{1,0:T(8,128)(2,1)S(1)}, u32[]{:S(2)}, u32[]{:S(2)}) %collective-permute-start.15) | collective-permute-done | bytes 131104 | tf_op jit(solution)/shard_map/ppermute | solution.py:266
  46.8 2.1 %collective-permute-done.12.refs_8_ = bf16[8,16,1024]{2,1,0:T(8,128)(2,1)S(1)} collective-permute-done((bf16[8,16,1024]{2,1,0:T(8,128)(2,1)S(1)}, bf16[8,16,1024]{2,1,0:T(8,128)(2,1)S(1)}, u32[]{:S(2)}, u32[]{:S(2)}) %collective-permute-start.12) | collective-permute-done | bytes 262176 | tf_op jit(solution)/shard_map/ppermute | solution.py:266
  49.5 1.0 %copy.20 = f32[64,1,1024]{2,1,0:T(1,128)} copy(f32[64,1,1024]{2,0,1:T(8,128)S(1)} %get-tuple-element.59) | data formatting | bytes 524288
  50.8 4.5 %filter_block.1.refs_0_ = bf16[896,128]{1,0:T(8,128)(2,1)S(1)} custom-call(s32[2]{0:T(128)S(1)} %pad_add_fusion.1.index, bf16[1,64,1024]{2,1,0:T(8,128)(2,1)S(1)} %bitcast.68, bf16[1,64,1024]{2,1,0:T(8,128)(2,1)S(1)} %bitcast.69, bf16[1,64,1024]{2,1,0:T(8,128)(2,1)S(1)} %bitcast.60, bf16[1,64,1024]{2,1,0:T(8,128)(2,1)S(1)} %bitcast.62, ...), custom_call_target="tpu_custom_call" | custom-call | flops 1811939328 | bytes 8388608 | tf_op jit(solution)/shard_map/filter_block/pallas_call | solution.py:185
  55.3 4.0 %collective-permute-start.21 = (bf16[896,128]{1,0:T(8,128)(2,1)S(1)}, bf16[896,128]{1,0:T(8,128)(2,1)S(1)}, u32[]{:S(2)}, u32[]{:S(2)}) collective-permute-start(bf16[896,128]{1,0:T(8,128)(2,1)S(1)} %filter_block.1.refs_0_), channel_id=1, source_target_pairs={{0,12},{4,8},{8,4},{12,0},{16,28},{20,24},{24,20},{28,16},{1,13},{... | collective-permute-start | bytes 688136 | tf_op jit(solution)/shard_map/ppermute | solution.py:266
  60.0 1.0 %copy.21 = f32[64,1,1024]{2,1,0:T(1,128)} copy(f32[64,1,1024]{2,0,1:T(8,128)S(1)} %add_bitcast_fusion) | data formatting | bytes 524288
  61.0 4.8 %collective-permute-done.21.refs_3_ = bf16[896,128]{1,0:T(8,128)(2,1)S(1)} collective-permute-done((bf16[896,128]{1,0:T(8,128)(2,1)S(1)}, bf16[896,128]{1,0:T(8,128)(2,1)S(1)}, u32[]{:S(2)}, u32[]{:S(2)}) %collective-permute-start.21) | collective-permute-done | bytes 229408 | tf_op jit(solution)/shard_map/ppermute | solution.py:266
  65.8 4.3 %collective-permute-done.20.refs_2_ = bf16[896,128]{1,0:T(8,128)(2,1)S(1)} collective-permute-done((bf16[896,128]{1,0:T(8,128)(2,1)S(1)}, bf16[896,128]{1,0:T(8,128)(2,1)S(1)}, u32[]{:S(2)}, u32[]{:S(2)}) %collective-permute-start.20) | collective-permute-done | bytes 229408 | tf_op jit(solution)/shard_map/ppermute | solution.py:266
  70.1 2.1 %join_blocks.1 = (f32[27,64,256]{2,1,0:T(8,128)}, f32[1,256]{1,0:T(1,128)}) custom-call(s32[1]{0:T(128)} %bitcast.24.index, bf16[896,128]{1,0:T(8,128)(2,1)S(1)} %filter_block.1.refs_0_, bf16[896,128]{1,0:T(8,128)(2,1)S(1)} %collective-permute-done.19.refs_1_, bf16[896,128]{1,0:T(8,128)(2,1)S(1)} %collective-permute-done.20.refs_2_, ...), custom_call_target="tpu_custom_call" | custom-call | flops 452984832 | bytes 4194304 | tf_op jit(solution)/shard_map/join_blocks/pallas_call | solution.py:243
  (48 shorter events, 3.4 us)
Async XLA Ops:
  0.6 6.9 %collective-permute-start.1 = (bf16[64,1024]{1,0:T(8,128)(2,1)}, bf16[64,1024]{1,0:T(8,128)(2,1)S(1)}, u32[]{:S(2)}, u32[]{:S(2)}) collective-permute-start(bf16[64,1024]{1,0:T(8,128)(2,1)} %bitcast.63), channel_id=1, source_target_pairs={{0,4},{4,0},{8,12},{12,8},{16,20},{20,16},{24,28},{28,24},{1,5},{5... | collective-permute-start | bytes 393224 | tf_op jit(solution)/shard_map/ppermute | solution.py:266
  3.6 3.9 %collective-permute-start = (bf16[64,1024]{1,0:T(8,128)(2,1)}, bf16[64,1024]{1,0:T(8,128)(2,1)S(1)}, u32[]{:S(2)}, u32[]{:S(2)}) collective-permute-start(bf16[64,1024]{1,0:T(8,128)(2,1)} %bitcast.64), channel_id=1, source_target_pairs={{4,8},{12,16},{20,24},{8,4},{16,12},{24,20},{5,9},{13,17},{21,25},... | collective-permute-start | bytes 393224 | tf_op jit(solution)/shard_map/ppermute | solution.py:271
  6.4 1.2 %copy-start.1 = (bf16[64,1,1024]{2,0,1:T(8,128)(2,1)S(1)}, bf16[64,1,1024]{2,0,1:T(8,128)(2,1)}, u32[]{:S(2)}) copy-start(bf16[64,1,1024]{2,0,1:T(8,128)(2,1)} %param.4) | copy-start | bytes 393220
  7.6 13.7 %copy-start.3 = (f32[64]{0:T(128)S(1)}, f32[64]{0:T(128)}, u32[]{:S(2)}) copy-start(f32[64]{0:T(128)} %param.6) | copy-start | bytes 772
  7.6 19.8 %copy-start.2 = (bf16[64,1,1024]{2,0,1:T(8,128)(2,1)S(1)}, bf16[64,1,1024]{2,0,1:T(8,128)(2,1)}, u32[]{:S(2)}) copy-start(bf16[64,1,1024]{2,0,1:T(8,128)(2,1)} %param.7) | copy-start | bytes 393220
  9.5 2.0 %collective-permute-start.2 = (f32[2,64,1024]{2,1,0:T(8,128)S(1)}, f32[2,64,1024]{2,1,0:T(8,128)S(1)}, u32[]{:S(2)}, u32[]{:S(2)}) collective-permute-start(f32[2,64,1024]{2,1,0:T(8,128)S(1)} %get-tuple-element.29), channel_id=1, source_target_pairs={{0,1},{1,0},{2,3},{3,2},{4,5},{5,4},{6,7},{7,6},{8,9},{9,8},{10,11... | collective-permute-start | bytes 1572872 | tf_op jit(solution)/shard_map/ppermute | solution.py:266
  11.5 9.8 %collective-permute-start.3 = (f32[64,1024]{1,0:T(8,128)S(1)}, f32[64,1024]{1,0:T(8,128)S(1)}, u32[]{:S(2)}, u32[]{:S(2)}) collective-permute-start(f32[64,1024]{1,0:T(8,128)S(1)} %fusion), channel_id=1, source_target_pairs={{0,2},{1,3},{2,0},{3,1},{4,6},{5,7},{6,4},{7,5},{8,10},{9,11},{10,... | collective-permute-start | bytes 786440 | tf_op jit(solution)/shard_map/ppermute | solution.py:266
  13.1 10.9 %collective-permute-start.5 = (bf16[64,1024]{1,0:T(8,128)(2,1)S(1)}, bf16[64,1024]{1,0:T(8,128)(2,1)S(1)}, u32[]{:S(2)}, u32[]{:S(2)}) collective-permute-start(bf16[64,1024]{1,0:T(8,128)(2,1)S(1)} %bitcast.66), channel_id=1, source_target_pairs={{0,8},{4,12},{8,0},{12,4},{16,24},{20,28},{24,16},{28,20},{1,9},{5... | collective-permute-start | bytes 393224 | tf_op jit(solution)/shard_map/ppermute | solution.py:266
  18.7 8.7 %collective-permute-start.4 = (bf16[64,1024]{1,0:T(8,128)(2,1)S(1)}, bf16[64,1024]{1,0:T(8,128)(2,1)S(1)}, u32[]{:S(2)}, u32[]{:S(2)}) collective-permute-start(bf16[64,1024]{1,0:T(8,128)(2,1)S(1)} %bitcast.67), channel_id=1, source_target_pairs={{0,16},{4,20},{8,24},{12,28},{16,0},{20,4},{24,8},{28,12},{1,17},{... | collective-permute-start | bytes 393224 | tf_op jit(solution)/shard_map/ppermute | solution.py:266
  21.4 17.0 %copy-start = (bf16[27,64,256]{2,1,0:T(8,128)(2,1)S(1)}, bf16[27,64,256]{2,1,0:T(8,128)(2,1)}, u32[]{:S(2)}) copy-start(bf16[27,64,256]{2,1,0:T(8,128)(2,1)} %refs_2_.1) | copy-start | bytes 2654212
  27.6 2.3 %collective-permute-start.6 = (bf16[64,1024]{1,0:T(8,128)(2,1)S(1)}, bf16[64,1024]{1,0:T(8,128)(2,1)S(1)}, u32[]{:S(2)}, u32[]{:S(2)}) collective-permute-start(bf16[64,1024]{1,0:T(8,128)(2,1)S(1)} %get-tuple-element.31), channel_id=1, source_target_pairs={{0,1},{1,0},{2,3},{3,2},{4,5},{5,4},{6,7},{7,6},{8,9},{9,8},{10,11... | collective-permute-start | bytes 393224 | tf_op jit(solution)/shard_map/ppermute | solution.py:266
  27.7 5.0 %collective-permute-start.8 = (bf16[2,16,1024]{2,1,0:T(8,128)(2,1)S(1)}, bf16[2,16,1024]{2,1,0:T(8,128)(2,1)S(1)}, u32[]{:S(2)}, u32[]{:S(2)}) collective-permute-start(bf16[2,16,1024]{2,1,0:T(8,128)(2,1)S(1)} %get-tuple-element.33), channel_id=1, source_target_pairs={{0,4},{4,0},{8,12},{12,8},{16,20},{20,16},{24,28},{28,24},{1,5},{5... | collective-permute-start | bytes 196616 | tf_op jit(solution)/shard_map/ppermute | solution.py:266
  28.3 9.5 %collective-permute-start.13 = (bf16[2,64,1024]{2,1,0:T(8,128)(2,1)S(1)}, bf16[2,64,1024]{2,1,0:T(8,128)(2,1)S(1)}, u32[]{:S(2)}, u32[]{:S(2)}) collective-permute-start(bf16[2,64,1024]{2,1,0:T(8,128)(2,1)S(1)} %pad_maximum_fusion), channel_id=1, source_target_pairs={{0,4},{4,0},{8,12},{12,8},{16,20},{20,16},{24,28},{28,24},{1,5},{5... | collective-permute-start | bytes 786440 | tf_op jit(solution)/shard_map/ppermute | solution.py:266
  29.9 8.5 %collective-permute-start.7 = (bf16[2,64,1024]{2,1,0:T(8,128)(2,1)S(1)}, bf16[2,64,1024]{2,1,0:T(8,128)(2,1)S(1)}, u32[]{:S(2)}, u32[]{:S(2)}) collective-permute-start(bf16[2,64,1024]{2,1,0:T(8,128)(2,1)S(1)} %pad_maximum_fusion.2.refs_0_), channel_id=1, source_target_pairs={{0,2},{1,3},{2,0},{3,1},{4,6},{5,7},{6,4},{7,5},{8,10},{9,11},{10,... | collective-permute-start | bytes 786440 | tf_op jit(solution)/shard_map/ppermute | solution.py:266
  32.6 8.6 %collective-permute-start.11 = (bf16[2,16,1024]{2,1,0:T(8,128)(2,1)S(1)}, bf16[2,16,1024]{2,1,0:T(8,128)(2,1)S(1)}, u32[]{:S(2)}, u32[]{:S(2)}) collective-permute-start(bf16[2,16,1024]{2,1,0:T(8,128)(2,1)S(1)} %get-tuple-element.60), channel_id=1, source_target_pairs={{0,24},{4,28},{8,16},{12,20},{16,8},{20,12},{24,0},{28,4},{1,25},{... | collective-permute-start | bytes 196616 | tf_op jit(solution)/shard_map/ppermute | solution.py:266
  35.2 6.0 %collective-permute-start.9 = (bf16[2,16,1024]{2,1,0:T(8,128)(2,1)S(1)}, bf16[2,16,1024]{2,1,0:T(8,128)(2,1)S(1)}, u32[]{:S(2)}, u32[]{:S(2)}) collective-permute-start(bf16[2,16,1024]{2,1,0:T(8,128)(2,1)S(1)} %get-tuple-element.60), channel_id=1, source_target_pairs={{0,8},{4,12},{8,0},{12,4},{16,24},{20,28},{24,16},{28,20},{1,9},{5... | collective-permute-start | bytes 196616 | tf_op jit(solution)/shard_map/ppermute | solution.py:266
  35.2 6.0 %collective-permute-start.10 = (bf16[2,16,1024]{2,1,0:T(8,128)(2,1)S(1)}, bf16[2,16,1024]{2,1,0:T(8,128)(2,1)S(1)}, u32[]{:S(2)}, u32[]{:S(2)}) collective-permute-start(bf16[2,16,1024]{2,1,0:T(8,128)(2,1)S(1)} %get-tuple-element.36), channel_id=1, source_target_pairs={{0,16},{4,20},{8,24},{12,28},{16,0},{20,4},{24,8},{28,12},{1,17},{... | collective-permute-start | bytes 196616 | tf_op jit(solution)/shard_map/ppermute | solution.py:266
  37.8 9.0 %collective-permute-start.14 = (bf16[2,64,1024]{2,1,0:T(8,128)(2,1)S(1)}, bf16[2,64,1024]{2,1,0:T(8,128)(2,1)S(1)}, u32[]{:S(2)}, u32[]{:S(2)}) collective-permute-start(bf16[2,64,1024]{2,1,0:T(8,128)(2,1)S(1)} %pad_maximum_fusion.1), channel_id=1, source_target_pairs={{0,8},{4,12},{8,0},{12,4},{16,24},{20,28},{24,16},{28,20},{1,9},{5... | collective-permute-start | bytes 786440 | tf_op jit(solution)/shard_map/ppermute | solution.py:266
  41.2 7.7 %collective-permute-start.12 = (bf16[8,16,1024]{2,1,0:T(8,128)(2,1)S(1)}, bf16[8,16,1024]{2,1,0:T(8,128)(2,1)S(1)}, u32[]{:S(2)}, u32[]{:S(2)}) collective-permute-start(bf16[8,16,1024]{2,1,0:T(8,128)(2,1)S(1)} %constant_dynamic-update-slice_fusion.refs_6_), channel_id=1, source_target_pairs={{0,2},{1,3},{2,0},{3,1},{4,6},{5,7},{6,4},{7,5},{8,10},{9,11},{10,... | collective-permute-start | bytes 786440 | tf_op jit(solution)/shard_map/ppermute | solution.py:266
  41.8 5.0 %collective-permute-start.15 = (bf16[64,1024]{1,0:T(8,128)(2,1)S(1)}, bf16[64,1024]{1,0:T(8,128)(2,1)S(1)}, u32[]{:S(2)}, u32[]{:S(2)}) collective-permute-start(bf16[64,1024]{1,0:T(8,128)(2,1)S(1)} %get-tuple-element.39), channel_id=1, source_target_pairs={{0,4},{4,0},{8,12},{12,8},{16,20},{20,16},{24,28},{28,24},{1,5},{5... | collective-permute-start | bytes 393224 | tf_op jit(solution)/shard_map/ppermute | solution.py:266
  42.3 4.5 %collective-permute-start.16 = (bf16[64,1024]{1,0:T(8,128)(2,1)S(1)}, bf16[64,1024]{1,0:T(8,128)(2,1)S(1)}, u32[]{:S(2)}, u32[]{:S(2)}) collective-permute-start(bf16[64,1024]{1,0:T(8,128)(2,1)S(1)} %get-tuple-element.40), channel_id=1, source_target_pairs={{4,8},{12,16},{20,24},{8,4},{16,12},{24,20},{5,9},{13,17},{21,25},... | collective-permute-start | bytes 393224 | tf_op jit(solution)/shard_map/ppermute | solution.py:271
  48.9 1.6 %collective-permute-start.17 = (bf16[8,16,1024]{2,1,0:T(8,128)(2,1)S(1)}, bf16[8,16,1024]{2,1,0:T(8,128)(2,1)S(1)}, u32[]{:S(2)}, u32[]{:S(2)}) collective-permute-start(bf16[8,16,1024]{2,1,0:T(8,128)(2,1)S(1)} %constant_dynamic-update-slice_fusion.refs_6_), channel_id=1, source_target_pairs={{0,1},{1,0},{2,3},{3,2},{4,5},{5,4},{6,7},{7,6},{8,9},{9,8},{10,11... | collective-permute-start | bytes 786440 | tf_op jit(solution)/shard_map/ppermute | solution.py:266
  48.9 1.9 %collective-permute-start.18 = (bf16[8,16,1024]{2,1,0:T(8,128)(2,1)S(1)}, bf16[8,16,1024]{2,1,0:T(8,128)(2,1)S(1)}, u32[]{:S(2)}, u32[]{:S(2)}) collective-permute-start(bf16[8,16,1024]{2,1,0:T(8,128)(2,1)S(1)} %collective-permute-done.12.refs_8_), channel_id=1, source_target_pairs={{0,1},{1,0},{2,3},{3,2},{4,5},{5,4},{6,7},{7,6},{8,9},{9,8},{10,11... | collective-permute-start | bytes 786440 | tf_op jit(solution)/shard_map/ppermute | solution.py:266
  55.3 10.4 %collective-permute-start.21 = (bf16[896,128]{1,0:T(8,128)(2,1)S(1)}, bf16[896,128]{1,0:T(8,128)(2,1)S(1)}, u32[]{:S(2)}, u32[]{:S(2)}) collective-permute-start(bf16[896,128]{1,0:T(8,128)(2,1)S(1)} %filter_block.1.refs_0_), channel_id=1, source_target_pairs={{0,12},{4,8},{8,4},{12,0},{16,28},{20,24},{24,20},{28,16},{1,13},{... | collective-permute-start | bytes 688136 | tf_op jit(solution)/shard_map/ppermute | solution.py:266
  59.3 10.8 %collective-permute-start.20 = (bf16[896,128]{1,0:T(8,128)(2,1)S(1)}, bf16[896,128]{1,0:T(8,128)(2,1)S(1)}, u32[]{:S(2)}, u32[]{:S(2)}) collective-permute-start(bf16[896,128]{1,0:T(8,128)(2,1)S(1)} %filter_block.1.refs_0_), channel_id=1, source_target_pairs={{0,8},{4,12},{8,0},{12,4},{16,24},{20,28},{24,16},{28,20},{1,9},{5... | collective-permute-start | bytes 688136 | tf_op jit(solution)/shard_map/ppermute | solution.py:266
  59.5 10.6 %collective-permute-start.19 = (bf16[896,128]{1,0:T(8,128)(2,1)S(1)}, bf16[896,128]{1,0:T(8,128)(2,1)S(1)}, u32[]{:S(2)}, u32[]{:S(2)}) collective-permute-start(bf16[896,128]{1,0:T(8,128)(2,1)S(1)} %filter_block.1.refs_0_), channel_id=1, source_target_pairs={{0,4},{4,0},{8,12},{12,8},{16,20},{20,16},{24,28},{28,24},{1,5},{5... | collective-permute-start | bytes 688136 | tf_op jit(solution)/shard_map/ppermute | solution.py:266

commit v10 on v9

--- a/solution.py
+++ b/solution.py
@@ -308,9 +308,9 @@
     near = [swapped(own, "space", flip) for flip in (4, 2)]
     pre_act = keep[0] + got[0] + out_bias[:, None]
     for j in range(1, groups // 2):
-        pre_act = pre_act + swapped(keep[j] + got[j], "chan", 2 * j)
-
-    pre_act, near = barrier((pre_act, near))
+        term = (keep[j] + got[j]).astype(BF16)
+        pre_act = pre_act + swapped(term, "chan", 2 * j).astype(F32)
+
     sigmoid = jax.nn.sigmoid(pre_act)
     activated = pre_act * sigmoid
     grad_pre = (
@@ -324,6 +324,7 @@
     kept = jnp.where(side == 0, split[:, 0], split[:, 1])
     given = jnp.where(side == 0, split[:, 1], split[:, 0])
     given, grad_pre = barrier((given, grad_pre))
+    beside, near = barrier((swapped(grad_pre, "chan", 1), near))
     pair = jnp.stack([kept, swapped(given, "space", 1)], axis=0)
     ahead = swapped(jnp.stack(near, axis=0), "space", 1)
     last = swapped(jnp.stack([near[0], ahead[0]], axis=0), "space", 2)
@@ -334,7 +335,7 @@
     for t in range(1, depth // 2):
         pieces.append(swapped(given if t & 1 else kept, "space", 2 * t))
 
-    grads = other_chips(jnp.stack([grad_pre, swapped(grad_pre, "chan", 1)], axis=0))
+    grads = other_chips(jnp.stack([grad_pre, beside], axis=0))
     in_grad, to_partner, to_outer = input_parts(where, grads, filters)
     pieces[0], to_partner, to_outer = barrier((pieces[0], to_partner, to_outer))
     blocks = other_chips(jnp.concatenate(pieces, axis=0))

time: 72.4 us -> 69.6 us (0.961)
  waiting for transfers between devices: 26.2 us -> 20.3 us
  starting transfers between devices: 28.2 us -> 31.2 us
    ppermute x20, waiting for transfers between devices: 26.2 us -> 20.3 us  [swapped(): return lax.ppermute(value, axis, [(i, i ^ mask) for i in range(count)])]
    ppermute x20, starting transfers between devices: 26.8 us -> 29.9 us  [swapped(): return lax.ppermute(value, axis, [(i, i ^ mask) for i in range(count)])]
  transfers between devices with their start and end apart: 22 -> 22, of which waited for: 10 -> 9; matrix products, arithmetic and copies ran while one was open for 8% -> 8% of each run, Pallas kernels for 4% -> 4%
where the time goes in v10:
time: 69.6 us; the launch traced here: 69.5 us
  starting transfers between devices  31.2 us (45%)
  waiting for transfers between devices  20.3 us (29%)
  Pallas kernels  11.3 us (16%)
  local copies, waits for them, and re-layouts  5.15 us (7%)
  between operations  0.86 us (1%)
    ppermute x20, starting transfers between devices, swapped(): return lax.ppermute(value, axis, [(i, i ^ mask) for i in range(count)])  29.9 us
    ppermute x20, waiting for transfers between devices, swapped(): return lax.ppermute(value, axis, [(i, i ^ mask) for i in range(count)])  20.3 us
    pallas_call x1, Pallas kernels, filter_block(): pl.pallas_call(functools.partial(filter_kernel, factor, groups, flips), o...  4.5 us
    pallas_call x1, Pallas kernels, input_parts(): pl.pallas_call(functools.partial(input_kernel, chans, chips), out_shape=[...  2.8 us
    unnamed x15, local copies, waits for them, and re-layouts  2.4 us
    pallas_call x1, Pallas kernels, join_blocks(): pl.pallas_call(functools.partial(join_kernel, share, chans), out_shape=[j...  2.11 us
    pallas_call x1, Pallas kernels, forward_parts(): pl.pallas_call(functools.partial(forward_kernel, chans), out_shape=[side,...  1.91 us
  transfers between devices with their start and end apart: 22, of which 9 were waited for; matrix products, arithmetic and copies ran while one was open for 8% of the time, Pallas kernels for 4%

profile of v10, /device:TPU:0, one launch (start us, length us, event | category | flops | bytes accessed | tf_op | source)
XLA Modules:
  0.0 69.5 jit_solution(4562012430884647768)
XLA Ops:
  0.6 3.0 %collective-permute-start.1 = (bf16[64,1024]{1,0:T(8,128)(2,1)}, bf16[64,1024]{1,0:T(8,128)(2,1)S(1)}, u32[]{:S(2)}, u32[]{:S(2)}) collective-permute-start(bf16[64,1024]{1,0:T(8,128)(2,1)} %bitcast.67), channel_id=1, source_target_pairs={{0,4},{4,0},{8,12},{12,8},{16,20},{20,16},{24,28},{28,24},{1,5},{5... | collective-permute-start | bytes 393224 | tf_op jit(solution)/shard_map/ppermute | solution.py:266
  3.6 0.7 collective-permute-start
  4.3 1.1 %constant_dynamic-slice_fusion = (bf16[1,576,256]{2,1,0:T(8,128)(2,1)S(1)}, bf16[1,576,256]{2,1,0:T(8,128)(2,1)S(1)}) fusion(bf16[3,576,256]{2,1,0:T(8,128)(2,1)} %bitcast.61, s32[]{:T(128)S(6)} %select_n.48, s32[]{:T(128)S(6)} %select_n.47), kind=kLoop, calls=%fused_computation.32 | loop fusion | bytes 1179656 | tf_op jit(solution)/shard_map/dynamic_slice | solution.py:303
  5.4 1.0 %slice.35 = bf16[9,64,256]{2,1,0:T(8,128)(2,1)S(1)} slice(bf16[27,64,256]{2,1,0:T(8,128)(2,1)} %refs_2_.1), slice={[9:18], [0:64], [0:256]} | slice | bytes 589824 | tf_op jit(solution)/shard_map/slice | solution.py:303
  7.6 1.9 %forward_parts.1 = (f32[2,64,1024]{2,1,0:T(8,128)S(1)}, f32[2,64,1024]{2,1,0:T(8,128)S(1)}) custom-call(s32[2]{0:T(128)S(1)} %pad_add_fusion.index, bf16[64,1024]{1,0:T(8,128)(2,1)S(1)} %bitcast.69, bf16[64,1024]{1,0:T(8,128)(2,1)S(1)} %collective-permute-done.1.partner, bf16[64,1024]{1,0:T(8,128)(2,1)S(1)} %collective-permute-done.outer, ...), custom_call_target="tpu_custom_call" | custom-call | flops 905969664 | bytes 6291456 | tf_op jit(solution)/shard_map/forward_parts/pallas_call | solution.py:64
  9.6 1.9 %collective-permute-done.2 = f32[2,64,1024]{2,1,0:T(8,128)S(1)} collective-permute-done((f32[2,64,1024]{2,1,0:T(8,128)S(1)}, f32[2,64,1024]{2,1,0:T(8,128)S(1)}, u32[]{:S(2)}, u32[]{:S(2)}) %collective-permute-start.2) | collective-permute-done | bytes 524320 | tf_op jit(solution)/shard_map/ppermute | solution.py:266
  11.5 1.6 %collective-permute-start.3 = (bf16[64,1024]{1,0:T(8,128)(2,1)S(1)}, bf16[64,1024]{1,0:T(8,128)(2,1)S(1)}, u32[]{:S(2)}, u32[]{:S(2)}) collective-permute-start(bf16[64,1024]{1,0:T(8,128)(2,1)S(1)} %fusion.6), channel_id=1, source_target_pairs={{0,2},{1,3},{2,0},{3,1},{4,6},{5,7},{6,4},{7,5},{8,10},{9,11},{10,... | collective-permute-start | bytes 393224 | tf_op jit(solution)/shard_map/ppermute | solution.py:266
  13.1 5.6 %collective-permute-start.6 = (bf16[64,1024]{1,0:T(8,128)(2,1)S(1)}, bf16[64,1024]{1,0:T(8,128)(2,1)S(1)}, u32[]{:S(2)}, u32[]{:S(2)}) collective-permute-start(bf16[64,1024]{1,0:T(8,128)(2,1)S(1)} %bitcast.70), channel_id=1, source_target_pairs={{0,8},{4,12},{8,0},{12,4},{16,24},{20,28},{24,16},{28,20},{1,9},{5... | collective-permute-start | bytes 393224 | tf_op jit(solution)/shard_map/ppermute | solution.py:266
  18.7 2.6 %collective-permute-start.5 = (bf16[64,1024]{1,0:T(8,128)(2,1)S(1)}, bf16[64,1024]{1,0:T(8,128)(2,1)S(1)}, u32[]{:S(2)}, u32[]{:S(2)}) collective-permute-start(bf16[64,1024]{1,0:T(8,128)(2,1)S(1)} %bitcast.71), channel_id=1, source_target_pairs={{0,16},{4,20},{8,24},{12,28},{16,0},{20,4},{24,8},{28,12},{1,17},{... | collective-permute-start | bytes 393224 | tf_op jit(solution)/shard_map/ppermute | solution.py:266
  21.9 2.2 %collective-permute-done.6 = bf16[64,1024]{1,0:T(8,128)(2,1)S(1)} collective-permute-done((bf16[64,1024]{1,0:T(8,128)(2,1)S(1)}, bf16[64,1024]{1,0:T(8,128)(2,1)S(1)}, u32[]{:S(2)}, u32[]{:S(2)}) %collective-permute-start.6) | collective-permute-done | bytes 131104 | tf_op jit(solution)/shard_map/ppermute | solution.py:266
  24.1 3.4 %collective-permute-done.5 = bf16[64,1024]{1,0:T(8,128)(2,1)S(1)} collective-permute-done((bf16[64,1024]{1,0:T(8,128)(2,1)S(1)}, bf16[64,1024]{1,0:T(8,128)(2,1)S(1)}, u32[]{:S(2)}, u32[]{:S(2)}) %collective-permute-start.5) | collective-permute-done | bytes 131104 | tf_op jit(solution)/shard_map/ppermute | solution.py:266
  27.5 0.6 collective-permute-start.13
  28.1 0.6 collective-permute-start.7
  28.7 2.5 %collective-permute-start.11 = (bf16[2,16,1024]{2,1,0:T(8,128)(2,1)S(1)}, bf16[2,16,1024]{2,1,0:T(8,128)(2,1)S(1)}, u32[]{:S(2)}, u32[]{:S(2)}) collective-permute-start(bf16[2,16,1024]{2,1,0:T(8,128)(2,1)S(1)} %get-tuple-element.60), channel_id=1, source_target_pairs={{0,24},{4,28},{8,16},{12,20},{16,8},{20,12},{24,0},{28,4},{1,25},{... | collective-permute-start | bytes 196616 | tf_op jit(solution)/shard_map/ppermute | solution.py:266
  31.2 2.0 %collective-permute-start.10 = (bf16[2,16,1024]{2,1,0:T(8,128)(2,1)S(1)}, bf16[2,16,1024]{2,1,0:T(8,128)(2,1)S(1)}, u32[]{:S(2)}, u32[]{:S(2)}) collective-permute-start(bf16[2,16,1024]{2,1,0:T(8,128)(2,1)S(1)} %get-tuple-element.36), channel_id=1, source_target_pairs={{0,16},{4,20},{8,24},{12,28},{16,0},{20,4},{24,8},{28,12},{1,17},{... | collective-permute-start | bytes 196616 | tf_op jit(solution)/shard_map/ppermute | solution.py:266
  33.1 0.8 %collective-permute-done.13.refs_4_ = bf16[2,64,1024]{2,1,0:T(8,128)(2,1)S(1)} collective-permute-done((bf16[2,64,1024]{2,1,0:T(8,128)(2,1)S(1)}, bf16[2,64,1024]{2,1,0:T(8,128)(2,1)S(1)}, u32[]{:S(2)}, u32[]{:S(2)}) %collective-permute-start.13) | collective-permute-done | bytes 262176 | tf_op jit(solution)/shard_map/ppermute | solution.py:266
  34.0 1.2 %collective-permute-start.14 = (bf16[2,64,1024]{2,1,0:T(8,128)(2,1)S(1)}, bf16[2,64,1024]{2,1,0:T(8,128)(2,1)S(1)}, u32[]{:S(2)}, u32[]{:S(2)}) collective-permute-start(bf16[2,64,1024]{2,1,0:T(8,128)(2,1)S(1)} %pad_maximum_fusion.1), channel_id=1, source_target_pairs={{0,8},{4,12},{8,0},{12,4},{16,24},{20,28},{24,16},{28,20},{1,9},{5... | collective-permute-start | bytes 786440 | tf_op jit(solution)/shard_map/ppermute | solution.py:266
  35.2 2.8 %input_parts.1 = (f32[64,1024]{1,0:T(8,128)S(1)}, bf16[64,1024]{1,0:T(8,128)(2,1)S(1)}, bf16[64,1024]{1,0:T(8,128)(2,1)S(1)}) custom-call(s32[2]{0:T(128)S(1)} %pad_add_fusion.index, bf16[2,64,1024]{2,1,0:T(8,128)(2,1)S(1)} %pad_maximum_fusion.2.refs_0_, bf16[2,64,1024]{2,1,0:T(8,128)(2,1)S(1)} %collective-permute-done.7.refs_1_, ...), custom_call_target="tpu_custom_call" | custom-call | flops 905969664 | bytes 6291456 | tf_op jit(solution)/shard_map/input_parts/pallas_call | solution.py:107
  38.1 0.8 %collective-permute-start.12 = (bf16[8,16,1024]{2,1,0:T(8,128)(2,1)S(1)}, bf16[8,16,1024]{2,1,0:T(8,128)(2,1)S(1)}, u32[]{:S(2)}, u32[]{:S(2)}) collective-permute-start(bf16[8,16,1024]{2,1,0:T(8,128)(2,1)S(1)} %constant_dynamic-update-slice_fusion.refs_6_), channel_id=1, source_target_pairs={{0,2},{1,3},{2,0},{3,1},{4,6},{5,7},{6,4},{7,5},{8,10},{9,11},{10,... | collective-permute-start | bytes 786440 | tf_op jit(solution)/shard_map/ppermute | solution.py:266
  38.9 1.6 %collective-permute-start.15 = (bf16[64,1024]{1,0:T(8,128)(2,1)S(1)}, bf16[64,1024]{1,0:T(8,128)(2,1)S(1)}, u32[]{:S(2)}, u32[]{:S(2)}) collective-permute-start(bf16[64,1024]{1,0:T(8,128)(2,1)S(1)} %get-tuple-element.39), channel_id=1, source_target_pairs={{0,4},{4,0},{8,12},{12,8},{16,20},{20,16},{24,28},{28,24},{1,5},{5... | collective-permute-start | bytes 393224 | tf_op jit(solution)/shard_map/ppermute | solution.py:266
  40.5 0.7 collective-permute-start.16
  41.1 2.7 %collective-permute-done.15 = bf16[64,1024]{1,0:T(8,128)(2,1)S(1)} collective-permute-done((bf16[64,1024]{1,0:T(8,128)(2,1)S(1)}, bf16[64,1024]{1,0:T(8,128)(2,1)S(1)}, u32[]{:S(2)}, u32[]{:S(2)}) %collective-permute-start.15) | collective-permute-done | bytes 131104 | tf_op jit(solution)/shard_map/ppermute | solution.py:266
  43.9 0.7 collective-permute-done.12.refs_8_
  44.5 0.5 collective-permute-start.18
  45.1 1.0 %copy.20 = f32[64,1,1024]{2,1,0:T(1,128)} copy(f32[64,1,1024]{2,0,1:T(8,128)S(1)} %get-tuple-element.57) | data formatting | bytes 524288
  46.4 4.5 %filter_block.1.refs_0_ = bf16[896,128]{1,0:T(8,128)(2,1)S(1)} custom-call(s32[2]{0:T(128)S(1)} %pad_add_fusion.1.index, bf16[1,64,1024]{2,1,0:T(8,128)(2,1)S(1)} %bitcast.72, bf16[1,64,1024]{2,1,0:T(8,128)(2,1)S(1)} %bitcast.73, bf16[1,64,1024]{2,1,0:T(8,128)(2,1)S(1)} %bitcast.64, bf16[1,64,1024]{2,1,0:T(8,128)(2,1)S(1)} %bitcast.66, ...), custom_call_target="tpu_custom_call" | custom-call | flops 1811939328 | bytes 8388608 | tf_op jit(solution)/shard_map/filter_block/pallas_call | solution.py:185
  50.9 5.5 %collective-permute-start.21 = (bf16[896,128]{1,0:T(8,128)(2,1)S(1)}, bf16[896,128]{1,0:T(8,128)(2,1)S(1)}, u32[]{:S(2)}, u32[]{:S(2)}) collective-permute-start(bf16[896,128]{1,0:T(8,128)(2,1)S(1)} %filter_block.1.refs_0_), channel_id=1, source_target_pairs={{0,12},{4,8},{8,4},{12,0},{16,28},{20,24},{24,20},{28,16},{1,13},{... | collective-permute-start | bytes 688136 | tf_op jit(solution)/shard_map/ppermute | solution.py:266
  56.6 1.4 %collective-permute-start.19 = (bf16[896,128]{1,0:T(8,128)(2,1)S(1)}, bf16[896,128]{1,0:T(8,128)(2,1)S(1)}, u32[]{:S(2)}, u32[]{:S(2)}) collective-permute-start(bf16[896,128]{1,0:T(8,128)(2,1)S(1)} %filter_block.1.refs_0_), channel_id=1, source_target_pairs={{0,4},{4,0},{8,12},{12,8},{16,20},{20,16},{24,28},{28,24},{1,5},{5... | collective-permute-start | bytes 688136 | tf_op jit(solution)/shard_map/ppermute | solution.py:266
  58.0 1.0 %copy.21 = f32[64,1,1024]{2,1,0:T(1,128)} copy(f32[64,1,1024]{2,0,1:T(8,128)S(1)} %add_bitcast_fusion) | data formatting | bytes 524288
  59.0 3.9 %collective-permute-done.21.refs_3_ = bf16[896,128]{1,0:T(8,128)(2,1)S(1)} collective-permute-done((bf16[896,128]{1,0:T(8,128)(2,1)S(1)}, bf16[896,128]{1,0:T(8,128)(2,1)S(1)}, u32[]{:S(2)}, u32[]{:S(2)}) %collective-permute-start.21) | collective-permute-done | bytes 229408 | tf_op jit(solution)/shard_map/ppermute | solution.py:266
  62.8 4.5 %collective-permute-done.20.refs_2_ = bf16[896,128]{1,0:T(8,128)(2,1)S(1)} collective-permute-done((bf16[896,128]{1,0:T(8,128)(2,1)S(1)}, bf16[896,128]{1,0:T(8,128)(2,1)S(1)}, u32[]{:S(2)}, u32[]{:S(2)}) %collective-permute-start.20) | collective-permute-done | bytes 229408 | tf_op jit(solution)/shard_map/ppermute | solution.py:266
  67.4 2.1 %join_blocks.1 = (f32[27,64,256]{2,1,0:T(8,128)}, f32[1,256]{1,0:T(1,128)}) custom-call(s32[1]{0:T(128)} %bitcast.24.index, bf16[896,128]{1,0:T(8,128)(2,1)S(1)} %filter_block.1.refs_0_, bf16[896,128]{1,0:T(8,128)(2,1)S(1)} %collective-permute-done.19.refs_1_, bf16[896,128]{1,0:T(8,128)(2,1)S(1)} %collective-permute-done.20.refs_2_, ...), custom_call_target="tpu_custom_call" | custom-call | flops 452984832 | bytes 4194304 | tf_op jit(solution)/shard_map/join_blocks/pallas_call | solution.py:243
  (47 shorter events, 2.7 us)
Async XLA Ops:
  0.6 6.9 %collective-permute-start.1 = (bf16[64,1024]{1,0:T(8,128)(2,1)}, bf16[64,1024]{1,0:T(8,128)(2,1)S(1)}, u32[]{:S(2)}, u32[]{:S(2)}) collective-permute-start(bf16[64,1024]{1,0:T(8,128)(2,1)} %bitcast.67), channel_id=1, source_target_pairs={{0,4},{4,0},{8,12},{12,8},{16,20},{20,16},{24,28},{28,24},{1,5},{5... | collective-permute-start | bytes 393224 | tf_op jit(solution)/shard_map/ppermute | solution.py:266
  3.6 3.9 %collective-permute-start = (bf16[64,1024]{1,0:T(8,128)(2,1)}, bf16[64,1024]{1,0:T(8,128)(2,1)S(1)}, u32[]{:S(2)}, u32[]{:S(2)}) collective-permute-start(bf16[64,1024]{1,0:T(8,128)(2,1)} %bitcast.68), channel_id=1, source_target_pairs={{4,8},{12,16},{20,24},{8,4},{16,12},{24,20},{5,9},{13,17},{21,25},... | collective-permute-start | bytes 393224 | tf_op jit(solution)/shard_map/ppermute | solution.py:271
  6.4 1.2 %copy-start.1 = (bf16[64,1,1024]{2,0,1:T(8,128)(2,1)S(1)}, bf16[64,1,1024]{2,0,1:T(8,128)(2,1)}, u32[]{:S(2)}) copy-start(bf16[64,1,1024]{2,0,1:T(8,128)(2,1)} %param.4) | copy-start | bytes 393220
  7.6 13.7 %copy-start.2 = (bf16[64,1,1024]{2,0,1:T(8,128)(2,1)S(1)}, bf16[64,1,1024]{2,0,1:T(8,128)(2,1)}, u32[]{:S(2)}) copy-start(bf16[64,1,1024]{2,0,1:T(8,128)(2,1)} %param.7) | copy-start | bytes 393220
  7.6 13.7 %copy-start.3 = (f32[64]{0:T(128)S(1)}, f32[64]{0:T(128)}, u32[]{:S(2)}) copy-start(f32[64]{0:T(128)} %param.6) | copy-start | bytes 772
  9.5 2.0 %collective-permute-start.2 = (f32[2,64,1024]{2,1,0:T(8,128)S(1)}, f32[2,64,1024]{2,1,0:T(8,128)S(1)}, u32[]{:S(2)}, u32[]{:S(2)}) collective-permute-start(f32[2,64,1024]{2,1,0:T(8,128)S(1)} %get-tuple-element.29), channel_id=1, source_target_pairs={{0,1},{1,0},{2,3},{3,2},{4,5},{5,4},{6,7},{7,6},{8,9},{9,8},{10,11... | collective-permute-start | bytes 1572872 | tf_op jit(solution)/shard_map/ppermute | solution.py:266
  11.5 9.8 %collective-permute-start.3 = (bf16[64,1024]{1,0:T(8,128)(2,1)S(1)}, bf16[64,1024]{1,0:T(8,128)(2,1)S(1)}, u32[]{:S(2)}, u32[]{:S(2)}) collective-permute-start(bf16[64,1024]{1,0:T(8,128)(2,1)S(1)} %fusion.6), channel_id=1, source_target_pairs={{0,2},{1,3},{2,0},{3,1},{4,6},{5,7},{6,4},{7,5},{8,10},{9,11},{10,... | collective-permute-start | bytes 393224 | tf_op jit(solution)/shard_map/ppermute | solution.py:266
  13.1 10.9 %collective-permute-start.6 = (bf16[64,1024]{1,0:T(8,128)(2,1)S(1)}, bf16[64,1024]{1,0:T(8,128)(2,1)S(1)}, u32[]{:S(2)}, u32[]{:S(2)}) collective-permute-start(bf16[64,1024]{1,0:T(8,128)(2,1)S(1)} %bitcast.70), channel_id=1, source_target_pairs={{0,8},{4,12},{8,0},{12,4},{16,24},{20,28},{24,16},{28,20},{1,9},{5... | collective-permute-start | bytes 393224 | tf_op jit(solution)/shard_map/ppermute | solution.py:266
  18.7 8.7 %collective-permute-start.5 = (bf16[64,1024]{1,0:T(8,128)(2,1)S(1)}, bf16[64,1024]{1,0:T(8,128)(2,1)S(1)}, u32[]{:S(2)}, u32[]{:S(2)}) collective-permute-start(bf16[64,1024]{1,0:T(8,128)(2,1)S(1)} %bitcast.71), channel_id=1, source_target_pairs={{0,16},{4,20},{8,24},{12,28},{16,0},{20,4},{24,8},{28,12},{1,17},{... | collective-permute-start | bytes 393224 | tf_op jit(solution)/shard_map/ppermute | solution.py:266
  21.3 13.9 %copy-start = (bf16[27,64,256]{2,1,0:T(8,128)(2,1)S(1)}, bf16[27,64,256]{2,1,0:T(8,128)(2,1)}, u32[]{:S(2)}) copy-start(bf16[27,64,256]{2,1,0:T(8,128)(2,1)} %refs_2_.1) | copy-start | bytes 2654212
  21.5 5.9 %collective-permute-start.4 = (bf16[64,1024]{1,0:T(8,128)(2,1)S(1)}, bf16[64,1024]{1,0:T(8,128)(2,1)S(1)}, u32[]{:S(2)}, u32[]{:S(2)}) collective-permute-start(bf16[64,1024]{1,0:T(8,128)(2,1)S(1)} %get-tuple-element.30), channel_id=1, source_target_pairs={{0,1},{1,0},{2,3},{3,2},{4,5},{5,4},{6,7},{7,6},{8,9},{9,8},{10,11... | collective-permute-start | bytes 393224 | tf_op jit(solution)/shard_map/ppermute | solution.py:266
  21.6 7.0 %collective-permute-start.8 = (bf16[2,16,1024]{2,1,0:T(8,128)(2,1)S(1)}, bf16[2,16,1024]{2,1,0:T(8,128)(2,1)S(1)}, u32[]{:S(2)}, u32[]{:S(2)}) collective-permute-start(bf16[2,16,1024]{2,1,0:T(8,128)(2,1)S(1)} %get-tuple-element.33), channel_id=1, source_target_pairs={{0,4},{4,0},{8,12},{12,8},{16,20},{20,16},{24,28},{28,24},{1,5},{5... | collective-permute-start | bytes 196616 | tf_op jit(solution)/shard_map/ppermute | solution.py:266
  27.5 6.4 %collective-permute-start.13 = (bf16[2,64,1024]{2,1,0:T(8,128)(2,1)S(1)}, bf16[2,64,1024]{2,1,0:T(8,128)(2,1)S(1)}, u32[]{:S(2)}, u32[]{:S(2)}) collective-permute-start(bf16[2,64,1024]{2,1,0:T(8,128)(2,1)S(1)} %pad_maximum_fusion), channel_id=1, source_target_pairs={{0,4},{4,0},{8,12},{12,8},{16,20},{20,16},{24,28},{28,24},{1,5},{5... | collective-permute-start | bytes 786440 | tf_op jit(solution)/shard_map/ppermute | solution.py:266
  28.1 7.1 %collective-permute-start.7 = (bf16[2,64,1024]{2,1,0:T(8,128)(2,1)S(1)}, bf16[2,64,1024]{2,1,0:T(8,128)(2,1)S(1)}, u32[]{:S(2)}, u32[]{:S(2)}) collective-permute-start(bf16[2,64,1024]{2,1,0:T(8,128)(2,1)S(1)} %pad_maximum_fusion.2.refs_0_), channel_id=1, source_target_pairs={{0,2},{1,3},{2,0},{3,1},{4,6},{5,7},{6,4},{7,5},{8,10},{9,11},{10,... | collective-permute-start | bytes 786440 | tf_op jit(solution)/shard_map/ppermute | solution.py:266
  28.7 9.4 %collective-permute-start.11 = (bf16[2,16,1024]{2,1,0:T(8,128)(2,1)S(1)}, bf16[2,16,1024]{2,1,0:T(8,128)(2,1)S(1)}, u32[]{:S(2)}, u32[]{:S(2)}) collective-permute-start(bf16[2,16,1024]{2,1,0:T(8,128)(2,1)S(1)} %get-tuple-element.60), channel_id=1, source_target_pairs={{0,24},{4,28},{8,16},{12,20},{16,8},{20,12},{24,0},{28,4},{1,25},{... | collective-permute-start | bytes 196616 | tf_op jit(solution)/shard_map/ppermute | solution.py:266
  31.2 6.8 %collective-permute-start.9 = (bf16[2,16,1024]{2,1,0:T(8,128)(2,1)S(1)}, bf16[2,16,1024]{2,1,0:T(8,128)(2,1)S(1)}, u32[]{:S(2)}, u32[]{:S(2)}) collective-permute-start(bf16[2,16,1024]{2,1,0:T(8,128)(2,1)S(1)} %get-tuple-element.60), channel_id=1, source_target_pairs={{0,8},{4,12},{8,0},{12,4},{16,24},{20,28},{24,16},{28,20},{1,9},{5... | collective-permute-start | bytes 196616 | tf_op jit(solution)/shard_map/ppermute | solution.py:266
  31.2 6.9 %collective-permute-start.10 = (bf16[2,16,1024]{2,1,0:T(8,128)(2,1)S(1)}, bf16[2,16,1024]{2,1,0:T(8,128)(2,1)S(1)}, u32[]{:S(2)}, u32[]{:S(2)}) collective-permute-start(bf16[2,16,1024]{2,1,0:T(8,128)(2,1)S(1)} %get-tuple-element.36), channel_id=1, source_target_pairs={{0,16},{4,20},{8,24},{12,28},{16,0},{20,4},{24,8},{28,12},{1,17},{... | collective-permute-start | bytes 196616 | tf_op jit(solution)/shard_map/ppermute | solution.py:266
  34.0 9.9 %collective-permute-start.14 = (bf16[2,64,1024]{2,1,0:T(8,128)(2,1)S(1)}, bf16[2,64,1024]{2,1,0:T(8,128)(2,1)S(1)}, u32[]{:S(2)}, u32[]{:S(2)}) collective-permute-start(bf16[2,64,1024]{2,1,0:T(8,128)(2,1)S(1)} %pad_maximum_fusion.1), channel_id=1, source_target_pairs={{0,8},{4,12},{8,0},{12,4},{16,24},{20,28},{24,16},{28,20},{1,9},{5... | collective-permute-start | bytes 786440 | tf_op jit(solution)/shard_map/ppermute | solution.py:266
  38.1 6.4 %collective-permute-start.12 = (bf16[8,16,1024]{2,1,0:T(8,128)(2,1)S(1)}, bf16[8,16,1024]{2,1,0:T(8,128)(2,1)S(1)}, u32[]{:S(2)}, u32[]{:S(2)}) collective-permute-start(bf16[8,16,1024]{2,1,0:T(8,128)(2,1)S(1)} %constant_dynamic-update-slice_fusion.refs_6_), channel_id=1, source_target_pairs={{0,2},{1,3},{2,0},{3,1},{4,6},{5,7},{6,4},{7,5},{8,10},{9,11},{10,... | collective-permute-start | bytes 786440 | tf_op jit(solution)/shard_map/ppermute | solution.py:266
  38.9 5.0 %collective-permute-start.15 = (bf16[64,1024]{1,0:T(8,128)(2,1)S(1)}, bf16[64,1024]{1,0:T(8,128)(2,1)S(1)}, u32[]{:S(2)}, u32[]{:S(2)}) collective-permute-start(bf16[64,1024]{1,0:T(8,128)(2,1)S(1)} %get-tuple-element.39), channel_id=1, source_target_pairs={{0,4},{4,0},{8,12},{12,8},{16,20},{20,16},{24,28},{28,24},{1,5},{5... | collective-permute-start | bytes 393224 | tf_op jit(solution)/shard_map/ppermute | solution.py:266
  40.5 3.4 %collective-permute-start.16 = (bf16[64,1024]{1,0:T(8,128)(2,1)S(1)}, bf16[64,1024]{1,0:T(8,128)(2,1)S(1)}, u32[]{:S(2)}, u32[]{:S(2)}) collective-permute-start(bf16[64,1024]{1,0:T(8,128)(2,1)S(1)} %get-tuple-element.40), channel_id=1, source_target_pairs={{4,8},{12,16},{20,24},{8,4},{16,12},{24,20},{5,9},{13,17},{21,25},... | collective-permute-start | bytes 393224 | tf_op jit(solution)/shard_map/ppermute | solution.py:271
  44.5 1.6 %collective-permute-start.17 = (bf16[8,16,1024]{2,1,0:T(8,128)(2,1)S(1)}, bf16[8,16,1024]{2,1,0:T(8,128)(2,1)S(1)}, u32[]{:S(2)}, u32[]{:S(2)}) collective-permute-start(bf16[8,16,1024]{2,1,0:T(8,128)(2,1)S(1)} %constant_dynamic-update-slice_fusion.refs_6_), channel_id=1, source_target_pairs={{0,1},{1,0},{2,3},{3,2},{4,5},{5,4},{6,7},{7,6},{8,9},{9,8},{10,11... | collective-permute-start | bytes 786440 | tf_op jit(solution)/shard_map/ppermute | solution.py:266
  44.5 1.9 %collective-permute-start.18 = (bf16[8,16,1024]{2,1,0:T(8,128)(2,1)S(1)}, bf16[8,16,1024]{2,1,0:T(8,128)(2,1)S(1)}, u32[]{:S(2)}, u32[]{:S(2)}) collective-permute-start(bf16[8,16,1024]{2,1,0:T(8,128)(2,1)S(1)} %collective-permute-done.12.refs_8_), channel_id=1, source_target_pairs={{0,1},{1,0},{2,3},{3,2},{4,5},{5,4},{6,7},{7,6},{8,9},{9,8},{10,11... | collective-permute-start | bytes 786440 | tf_op jit(solution)/shard_map/ppermute | solution.py:266
  50.9 11.9 %collective-permute-start.21 = (bf16[896,128]{1,0:T(8,128)(2,1)S(1)}, bf16[896,128]{1,0:T(8,128)(2,1)S(1)}, u32[]{:S(2)}, u32[]{:S(2)}) collective-permute-start(bf16[896,128]{1,0:T(8,128)(2,1)S(1)} %filter_block.1.refs_0_), channel_id=1, source_target_pairs={{0,12},{4,8},{8,4},{12,0},{16,28},{20,24},{24,20},{28,16},{1,13},{... | collective-permute-start | bytes 688136 | tf_op jit(solution)/shard_map/ppermute | solution.py:266
  56.4 10.9 %collective-permute-start.20 = (bf16[896,128]{1,0:T(8,128)(2,1)S(1)}, bf16[896,128]{1,0:T(8,128)(2,1)S(1)}, u32[]{:S(2)}, u32[]{:S(2)}) collective-permute-start(bf16[896,128]{1,0:T(8,128)(2,1)S(1)} %filter_block.1.refs_0_), channel_id=1, source_target_pairs={{0,8},{4,12},{8,0},{12,4},{16,24},{20,28},{24,16},{28,20},{1,9},{5... | collective-permute-start | bytes 688136 | tf_op jit(solution)/shard_map/ppermute | solution.py:266
  56.6 10.8 %collective-permute-start.19 = (bf16[896,128]{1,0:T(8,128)(2,1)S(1)}, bf16[896,128]{1,0:T(8,128)(2,1)S(1)}, u32[]{:S(2)}, u32[]{:S(2)}) collective-permute-start(bf16[896,128]{1,0:T(8,128)(2,1)S(1)} %filter_block.1.refs_0_), channel_id=1, source_target_pairs={{0,4},{4,0},{8,12},{12,8},{16,20},{20,16},{24,28},{28,24},{1,5},{5... | collective-permute-start | bytes 688136 | tf_op jit(solution)/shard_map/ppermute | solution.py:266

commit v11 on v10

--- a/solution.py
+++ b/solution.py
@@ -7,6 +7,7 @@
 from jax.experimental import pallas as pl
 from jax.experimental.pallas import tpu as pltpu
 from jax.sharding import PartitionSpec as P
+import numpy as np
 
 TAPS = 27
 PLANE_H = 32
@@ -203,26 +204,24 @@
     )(index, *held, *grads)
 
 
-def join_kernel(share, chans, index, *refs):
-    blocks, (out, bias, right, held, done) = refs[:4], refs[4:]
+def spread(share, lanes, total):
+    slot = np.arange(4 * lanes) % (lanes // 2)
+    quarter, odd = np.arange(4 * lanes) // lanes, np.arange(4 * lanes) % lanes // (lanes // 2)
+    home = odd * total + (slot // share) * (4 * share) + quarter * share + slot % share
+    return jnp.asarray(home[:, None] == np.arange(2 * total), BF16)
+
+
+def join_kernel(chans, index, *refs):
+    blocks, (right, out, bias, left, held, done) = refs[:4], refs[4:]
     lanes, total = blocks[0].shape[1], out.shape[2]
-    width = lanes // 2
-    lane = lax.broadcasted_iota(jnp.int32, (lanes, total), 0)
-    column = lax.broadcasted_iota(jnp.int32, (lanes, total), 1)
-    slot = lane % width
-    for odd in range(2):
-        for r in range(4):
-            home = (slot // share) * (4 * share) + (index[0] ^ r) * share + slot % share
-            hit = (column == home) & (lane // width == odd)
-            right[r * lanes : (r + 1) * lanes, odd * total : (odd + 1) * total] = jnp.where(
-                hit, 1.0, 0.0
-            ).astype(BF16)
+    for r in range(4):
+        at = pl.multiple_of((index[0] ^ r) * lanes, lanes)
+        left[:, pl.ds(at, lanes)] = blocks[r][...]
     copies = []
     for k, (first, last) in enumerate(CHUNKS):
         pairs = range(first // 2, (last + 1) // 2)
         at = slice(pairs[0] * chans, (pairs[-1] + 1) * chans)
-        left = jnp.concatenate([block[at, :] for block in blocks], axis=1)
-        both = jnp.dot(left, right[...], preferred_element_type=F32)
+        both = jnp.dot(left[at, :], right[...], preferred_element_type=F32)
         for pair in pairs:
             row = (pair - pairs[0]) * chans
             held[2 * pair] = both[row : row + chans, :total]
@@ -241,15 +240,15 @@
     lanes = blocks[0].shape[1]
     total = 2 * lanes
     return pl.pallas_call(
-        functools.partial(join_kernel, share, chans),
+        functools.partial(join_kernel, chans),
         out_shape=[
             jax.ShapeDtypeStruct((TAPS, chans, total), F32),
             jax.ShapeDtypeStruct((1, total), F32),
         ],
-        in_specs=[SMEM] + [VMEM] * 4,
+        in_specs=[SMEM] + [VMEM] * 5,
         out_specs=[pl.BlockSpec(memory_space=pl.ANY), VMEM],
         scratch_shapes=[
-            pltpu.VMEM((4 * lanes, 2 * total), BF16),
+            pltpu.VMEM((blocks[0].shape[0], 4 * lanes), BF16),
             pltpu.VMEM((TAPS, chans, total), F32),
             pltpu.SemaphoreType.DMA((len(CHUNKS),)),
         ],
@@ -258,7 +257,7 @@
             flops=4 * TAPS * chans * total * lanes * 2, bytes_accessed=4 << 20, transcendentals=0
         ),
         name="join_blocks",
-    )(index, *blocks)
+    )(index, *blocks, spread(share, lanes, total))
 
 
 def swapped(value, axis, mask):
@@ -327,7 +326,6 @@
     beside, near = barrier((swapped(grad_pre, "chan", 1), near))
     pair = jnp.stack([kept, swapped(given, "space", 1)], axis=0)
     ahead = swapped(jnp.stack(near, axis=0), "space", 1)
-    last = swapped(jnp.stack([near[0], ahead[0]], axis=0), "space", 2)
     side = (space >> 1) & 1
     kept = jnp.where(side == 0, pair[:, 0], pair[:, 1])
     given = jnp.where(side == 0, pair[:, 1], pair[:, 0])
@@ -337,10 +335,11 @@
 
     grads = other_chips(jnp.stack([grad_pre, beside], axis=0))
     in_grad, to_partner, to_outer = input_parts(where, grads, filters)
-    pieces[0], to_partner, to_outer = barrier((pieces[0], to_partner, to_outer))
+    pieces[0], to_partner, to_outer, ahead = barrier((pieces[0], to_partner, to_outer, ahead))
+    last = swapped(jnp.stack([near[0], ahead[0]], axis=0), "space", 2)
     blocks = other_chips(jnp.concatenate(pieces, axis=0))
     from_partner, from_outer = swapped(to_partner, "space", 1), exchanged(to_outer)
-    blocks, last, from_partner, from_outer = barrier((blocks, last, from_partner, from_outer))
+    blocks, from_partner, from_outer = barrier((blocks, from_partner, from_outer))
     blocks = both_cores(blocks)
     in_grad = in_grad + from_partner.astype(F32) + from_outer.astype(F32)
 

time: 69.6 us -> 69 us (level)
  starting transfers between devices: 31.2 us -> 30.4 us
    ppermute x20, starting transfers between devices: 29.9 us -> 29.1 us  [swapped(): return lax.ppermute(value, axis, [(i, i ^ mask) for i in range(count)])]
    unnamed x15 -> x17, local copies, waits for them, and re-layouts: 2.4 us -> 2.4 us
  transfers between devices with their start and end apart: 22 -> 22, of which waited for: 9 -> 7; matrix products, arithmetic and copies ran while one was open for 8% -> 8% of each run, Pallas kernels for 4% -> 4%
where the time goes in v11:
time: 69 us; the launch traced here: 68.8 us
  starting transfers between devices  30.4 us (44%)
  waiting for transfers between devices  20.4 us (30%)
  Pallas kernels  11.5 us (17%)
  local copies, waits for them, and re-layouts  5.16 us (7%)
  between operations  0.89 us (1%)
    ppermute x20, starting transfers between devices, swapped(): return lax.ppermute(value, axis, [(i, i ^ mask) for i in range(count)])  29.1 us
    ppermute x20, waiting for transfers between devices, swapped(): return lax.ppermute(value, axis, [(i, i ^ mask) for i in range(count)])  20.4 us
    pallas_call x1, Pallas kernels, filter_block(): pl.pallas_call(functools.partial(filter_kernel, factor, groups, flips), o...  4.5 us
    pallas_call x1, Pallas kernels, input_parts(): pl.pallas_call(functools.partial(input_kernel, chans, chips), out_shape=[...  2.8 us
    unnamed x17, local copies, waits for them, and re-layouts  2.4 us
    pallas_call x1, Pallas kernels, join_blocks(): pl.pallas_call(functools.partial(join_kernel, chans), out_shape=[jax.Shap...  2.25 us
    pallas_call x1, Pallas kernels, forward_parts(): pl.pallas_call(functools.partial(forward_kernel, chans), out_shape=[side,...  1.91 us
  transfers between devices with their start and end apart: 22, of which 7 were waited for; matrix products, arithmetic and copies ran while one was open for 8% of the time, Pallas kernels for 4%

profile of v11, /device:TPU:0, one launch (start us, length us, event | category | flops | bytes accessed | tf_op | source)
XLA Modules:
  0.0 68.8 jit_solution(1040888429594731111)
XLA Ops:
  0.6 3.0 %collective-permute-start.1 = (bf16[64,1024]{1,0:T(8,128)(2,1)}, bf16[64,1024]{1,0:T(8,128)(2,1)S(1)}, u32[]{:S(2)}, u32[]{:S(2)}) collective-permute-start(bf16[64,1024]{1,0:T(8,128)(2,1)} %bitcast.67), channel_id=1, source_target_pairs={{0,4},{4,0},{8,12},{12,8},{16,20},{20,16},{24,28},{28,24},{1,5},{5... | collective-permute-start | bytes 393224 | tf_op jit(solution)/shard_map/ppermute | solution.py:265
  3.6 0.7 collective-permute-start
  4.3 1.1 %constant_dynamic-slice_fusion = (bf16[1,576,256]{2,1,0:T(8,128)(2,1)S(1)}, bf16[1,576,256]{2,1,0:T(8,128)(2,1)S(1)}) fusion(bf16[3,576,256]{2,1,0:T(8,128)(2,1)} %bitcast.61, s32[]{:T(128)S(6)} %select_n.48, s32[]{:T(128)S(6)} %select_n.47), kind=kLoop, calls=%fused_computation.32 | loop fusion | bytes 1179656 | tf_op jit(solution)/shard_map/dynamic_slice | solution.py:302
  5.4 1.0 %slice.35 = bf16[9,64,256]{2,1,0:T(8,128)(2,1)S(1)} slice(bf16[27,64,256]{2,1,0:T(8,128)(2,1)} %refs_2_.1), slice={[9:18], [0:64], [0:256]} | slice | bytes 589824 | tf_op jit(solution)/shard_map/slice | solution.py:302
  7.0 0.5 concatenate.6
  7.6 1.9 %forward_parts.1 = (f32[2,64,1024]{2,1,0:T(8,128)S(1)}, f32[2,64,1024]{2,1,0:T(8,128)S(1)}) custom-call(s32[2]{0:T(128)S(1)} %pad_add_fusion.index, bf16[64,1024]{1,0:T(8,128)(2,1)S(1)} %bitcast.69, bf16[64,1024]{1,0:T(8,128)(2,1)S(1)} %collective-permute-done.1.partner, bf16[64,1024]{1,0:T(8,128)(2,1)S(1)} %collective-permute-done.outer, ...), custom_call_target="tpu_custom_call" | custom-call | flops 905969664 | bytes 6291456 | tf_op jit(solution)/shard_map/forward_parts/pallas_call | solution.py:65
  9.6 1.9 %collective-permute-done.2 = f32[2,64,1024]{2,1,0:T(8,128)S(1)} collective-permute-done((f32[2,64,1024]{2,1,0:T(8,128)S(1)}, f32[2,64,1024]{2,1,0:T(8,128)S(1)}, u32[]{:S(2)}, u32[]{:S(2)}) %collective-permute-start.2) | collective-permute-done | bytes 524320 | tf_op jit(solution)/shard_map/ppermute | solution.py:265
  11.5 1.6 %collective-permute-start.3 = (bf16[64,1024]{1,0:T(8,128)(2,1)S(1)}, bf16[64,1024]{1,0:T(8,128)(2,1)S(1)}, u32[]{:S(2)}, u32[]{:S(2)}) collective-permute-start(bf16[64,1024]{1,0:T(8,128)(2,1)S(1)} %fusion.6), channel_id=1, source_target_pairs={{0,2},{1,3},{2,0},{3,1},{4,6},{5,7},{6,4},{7,5},{8,10},{9,11},{10,... | collective-permute-start | bytes 393224 | tf_op jit(solution)/shard_map/ppermute | solution.py:265
  13.1 5.6 %collective-permute-start.6 = (bf16[64,1024]{1,0:T(8,128)(2,1)S(1)}, bf16[64,1024]{1,0:T(8,128)(2,1)S(1)}, u32[]{:S(2)}, u32[]{:S(2)}) collective-permute-start(bf16[64,1024]{1,0:T(8,128)(2,1)S(1)} %bitcast.70), channel_id=1, source_target_pairs={{0,8},{4,12},{8,0},{12,4},{16,24},{20,28},{24,16},{28,20},{1,9},{5... | collective-permute-start | bytes 393224 | tf_op jit(solution)/shard_map/ppermute | solution.py:265
  18.7 2.6 %collective-permute-start.5 = (bf16[64,1024]{1,0:T(8,128)(2,1)S(1)}, bf16[64,1024]{1,0:T(8,128)(2,1)S(1)}, u32[]{:S(2)}, u32[]{:S(2)}) collective-permute-start(bf16[64,1024]{1,0:T(8,128)(2,1)S(1)} %bitcast.71), channel_id=1, source_target_pairs={{0,16},{4,20},{8,24},{12,28},{16,0},{20,4},{24,8},{28,12},{1,17},{... | collective-permute-start | bytes 393224 | tf_op jit(solution)/shard_map/ppermute | solution.py:265
  21.9 2.2 %collective-permute-done.6 = bf16[64,1024]{1,0:T(8,128)(2,1)S(1)} collective-permute-done((bf16[64,1024]{1,0:T(8,128)(2,1)S(1)}, bf16[64,1024]{1,0:T(8,128)(2,1)S(1)}, u32[]{:S(2)}, u32[]{:S(2)}) %collective-permute-start.6) | collective-permute-done | bytes 131104 | tf_op jit(solution)/shard_map/ppermute | solution.py:265
  24.1 3.4 %collective-permute-done.5 = bf16[64,1024]{1,0:T(8,128)(2,1)S(1)} collective-permute-done((bf16[64,1024]{1,0:T(8,128)(2,1)S(1)}, bf16[64,1024]{1,0:T(8,128)(2,1)S(1)}, u32[]{:S(2)}, u32[]{:S(2)}) %collective-permute-start.5) | collective-permute-done | bytes 131104 | tf_op jit(solution)/shard_map/ppermute | solution.py:265
  27.5 0.6 collective-permute-start.7
  28.1 0.6 collective-permute-start.9
  28.7 2.5 %collective-permute-start.12 = (bf16[2,16,1024]{2,1,0:T(8,128)(2,1)S(1)}, bf16[2,16,1024]{2,1,0:T(8,128)(2,1)S(1)}, u32[]{:S(2)}, u32[]{:S(2)}) collective-permute-start(bf16[2,16,1024]{2,1,0:T(8,128)(2,1)S(1)} %get-tuple-element.60), channel_id=1, source_target_pairs={{0,24},{4,28},{8,16},{12,20},{16,8},{20,12},{24,0},{28,4},{1,25},{... | collective-permute-start | bytes 196616 | tf_op jit(solution)/shard_map/ppermute | solution.py:265
  31.2 2.0 %collective-permute-start.11 = (bf16[2,16,1024]{2,1,0:T(8,128)(2,1)S(1)}, bf16[2,16,1024]{2,1,0:T(8,128)(2,1)S(1)}, u32[]{:S(2)}, u32[]{:S(2)}) collective-permute-start(bf16[2,16,1024]{2,1,0:T(8,128)(2,1)S(1)} %get-tuple-element.38), channel_id=1, source_target_pairs={{0,16},{4,20},{8,24},{12,28},{16,0},{20,4},{24,8},{28,12},{1,17},{... | collective-permute-start | bytes 196616 | tf_op jit(solution)/shard_map/ppermute | solution.py:265
  33.1 0.8 %collective-permute-done.7.refs_1_ = bf16[2,64,1024]{2,1,0:T(8,128)(2,1)S(1)} collective-permute-done((bf16[2,64,1024]{2,1,0:T(8,128)(2,1)S(1)}, bf16[2,64,1024]{2,1,0:T(8,128)(2,1)S(1)}, u32[]{:S(2)}, u32[]{:S(2)}) %collective-permute-start.7) | collective-permute-done | bytes 262176 | tf_op jit(solution)/shard_map/ppermute | solution.py:265
  33.9 2.8 %input_parts.1 = (f32[64,1024]{1,0:T(8,128)S(1)}, bf16[64,1024]{1,0:T(8,128)(2,1)S(1)}, bf16[64,1024]{1,0:T(8,128)(2,1)S(1)}) custom-call(s32[2]{0:T(128)S(1)} %pad_add_fusion.index, bf16[2,64,1024]{2,1,0:T(8,128)(2,1)S(1)} %pad_maximum_fusion.2.refs_0_, bf16[2,64,1024]{2,1,0:T(8,128)(2,1)S(1)} %collective-permute-done.7.refs_1_, ...), custom_call_target="tpu_custom_call" | custom-call | flops 905969664 | bytes 6291456 | tf_op jit(solution)/shard_map/input_parts/pallas_call | solution.py:108
  36.8 1.3 %collective-permute-start.13 = (bf16[8,16,1024]{2,1,0:T(8,128)(2,1)S(1)}, bf16[8,16,1024]{2,1,0:T(8,128)(2,1)S(1)}, u32[]{:S(2)}, u32[]{:S(2)}) collective-permute-start(bf16[8,16,1024]{2,1,0:T(8,128)(2,1)S(1)} %constant_dynamic-update-slice_fusion.refs_6_), channel_id=1, source_target_pairs={{0,2},{1,3},{2,0},{3,1},{4,6},{5,7},{6,4},{7,5},{8,10},{9,11},{10,... | collective-permute-start | bytes 786440 | tf_op jit(solution)/shard_map/ppermute | solution.py:265
  38.1 1.6 %collective-permute-start.14 = (bf16[64,1024]{1,0:T(8,128)(2,1)S(1)}, bf16[64,1024]{1,0:T(8,128)(2,1)S(1)}, u32[]{:S(2)}, u32[]{:S(2)}) collective-permute-start(bf16[64,1024]{1,0:T(8,128)(2,1)S(1)} %get-tuple-element.39), channel_id=1, source_target_pairs={{0,4},{4,0},{8,12},{12,8},{16,20},{20,16},{24,28},{28,24},{1,5},{5... | collective-permute-start | bytes 393224 | tf_op jit(solution)/shard_map/ppermute | solution.py:265
  39.7 0.7 collective-permute-start.15
  40.4 3.2 %collective-permute-start.16 = (bf16[2,64,1024]{2,1,0:T(8,128)(2,1)S(1)}, bf16[2,64,1024]{2,1,0:T(8,128)(2,1)S(1)}, u32[]{:S(2)}, u32[]{:S(2)}) collective-permute-start(bf16[2,64,1024]{2,1,0:T(8,128)(2,1)S(1)} %pad_maximum_fusion), channel_id=1, source_target_pairs={{0,8},{4,12},{8,0},{12,4},{16,24},{20,28},{24,16},{28,20},{1,9},{5... | collective-permute-start | bytes 786440 | tf_op jit(solution)/shard_map/ppermute | solution.py:265
  43.7 0.5 collective-permute-start.18
  44.3 1.0 %copy.21 = f32[64,1,1024]{2,1,0:T(1,128)} copy(f32[64,1,1024]{2,0,1:T(8,128)S(1)} %get-tuple-element.57) | data formatting | bytes 524288
  45.3 4.0 %collective-permute-done.16.refs_5_ = bf16[2,64,1024]{2,1,0:T(8,128)(2,1)S(1)} collective-permute-done((bf16[2,64,1024]{2,1,0:T(8,128)(2,1)S(1)}, bf16[2,64,1024]{2,1,0:T(8,128)(2,1)S(1)}, u32[]{:S(2)}, u32[]{:S(2)}) %collective-permute-start.16) | collective-permute-done | bytes 262176 | tf_op jit(solution)/shard_map/ppermute | solution.py:265
  49.3 4.5 %filter_block.1.refs_0_ = bf16[896,128]{1,0:T(8,128)(2,1)S(1)} custom-call(s32[2]{0:T(128)S(1)} %pad_add_fusion.1.index, bf16[1,64,1024]{2,1,0:T(8,128)(2,1)S(1)} %bitcast.72, bf16[1,64,1024]{2,1,0:T(8,128)(2,1)S(1)} %bitcast.73, bf16[1,64,1024]{2,1,0:T(8,128)(2,1)S(1)} %bitcast.64, bf16[1,64,1024]{2,1,0:T(8,128)(2,1)S(1)} %bitcast.66, ...), custom_call_target="tpu_custom_call" | custom-call | flops 1811939328 | bytes 8388608 | tf_op jit(solution)/shard_map/filter_block/pallas_call | solution.py:186
  53.8 2.8 %collective-permute-start.21 = (bf16[896,128]{1,0:T(8,128)(2,1)S(1)}, bf16[896,128]{1,0:T(8,128)(2,1)S(1)}, u32[]{:S(2)}, u32[]{:S(2)}) collective-permute-start(bf16[896,128]{1,0:T(8,128)(2,1)S(1)} %filter_block.1.refs_0_), channel_id=1, source_target_pairs={{0,12},{4,8},{8,4},{12,0},{16,28},{20,24},{24,20},{28,16},{1,13},{... | collective-permute-start | bytes 688136 | tf_op jit(solution)/shard_map/ppermute | solution.py:265
  56.6 0.8 %collective-permute-start.20 = (bf16[896,128]{1,0:T(8,128)(2,1)S(1)}, bf16[896,128]{1,0:T(8,128)(2,1)S(1)}, u32[]{:S(2)}, u32[]{:S(2)}) collective-permute-start(bf16[896,128]{1,0:T(8,128)(2,1)S(1)} %filter_block.1.refs_0_), channel_id=1, source_target_pairs={{0,8},{4,12},{8,0},{12,4},{16,24},{20,28},{24,16},{28,20},{1,9},{5... | collective-permute-start | bytes 688136 | tf_op jit(solution)/shard_map/ppermute | solution.py:265
  57.5 1.0 %copy.22 = f32[64,1,1024]{2,1,0:T(1,128)} copy(f32[64,1,1024]{2,0,1:T(8,128)S(1)} %add_bitcast_fusion) | data formatting | bytes 524288
  58.4 4.9 %collective-permute-done.21.refs_3_ = bf16[896,128]{1,0:T(8,128)(2,1)S(1)} collective-permute-done((bf16[896,128]{1,0:T(8,128)(2,1)S(1)}, bf16[896,128]{1,0:T(8,128)(2,1)S(1)}, u32[]{:S(2)}, u32[]{:S(2)}) %collective-permute-start.21) | collective-permute-done | bytes 229408 | tf_op jit(solution)/shard_map/ppermute | solution.py:265
  63.3 3.3 %collective-permute-done.20.refs_2_ = bf16[896,128]{1,0:T(8,128)(2,1)S(1)} collective-permute-done((bf16[896,128]{1,0:T(8,128)(2,1)S(1)}, bf16[896,128]{1,0:T(8,128)(2,1)S(1)}, u32[]{:S(2)}, u32[]{:S(2)}) %collective-permute-start.20) | collective-permute-done | bytes 229408 | tf_op jit(solution)/shard_map/ppermute | solution.py:265
  66.6 2.3 %join_blocks.1 = (f32[27,64,256]{2,1,0:T(8,128)}, f32[1,256]{1,0:T(1,128)}) custom-call(s32[1]{0:T(128)} %bitcast.24.index, bf16[896,128]{1,0:T(8,128)(2,1)S(1)} %filter_block.1.refs_0_, bf16[896,128]{1,0:T(8,128)(2,1)S(1)} %collective-permute-done.19.refs_1_, bf16[896,128]{1,0:T(8,128)(2,1)S(1)} %collective-permute-done.20.refs_2_, ...), custom_call_target="tpu_custom_call" | custom-call | flops 452984832 | bytes 4194304 | tf_op jit(solution)/shard_map/join_blocks/pallas_call | solution.py:242
  (49 shorter events, 1.8 us)
Async XLA Ops:
  0.6 6.9 %collective-permute-start.1 = (bf16[64,1024]{1,0:T(8,128)(2,1)}, bf16[64,1024]{1,0:T(8,128)(2,1)S(1)}, u32[]{:S(2)}, u32[]{:S(2)}) collective-permute-start(bf16[64,1024]{1,0:T(8,128)(2,1)} %bitcast.67), channel_id=1, source_target_pairs={{0,4},{4,0},{8,12},{12,8},{16,20},{20,16},{24,28},{28,24},{1,5},{5... | collective-permute-start | bytes 393224 | tf_op jit(solution)/shard_map/ppermute | solution.py:265
  3.6 3.9 %collective-permute-start = (bf16[64,1024]{1,0:T(8,128)(2,1)}, bf16[64,1024]{1,0:T(8,128)(2,1)S(1)}, u32[]{:S(2)}, u32[]{:S(2)}) collective-permute-start(bf16[64,1024]{1,0:T(8,128)(2,1)} %bitcast.68), channel_id=1, source_target_pairs={{4,8},{12,16},{20,24},{8,4},{16,12},{24,20},{5,9},{13,17},{21,25},... | collective-permute-start | bytes 393224 | tf_op jit(solution)/shard_map/ppermute | solution.py:270
  6.4 1.2 %copy-start.1 = (bf16[64,1,1024]{2,0,1:T(8,128)(2,1)S(1)}, bf16[64,1,1024]{2,0,1:T(8,128)(2,1)}, u32[]{:S(2)}) copy-start(bf16[64,1,1024]{2,0,1:T(8,128)(2,1)} %param.5) | copy-start | bytes 393220
  7.6 13.7 %copy-start.3 = (bf16[64,1,1024]{2,0,1:T(8,128)(2,1)S(1)}, bf16[64,1,1024]{2,0,1:T(8,128)(2,1)}, u32[]{:S(2)}) copy-start(bf16[64,1,1024]{2,0,1:T(8,128)(2,1)} %param.8) | copy-start | bytes 393220
  7.6 13.7 %copy-start.4 = (f32[64]{0:T(128)S(1)}, f32[64]{0:T(128)}, u32[]{:S(2)}) copy-start(f32[64]{0:T(128)} %param.7) | copy-start | bytes 772
  9.5 24.4 %copy-start = (bf16[27,64,256]{2,1,0:T(8,128)(2,1)S(1)}, bf16[27,64,256]{2,1,0:T(8,128)(2,1)}, u32[]{:S(2)}) copy-start(bf16[27,64,256]{2,1,0:T(8,128)(2,1)} %refs_2_.1) | copy-start | bytes 2654212
  9.5 2.0 %collective-permute-start.2 = (f32[2,64,1024]{2,1,0:T(8,128)S(1)}, f32[2,64,1024]{2,1,0:T(8,128)S(1)}, u32[]{:S(2)}, u32[]{:S(2)}) collective-permute-start(f32[2,64,1024]{2,1,0:T(8,128)S(1)} %get-tuple-element.29), channel_id=1, source_target_pairs={{0,1},{1,0},{2,3},{3,2},{4,5},{5,4},{6,7},{7,6},{8,9},{9,8},{10,11... | collective-permute-start | bytes 1572872 | tf_op jit(solution)/shard_map/ppermute | solution.py:265
  11.5 9.8 %collective-permute-start.3 = (bf16[64,1024]{1,0:T(8,128)(2,1)S(1)}, bf16[64,1024]{1,0:T(8,128)(2,1)S(1)}, u32[]{:S(2)}, u32[]{:S(2)}) collective-permute-start(bf16[64,1024]{1,0:T(8,128)(2,1)S(1)} %fusion.6), channel_id=1, source_target_pairs={{0,2},{1,3},{2,0},{3,1},{4,6},{5,7},{6,4},{7,5},{8,10},{9,11},{10,... | collective-permute-start | bytes 393224 | tf_op jit(solution)/shard_map/ppermute | solution.py:265
  13.1 10.9 %collective-permute-start.6 = (bf16[64,1024]{1,0:T(8,128)(2,1)S(1)}, bf16[64,1024]{1,0:T(8,128)(2,1)S(1)}, u32[]{:S(2)}, u32[]{:S(2)}) collective-permute-start(bf16[64,1024]{1,0:T(8,128)(2,1)S(1)} %bitcast.70), channel_id=1, source_target_pairs={{0,8},{4,12},{8,0},{12,4},{16,24},{20,28},{24,16},{28,20},{1,9},{5... | collective-permute-start | bytes 393224 | tf_op jit(solution)/shard_map/ppermute | solution.py:265
  18.7 8.7 %collective-permute-start.5 = (bf16[64,1024]{1,0:T(8,128)(2,1)S(1)}, bf16[64,1024]{1,0:T(8,128)(2,1)S(1)}, u32[]{:S(2)}, u32[]{:S(2)}) collective-permute-start(bf16[64,1024]{1,0:T(8,128)(2,1)S(1)} %bitcast.71), channel_id=1, source_target_pairs={{0,16},{4,20},{8,24},{12,28},{16,0},{20,4},{24,8},{28,12},{1,17},{... | collective-permute-start | bytes 393224 | tf_op jit(solution)/shard_map/ppermute | solution.py:265
  21.6 5.9 %collective-permute-start.4 = (bf16[64,1024]{1,0:T(8,128)(2,1)S(1)}, bf16[64,1024]{1,0:T(8,128)(2,1)S(1)}, u32[]{:S(2)}, u32[]{:S(2)}) collective-permute-start(bf16[64,1024]{1,0:T(8,128)(2,1)S(1)} %get-tuple-element.30), channel_id=1, source_target_pairs={{0,1},{1,0},{2,3},{3,2},{4,5},{5,4},{6,7},{7,6},{8,9},{9,8},{10,11... | collective-permute-start | bytes 393224 | tf_op jit(solution)/shard_map/ppermute | solution.py:265
  21.6 7.0 %collective-permute-start.8 = (bf16[2,16,1024]{2,1,0:T(8,128)(2,1)S(1)}, bf16[2,16,1024]{2,1,0:T(8,128)(2,1)S(1)}, u32[]{:S(2)}, u32[]{:S(2)}) collective-permute-start(bf16[2,16,1024]{2,1,0:T(8,128)(2,1)S(1)} %get-tuple-element.33), channel_id=1, source_target_pairs={{0,4},{4,0},{8,12},{12,8},{16,20},{20,16},{24,28},{28,24},{1,5},{5... | collective-permute-start | bytes 196616 | tf_op jit(solution)/shard_map/ppermute | solution.py:265
  27.5 6.4 %collective-permute-start.7 = (bf16[2,64,1024]{2,1,0:T(8,128)(2,1)S(1)}, bf16[2,64,1024]{2,1,0:T(8,128)(2,1)S(1)}, u32[]{:S(2)}, u32[]{:S(2)}) collective-permute-start(bf16[2,64,1024]{2,1,0:T(8,128)(2,1)S(1)} %pad_maximum_fusion.2.refs_0_), channel_id=1, source_target_pairs={{0,2},{1,3},{2,0},{3,1},{4,6},{5,7},{6,4},{7,5},{8,10},{9,11},{10,... | collective-permute-start | bytes 786440 | tf_op jit(solution)/shard_map/ppermute | solution.py:265
  28.1 8.7 %collective-permute-start.9 = (bf16[2,64,1024]{2,1,0:T(8,128)(2,1)S(1)}, bf16[2,64,1024]{2,1,0:T(8,128)(2,1)S(1)}, u32[]{:S(2)}, u32[]{:S(2)}) collective-permute-start(bf16[2,64,1024]{2,1,0:T(8,128)(2,1)S(1)} %pad_maximum_fusion.1), channel_id=1, source_target_pairs={{0,4},{4,0},{8,12},{12,8},{16,20},{20,16},{24,28},{28,24},{1,5},{5... | collective-permute-start | bytes 786440 | tf_op jit(solution)/shard_map/ppermute | solution.py:265
  28.7 8.1 %collective-permute-start.12 = (bf16[2,16,1024]{2,1,0:T(8,128)(2,1)S(1)}, bf16[2,16,1024]{2,1,0:T(8,128)(2,1)S(1)}, u32[]{:S(2)}, u32[]{:S(2)}) collective-permute-start(bf16[2,16,1024]{2,1,0:T(8,128)(2,1)S(1)} %get-tuple-element.60), channel_id=1, source_target_pairs={{0,24},{4,28},{8,16},{12,20},{16,8},{20,12},{24,0},{28,4},{1,25},{... | collective-permute-start | bytes 196616 | tf_op jit(solution)/shard_map/ppermute | solution.py:265
  31.2 5.6 %collective-permute-start.10 = (bf16[2,16,1024]{2,1,0:T(8,128)(2,1)S(1)}, bf16[2,16,1024]{2,1,0:T(8,128)(2,1)S(1)}, u32[]{:S(2)}, u32[]{:S(2)}) collective-permute-start(bf16[2,16,1024]{2,1,0:T(8,128)(2,1)S(1)} %get-tuple-element.60), channel_id=1, source_target_pairs={{0,8},{4,12},{8,0},{12,4},{16,24},{20,28},{24,16},{28,20},{1,9},{5... | collective-permute-start | bytes 196616 | tf_op jit(solution)/shard_map/ppermute | solution.py:265
  31.2 5.6 %collective-permute-start.11 = (bf16[2,16,1024]{2,1,0:T(8,128)(2,1)S(1)}, bf16[2,16,1024]{2,1,0:T(8,128)(2,1)S(1)}, u32[]{:S(2)}, u32[]{:S(2)}) collective-permute-start(bf16[2,16,1024]{2,1,0:T(8,128)(2,1)S(1)} %get-tuple-element.38), channel_id=1, source_target_pairs={{0,16},{4,20},{8,24},{12,28},{16,0},{20,4},{24,8},{28,12},{1,17},{... | collective-permute-start | bytes 196616 | tf_op jit(solution)/shard_map/ppermute | solution.py:265
  36.8 6.8 %collective-permute-start.13 = (bf16[8,16,1024]{2,1,0:T(8,128)(2,1)S(1)}, bf16[8,16,1024]{2,1,0:T(8,128)(2,1)S(1)}, u32[]{:S(2)}, u32[]{:S(2)}) collective-permute-start(bf16[8,16,1024]{2,1,0:T(8,128)(2,1)S(1)} %constant_dynamic-update-slice_fusion.refs_6_), channel_id=1, source_target_pairs={{0,2},{1,3},{2,0},{3,1},{4,6},{5,7},{6,4},{7,5},{8,10},{9,11},{10,... | collective-permute-start | bytes 786440 | tf_op jit(solution)/shard_map/ppermute | solution.py:265
  38.1 5.5 %collective-permute-start.14 = (bf16[64,1024]{1,0:T(8,128)(2,1)S(1)}, bf16[64,1024]{1,0:T(8,128)(2,1)S(1)}, u32[]{:S(2)}, u32[]{:S(2)}) collective-permute-start(bf16[64,1024]{1,0:T(8,128)(2,1)S(1)} %get-tuple-element.39), channel_id=1, source_target_pairs={{0,4},{4,0},{8,12},{12,8},{16,20},{20,16},{24,28},{28,24},{1,5},{5... | collective-permute-start | bytes 393224 | tf_op jit(solution)/shard_map/ppermute | solution.py:265
  39.7 4.0 %collective-permute-start.15 = (bf16[64,1024]{1,0:T(8,128)(2,1)S(1)}, bf16[64,1024]{1,0:T(8,128)(2,1)S(1)}, u32[]{:S(2)}, u32[]{:S(2)}) collective-permute-start(bf16[64,1024]{1,0:T(8,128)(2,1)S(1)} %get-tuple-element.40), channel_id=1, source_target_pairs={{4,8},{12,16},{20,24},{8,4},{16,12},{24,20},{5,9},{13,17},{21,25},... | collective-permute-start | bytes 393224 | tf_op jit(solution)/shard_map/ppermute | solution.py:270
  40.4 8.9 %collective-permute-start.16 = (bf16[2,64,1024]{2,1,0:T(8,128)(2,1)S(1)}, bf16[2,64,1024]{2,1,0:T(8,128)(2,1)S(1)}, u32[]{:S(2)}, u32[]{:S(2)}) collective-permute-start(bf16[2,64,1024]{2,1,0:T(8,128)(2,1)S(1)} %pad_maximum_fusion), channel_id=1, source_target_pairs={{0,8},{4,12},{8,0},{12,4},{16,24},{20,28},{24,16},{28,20},{1,9},{5... | collective-permute-start | bytes 786440 | tf_op jit(solution)/shard_map/ppermute | solution.py:265
  43.7 5.6 %collective-permute-start.17 = (bf16[8,16,1024]{2,1,0:T(8,128)(2,1)S(1)}, bf16[8,16,1024]{2,1,0:T(8,128)(2,1)S(1)}, u32[]{:S(2)}, u32[]{:S(2)}) collective-permute-start(bf16[8,16,1024]{2,1,0:T(8,128)(2,1)S(1)} %constant_dynamic-update-slice_fusion.refs_6_), channel_id=1, source_target_pairs={{0,1},{1,0},{2,3},{3,2},{4,5},{5,4},{6,7},{7,6},{8,9},{9,8},{10,11... | collective-permute-start | bytes 786440 | tf_op jit(solution)/shard_map/ppermute | solution.py:265
  43.7 5.6 %collective-permute-start.18 = (bf16[8,16,1024]{2,1,0:T(8,128)(2,1)S(1)}, bf16[8,16,1024]{2,1,0:T(8,128)(2,1)S(1)}, u32[]{:S(2)}, u32[]{:S(2)}) collective-permute-start(bf16[8,16,1024]{2,1,0:T(8,128)(2,1)S(1)} %collective-permute-done.13.refs_8_), channel_id=1, source_target_pairs={{0,1},{1,0},{2,3},{3,2},{4,5},{5,4},{6,7},{7,6},{8,9},{9,8},{10,11... | collective-permute-start | bytes 786440 | tf_op jit(solution)/shard_map/ppermute | solution.py:265
  49.3 17.2 %copy-start.2 = (bf16[512,512]{1,0:T(8,128)(2,1)S(1)}, bf16[512,512]{1,0:T(8,128)(2,1)}, u32[]{:S(2)}) copy-start(bf16[512,512]{1,0:T(8,128)(2,1)} %constant.21.clone.refs_4_) | copy-start | bytes 1572868
  53.8 9.5 %collective-permute-start.21 = (bf16[896,128]{1,0:T(8,128)(2,1)S(1)}, bf16[896,128]{1,0:T(8,128)(2,1)S(1)}, u32[]{:S(2)}, u32[]{:S(2)}) collective-permute-start(bf16[896,128]{1,0:T(8,128)(2,1)S(1)} %filter_block.1.refs_0_), channel_id=1, source_target_pairs={{0,12},{4,8},{8,4},{12,0},{16,28},{20,24},{24,20},{28,16},{1,13},{... | collective-permute-start | bytes 688136 | tf_op jit(solution)/shard_map/ppermute | solution.py:265
  56.6 9.9 %collective-permute-start.20 = (bf16[896,128]{1,0:T(8,128)(2,1)S(1)}, bf16[896,128]{1,0:T(8,128)(2,1)S(1)}, u32[]{:S(2)}, u32[]{:S(2)}) collective-permute-start(bf16[896,128]{1,0:T(8,128)(2,1)S(1)} %filter_block.1.refs_0_), channel_id=1, source_target_pairs={{0,8},{4,12},{8,0},{12,4},{16,24},{20,28},{24,16},{28,20},{1,9},{5... | collective-permute-start | bytes 688136 | tf_op jit(solution)/shard_map/ppermute | solution.py:265
  57.4 9.2 %collective-permute-start.19 = (bf16[896,128]{1,0:T(8,128)(2,1)S(1)}, bf16[896,128]{1,0:T(8,128)(2,1)S(1)}, u32[]{:S(2)}, u32[]{:S(2)}) collective-permute-start(bf16[896,128]{1,0:T(8,128)(2,1)S(1)} %filter_block.1.refs_0_), channel_id=1, source_target_pairs={{0,4},{4,0},{8,12},{12,8},{16,20},{20,16},{24,28},{28,24},{1,5},{5... | collective-permute-start | bytes 688136 | tf_op jit(solution)/shard_map/ppermute | solution.py:265

commit v12 on v11

--- a/solution.py
+++ b/solution.py
@@ -43,14 +43,43 @@
             step(q)
 
 
-def forward_kernel(chans, index, own, partner, outer, weights, keep, give, stack, total):
-    for k, plane in enumerate((own, partner, outer)):
+def stacked(stack, planes):
+    for k, plane in enumerate(planes):
         cells = plane[...]
+        chans = cells.shape[0]
         for b in range(3):
             for e in range(3):
                 start = (9 * k + 3 * b + e) * chans
                 stack[start : start + chans, :] = moved(cells, b - 1, e - 1)
-    total[...] = jnp.dot(weights[...], stack[...], preferred_element_type=F32)
+    return stack[...]
+
+
+def near_kernel(own, partner, weights, total, stack):
+    total[...] = jnp.dot(
+        weights[...], stacked(stack, (own, partner)), preferred_element_type=F32
+    )
+
+
+def near_part(own, partner, weights):
+    outs, depth = weights.shape
+    return pl.pallas_call(
+        near_kernel,
+        out_shape=jax.ShapeDtypeStruct((outs, CELLS), F32),
+        in_specs=[VMEM] * 3,
+        out_specs=VMEM,
+        scratch_shapes=[pltpu.VMEM((depth, CELLS), BF16)],
+        compiler_params=pltpu.CompilerParams(vmem_limit_bytes=16 << 20),
+        cost_estimate=pl.CostEstimate(
+            flops=2 * outs * depth * CELLS, bytes_accessed=4 << 20, transcendentals=0
+        ),
+        name="near_part",
+    )(own, partner, weights)
+
+
+def forward_kernel(chans, index, most, outer, weights, keep, give, stack, total):
+    total[...] = most[...] + jnp.dot(
+        weights[...], stacked(stack, (outer,)), preferred_element_type=F32
+    )
     for j in range(keep.shape[0]):
         start = pl.multiple_of((index[0] ^ (2 * j)) * chans, chans)
         keep[j] = total[pl.ds(start, chans), :]
@@ -58,25 +87,22 @@
         give[j] = total[pl.ds(start, chans), :]
 
 
-def forward_parts(index, own, partner, outer, weights):
-    chans = own.shape[0]
-    outs = weights.shape[0]
+def forward_parts(index, most, outer, weights):
+    chans = outer.shape[0]
+    outs, depth = weights.shape
     side = jax.ShapeDtypeStruct((outs // chans // 2, chans, CELLS), F32)
     return pl.pallas_call(
         functools.partial(forward_kernel, chans),
         out_shape=[side, side],
-        in_specs=[SMEM] + [VMEM] * 4,
+        in_specs=[SMEM] + [VMEM] * 3,
         out_specs=[VMEM] * 2,
-        scratch_shapes=[
-            pltpu.VMEM((TAPS * chans, CELLS), BF16),
-            pltpu.VMEM((outs, CELLS), F32),
-        ],
-        compiler_params=pltpu.CompilerParams(vmem_limit_bytes=20 << 20),
-        cost_estimate=pl.CostEstimate(
-            flops=2 * outs * TAPS * chans * CELLS, bytes_accessed=6 << 20, transcendentals=0
+        scratch_shapes=[pltpu.VMEM((depth, CELLS), BF16), pltpu.VMEM((outs, CELLS), F32)],
+        compiler_params=pltpu.CompilerParams(vmem_limit_bytes=16 << 20),
+        cost_estimate=pl.CostEstimate(
+            flops=2 * outs * depth * CELLS, bytes_accessed=4 << 20, transcendentals=0
         ),
         name="forward_parts",
-    )(index, own, partner, outer, weights)
+    )(index, most, outer, weights)
 
 
 def input_kernel(chans, chips, index, *refs):
@@ -293,15 +319,15 @@
     barrier = lax.optimization_barrier
 
     own = features.reshape(chans, cells)
-    partner, outer = swapped(own, "space", 1), exchanged(own)
-    outer, partner = barrier((outer, partner))
+    partner = swapped(own, "space", 1)
     side = space & 1
     where = jnp.stack([chan, side])
+    again, where = lax.optimization_barrier((own, where))
+    outer = exchanged(again)
     slabs = filters.reshape(3, 9 * chans, total_out)
-    weights = jnp.concatenate(
-        [slabs[1], slabs[2 * (1 - side)], slabs[2 * side]], axis=0
-    ).T
-    keep, give = forward_parts(where, own, partner, outer, weights)
+    inner = jnp.concatenate([slabs[1], slabs[2 * (1 - side)]], axis=0).T
+    most = near_part(own, partner, inner)
+    keep, give = forward_parts(where, most, outer, slabs[2 * side].T)
 
     got = swapped(give, "chan", 1)
     near = [swapped(own, "space", flip) for flip in (4, 2)]

time: 69 us -> 68.5 us (level)
  local copies, waits for them, and re-layouts: 5.16 us -> 3.65 us
  waiting for transfers between devices: 20.4 us -> 21.4 us
    dynamic_slice x1, local copies, waits for them, and re-layouts: 1.09 us -> 0.05 us  [body(): keep, give = forward_parts(where, most, outer, slabs[2 * side].T)]
    ppermute x20, waiting for transfers between devices: 20.4 us -> 21.4 us  [swapped(): return lax.ppermute(value, axis, [(i, i ^ mask) for i in range(count)])]
    pallas_call x0 -> x1, Pallas kernels: none -> 1 us  [near_part(): pl.pallas_call(near_kernel, out_shape=jax.ShapeDtypeStruct((outs, CELLS),...]
  transfers between devices with their start and end apart: 22 -> 22, of which waited for: 7 -> 8; matrix products, arithmetic and copies ran while one was open for 8% -> 6% of each run, Pallas kernels for 4% -> 6%
where the time goes in v12:
time: 68.5 us; the launch traced here: 68.3 us
  starting transfers between devices  29.8 us (44%)
  waiting for transfers between devices  21.4 us (31%)
  Pallas kernels  11.9 us (17%)
  local copies, waits for them, and re-layouts  3.65 us (5%)
  between operations  0.91 us (1%)
  other arithmetic  0.71 us (1%)
    ppermute x20, starting transfers between devices, swapped(): return lax.ppermute(value, axis, [(i, i ^ mask) for i in range(count)])  28.5 us
    ppermute x20, waiting for transfers between devices, swapped(): return lax.ppermute(value, axis, [(i, i ^ mask) for i in range(count)])  21.4 us
    pallas_call x1, Pallas kernels, filter_block(): pl.pallas_call(functools.partial(filter_kernel, factor, groups, flips), o...  4.51 us
    pallas_call x1, Pallas kernels, input_parts(): pl.pallas_call(functools.partial(input_kernel, chans, chips), out_shape=[...  2.79 us
    unnamed x17, local copies, waits for them, and re-layouts  2.4 us
    pallas_call x1, Pallas kernels, join_blocks(): pl.pallas_call(functools.partial(join_kernel, chans), out_shape=[jax.Shap...  2.25 us
  transfers between devices with their start and end apart: 22, of which 8 were waited for; matrix products, arithmetic and copies ran while one was open for 6% of the time, Pallas kernels for 6%

profile of v12, /device:TPU:0, one launch (start us, length us, event | category | flops | bytes accessed | tf_op | source)
XLA Modules:
  0.0 68.3 jit_solution(2205673169697432292)
XLA Ops:
  0.6 3.0 %collective-permute-start = (bf16[64,1024]{1,0:T(8,128)(2,1)}, bf16[64,1024]{1,0:T(8,128)(2,1)S(1)}, u32[]{:S(2)}, u32[]{:S(2)}) collective-permute-start(bf16[64,1024]{1,0:T(8,128)(2,1)} %bitcast.70), channel_id=1, source_target_pairs={{0,4},{4,0},{8,12},{12,8},{16,20},{20,16},{24,28},{28,24},{1,5},{5... | collective-permute-start | bytes 393224 | tf_op jit(solution)/shard_map/ppermute | solution.py:291
  3.7 0.7 collective-permute-start.1
  4.4 1.0 %slice.35 = bf16[9,64,256]{2,1,0:T(8,128)(2,1)S(1)} slice(bf16[27,64,256]{2,1,0:T(8,128)(2,1)} %refs_2_.1), slice={[9:18], [0:64], [0:256]} | slice | bytes 589824 | tf_op jit(solution)/shard_map/slice | solution.py:328
  6.2 1.1 %collective-permute-done.partner = bf16[64,1024]{1,0:T(8,128)(2,1)S(1)} collective-permute-done((bf16[64,1024]{1,0:T(8,128)(2,1)}, bf16[64,1024]{1,0:T(8,128)(2,1)S(1)}, u32[]{:S(2)}, u32[]{:S(2)}) %collective-permute-start) | collective-permute-done | bytes 131104 | tf_op jit(solution)/shard_map/ppermute | solution.py:291
  7.4 1.0 %near_part.1.most = f32[256,1024]{1,0:T(8,128)S(1)} custom-call(bf16[64,1024]{1,0:T(8,128)(2,1)S(1)} %bitcast.72, bf16[64,1024]{1,0:T(8,128)(2,1)S(1)} %collective-permute-done.partner, bf16[256,1152]{1,0:T(8,128)(2,1)S(1)} %maximum_bitcast_fusion.weights), custom_call_target="tpu_custom_call" | custom-call | flops 603979776 | bytes 4194304 | tf_op jit(solution)/shard_map/near_part/pallas_call | solution.py:65
  8.4 1.3 %forward_parts.1 = (f32[2,64,1024]{2,1,0:T(8,128)S(1)}, f32[2,64,1024]{2,1,0:T(8,128)S(1)}) custom-call(s32[2]{0:T(128)S(1)} %pad_add_fusion.index, f32[256,1024]{1,0:T(8,128)S(1)} %near_part.1.most, bf16[64,1024]{1,0:T(8,128)(2,1)S(1)} %collective-permute-done.1.outer, bf16[256,576]{1,0:T(8,128)(2,1)S(1)} %bitcast.63), custom_call_target="tpu_custom_call" | custom-call | flops 301989888 | bytes 4194304 | tf_op jit(solution)/shard_map/forward_parts/pallas_call | solution.py:94
  9.8 1.9 %collective-permute-done.2 = f32[2,64,1024]{2,1,0:T(8,128)S(1)} collective-permute-done((f32[2,64,1024]{2,1,0:T(8,128)S(1)}, f32[2,64,1024]{2,1,0:T(8,128)S(1)}, u32[]{:S(2)}, u32[]{:S(2)}) %collective-permute-start.2) | collective-permute-done | bytes 524320 | tf_op jit(solution)/shard_map/ppermute | solution.py:291
  11.7 1.8 %collective-permute-start.3 = (bf16[64,1024]{1,0:T(8,128)(2,1)S(1)}, bf16[64,1024]{1,0:T(8,128)(2,1)S(1)}, u32[]{:S(2)}, u32[]{:S(2)}) collective-permute-start(bf16[64,1024]{1,0:T(8,128)(2,1)S(1)} %fusion.6), channel_id=1, source_target_pairs={{0,2},{1,3},{2,0},{3,1},{4,6},{5,7},{6,4},{7,5},{8,10},{9,11},{10,... | collective-permute-start | bytes 393224 | tf_op jit(solution)/shard_map/ppermute | solution.py:291
  13.6 4.6 %collective-permute-start.6 = (bf16[64,1024]{1,0:T(8,128)(2,1)S(1)}, bf16[64,1024]{1,0:T(8,128)(2,1)S(1)}, u32[]{:S(2)}, u32[]{:S(2)}) collective-permute-start(bf16[64,1024]{1,0:T(8,128)(2,1)S(1)} %bitcast.73), channel_id=1, source_target_pairs={{0,8},{4,12},{8,0},{12,4},{16,24},{20,28},{24,16},{28,20},{1,9},{5... | collective-permute-start | bytes 393224 | tf_op jit(solution)/shard_map/ppermute | solution.py:291
  18.2 2.6 %collective-permute-start.5 = (bf16[64,1024]{1,0:T(8,128)(2,1)S(1)}, bf16[64,1024]{1,0:T(8,128)(2,1)S(1)}, u32[]{:S(2)}, u32[]{:S(2)}) collective-permute-start(bf16[64,1024]{1,0:T(8,128)(2,1)S(1)} %bitcast.74), channel_id=1, source_target_pairs={{0,16},{4,20},{8,24},{12,28},{16,0},{20,4},{24,8},{28,12},{1,17},{... | collective-permute-start | bytes 393224 | tf_op jit(solution)/shard_map/ppermute | solution.py:291
  21.4 2.1 %collective-permute-done.6 = bf16[64,1024]{1,0:T(8,128)(2,1)S(1)} collective-permute-done((bf16[64,1024]{1,0:T(8,128)(2,1)S(1)}, bf16[64,1024]{1,0:T(8,128)(2,1)S(1)}, u32[]{:S(2)}, u32[]{:S(2)}) %collective-permute-start.6) | collective-permute-done | bytes 131104 | tf_op jit(solution)/shard_map/ppermute | solution.py:291
  23.6 3.3 %collective-permute-done.5 = bf16[64,1024]{1,0:T(8,128)(2,1)S(1)} collective-permute-done((bf16[64,1024]{1,0:T(8,128)(2,1)S(1)}, bf16[64,1024]{1,0:T(8,128)(2,1)S(1)}, u32[]{:S(2)}, u32[]{:S(2)}) %collective-permute-start.5) | collective-permute-done | bytes 131104 | tf_op jit(solution)/shard_map/ppermute | solution.py:291
  26.9 0.6 collective-permute-start.7
  27.5 0.6 collective-permute-start.9
  28.2 2.5 %collective-permute-start.12 = (bf16[2,16,1024]{2,1,0:T(8,128)(2,1)S(1)}, bf16[2,16,1024]{2,1,0:T(8,128)(2,1)S(1)}, u32[]{:S(2)}, u32[]{:S(2)}) collective-permute-start(bf16[2,16,1024]{2,1,0:T(8,128)(2,1)S(1)} %get-tuple-element.60), channel_id=1, source_target_pairs={{0,24},{4,28},{8,16},{12,20},{16,8},{20,12},{24,0},{28,4},{1,25},{... | collective-permute-start | bytes 196616 | tf_op jit(solution)/shard_map/ppermute | solution.py:291
  30.7 2.0 %collective-permute-start.11 = (bf16[2,16,1024]{2,1,0:T(8,128)(2,1)S(1)}, bf16[2,16,1024]{2,1,0:T(8,128)(2,1)S(1)}, u32[]{:S(2)}, u32[]{:S(2)}) collective-permute-start(bf16[2,16,1024]{2,1,0:T(8,128)(2,1)S(1)} %get-tuple-element.38), channel_id=1, source_target_pairs={{0,16},{4,20},{8,24},{12,28},{16,0},{20,4},{24,8},{28,12},{1,17},{... | collective-permute-start | bytes 196616 | tf_op jit(solution)/shard_map/ppermute | solution.py:291
  32.6 0.7 %collective-permute-done.7.refs_1_ = bf16[2,64,1024]{2,1,0:T(8,128)(2,1)S(1)} collective-permute-done((bf16[2,64,1024]{2,1,0:T(8,128)(2,1)S(1)}, bf16[2,64,1024]{2,1,0:T(8,128)(2,1)S(1)}, u32[]{:S(2)}, u32[]{:S(2)}) %collective-permute-start.7) | collective-permute-done | bytes 262176 | tf_op jit(solution)/shard_map/ppermute | solution.py:291
  33.4 2.8 %input_parts.1 = (f32[64,1024]{1,0:T(8,128)S(1)}, bf16[64,1024]{1,0:T(8,128)(2,1)S(1)}, bf16[64,1024]{1,0:T(8,128)(2,1)S(1)}) custom-call(s32[2]{0:T(128)S(1)} %pad_add_fusion.index, bf16[2,64,1024]{2,1,0:T(8,128)(2,1)S(1)} %pad_maximum_fusion.2.refs_0_, bf16[2,64,1024]{2,1,0:T(8,128)(2,1)S(1)} %collective-permute-done.7.refs_1_, ...), custom_call_target="tpu_custom_call" | custom-call | flops 905969664 | bytes 6291456 | tf_op jit(solution)/shard_map/input_parts/pallas_call | solution.py:134
  36.3 1.3 %collective-permute-start.13 = (bf16[8,16,1024]{2,1,0:T(8,128)(2,1)S(1)}, bf16[8,16,1024]{2,1,0:T(8,128)(2,1)S(1)}, u32[]{:S(2)}, u32[]{:S(2)}) collective-permute-start(bf16[8,16,1024]{2,1,0:T(8,128)(2,1)S(1)} %constant_dynamic-update-slice_fusion.refs_6_), channel_id=1, source_target_pairs={{0,2},{1,3},{2,0},{3,1},{4,6},{5,7},{6,4},{7,5},{8,10},{9,11},{10,... | collective-permute-start | bytes 786440 | tf_op jit(solution)/shard_map/ppermute | solution.py:291
  37.6 1.5 %collective-permute-start.14 = (bf16[64,1024]{1,0:T(8,128)(2,1)S(1)}, bf16[64,1024]{1,0:T(8,128)(2,1)S(1)}, u32[]{:S(2)}, u32[]{:S(2)}) collective-permute-start(bf16[64,1024]{1,0:T(8,128)(2,1)S(1)} %get-tuple-element.39), channel_id=1, source_target_pairs={{0,4},{4,0},{8,12},{12,8},{16,20},{20,16},{24,28},{28,24},{1,5},{5... | collective-permute-start | bytes 393224 | tf_op jit(solution)/shard_map/ppermute | solution.py:291
  39.2 0.7 collective-permute-start.15
  39.9 3.2 %collective-permute-start.16 = (bf16[2,64,1024]{2,1,0:T(8,128)(2,1)S(1)}, bf16[2,64,1024]{2,1,0:T(8,128)(2,1)S(1)}, u32[]{:S(2)}, u32[]{:S(2)}) collective-permute-start(bf16[2,64,1024]{2,1,0:T(8,128)(2,1)S(1)} %pad_maximum_fusion), channel_id=1, source_target_pairs={{0,8},{4,12},{8,0},{12,4},{16,24},{20,28},{24,16},{28,20},{1,9},{5... | collective-permute-start | bytes 786440 | tf_op jit(solution)/shard_map/ppermute | solution.py:291
  43.2 0.5 collective-permute-start.18
  43.8 1.0 %copy.21 = f32[64,1,1024]{2,1,0:T(1,128)} copy(f32[64,1,1024]{2,0,1:T(8,128)S(1)} %get-tuple-element.57) | data formatting | bytes 524288
  44.8 4.0 %collective-permute-done.16.refs_5_ = bf16[2,64,1024]{2,1,0:T(8,128)(2,1)S(1)} collective-permute-done((bf16[2,64,1024]{2,1,0:T(8,128)(2,1)S(1)}, bf16[2,64,1024]{2,1,0:T(8,128)(2,1)S(1)}, u32[]{:S(2)}, u32[]{:S(2)}) %collective-permute-start.16) | collective-permute-done | bytes 262176 | tf_op jit(solution)/shard_map/ppermute | solution.py:291
  48.8 4.5 %filter_block.1.refs_0_ = bf16[896,128]{1,0:T(8,128)(2,1)S(1)} custom-call(s32[2]{0:T(128)S(1)} %pad_add_fusion.1.index, bf16[1,64,1024]{2,1,0:T(8,128)(2,1)S(1)} %bitcast.75, bf16[1,64,1024]{2,1,0:T(8,128)(2,1)S(1)} %bitcast.76, bf16[1,64,1024]{2,1,0:T(8,128)(2,1)S(1)} %bitcast.67, bf16[1,64,1024]{2,1,0:T(8,128)(2,1)S(1)} %bitcast.69, ...), custom_call_target="tpu_custom_call" | custom-call | flops 1811939328 | bytes 8388608 | tf_op jit(solution)/shard_map/filter_block/pallas_call | solution.py:212
  53.3 2.8 %collective-permute-start.21 = (bf16[896,128]{1,0:T(8,128)(2,1)S(1)}, bf16[896,128]{1,0:T(8,128)(2,1)S(1)}, u32[]{:S(2)}, u32[]{:S(2)}) collective-permute-start(bf16[896,128]{1,0:T(8,128)(2,1)S(1)} %filter_block.1.refs_0_), channel_id=1, source_target_pairs={{0,12},{4,8},{8,4},{12,0},{16,28},{20,24},{24,20},{28,16},{1,13},{... | collective-permute-start | bytes 688136 | tf_op jit(solution)/shard_map/ppermute | solution.py:291
  56.1 0.8 %collective-permute-start.20 = (bf16[896,128]{1,0:T(8,128)(2,1)S(1)}, bf16[896,128]{1,0:T(8,128)(2,1)S(1)}, u32[]{:S(2)}, u32[]{:S(2)}) collective-permute-start(bf16[896,128]{1,0:T(8,128)(2,1)S(1)} %filter_block.1.refs_0_), channel_id=1, source_target_pairs={{0,8},{4,12},{8,0},{12,4},{16,24},{20,28},{24,16},{28,20},{1,9},{5... | collective-permute-start | bytes 688136 | tf_op jit(solution)/shard_map/ppermute | solution.py:291
  56.9 1.0 %copy.22 = f32[64,1,1024]{2,1,0:T(1,128)} copy(f32[64,1,1024]{2,0,1:T(8,128)S(1)} %add_bitcast_fusion) | data formatting | bytes 524288
  57.9 4.9 %collective-permute-done.21.refs_3_ = bf16[896,128]{1,0:T(8,128)(2,1)S(1)} collective-permute-done((bf16[896,128]{1,0:T(8,128)(2,1)S(1)}, bf16[896,128]{1,0:T(8,128)(2,1)S(1)}, u32[]{:S(2)}, u32[]{:S(2)}) %collective-permute-start.21) | collective-permute-done | bytes 229408 | tf_op jit(solution)/shard_map/ppermute | solution.py:291
  62.8 3.3 %collective-permute-done.20.refs_2_ = bf16[896,128]{1,0:T(8,128)(2,1)S(1)} collective-permute-done((bf16[896,128]{1,0:T(8,128)(2,1)S(1)}, bf16[896,128]{1,0:T(8,128)(2,1)S(1)}, u32[]{:S(2)}, u32[]{:S(2)}) %collective-permute-start.20) | collective-permute-done | bytes 229408 | tf_op jit(solution)/shard_map/ppermute | solution.py:291
  66.0 2.3 %join_blocks.1 = (f32[27,64,256]{2,1,0:T(8,128)}, f32[1,256]{1,0:T(1,128)}) custom-call(s32[1]{0:T(128)} %bitcast.25.index, bf16[896,128]{1,0:T(8,128)(2,1)S(1)} %filter_block.1.refs_0_, bf16[896,128]{1,0:T(8,128)(2,1)S(1)} %collective-permute-done.19.refs_1_, bf16[896,128]{1,0:T(8,128)(2,1)S(1)} %collective-permute-done.20.refs_2_, ...), custom_call_target="tpu_custom_call" | custom-call | flops 452984832 | bytes 4194304 | tf_op jit(solution)/shard_map/join_blocks/pallas_call | solution.py:268
  (50 shorter events, 2.0 us)
Async XLA Ops:
  0.6 5.0 %copy-start = (bf16[27,64,256]{2,1,0:T(8,128)(2,1)S(1)}, bf16[27,64,256]{2,1,0:T(8,128)(2,1)}, u32[]{:S(2)}) copy-start(bf16[27,64,256]{2,1,0:T(8,128)(2,1)} %refs_2_.1) | copy-start | bytes 2654212
  0.6 6.7 %collective-permute-start = (bf16[64,1024]{1,0:T(8,128)(2,1)}, bf16[64,1024]{1,0:T(8,128)(2,1)S(1)}, u32[]{:S(2)}, u32[]{:S(2)}) collective-permute-start(bf16[64,1024]{1,0:T(8,128)(2,1)} %bitcast.70), channel_id=1, source_target_pairs={{0,4},{4,0},{8,12},{12,8},{16,20},{20,16},{24,28},{28,24},{1,5},{5... | collective-permute-start | bytes 393224 | tf_op jit(solution)/shard_map/ppermute | solution.py:291
  3.7 4.7 %collective-permute-start.1 = (bf16[64,1024]{1,0:T(8,128)(2,1)}, bf16[64,1024]{1,0:T(8,128)(2,1)S(1)}, u32[]{:S(2)}, u32[]{:S(2)}) collective-permute-start(bf16[64,1024]{1,0:T(8,128)(2,1)} %bitcast.71), channel_id=1, source_target_pairs={{4,8},{12,16},{20,24},{8,4},{16,12},{24,20},{5,9},{13,17},{21,25},... | collective-permute-start | bytes 393224 | tf_op jit(solution)/shard_map/ppermute | solution.py:296
  5.7 1.7 %copy-start.1 = (bf16[64,1,1024]{2,0,1:T(8,128)(2,1)S(1)}, bf16[64,1,1024]{2,0,1:T(8,128)(2,1)}, u32[]{:S(2)}) copy-start(bf16[64,1,1024]{2,0,1:T(8,128)(2,1)} %param.5) | copy-start | bytes 393220
  8.4 12.4 %copy-start.3 = (bf16[64,1,1024]{2,0,1:T(8,128)(2,1)S(1)}, bf16[64,1,1024]{2,0,1:T(8,128)(2,1)}, u32[]{:S(2)}) copy-start(bf16[64,1,1024]{2,0,1:T(8,128)(2,1)} %param.8) | copy-start | bytes 393220
  8.4 12.4 %copy-start.4 = (f32[64]{0:T(128)S(1)}, f32[64]{0:T(128)}, u32[]{:S(2)}) copy-start(f32[64]{0:T(128)} %param.7) | copy-start | bytes 772
  9.7 2.0 %collective-permute-start.2 = (f32[2,64,1024]{2,1,0:T(8,128)S(1)}, f32[2,64,1024]{2,1,0:T(8,128)S(1)}, u32[]{:S(2)}, u32[]{:S(2)}) collective-permute-start(f32[2,64,1024]{2,1,0:T(8,128)S(1)} %get-tuple-element.29), channel_id=1, source_target_pairs={{0,1},{1,0},{2,3},{3,2},{4,5},{5,4},{6,7},{7,6},{8,9},{9,8},{10,11... | collective-permute-start | bytes 1572872 | tf_op jit(solution)/shard_map/ppermute | solution.py:291
  11.7 9.0 %collective-permute-start.3 = (bf16[64,1024]{1,0:T(8,128)(2,1)S(1)}, bf16[64,1024]{1,0:T(8,128)(2,1)S(1)}, u32[]{:S(2)}, u32[]{:S(2)}) collective-permute-start(bf16[64,1024]{1,0:T(8,128)(2,1)S(1)} %fusion.6), channel_id=1, source_target_pairs={{0,2},{1,3},{2,0},{3,1},{4,6},{5,7},{6,4},{7,5},{8,10},{9,11},{10,... | collective-permute-start | bytes 393224 | tf_op jit(solution)/shard_map/ppermute | solution.py:291
  13.6 10.0 %collective-permute-start.6 = (bf16[64,1024]{1,0:T(8,128)(2,1)S(1)}, bf16[64,1024]{1,0:T(8,128)(2,1)S(1)}, u32[]{:S(2)}, u32[]{:S(2)}) collective-permute-start(bf16[64,1024]{1,0:T(8,128)(2,1)S(1)} %bitcast.73), channel_id=1, source_target_pairs={{0,8},{4,12},{8,0},{12,4},{16,24},{20,28},{24,16},{28,20},{1,9},{5... | collective-permute-start | bytes 393224 | tf_op jit(solution)/shard_map/ppermute | solution.py:291
  18.2 8.7 %collective-permute-start.5 = (bf16[64,1024]{1,0:T(8,128)(2,1)S(1)}, bf16[64,1024]{1,0:T(8,128)(2,1)S(1)}, u32[]{:S(2)}, u32[]{:S(2)}) collective-permute-start(bf16[64,1024]{1,0:T(8,128)(2,1)S(1)} %bitcast.74), channel_id=1, source_target_pairs={{0,16},{4,20},{8,24},{12,28},{16,0},{20,4},{24,8},{28,12},{1,17},{... | collective-permute-start | bytes 393224 | tf_op jit(solution)/shard_map/ppermute | solution.py:291
  21.0 5.9 %collective-permute-start.4 = (bf16[64,1024]{1,0:T(8,128)(2,1)S(1)}, bf16[64,1024]{1,0:T(8,128)(2,1)S(1)}, u32[]{:S(2)}, u32[]{:S(2)}) collective-permute-start(bf16[64,1024]{1,0:T(8,128)(2,1)S(1)} %get-tuple-element.30), channel_id=1, source_target_pairs={{0,1},{1,0},{2,3},{3,2},{4,5},{5,4},{6,7},{7,6},{8,9},{9,8},{10,11... | collective-permute-start | bytes 393224 | tf_op jit(solution)/shard_map/ppermute | solution.py:291
  21.1 7.1 %collective-permute-start.8 = (bf16[2,16,1024]{2,1,0:T(8,128)(2,1)S(1)}, bf16[2,16,1024]{2,1,0:T(8,128)(2,1)S(1)}, u32[]{:S(2)}, u32[]{:S(2)}) collective-permute-start(bf16[2,16,1024]{2,1,0:T(8,128)(2,1)S(1)} %get-tuple-element.33), channel_id=1, source_target_pairs={{0,4},{4,0},{8,12},{12,8},{16,20},{20,16},{24,28},{28,24},{1,5},{5... | collective-permute-start | bytes 196616 | tf_op jit(solution)/shard_map/ppermute | solution.py:291
  26.9 6.4 %collective-permute-start.7 = (bf16[2,64,1024]{2,1,0:T(8,128)(2,1)S(1)}, bf16[2,64,1024]{2,1,0:T(8,128)(2,1)S(1)}, u32[]{:S(2)}, u32[]{:S(2)}) collective-permute-start(bf16[2,64,1024]{2,1,0:T(8,128)(2,1)S(1)} %pad_maximum_fusion.2.refs_0_), channel_id=1, source_target_pairs={{0,2},{1,3},{2,0},{3,1},{4,6},{5,7},{6,4},{7,5},{8,10},{9,11},{10,... | collective-permute-start | bytes 786440 | tf_op jit(solution)/shard_map/ppermute | solution.py:291
  27.5 8.6 %collective-permute-start.9 = (bf16[2,64,1024]{2,1,0:T(8,128)(2,1)S(1)}, bf16[2,64,1024]{2,1,0:T(8,128)(2,1)S(1)}, u32[]{:S(2)}, u32[]{:S(2)}) collective-permute-start(bf16[2,64,1024]{2,1,0:T(8,128)(2,1)S(1)} %pad_maximum_fusion.1), channel_id=1, source_target_pairs={{0,4},{4,0},{8,12},{12,8},{16,20},{20,16},{24,28},{28,24},{1,5},{5... | collective-permute-start | bytes 786440 | tf_op jit(solution)/shard_map/ppermute | solution.py:291
  28.2 8.1 %collective-permute-start.12 = (bf16[2,16,1024]{2,1,0:T(8,128)(2,1)S(1)}, bf16[2,16,1024]{2,1,0:T(8,128)(2,1)S(1)}, u32[]{:S(2)}, u32[]{:S(2)}) collective-permute-start(bf16[2,16,1024]{2,1,0:T(8,128)(2,1)S(1)} %get-tuple-element.60), channel_id=1, source_target_pairs={{0,24},{4,28},{8,16},{12,20},{16,8},{20,12},{24,0},{28,4},{1,25},{... | collective-permute-start | bytes 196616 | tf_op jit(solution)/shard_map/ppermute | solution.py:291
  30.7 5.5 %collective-permute-start.10 = (bf16[2,16,1024]{2,1,0:T(8,128)(2,1)S(1)}, bf16[2,16,1024]{2,1,0:T(8,128)(2,1)S(1)}, u32[]{:S(2)}, u32[]{:S(2)}) collective-permute-start(bf16[2,16,1024]{2,1,0:T(8,128)(2,1)S(1)} %get-tuple-element.60), channel_id=1, source_target_pairs={{0,8},{4,12},{8,0},{12,4},{16,24},{20,28},{24,16},{28,20},{1,9},{5... | collective-permute-start | bytes 196616 | tf_op jit(solution)/shard_map/ppermute | solution.py:291
  30.7 5.6 %collective-permute-start.11 = (bf16[2,16,1024]{2,1,0:T(8,128)(2,1)S(1)}, bf16[2,16,1024]{2,1,0:T(8,128)(2,1)S(1)}, u32[]{:S(2)}, u32[]{:S(2)}) collective-permute-start(bf16[2,16,1024]{2,1,0:T(8,128)(2,1)S(1)} %get-tuple-element.38), channel_id=1, source_target_pairs={{0,16},{4,20},{8,24},{12,28},{16,0},{20,4},{24,8},{28,12},{1,17},{... | collective-permute-start | bytes 196616 | tf_op jit(solution)/shard_map/ppermute | solution.py:291
  36.3 6.9 %collective-permute-start.13 = (bf16[8,16,1024]{2,1,0:T(8,128)(2,1)S(1)}, bf16[8,16,1024]{2,1,0:T(8,128)(2,1)S(1)}, u32[]{:S(2)}, u32[]{:S(2)}) collective-permute-start(bf16[8,16,1024]{2,1,0:T(8,128)(2,1)S(1)} %constant_dynamic-update-slice_fusion.refs_6_), channel_id=1, source_target_pairs={{0,2},{1,3},{2,0},{3,1},{4,6},{5,7},{6,4},{7,5},{8,10},{9,11},{10,... | collective-permute-start | bytes 786440 | tf_op jit(solution)/shard_map/ppermute | solution.py:291
  37.6 5.5 %collective-permute-start.14 = (bf16[64,1024]{1,0:T(8,128)(2,1)S(1)}, bf16[64,1024]{1,0:T(8,128)(2,1)S(1)}, u32[]{:S(2)}, u32[]{:S(2)}) collective-permute-start(bf16[64,1024]{1,0:T(8,128)(2,1)S(1)} %get-tuple-element.39), channel_id=1, source_target_pairs={{0,4},{4,0},{8,12},{12,8},{16,20},{20,16},{24,28},{28,24},{1,5},{5... | collective-permute-start | bytes 393224 | tf_op jit(solution)/shard_map/ppermute | solution.py:291
  39.2 4.0 %collective-permute-start.15 = (bf16[64,1024]{1,0:T(8,128)(2,1)S(1)}, bf16[64,1024]{1,0:T(8,128)(2,1)S(1)}, u32[]{:S(2)}, u32[]{:S(2)}) collective-permute-start(bf16[64,1024]{1,0:T(8,128)(2,1)S(1)} %get-tuple-element.40), channel_id=1, source_target_pairs={{4,8},{12,16},{20,24},{8,4},{16,12},{24,20},{5,9},{13,17},{21,25},... | collective-permute-start | bytes 393224 | tf_op jit(solution)/shard_map/ppermute | solution.py:296
  39.9 8.9 %collective-permute-start.16 = (bf16[2,64,1024]{2,1,0:T(8,128)(2,1)S(1)}, bf16[2,64,1024]{2,1,0:T(8,128)(2,1)S(1)}, u32[]{:S(2)}, u32[]{:S(2)}) collective-permute-start(bf16[2,64,1024]{2,1,0:T(8,128)(2,1)S(1)} %pad_maximum_fusion), channel_id=1, source_target_pairs={{0,8},{4,12},{8,0},{12,4},{16,24},{20,28},{24,16},{28,20},{1,9},{5... | collective-permute-start | bytes 786440 | tf_op jit(solution)/shard_map/ppermute | solution.py:291
  43.1 5.6 %collective-permute-start.17 = (bf16[8,16,1024]{2,1,0:T(8,128)(2,1)S(1)}, bf16[8,16,1024]{2,1,0:T(8,128)(2,1)S(1)}, u32[]{:S(2)}, u32[]{:S(2)}) collective-permute-start(bf16[8,16,1024]{2,1,0:T(8,128)(2,1)S(1)} %constant_dynamic-update-slice_fusion.refs_6_), channel_id=1, source_target_pairs={{0,1},{1,0},{2,3},{3,2},{4,5},{5,4},{6,7},{7,6},{8,9},{9,8},{10,11... | collective-permute-start | bytes 786440 | tf_op jit(solution)/shard_map/ppermute | solution.py:291
  43.2 5.5 %collective-permute-start.18 = (bf16[8,16,1024]{2,1,0:T(8,128)(2,1)S(1)}, bf16[8,16,1024]{2,1,0:T(8,128)(2,1)S(1)}, u32[]{:S(2)}, u32[]{:S(2)}) collective-permute-start(bf16[8,16,1024]{2,1,0:T(8,128)(2,1)S(1)} %collective-permute-done.13.refs_8_), channel_id=1, source_target_pairs={{0,1},{1,0},{2,3},{3,2},{4,5},{5,4},{6,7},{7,6},{8,9},{9,8},{10,11... | collective-permute-start | bytes 786440 | tf_op jit(solution)/shard_map/ppermute | solution.py:291
  53.3 12.8 %copy-start.2 = (bf16[512,512]{1,0:T(8,128)(2,1)S(1)}, bf16[512,512]{1,0:T(8,128)(2,1)}, u32[]{:S(2)}) copy-start(bf16[512,512]{1,0:T(8,128)(2,1)} %constant.21.clone.refs_4_) | copy-start | bytes 1572868
  53.3 9.5 %collective-permute-start.21 = (bf16[896,128]{1,0:T(8,128)(2,1)S(1)}, bf16[896,128]{1,0:T(8,128)(2,1)S(1)}, u32[]{:S(2)}, u32[]{:S(2)}) collective-permute-start(bf16[896,128]{1,0:T(8,128)(2,1)S(1)} %filter_block.1.refs_0_), channel_id=1, source_target_pairs={{0,12},{4,8},{8,4},{12,0},{16,28},{20,24},{24,20},{28,16},{1,13},{... | collective-permute-start | bytes 688136 | tf_op jit(solution)/shard_map/ppermute | solution.py:291
  56.1 9.9 %collective-permute-start.20 = (bf16[896,128]{1,0:T(8,128)(2,1)S(1)}, bf16[896,128]{1,0:T(8,128)(2,1)S(1)}, u32[]{:S(2)}, u32[]{:S(2)}) collective-permute-start(bf16[896,128]{1,0:T(8,128)(2,1)S(1)} %filter_block.1.refs_0_), channel_id=1, source_target_pairs={{0,8},{4,12},{8,0},{12,4},{16,24},{20,28},{24,16},{28,20},{1,9},{5... | collective-permute-start | bytes 688136 | tf_op jit(solution)/shard_map/ppermute | solution.py:291
  56.9 9.2 %collective-permute-start.19 = (bf16[896,128]{1,0:T(8,128)(2,1)S(1)}, bf16[896,128]{1,0:T(8,128)(2,1)S(1)}, u32[]{:S(2)}, u32[]{:S(2)}) collective-permute-start(bf16[896,128]{1,0:T(8,128)(2,1)S(1)} %filter_block.1.refs_0_), channel_id=1, source_target_pairs={{0,4},{4,0},{8,12},{12,8},{16,20},{20,16},{24,28},{28,24},{1,5},{5... | collective-permute-start | bytes 688136 | tf_op jit(solution)/shard_map/ppermute | solution.py:291

commit v13 on v12

--- a/solution.py
+++ b/solution.py
@@ -364,18 +364,18 @@
     pieces[0], to_partner, to_outer, ahead = barrier((pieces[0], to_partner, to_outer, ahead))
     last = swapped(jnp.stack([near[0], ahead[0]], axis=0), "space", 2)
     blocks = other_chips(jnp.concatenate(pieces, axis=0))
-    from_partner, from_outer = swapped(to_partner, "space", 1), exchanged(to_outer)
-    blocks, from_partner, from_outer = barrier((blocks, from_partner, from_outer))
+    from_partner = swapped(to_partner, "space", 1)
+    blocks, from_partner = barrier((blocks, from_partner))
     blocks = both_cores(blocks)
-    in_grad = in_grad + from_partner.astype(F32) + from_outer.astype(F32)
-
     held = [v[None] for v in (own, partner, *near)] + [ahead, last]
     flips = [(0,), (1,), (4,), (2,), (5, 3), (6, 7)]
     for mask in [1 << k for k in range(3, depth.bit_length() - 1)]:
         held.append(swapped(jnp.concatenate(held, axis=0), "space", mask))
         flips.append(tuple(f ^ mask for some in flips for f in some))
     part = filter_block(jnp.stack([space, chan]), held, flips, blocks, factor)
+    part, to_outer = barrier((part, to_outer))
     parts = [part] + [swapped(part, "space", r) for r in range(1, 4)]
+    in_grad = in_grad + from_partner.astype(F32) + exchanged(to_outer).astype(F32)
     joined, bias = join_blocks((space & 3).reshape(1), parts, share, chans)
     return (
         activated.reshape(chans, planes, cells),

time: 68.5 us -> 69.9 us (1.020)
  starting transfers between devices: 29.8 us -> 30.9 us
    ppermute x20, starting transfers between devices: 28.5 us -> 29.4 us  [swapped(): return lax.ppermute(value, axis, [(i, i ^ mask) for i in range(count)])]
  transfers between devices with their start and end apart: 22 -> 22, of which waited for: 8 -> 10; matrix products, arithmetic and copies ran while one was open for 6% -> 6% of each run, Pallas kernels for 6% -> 5%
where the time goes in v13:
time: 69.9 us; the launch traced here: 69.7 us
  starting transfers between devices  30.9 us (44%)
  waiting for transfers between devices  21.7 us (31%)
  Pallas kernels  11.9 us (17%)
  local copies, waits for them, and re-layouts  3.65 us (5%)
  between operations  0.9 us (1%)
  other arithmetic  0.71 us (1%)
    ppermute x20, starting transfers between devices, swapped(): return lax.ppermute(value, axis, [(i, i ^ mask) for i in range(count)])  29.4 us
    ppermute x20, waiting for transfers between devices, swapped(): return lax.ppermute(value, axis, [(i, i ^ mask) for i in range(count)])  21.7 us
    pallas_call x1, Pallas kernels, filter_block(): pl.pallas_call(functools.partial(filter_kernel, factor, groups, flips), o...  4.51 us
    pallas_call x1, Pallas kernels, input_parts(): pl.pallas_call(functools.partial(input_kernel, chans, chips), out_shape=[...  2.79 us
    unnamed x17, local copies, waits for them, and re-layouts  2.4 us
    pallas_call x1, Pallas kernels, join_blocks(): pl.pallas_call(functools.partial(join_kernel, chans), out_shape=[jax.Shap...  2.25 us
    ppermute x2, starting transfers between devices, exchanged(): return lax.ppermute(value, 'space', pairs + [(j, i) for i, j in pairs])  1.45 us
  transfers between devices with their start and end apart: 22, of which 10 were waited for; matrix products, arithmetic and copies ran while one was open for 6% of the time, Pallas kernels for 5%

profile of v13, /device:TPU:0, one launch (start us, length us, event | category | flops | bytes accessed | tf_op | source)
XLA Modules:
  0.0 69.7 jit_solution(17034741528945252950)
XLA Ops:
  0.6 3.0 %collective-permute-start = (bf16[64,1024]{1,0:T(8,128)(2,1)}, bf16[64,1024]{1,0:T(8,128)(2,1)S(1)}, u32[]{:S(2)}, u32[]{:S(2)}) collective-permute-start(bf16[64,1024]{1,0:T(8,128)(2,1)} %bitcast.70), channel_id=1, source_target_pairs={{0,4},{4,0},{8,12},{12,8},{16,20},{20,16},{24,28},{28,24},{1,5},{5... | collective-permute-start | bytes 393224 | tf_op jit(solution)/shard_map/ppermute | solution.py:291
  3.7 0.7 collective-permute-start.1
  4.4 1.0 %slice.35 = bf16[9,64,256]{2,1,0:T(8,128)(2,1)S(1)} slice(bf16[27,64,256]{2,1,0:T(8,128)(2,1)} %refs_2_.1), slice={[9:18], [0:64], [0:256]} | slice | bytes 589824 | tf_op jit(solution)/shard_map/slice | solution.py:328
  6.2 1.1 %collective-permute-done.partner = bf16[64,1024]{1,0:T(8,128)(2,1)S(1)} collective-permute-done((bf16[64,1024]{1,0:T(8,128)(2,1)}, bf16[64,1024]{1,0:T(8,128)(2,1)S(1)}, u32[]{:S(2)}, u32[]{:S(2)}) %collective-permute-start) | collective-permute-done | bytes 131104 | tf_op jit(solution)/shard_map/ppermute | solution.py:291
  7.4 1.0 %near_part.1.most = f32[256,1024]{1,0:T(8,128)S(1)} custom-call(bf16[64,1024]{1,0:T(8,128)(2,1)S(1)} %bitcast.72, bf16[64,1024]{1,0:T(8,128)(2,1)S(1)} %collective-permute-done.partner, bf16[256,1152]{1,0:T(8,128)(2,1)S(1)} %maximum_bitcast_fusion.weights), custom_call_target="tpu_custom_call" | custom-call | flops 603979776 | bytes 4194304 | tf_op jit(solution)/shard_map/near_part/pallas_call | solution.py:65
  8.4 1.3 %forward_parts.1 = (f32[2,64,1024]{2,1,0:T(8,128)S(1)}, f32[2,64,1024]{2,1,0:T(8,128)S(1)}) custom-call(s32[2]{0:T(128)S(1)} %pad_add_fusion.index, f32[256,1024]{1,0:T(8,128)S(1)} %near_part.1.most, bf16[64,1024]{1,0:T(8,128)(2,1)S(1)} %collective-permute-done.1.outer, bf16[256,576]{1,0:T(8,128)(2,1)S(1)} %bitcast.63), custom_call_target="tpu_custom_call" | custom-call | flops 301989888 | bytes 4194304 | tf_op jit(solution)/shard_map/forward_parts/pallas_call | solution.py:94
  9.8 1.9 %collective-permute-done.2 = f32[2,64,1024]{2,1,0:T(8,128)S(1)} collective-permute-done((f32[2,64,1024]{2,1,0:T(8,128)S(1)}, f32[2,64,1024]{2,1,0:T(8,128)S(1)}, u32[]{:S(2)}, u32[]{:S(2)}) %collective-permute-start.2) | collective-permute-done | bytes 524320 | tf_op jit(solution)/shard_map/ppermute | solution.py:291
  11.7 1.8 %collective-permute-start.3 = (bf16[64,1024]{1,0:T(8,128)(2,1)S(1)}, bf16[64,1024]{1,0:T(8,128)(2,1)S(1)}, u32[]{:S(2)}, u32[]{:S(2)}) collective-permute-start(bf16[64,1024]{1,0:T(8,128)(2,1)S(1)} %fusion.6), channel_id=1, source_target_pairs={{0,2},{1,3},{2,0},{3,1},{4,6},{5,7},{6,4},{7,5},{8,10},{9,11},{10,... | collective-permute-start | bytes 393224 | tf_op jit(solution)/shard_map/ppermute | solution.py:291
  13.6 4.6 %collective-permute-start.6 = (bf16[64,1024]{1,0:T(8,128)(2,1)S(1)}, bf16[64,1024]{1,0:T(8,128)(2,1)S(1)}, u32[]{:S(2)}, u32[]{:S(2)}) collective-permute-start(bf16[64,1024]{1,0:T(8,128)(2,1)S(1)} %bitcast.73), channel_id=1, source_target_pairs={{0,8},{4,12},{8,0},{12,4},{16,24},{20,28},{24,16},{28,20},{1,9},{5... | collective-permute-start | bytes 393224 | tf_op jit(solution)/shard_map/ppermute | solution.py:291
  18.2 2.6 %collective-permute-start.5 = (bf16[64,1024]{1,0:T(8,128)(2,1)S(1)}, bf16[64,1024]{1,0:T(8,128)(2,1)S(1)}, u32[]{:S(2)}, u32[]{:S(2)}) collective-permute-start(bf16[64,1024]{1,0:T(8,128)(2,1)S(1)} %bitcast.74), channel_id=1, source_target_pairs={{0,16},{4,20},{8,24},{12,28},{16,0},{20,4},{24,8},{28,12},{1,17},{... | collective-permute-start | bytes 393224 | tf_op jit(solution)/shard_map/ppermute | solution.py:291
  21.4 2.1 %collective-permute-done.6 = bf16[64,1024]{1,0:T(8,128)(2,1)S(1)} collective-permute-done((bf16[64,1024]{1,0:T(8,128)(2,1)S(1)}, bf16[64,1024]{1,0:T(8,128)(2,1)S(1)}, u32[]{:S(2)}, u32[]{:S(2)}) %collective-permute-start.6) | collective-permute-done | bytes 131104 | tf_op jit(solution)/shard_map/ppermute | solution.py:291
  23.6 3.3 %collective-permute-done.5 = bf16[64,1024]{1,0:T(8,128)(2,1)S(1)} collective-permute-done((bf16[64,1024]{1,0:T(8,128)(2,1)S(1)}, bf16[64,1024]{1,0:T(8,128)(2,1)S(1)}, u32[]{:S(2)}, u32[]{:S(2)}) %collective-permute-start.5) | collective-permute-done | bytes 131104 | tf_op jit(solution)/shard_map/ppermute | solution.py:291
  26.9 0.6 collective-permute-start.7
  27.5 0.6 collective-permute-start.9
  28.2 2.5 %collective-permute-start.12 = (bf16[2,16,1024]{2,1,0:T(8,128)(2,1)S(1)}, bf16[2,16,1024]{2,1,0:T(8,128)(2,1)S(1)}, u32[]{:S(2)}, u32[]{:S(2)}) collective-permute-start(bf16[2,16,1024]{2,1,0:T(8,128)(2,1)S(1)} %get-tuple-element.62), channel_id=1, source_target_pairs={{0,24},{4,28},{8,16},{12,20},{16,8},{20,12},{24,0},{28,4},{1,25},{... | collective-permute-start | bytes 196616 | tf_op jit(solution)/shard_map/ppermute | solution.py:291
  30.7 2.0 %collective-permute-start.11 = (bf16[2,16,1024]{2,1,0:T(8,128)(2,1)S(1)}, bf16[2,16,1024]{2,1,0:T(8,128)(2,1)S(1)}, u32[]{:S(2)}, u32[]{:S(2)}) collective-permute-start(bf16[2,16,1024]{2,1,0:T(8,128)(2,1)S(1)} %get-tuple-element.39), channel_id=1, source_target_pairs={{0,16},{4,20},{8,24},{12,28},{16,0},{20,4},{24,8},{28,12},{1,17},{... | collective-permute-start | bytes 196616 | tf_op jit(solution)/shard_map/ppermute | solution.py:291
  32.6 0.7 %collective-permute-done.7.refs_1_ = bf16[2,64,1024]{2,1,0:T(8,128)(2,1)S(1)} collective-permute-done((bf16[2,64,1024]{2,1,0:T(8,128)(2,1)S(1)}, bf16[2,64,1024]{2,1,0:T(8,128)(2,1)S(1)}, u32[]{:S(2)}, u32[]{:S(2)}) %collective-permute-start.7) | collective-permute-done | bytes 262176 | tf_op jit(solution)/shard_map/ppermute | solution.py:291
  33.4 2.8 %input_parts.1 = (f32[64,1024]{1,0:T(8,128)S(1)}, bf16[64,1024]{1,0:T(8,128)(2,1)S(1)}, bf16[64,1024]{1,0:T(8,128)(2,1)S(1)}) custom-call(s32[2]{0:T(128)S(1)} %pad_add_fusion.index, bf16[2,64,1024]{2,1,0:T(8,128)(2,1)S(1)} %pad_maximum_fusion.2.refs_0_, bf16[2,64,1024]{2,1,0:T(8,128)(2,1)S(1)} %collective-permute-done.7.refs_1_, ...), custom_call_target="tpu_custom_call" | custom-call | flops 905969664 | bytes 6291456 | tf_op jit(solution)/shard_map/input_parts/pallas_call | solution.py:134
  36.3 1.3 %collective-permute-start.13 = (bf16[8,16,1024]{2,1,0:T(8,128)(2,1)S(1)}, bf16[8,16,1024]{2,1,0:T(8,128)(2,1)S(1)}, u32[]{:S(2)}, u32[]{:S(2)}) collective-permute-start(bf16[8,16,1024]{2,1,0:T(8,128)(2,1)S(1)} %constant_dynamic-update-slice_fusion.refs_6_), channel_id=1, source_target_pairs={{0,2},{1,3},{2,0},{3,1},{4,6},{5,7},{6,4},{7,5},{8,10},{9,11},{10,... | collective-permute-start | bytes 786440 | tf_op jit(solution)/shard_map/ppermute | solution.py:291
  37.6 1.5 %collective-permute-start.14 = (bf16[64,1024]{1,0:T(8,128)(2,1)S(1)}, bf16[64,1024]{1,0:T(8,128)(2,1)S(1)}, u32[]{:S(2)}, u32[]{:S(2)}) collective-permute-start(bf16[64,1024]{1,0:T(8,128)(2,1)S(1)} %get-tuple-element.40), channel_id=1, source_target_pairs={{0,4},{4,0},{8,12},{12,8},{16,20},{20,16},{24,28},{28,24},{1,5},{5... | collective-permute-start | bytes 393224 | tf_op jit(solution)/shard_map/ppermute | solution.py:291
  39.2 1.9 %collective-permute-start.15 = (bf16[2,64,1024]{2,1,0:T(8,128)(2,1)S(1)}, bf16[2,64,1024]{2,1,0:T(8,128)(2,1)S(1)}, u32[]{:S(2)}, u32[]{:S(2)}) collective-permute-start(bf16[2,64,1024]{2,1,0:T(8,128)(2,1)S(1)} %pad_maximum_fusion), channel_id=1, source_target_pairs={{0,8},{4,12},{8,0},{12,4},{16,24},{20,28},{24,16},{28,20},{1,9},{5... | collective-permute-start | bytes 786440 | tf_op jit(solution)/shard_map/ppermute | solution.py:291
  41.1 1.5 %collective-permute-done.14 = bf16[64,1024]{1,0:T(8,128)(2,1)S(1)} collective-permute-done((bf16[64,1024]{1,0:T(8,128)(2,1)S(1)}, bf16[64,1024]{1,0:T(8,128)(2,1)S(1)}, u32[]{:S(2)}, u32[]{:S(2)}) %collective-permute-start.14) | collective-permute-done | bytes 131104 | tf_op jit(solution)/shard_map/ppermute | solution.py:291
  43.3 2.4 %collective-permute-done.15.refs_5_ = bf16[2,64,1024]{2,1,0:T(8,128)(2,1)S(1)} collective-permute-done((bf16[2,64,1024]{2,1,0:T(8,128)(2,1)S(1)}, bf16[2,64,1024]{2,1,0:T(8,128)(2,1)S(1)}, u32[]{:S(2)}, u32[]{:S(2)}) %collective-permute-start.15) | collective-permute-done | bytes 262176 | tf_op jit(solution)/shard_map/ppermute | solution.py:291
  45.7 4.5 %filter_block.1.refs_0_ = bf16[896,128]{1,0:T(8,128)(2,1)S(1)} custom-call(s32[2]{0:T(128)S(1)} %pad_add_fusion.1.index, bf16[1,64,1024]{2,1,0:T(8,128)(2,1)S(1)} %bitcast.75, bf16[1,64,1024]{2,1,0:T(8,128)(2,1)S(1)} %bitcast.76, bf16[1,64,1024]{2,1,0:T(8,128)(2,1)S(1)} %bitcast.67, bf16[1,64,1024]{2,1,0:T(8,128)(2,1)S(1)} %bitcast.69, ...), custom_call_target="tpu_custom_call" | custom-call | flops 1811939328 | bytes 8388608 | tf_op jit(solution)/shard_map/filter_block/pallas_call | solution.py:212
  50.2 0.8 %collective-permute-start.18 = (bf16[64,1024]{1,0:T(8,128)(2,1)S(1)}, bf16[64,1024]{1,0:T(8,128)(2,1)S(1)}, u32[]{:S(2)}, u32[]{:S(2)}) collective-permute-start(bf16[64,1024]{1,0:T(8,128)(2,1)S(1)} %get-tuple-element.46), channel_id=1, source_target_pairs={{4,8},{12,16},{20,24},{8,4},{16,12},{24,20},{5,9},{13,17},{21,25},... | collective-permute-start | bytes 393224 | tf_op jit(solution)/shard_map/ppermute | solution.py:296
  51.0 1.0 %copy.21 = f32[64,1,1024]{2,1,0:T(1,128)} copy(f32[64,1,1024]{2,0,1:T(8,128)S(1)} %get-tuple-element.59) | data formatting | bytes 524288
  51.9 4.4 %collective-permute-start.21 = (bf16[896,128]{1,0:T(8,128)(2,1)S(1)}, bf16[896,128]{1,0:T(8,128)(2,1)S(1)}, u32[]{:S(2)}, u32[]{:S(2)}) collective-permute-start(bf16[896,128]{1,0:T(8,128)(2,1)S(1)} %filter_block.1.refs_0_), channel_id=1, source_target_pairs={{0,12},{4,8},{8,4},{12,0},{16,28},{20,24},{24,20},{28,16},{1,13},{... | collective-permute-start | bytes 688136 | tf_op jit(solution)/shard_map/ppermute | solution.py:291
  56.4 1.6 %collective-permute-start.20 = (bf16[896,128]{1,0:T(8,128)(2,1)S(1)}, bf16[896,128]{1,0:T(8,128)(2,1)S(1)}, u32[]{:S(2)}, u32[]{:S(2)}) collective-permute-start(bf16[896,128]{1,0:T(8,128)(2,1)S(1)} %filter_block.1.refs_0_), channel_id=1, source_target_pairs={{0,8},{4,12},{8,0},{12,4},{16,24},{20,28},{24,16},{28,20},{1,9},{5... | collective-permute-start | bytes 688136 | tf_op jit(solution)/shard_map/ppermute | solution.py:291
  58.0 1.0 %copy.22 = f32[64,1,1024]{2,1,0:T(1,128)} copy(f32[64,1,1024]{2,0,1:T(8,128)S(1)} %add_bitcast_fusion) | data formatting | bytes 524288
  59.0 4.6 %collective-permute-done.21.refs_3_ = bf16[896,128]{1,0:T(8,128)(2,1)S(1)} collective-permute-done((bf16[896,128]{1,0:T(8,128)(2,1)S(1)}, bf16[896,128]{1,0:T(8,128)(2,1)S(1)}, u32[]{:S(2)}, u32[]{:S(2)}) %collective-permute-start.21) | collective-permute-done | bytes 229408 | tf_op jit(solution)/shard_map/ppermute | solution.py:291
  63.5 3.9 %collective-permute-done.20.refs_2_ = bf16[896,128]{1,0:T(8,128)(2,1)S(1)} collective-permute-done((bf16[896,128]{1,0:T(8,128)(2,1)S(1)}, bf16[896,128]{1,0:T(8,128)(2,1)S(1)}, u32[]{:S(2)}, u32[]{:S(2)}) %collective-permute-start.20) | collective-permute-done | bytes 229408 | tf_op jit(solution)/shard_map/ppermute | solution.py:291
  67.4 2.2 %join_blocks.1 = (f32[27,64,256]{2,1,0:T(8,128)}, f32[1,256]{1,0:T(1,128)}) custom-call(s32[1]{0:T(128)} %bitcast.28.index, bf16[896,128]{1,0:T(8,128)(2,1)S(1)} %filter_block.1.refs_0_, bf16[896,128]{1,0:T(8,128)(2,1)S(1)} %collective-permute-done.19.refs_1_, bf16[896,128]{1,0:T(8,128)(2,1)S(1)} %collective-permute-done.20.refs_2_, ...), custom_call_target="tpu_custom_call" | custom-call | flops 452984832 | bytes 4194304 | tf_op jit(solution)/shard_map/join_blocks/pallas_call | solution.py:268
  (50 shorter events, 2.6 us)
Async XLA Ops:
  0.6 5.0 %copy-start = (bf16[27,64,256]{2,1,0:T(8,128)(2,1)S(1)}, bf16[27,64,256]{2,1,0:T(8,128)(2,1)}, u32[]{:S(2)}) copy-start(bf16[27,64,256]{2,1,0:T(8,128)(2,1)} %refs_2_.1) | copy-start | bytes 2654212
  0.6 6.7 %collective-permute-start = (bf16[64,1024]{1,0:T(8,128)(2,1)}, bf16[64,1024]{1,0:T(8,128)(2,1)S(1)}, u32[]{:S(2)}, u32[]{:S(2)}) collective-permute-start(bf16[64,1024]{1,0:T(8,128)(2,1)} %bitcast.70), channel_id=1, source_target_pairs={{0,4},{4,0},{8,12},{12,8},{16,20},{20,16},{24,28},{28,24},{1,5},{5... | collective-permute-start | bytes 393224 | tf_op jit(solution)/shard_map/ppermute | solution.py:291
  3.7 4.7 %collective-permute-start.1 = (bf16[64,1024]{1,0:T(8,128)(2,1)}, bf16[64,1024]{1,0:T(8,128)(2,1)S(1)}, u32[]{:S(2)}, u32[]{:S(2)}) collective-permute-start(bf16[64,1024]{1,0:T(8,128)(2,1)} %bitcast.71), channel_id=1, source_target_pairs={{4,8},{12,16},{20,24},{8,4},{16,12},{24,20},{5,9},{13,17},{21,25},... | collective-permute-start | bytes 393224 | tf_op jit(solution)/shard_map/ppermute | solution.py:296
  5.7 1.7 %copy-start.1 = (bf16[64,1,1024]{2,0,1:T(8,128)(2,1)S(1)}, bf16[64,1,1024]{2,0,1:T(8,128)(2,1)}, u32[]{:S(2)}) copy-start(bf16[64,1,1024]{2,0,1:T(8,128)(2,1)} %param.5) | copy-start | bytes 393220
  8.4 12.4 %copy-start.3 = (bf16[64,1,1024]{2,0,1:T(8,128)(2,1)S(1)}, bf16[64,1,1024]{2,0,1:T(8,128)(2,1)}, u32[]{:S(2)}) copy-start(bf16[64,1,1024]{2,0,1:T(8,128)(2,1)} %param.8) | copy-start | bytes 393220
  8.4 12.4 %copy-start.4 = (f32[64]{0:T(128)S(1)}, f32[64]{0:T(128)}, u32[]{:S(2)}) copy-start(f32[64]{0:T(128)} %param.7) | copy-start | bytes 772
  9.7 2.0 %collective-permute-start.2 = (f32[2,64,1024]{2,1,0:T(8,128)S(1)}, f32[2,64,1024]{2,1,0:T(8,128)S(1)}, u32[]{:S(2)}, u32[]{:S(2)}) collective-permute-start(f32[2,64,1024]{2,1,0:T(8,128)S(1)} %get-tuple-element.30), channel_id=1, source_target_pairs={{0,1},{1,0},{2,3},{3,2},{4,5},{5,4},{6,7},{7,6},{8,9},{9,8},{10,11... | collective-permute-start | bytes 1572872 | tf_op jit(solution)/shard_map/ppermute | solution.py:291
  11.7 9.0 %collective-permute-start.3 = (bf16[64,1024]{1,0:T(8,128)(2,1)S(1)}, bf16[64,1024]{1,0:T(8,128)(2,1)S(1)}, u32[]{:S(2)}, u32[]{:S(2)}) collective-permute-start(bf16[64,1024]{1,0:T(8,128)(2,1)S(1)} %fusion.6), channel_id=1, source_target_pairs={{0,2},{1,3},{2,0},{3,1},{4,6},{5,7},{6,4},{7,5},{8,10},{9,11},{10,... | collective-permute-start | bytes 393224 | tf_op jit(solution)/shard_map/ppermute | solution.py:291
  13.6 10.0 %collective-permute-start.6 = (bf16[64,1024]{1,0:T(8,128)(2,1)S(1)}, bf16[64,1024]{1,0:T(8,128)(2,1)S(1)}, u32[]{:S(2)}, u32[]{:S(2)}) collective-permute-start(bf16[64,1024]{1,0:T(8,128)(2,1)S(1)} %bitcast.73), channel_id=1, source_target_pairs={{0,8},{4,12},{8,0},{12,4},{16,24},{20,28},{24,16},{28,20},{1,9},{5... | collective-permute-start | bytes 393224 | tf_op jit(solution)/shard_map/ppermute | solution.py:291
  18.2 8.7 %collective-permute-start.5 = (bf16[64,1024]{1,0:T(8,128)(2,1)S(1)}, bf16[64,1024]{1,0:T(8,128)(2,1)S(1)}, u32[]{:S(2)}, u32[]{:S(2)}) collective-permute-start(bf16[64,1024]{1,0:T(8,128)(2,1)S(1)} %bitcast.74), channel_id=1, source_target_pairs={{0,16},{4,20},{8,24},{12,28},{16,0},{20,4},{24,8},{28,12},{1,17},{... | collective-permute-start | bytes 393224 | tf_op jit(solution)/shard_map/ppermute | solution.py:291
  21.0 5.9 %collective-permute-start.4 = (bf16[64,1024]{1,0:T(8,128)(2,1)S(1)}, bf16[64,1024]{1,0:T(8,128)(2,1)S(1)}, u32[]{:S(2)}, u32[]{:S(2)}) collective-permute-start(bf16[64,1024]{1,0:T(8,128)(2,1)S(1)} %get-tuple-element.31), channel_id=1, source_target_pairs={{0,1},{1,0},{2,3},{3,2},{4,5},{5,4},{6,7},{7,6},{8,9},{9,8},{10,11... | collective-permute-start | bytes 393224 | tf_op jit(solution)/shard_map/ppermute | solution.py:291
  21.1 7.1 %collective-permute-start.8 = (bf16[2,16,1024]{2,1,0:T(8,128)(2,1)S(1)}, bf16[2,16,1024]{2,1,0:T(8,128)(2,1)S(1)}, u32[]{:S(2)}, u32[]{:S(2)}) collective-permute-start(bf16[2,16,1024]{2,1,0:T(8,128)(2,1)S(1)} %get-tuple-element.34), channel_id=1, source_target_pairs={{0,4},{4,0},{8,12},{12,8},{16,20},{20,16},{24,28},{28,24},{1,5},{5... | collective-permute-start | bytes 196616 | tf_op jit(solution)/shard_map/ppermute | solution.py:291
  26.9 6.4 %collective-permute-start.7 = (bf16[2,64,1024]{2,1,0:T(8,128)(2,1)S(1)}, bf16[2,64,1024]{2,1,0:T(8,128)(2,1)S(1)}, u32[]{:S(2)}, u32[]{:S(2)}) collective-permute-start(bf16[2,64,1024]{2,1,0:T(8,128)(2,1)S(1)} %pad_maximum_fusion.2.refs_0_), channel_id=1, source_target_pairs={{0,2},{1,3},{2,0},{3,1},{4,6},{5,7},{6,4},{7,5},{8,10},{9,11},{10,... | collective-permute-start | bytes 786440 | tf_op jit(solution)/shard_map/ppermute | solution.py:291
  27.5 8.6 %collective-permute-start.9 = (bf16[2,64,1024]{2,1,0:T(8,128)(2,1)S(1)}, bf16[2,64,1024]{2,1,0:T(8,128)(2,1)S(1)}, u32[]{:S(2)}, u32[]{:S(2)}) collective-permute-start(bf16[2,64,1024]{2,1,0:T(8,128)(2,1)S(1)} %pad_maximum_fusion.1), channel_id=1, source_target_pairs={{0,4},{4,0},{8,12},{12,8},{16,20},{20,16},{24,28},{28,24},{1,5},{5... | collective-permute-start | bytes 786440 | tf_op jit(solution)/shard_map/ppermute | solution.py:291
  28.2 8.1 %collective-permute-start.12 = (bf16[2,16,1024]{2,1,0:T(8,128)(2,1)S(1)}, bf16[2,16,1024]{2,1,0:T(8,128)(2,1)S(1)}, u32[]{:S(2)}, u32[]{:S(2)}) collective-permute-start(bf16[2,16,1024]{2,1,0:T(8,128)(2,1)S(1)} %get-tuple-element.62), channel_id=1, source_target_pairs={{0,24},{4,28},{8,16},{12,20},{16,8},{20,12},{24,0},{28,4},{1,25},{... | collective-permute-start | bytes 196616 | tf_op jit(solution)/shard_map/ppermute | solution.py:291
  30.7 5.5 %collective-permute-start.10 = (bf16[2,16,1024]{2,1,0:T(8,128)(2,1)S(1)}, bf16[2,16,1024]{2,1,0:T(8,128)(2,1)S(1)}, u32[]{:S(2)}, u32[]{:S(2)}) collective-permute-start(bf16[2,16,1024]{2,1,0:T(8,128)(2,1)S(1)} %get-tuple-element.62), channel_id=1, source_target_pairs={{0,8},{4,12},{8,0},{12,4},{16,24},{20,28},{24,16},{28,20},{1,9},{5... | collective-permute-start | bytes 196616 | tf_op jit(solution)/shard_map/ppermute | solution.py:291
  30.7 5.6 %collective-permute-start.11 = (bf16[2,16,1024]{2,1,0:T(8,128)(2,1)S(1)}, bf16[2,16,1024]{2,1,0:T(8,128)(2,1)S(1)}, u32[]{:S(2)}, u32[]{:S(2)}) collective-permute-start(bf16[2,16,1024]{2,1,0:T(8,128)(2,1)S(1)} %get-tuple-element.39), channel_id=1, source_target_pairs={{0,16},{4,20},{8,24},{12,28},{16,0},{20,4},{24,8},{28,12},{1,17},{... | collective-permute-start | bytes 196616 | tf_op jit(solution)/shard_map/ppermute | solution.py:291
  36.3 6.4 %collective-permute-start.13 = (bf16[8,16,1024]{2,1,0:T(8,128)(2,1)S(1)}, bf16[8,16,1024]{2,1,0:T(8,128)(2,1)S(1)}, u32[]{:S(2)}, u32[]{:S(2)}) collective-permute-start(bf16[8,16,1024]{2,1,0:T(8,128)(2,1)S(1)} %constant_dynamic-update-slice_fusion.refs_6_), channel_id=1, source_target_pairs={{0,2},{1,3},{2,0},{3,1},{4,6},{5,7},{6,4},{7,5},{8,10},{9,11},{10,... | collective-permute-start | bytes 786440 | tf_op jit(solution)/shard_map/ppermute | solution.py:291
  37.6 5.0 %collective-permute-start.14 = (bf16[64,1024]{1,0:T(8,128)(2,1)S(1)}, bf16[64,1024]{1,0:T(8,128)(2,1)S(1)}, u32[]{:S(2)}, u32[]{:S(2)}) collective-permute-start(bf16[64,1024]{1,0:T(8,128)(2,1)S(1)} %get-tuple-element.40), channel_id=1, source_target_pairs={{0,4},{4,0},{8,12},{12,8},{16,20},{20,16},{24,28},{28,24},{1,5},{5... | collective-permute-start | bytes 393224 | tf_op jit(solution)/shard_map/ppermute | solution.py:291
  39.2 6.4 %collective-permute-start.15 = (bf16[2,64,1024]{2,1,0:T(8,128)(2,1)S(1)}, bf16[2,64,1024]{2,1,0:T(8,128)(2,1)S(1)}, u32[]{:S(2)}, u32[]{:S(2)}) collective-permute-start(bf16[2,64,1024]{2,1,0:T(8,128)(2,1)S(1)} %pad_maximum_fusion), channel_id=1, source_target_pairs={{0,8},{4,12},{8,0},{12,4},{16,24},{20,28},{24,16},{28,20},{1,9},{5... | collective-permute-start | bytes 786440 | tf_op jit(solution)/shard_map/ppermute | solution.py:291
  42.7 2.9 %collective-permute-start.16 = (bf16[8,16,1024]{2,1,0:T(8,128)(2,1)S(1)}, bf16[8,16,1024]{2,1,0:T(8,128)(2,1)S(1)}, u32[]{:S(2)}, u32[]{:S(2)}) collective-permute-start(bf16[8,16,1024]{2,1,0:T(8,128)(2,1)S(1)} %constant_dynamic-update-slice_fusion.refs_6_), channel_id=1, source_target_pairs={{0,1},{1,0},{2,3},{3,2},{4,5},{5,4},{6,7},{7,6},{8,9},{9,8},{10,11... | collective-permute-start | bytes 786440 | tf_op jit(solution)/shard_map/ppermute | solution.py:291
  42.7 2.9 %collective-permute-start.17 = (bf16[8,16,1024]{2,1,0:T(8,128)(2,1)S(1)}, bf16[8,16,1024]{2,1,0:T(8,128)(2,1)S(1)}, u32[]{:S(2)}, u32[]{:S(2)}) collective-permute-start(bf16[8,16,1024]{2,1,0:T(8,128)(2,1)S(1)} %collective-permute-done.13.refs_8_), channel_id=1, source_target_pairs={{0,1},{1,0},{2,3},{3,2},{4,5},{5,4},{6,7},{7,6},{8,9},{9,8},{10,11... | collective-permute-start | bytes 786440 | tf_op jit(solution)/shard_map/ppermute | solution.py:291
  50.2 17.3 %copy-start.2 = (bf16[512,512]{1,0:T(8,128)(2,1)S(1)}, bf16[512,512]{1,0:T(8,128)(2,1)}, u32[]{:S(2)}) copy-start(bf16[512,512]{1,0:T(8,128)(2,1)} %constant.21.clone.refs_4_) | copy-start | bytes 1572868
  50.2 7.8 %collective-permute-start.18 = (bf16[64,1024]{1,0:T(8,128)(2,1)S(1)}, bf16[64,1024]{1,0:T(8,128)(2,1)S(1)}, u32[]{:S(2)}, u32[]{:S(2)}) collective-permute-start(bf16[64,1024]{1,0:T(8,128)(2,1)S(1)} %get-tuple-element.46), channel_id=1, source_target_pairs={{4,8},{12,16},{20,24},{8,4},{16,12},{24,20},{5,9},{13,17},{21,25},... | collective-permute-start | bytes 393224 | tf_op jit(solution)/shard_map/ppermute | solution.py:296
  51.9 11.6 %collective-permute-start.21 = (bf16[896,128]{1,0:T(8,128)(2,1)S(1)}, bf16[896,128]{1,0:T(8,128)(2,1)S(1)}, u32[]{:S(2)}, u32[]{:S(2)}) collective-permute-start(bf16[896,128]{1,0:T(8,128)(2,1)S(1)} %filter_block.1.refs_0_), channel_id=1, source_target_pairs={{0,12},{4,8},{8,4},{12,0},{16,28},{20,24},{24,20},{28,16},{1,13},{... | collective-permute-start | bytes 688136 | tf_op jit(solution)/shard_map/ppermute | solution.py:291
  56.4 11.1 %collective-permute-start.20 = (bf16[896,128]{1,0:T(8,128)(2,1)S(1)}, bf16[896,128]{1,0:T(8,128)(2,1)S(1)}, u32[]{:S(2)}, u32[]{:S(2)}) collective-permute-start(bf16[896,128]{1,0:T(8,128)(2,1)S(1)} %filter_block.1.refs_0_), channel_id=1, source_target_pairs={{0,8},{4,12},{8,0},{12,4},{16,24},{20,28},{24,16},{28,20},{1,9},{5... | collective-permute-start | bytes 688136 | tf_op jit(solution)/shard_map/ppermute | solution.py:291
  57.9 9.5 %collective-permute-start.19 = (bf16[896,128]{1,0:T(8,128)(2,1)S(1)}, bf16[896,128]{1,0:T(8,128)(2,1)S(1)}, u32[]{:S(2)}, u32[]{:S(2)}) collective-permute-start(bf16[896,128]{1,0:T(8,128)(2,1)S(1)} %filter_block.1.refs_0_), channel_id=1, source_target_pairs={{0,4},{4,0},{8,12},{12,8},{16,20},{20,16},{24,28},{28,24},{1,5},{5... | collective-permute-start | bytes 688136 | tf_op jit(solution)/shard_map/ppermute | solution.py:291
